TPU v7x, 32 devices: a whole 2x2x4 slice. The times are simulated.
32 devices in a mesh: dp: 4 (over y, x), expert: 8 (over z, core).
Axes of the slice: x: 2, y: 2, z: 4, core: 2. Of those that a mesh axis runs over, the one named last changes fastest.
Arguments:
- tokens: bfloat16 [8704, 2048], P(('dp', 'expert')), may hold values from -6 to 6
- teacher: bfloat16 [8704, 2048], P(('dp', 'expert')), may hold values from -6 to 6
- att_routes: int32 [8704, 2], P(('dp', 'expert')), may hold values from 0 to 7, all different within a row; in each aligned block of 272 rows (0 to 271, 272 to 543, ...) at most 88 rows name the same one
- ffn_routes: int32 [8704, 2], P(('dp', 'expert')), may hold values from 0 to 3, all different within a row; in each aligned block of 272 rows (0 to 271, 272 to 543, ...) at most 176 rows name the same one
- parent: int32 [4, 13], P('dp'), may hold values from 0 to 4, as said below
- valid: int32 [4], replicated, may hold values from 1632 to 2176
- gain_one: float32 [2048], replicated, may hold values from 0.5 to 1.5
- kv_weight: bfloat16 [2048, 4096], P('expert'), may hold values from -0.125 to 0.125
- att_router: float32 [2048, 8], replicated, may hold values from -0.125 to 0.125
- q_weight: bfloat16 [2048, 16384], P(None, 'expert'), may hold values from -0.125 to 0.125
- o_weight: bfloat16 [2048, 16384], P(None, 'expert'), may hold values from -1 to 1
- gain_two: float32 [2048], replicated, may hold values from 0.5 to 1.5
- ffn_router: float32 [2048, 4], replicated, may hold values from -0.125 to 0.125
- gate_weight: bfloat16 [2048, 22528], P(None, 'expert'), may hold values from -0.125 to 0.125
- up_weight: bfloat16 [2048, 22528], P(None, 'expert'), may hold values from -0.125 to 0.125
- down_weight: bfloat16 [2048, 22528], P(None, 'expert'), may hold values from -0.078125 to 0.078125
Outputs:
- output: bfloat16 [8704, 2048], P(('dp', 'expert'))
- grad_input: bfloat16 [8704, 2048], P(('dp', 'expert'))
- grad_gain_one: float32 [2048], P(('dp', 'expert'))
- grad_kv_weight: float32 [2048, 4096], P(('dp', 'expert'))
- grad_att_router: float32 [2048, 8], P(('dp', 'expert'))
- grad_q_weight: float32 [2048, 16384], P('dp', 'expert')
- grad_o_weight: float32 [2048, 16384], P('dp', 'expert')
- grad_gain_two: float32 [2048], P(('dp', 'expert'))
- grad_ffn_router: float32 [2048, 4], P(('dp', 'expert'))
- grad_gate_weight: float32 [2048, 22528], P('dp', 'expert')
- grad_up_weight: float32 [2048, 22528], P('dp', 'expert')
- grad_down_weight: float32 [2048, 22528], P('dp', 'expert')
Inputs may be any that keep to these rules, and one draw needn't show every extreme that they name: `att_routes`: in the rows of one device no attention expert is named by more than 88 rows; a row's two experts differ. `ffn_routes`: in the rows of one device no feed-forward expert is named by more than 176 rows; a row's two experts differ. segment 0 is the trunk, 1 to 4 the branches, 5 to 12 the leaves; trunk and branches have parent 0; each branch is the parent of exactly two leaves. `valid`: tokens of a tree at places below its count enter the loss.
All inputs are finite; a program needn't handle non-finite values.
Results may differ from a plain program's by a relative error of at most 0.015.
Values may be sent and summed in bfloat16 or wider, within the bound.
A program may use at most 384 MiB of HBM per device.

v0:
```python
import jax
import jax.numpy as jnp
from jax import lax
from jax.sharding import PartitionSpec as P

D = 2048
HEADS = 16
HEAD = 128
ATT_EXPERTS = 8
FFN_EXPERTS = 4
TRUNK = 1024
SEG = 96
TREE_LEN = 2176


epsilon = 1e-06
highest = lax.Precision.HIGHEST


def tree_layout(places):
    after_trunk = places - TRUNK
    after_branch = after_trunk - 4 * SEG
    segments = jnp.where(
        places < TRUNK,
        0,
        jnp.where(after_branch < 0, 1 + after_trunk // SEG, 5 + after_branch // SEG),
    )
    depths = jnp.where(
        places < TRUNK,
        places,
        jnp.where(after_branch < 0, TRUNK + after_trunk % SEG, TRUNK + SEG + after_branch % SEG),
    )
    return (segments.astype(jnp.int32), depths.astype(jnp.int32))


def rotate(values, depths, direction):
    half_size = values.shape[-1] // 2
    frequency = 10000.0 ** (-jnp.arange(half_size, dtype=jnp.float32) * 2.0 / values.shape[-1])
    angles = depths.astype(jnp.float32)[:, None] * frequency[None, :]
    cosine = jnp.cos(angles)[:, None, :]
    sine = jnp.sin(angles)[:, None, :] * direction
    first = values[..., :half_size]
    second = values[..., half_size:]
    return jnp.concatenate(
        [first * cosine - second * sine, second * cosine + first * sine], axis=-1
    )


def ancestor_mask(parent, query_places, key_places):
    tree_count = parent.shape[0]
    nodes = jnp.arange(13, dtype=jnp.int32)
    grand = jnp.sum(
        jnp.where(parent[:, :, None] == nodes[None, None, :], parent[:, None, :], 0), axis=2
    )
    related = (
        (nodes[None, None, :] == nodes[None, :, None])
        | (nodes[None, None, :] == parent[:, :, None])
        | (nodes[None, None, :] == grand[:, :, None])
    )
    same_tree = jnp.eye(tree_count, dtype=bool)
    table = (
        (same_tree[:, None, :, None] & related[:, :, None, :])
        .reshape(tree_count * 13, tree_count * 13)
        .astype(jnp.float32)
    )
    query_segment, unused_one = tree_layout(query_places % TREE_LEN)
    key_segment, unused_two = tree_layout(key_places % TREE_LEN)
    query_label = query_places // TREE_LEN * 13 + query_segment
    key_label = key_places // TREE_LEN * 13 + key_segment
    labels = jnp.arange(tree_count * 13, dtype=jnp.int32)
    query_onehot = (query_label[:, None] == labels[None, :]).astype(jnp.float32)
    key_onehot = (key_label[:, None] == labels[None, :]).astype(jnp.float32)
    reach = jnp.dot(jnp.dot(query_onehot, table), key_onehot.T)
    return (reach > 0.5) & (key_places[None, :] <= query_places[:, None])


def dispatch_plan(routes, experts, capacity):
    labels = jnp.arange(experts, dtype=jnp.int32)
    first = routes[:, 0:1] == labels[None, :]
    second = routes[:, 1:2] == labels[None, :]
    chosen = (first | second).astype(jnp.int32)
    ranking = jnp.cumsum(chosen, axis=0) - 1
    slot_ids = jnp.arange(capacity, dtype=jnp.int32)
    plan = (chosen.T[:, None, :] == 1) & (ranking.T[:, None, :] == slot_ids[None, :, None])
    return (plan, first.astype(jnp.float32), second.astype(jnp.float32))


def gate_values(hidden, router, first, second):
    logits = jnp.dot(hidden.astype(jnp.float32), router, precision=highest)
    picked = jnp.stack([jnp.sum(logits * first, axis=1), jnp.sum(logits * second, axis=1)], axis=1)
    gates = jax.nn.softmax(picked, axis=1)
    return (gates, gates[:, 0:1] * first + gates[:, 1:2] * second)


def router_grads(hidden, router, gates, first, second, weight_grad):
    picked_grad = jnp.stack(
        [jnp.sum(weight_grad * first, axis=1), jnp.sum(weight_grad * second, axis=1)], axis=1
    )
    logit_pick = gates * (picked_grad - jnp.sum(gates * picked_grad, axis=1, keepdims=True))
    logit_grad = logit_pick[:, 0:1] * first + logit_pick[:, 1:2] * second
    router_grad = jnp.dot(hidden.astype(jnp.float32).T, logit_grad, precision=highest)
    hidden_grad = jnp.dot(logit_grad, router.T, precision=highest)
    return (router_grad, hidden_grad)


def pack_rows(plan, hidden, copies):
    filled = jnp.einsum(
        "ecr,rd->ecd", plan.astype(jnp.bfloat16), hidden, preferred_element_type=jnp.float32
    ).astype(jnp.bfloat16)
    return jnp.repeat(filled, copies, axis=0)


def slot_places(plan, places):
    return jnp.sum(jnp.where(plan, places[None, None, :], 0), axis=2)


def combine_rows(plan_float, weights, slots):
    mixing = plan_float * weights.T[:, None, :]
    return jnp.einsum("ecr,ecd->rd", mixing, slots, precision=highest)


def rms_parts(values):
    inverse = lax.rsqrt(jnp.mean(values * values, axis=-1, keepdims=True) + epsilon)
    return (values * inverse, inverse)


def norm_back(grad_normed, normed, inverse):
    return inverse * (grad_normed - normed * jnp.mean(grad_normed * normed, axis=-1, keepdims=True))


def expert_backward_slots(plan_float, weights, slot_outputs, upstream, copies):
    upstream_slots = jnp.einsum("ecr,rd->ecd", plan_float, upstream, precision=highest)
    weight_grad = jnp.einsum(
        "ecr,ec->re", plan_float, jnp.sum(upstream_slots * slot_outputs, axis=2), precision=highest
    )
    slot_gate = jnp.einsum("ecr,re->ec", plan_float, weights, precision=highest)
    sending = jnp.repeat(
        (upstream_slots * slot_gate[:, :, None]).astype(jnp.bfloat16), copies, axis=0
    )
    return (sending, weight_grad)


def body(
    tokens,
    teacher,
    att_routes,
    ffn_routes,
    parent,
    valid,
    gain_one,
    kv_weight,
    att_router,
    q_weight,
    o_weight,
    gain_two,
    ffn_router,
    gate_weight,
    up_weight,
    down_weight,
):
    row_count = tokens.shape[0]
    devices = lax.axis_size("expert")
    my_index = lax.axis_index("expert")
    att_copies = devices // ATT_EXPERTS
    ffn_copies = devices // FFN_EXPERTS
    att_capacity = row_count * 13 // 40
    ffn_capacity = row_count * 13 // 20
    group_rows = row_count * devices
    heads_local = q_weight.shape[1] // HEAD
    width = HEADS * HEAD
    score_scale = HEAD ** (-0.5)
    own_places = my_index * row_count + jnp.arange(row_count, dtype=jnp.int32)
    unused_segment, own_depths = tree_layout(own_places % TREE_LEN)
    x_in = tokens.astype(jnp.float32)
    normed_one, inverse_one = rms_parts(x_in)
    hidden = (normed_one * gain_one).astype(jnp.bfloat16)
    kv_full = lax.all_gather(kv_weight, "expert", axis=0, tiled=True)
    kv_rows = jnp.dot(hidden, kv_full, preferred_element_type=jnp.float32)
    key_rows = rotate(kv_rows[:, :width].reshape(row_count, HEADS, HEAD), own_depths, 1.0).astype(
        jnp.bfloat16
    )
    value_rows = kv_rows[:, width:].reshape(row_count, HEADS, HEAD).astype(jnp.bfloat16)
    kv_heads = jnp.concatenate([key_rows, value_rows], axis=1).transpose(1, 0, 2)
    kv_group = lax.all_gather(kv_heads, "expert", axis=1, tiled=True)
    att_plan, att_first, att_second = dispatch_plan(att_routes, ATT_EXPERTS, att_capacity)
    att_plan_float = att_plan.astype(jnp.float32)
    att_gates, att_weights = gate_values(hidden, att_router, att_first, att_second)
    send_rows = pack_rows(att_plan, hidden, att_copies)
    send_places = jnp.repeat(slot_places(att_plan, own_places), att_copies, axis=0)
    recv_rows, recv_places = (
        lax.all_to_all(send_rows, "expert", split_axis=0, concat_axis=0, tiled=True),
        lax.all_to_all(send_places, "expert", split_axis=0, concat_axis=0, tiled=True),
    )
    query_inputs = recv_rows.reshape(-1, D)
    query_places = recv_places.reshape(-1)
    head_start = my_index % att_copies * heads_local
    key_heads = lax.dynamic_slice_in_dim(kv_group, head_start, heads_local, 0)
    value_heads = lax.dynamic_slice_in_dim(kv_group, HEADS + head_start, heads_local, 0)
    allowed = ancestor_mask(parent, query_places, jnp.arange(group_rows, dtype=jnp.int32))
    unused_query_segment, query_depths = tree_layout(query_places % TREE_LEN)
    query_pre = jnp.dot(query_inputs, q_weight, preferred_element_type=jnp.float32)
    queries = (
        rotate(query_pre.reshape(-1, heads_local, HEAD), query_depths, 1.0)
        .astype(jnp.bfloat16)
        .transpose(1, 0, 2)
    )

    def head_forward(item):
        query_head, key_head, value_head = item
        scores = jnp.where(
            allowed,
            jnp.dot(query_head, key_head.T, preferred_element_type=jnp.float32) * score_scale,
            -1e30,
        )
        highest_score = jnp.max(scores, axis=1, keepdims=True)
        exponent = jnp.exp(scores - highest_score)
        totals = jnp.sum(exponent, axis=1, keepdims=True)
        probs = (exponent / totals).astype(jnp.bfloat16)
        return (
            jnp.dot(probs, value_head, preferred_element_type=jnp.float32),
            highest_score,
            totals,
        )

    att_float, score_tops, score_totals = lax.map(head_forward, (queries, key_heads, value_heads))
    att_rows = att_float.transpose(1, 0, 2).reshape(-1, heads_local * HEAD).astype(jnp.bfloat16)
    att_partial = lax.dot_general(
        att_rows, o_weight, (((1,), (1,)), ((), ())), preferred_element_type=jnp.float32
    )
    att_back = lax.all_to_all(
        att_partial.reshape(devices, att_capacity, D),
        "expert",
        split_axis=0,
        concat_axis=0,
        tiled=True,
    )
    att_slots = att_back.reshape(ATT_EXPERTS, att_copies, att_capacity, D).sum(axis=1)
    x_mid = x_in + combine_rows(att_plan_float, att_weights, att_slots)
    normed_two, inverse_two = rms_parts(x_mid)
    hidden_two = (normed_two * gain_two).astype(jnp.bfloat16)
    ffn_plan, ffn_first, ffn_second = dispatch_plan(ffn_routes, FFN_EXPERTS, ffn_capacity)
    ffn_plan_float = ffn_plan.astype(jnp.float32)
    ffn_gates, ffn_weights = gate_values(hidden_two, ffn_router, ffn_first, ffn_second)
    ffn_send = pack_rows(ffn_plan, hidden_two, ffn_copies)
    ffn_inputs = lax.all_to_all(
        ffn_send, "expert", split_axis=0, concat_axis=0, tiled=True
    ).reshape(-1, D)
    gate_pre = jnp.dot(ffn_inputs, gate_weight, preferred_element_type=jnp.float32)
    up_pre = jnp.dot(ffn_inputs, up_weight, preferred_element_type=jnp.float32)
    sigmoid_gate = jax.nn.sigmoid(gate_pre)
    silu_gate = gate_pre * sigmoid_gate
    activated = (silu_gate * up_pre).astype(jnp.bfloat16)
    ffn_partial = lax.dot_general(
        activated, down_weight, (((1,), (1,)), ((), ())), preferred_element_type=jnp.float32
    )
    ffn_back = lax.all_to_all(
        ffn_partial.reshape(devices, ffn_capacity, D).astype(jnp.bfloat16),
        "expert",
        split_axis=0,
        concat_axis=0,
        tiled=True,
    ).astype(jnp.float32)
    ffn_slots = ffn_back.reshape(FFN_EXPERTS, ffn_copies, ffn_capacity, D).sum(axis=1)
    result = x_mid + combine_rows(ffn_plan_float, ffn_weights, ffn_slots)
    tree_local = own_places // TREE_LEN
    tree_global = lax.axis_index("dp") * parent.shape[0] + tree_local
    tree_labels = jnp.arange(valid.shape[0], dtype=jnp.int32)
    limits = jnp.sum(
        jnp.where(tree_global[:, None] == tree_labels[None, :], valid[None, :], 0), axis=1
    )
    counted = own_places % TREE_LEN < limits
    loss_factor = valid.shape[0] * TREE_LEN / jnp.sum(valid).astype(jnp.float32)
    grad_result = jnp.where(
        counted[:, None], (result - teacher.astype(jnp.float32)) * loss_factor, 0.0
    )
    ffn_grad_send, ffn_weight_grad = expert_backward_slots(
        ffn_plan_float, ffn_weights, ffn_slots, grad_result, ffn_copies
    )
    grad_ffn_out = lax.all_to_all(
        ffn_grad_send, "expert", split_axis=0, concat_axis=0, tiled=True
    ).reshape(-1, D)
    grad_down = lax.dot_general(
        grad_ffn_out, activated, (((0,), (0,)), ((), ())), preferred_element_type=jnp.float32
    )
    grad_activated = jnp.dot(grad_ffn_out, down_weight, preferred_element_type=jnp.float32)
    grad_gate_pre = (
        grad_activated * up_pre * sigmoid_gate * (1.0 + gate_pre * (1.0 - sigmoid_gate))
    ).astype(jnp.bfloat16)
    grad_up_pre = (grad_activated * silu_gate).astype(jnp.bfloat16)
    grad_gate = lax.dot_general(
        ffn_inputs, grad_gate_pre, (((0,), (0,)), ((), ())), preferred_element_type=jnp.float32
    )
    grad_up = lax.dot_general(
        ffn_inputs, grad_up_pre, (((0,), (0,)), ((), ())), preferred_element_type=jnp.float32
    )
    grad_ffn_in = lax.dot_general(
        grad_gate_pre, gate_weight, (((1,), (1,)), ((), ())), preferred_element_type=jnp.float32
    )
    grad_ffn_in = grad_ffn_in + lax.dot_general(
        grad_up_pre, up_weight, (((1,), (1,)), ((), ())), preferred_element_type=jnp.float32
    )
    ffn_grad_back = lax.all_to_all(
        grad_ffn_in.reshape(devices, ffn_capacity, D).astype(jnp.bfloat16),
        "expert",
        split_axis=0,
        concat_axis=0,
        tiled=True,
    ).astype(jnp.float32)
    ffn_grad_slots = ffn_grad_back.reshape(FFN_EXPERTS, ffn_copies, ffn_capacity, D).sum(axis=1)
    grad_hidden_two = jnp.einsum("ecr,ecd->rd", ffn_plan_float, ffn_grad_slots, precision=highest)
    grad_ffn_router, hidden_two_extra = router_grads(
        hidden_two, ffn_router, ffn_gates, ffn_first, ffn_second, ffn_weight_grad
    )
    grad_hidden_two = grad_hidden_two + hidden_two_extra
    grad_gain_two = jnp.sum(grad_hidden_two * normed_two, axis=0)
    grad_mid = grad_result + norm_back(grad_hidden_two * gain_two, normed_two, inverse_two)
    att_grad_send, att_weight_grad = expert_backward_slots(
        att_plan_float, att_weights, att_slots, grad_mid, att_copies
    )
    grad_att_out = lax.all_to_all(
        att_grad_send, "expert", split_axis=0, concat_axis=0, tiled=True
    ).reshape(-1, D)
    grad_o = lax.dot_general(
        grad_att_out, att_rows, (((0,), (0,)), ((), ())), preferred_element_type=jnp.float32
    )
    grad_heads = jnp.dot(grad_att_out, o_weight, preferred_element_type=jnp.float32).astype(
        jnp.bfloat16
    )
    grad_heads = grad_heads.reshape(-1, heads_local, HEAD).transpose(1, 0, 2)

    def head_backward(item):
        query_head, key_head, value_head, grad_head, highest_score, totals = item
        scores = jnp.where(
            allowed,
            jnp.dot(query_head, key_head.T, preferred_element_type=jnp.float32) * score_scale,
            -1e30,
        )
        probs = jnp.exp(scores - highest_score) / totals
        grad_probs = jnp.dot(grad_head, value_head.T, preferred_element_type=jnp.float32)
        centre = jnp.sum(probs * grad_probs, axis=1, keepdims=True)
        grad_scores = (probs * (grad_probs - centre)).astype(jnp.bfloat16)
        grad_query = (
            jnp.dot(grad_scores, key_head, preferred_element_type=jnp.float32) * score_scale
        )
        grad_key = (
            lax.dot_general(
                grad_scores,
                query_head,
                (((0,), (0,)), ((), ())),
                preferred_element_type=jnp.float32,
            )
            * score_scale
        )
        grad_value = lax.dot_general(
            probs.astype(jnp.bfloat16),
            grad_head,
            (((0,), (0,)), ((), ())),
            preferred_element_type=jnp.float32,
        )
        return (grad_query, grad_key, grad_value)

    grad_query_rot, grad_key_rot, grad_value_all = lax.map(
        head_backward, (queries, key_heads, value_heads, grad_heads, score_tops, score_totals)
    )
    grad_query_pre = (
        rotate(grad_query_rot.transpose(1, 0, 2), query_depths, -1.0)
        .reshape(-1, heads_local * HEAD)
        .astype(jnp.bfloat16)
    )
    grad_q = lax.dot_general(
        query_inputs, grad_query_pre, (((0,), (0,)), ((), ())), preferred_element_type=jnp.float32
    )
    grad_query_in = lax.dot_general(
        grad_query_pre, q_weight, (((1,), (1,)), ((), ())), preferred_element_type=jnp.float32
    )
    att_grad_back = lax.all_to_all(
        grad_query_in.reshape(devices, att_capacity, D).astype(jnp.bfloat16),
        "expert",
        split_axis=0,
        concat_axis=0,
        tiled=True,
    ).astype(jnp.float32)
    att_grad_slots = att_grad_back.reshape(ATT_EXPERTS, att_copies, att_capacity, D).sum(axis=1)
    grad_hidden_one = jnp.einsum("ecr,ecd->rd", att_plan_float, att_grad_slots, precision=highest)
    grad_full = jnp.zeros((2 * HEADS, group_rows, HEAD), jnp.float32)
    grad_full = lax.dynamic_update_slice_in_dim(grad_full, grad_key_rot, head_start, 0)
    grad_full = lax.dynamic_update_slice_in_dim(grad_full, grad_value_all, HEADS + head_start, 0)
    grad_kv_own = lax.psum_scatter(
        grad_full.astype(jnp.bfloat16), "expert", scatter_dimension=1, tiled=True
    ).astype(jnp.float32)
    grad_key_rows = rotate(grad_kv_own[:HEADS].transpose(1, 0, 2), own_depths, -1.0).reshape(
        row_count, width
    )
    grad_value_rows = grad_kv_own[HEADS:].transpose(1, 0, 2).reshape(row_count, width)
    grad_kv_rows = jnp.concatenate([grad_key_rows, grad_value_rows], axis=1).astype(jnp.bfloat16)
    grad_kv = lax.dot_general(
        hidden, grad_kv_rows, (((0,), (0,)), ((), ())), preferred_element_type=jnp.float32
    )
    grad_hidden_one = grad_hidden_one + lax.dot_general(
        grad_kv_rows, kv_full, (((1,), (1,)), ((), ())), preferred_element_type=jnp.float32
    )
    grad_att_router, hidden_one_extra = router_grads(
        hidden, att_router, att_gates, att_first, att_second, att_weight_grad
    )
    grad_hidden_one = grad_hidden_one + hidden_one_extra
    grad_gain_one = jnp.sum(grad_hidden_one * normed_one, axis=0)
    grad_input = grad_mid + norm_back(grad_hidden_one * gain_one, normed_one, inverse_one)
    summed_q, summed_o, summed_gate, summed_up, summed_down = (
        lax.psum_scatter(grad_q.astype(jnp.bfloat16), "dp", scatter_dimension=0, tiled=True).astype(
            jnp.float32
        ),
        lax.psum_scatter(grad_o.astype(jnp.bfloat16), "dp", scatter_dimension=0, tiled=True).astype(
            jnp.float32
        ),
        lax.psum_scatter(
            grad_gate.astype(jnp.bfloat16), "dp", scatter_dimension=0, tiled=True
        ).astype(jnp.float32),
        lax.psum_scatter(
            grad_up.astype(jnp.bfloat16), "dp", scatter_dimension=0, tiled=True
        ).astype(jnp.float32),
        lax.psum_scatter(
            grad_down.astype(jnp.bfloat16), "dp", scatter_dimension=0, tiled=True
        ).astype(jnp.float32),
    )
    shared_gain_one, shared_kv, shared_att_router, shared_gain_two, shared_ffn_router = (
        lax.psum_scatter(grad_gain_one, ("dp", "expert"), scatter_dimension=0, tiled=True),
        lax.psum_scatter(grad_kv, ("dp", "expert"), scatter_dimension=0, tiled=True),
        lax.psum_scatter(grad_att_router, ("dp", "expert"), scatter_dimension=0, tiled=True),
        lax.psum_scatter(grad_gain_two, ("dp", "expert"), scatter_dimension=0, tiled=True),
        lax.psum_scatter(grad_ffn_router, ("dp", "expert"), scatter_dimension=0, tiled=True),
    )
    return (
        result.astype(jnp.bfloat16),
        grad_input.astype(jnp.bfloat16),
        shared_gain_one,
        shared_kv,
        shared_att_router,
        summed_q,
        summed_o,
        shared_gain_two,
        shared_ffn_router,
        summed_gate,
        summed_up,
        summed_down,
    )


def solution(mesh):
    in_specs = (
        P(("dp", "expert"), None),
        P(("dp", "expert"), None),
        P(("dp", "expert"), None),
        P(("dp", "expert"), None),
        P("dp", None),
        P(),
        P(),
        P("expert", None),
        P(),
        P(None, "expert"),
        P(None, "expert"),
        P(),
        P(),
        P(None, "expert"),
        P(None, "expert"),
        P(None, "expert"),
    )
    out_specs = (
        P(("dp", "expert"), None),
        P(("dp", "expert"), None),
        P(("dp", "expert")),
        P(("dp", "expert"), None),
        P(("dp", "expert"), None),
        P("dp", "expert"),
        P("dp", "expert"),
        P(("dp", "expert")),
        P(("dp", "expert"), None),
        P("dp", "expert"),
        P("dp", "expert"),
        P("dp", "expert"),
    )
    return jax.shard_map(body, mesh=mesh, in_specs=in_specs, out_specs=out_specs, check_vma=False)
```

profile of v0, /device:TPU:0, one launch (start us, length us, event | category | flops | bytes accessed | tf_op | source)
XLA Modules:
  0.0 3102.9 jit_solution(4555319346405230609)
XLA Ops:
  10.8 152.7 %all-gather.3.cloned.1.call-done = bf16[2048,4096]{1,0:T(8,128)(2,1)} async-done(((bf16[256,4096]{1,0:T(8,128)(2,1)}), bf16[2048,4096]{1,0:T(8,128)(2,1)}) %all-gather.3.cloned.1.call-update) | async-done | bytes 16777232 | tf_op jit(solution)/shard_map/all_gather | solution.py:177
  163.5 8.5 fusion.240
  193.1 12.4 copy.77
  214.0 124.1 %all-to-all-done = bf16[8,88,2048]{2,1,0:T(8,128)(2,1)} async-done(((bf16[8,88,2048]{2,1,0:T(8,128)(2,1)}), bf16[8,88,2048]{2,1,0:T(8,128)(2,1)}, u32[]{:S(2)}, u32[]{:S(2)}) %all-to-all-start) | async-done | bytes 2883616 | tf_op jit(solution)/shard_map/all_to_all | solution.py:191
  338.1 9.5 fusion.248
  352.8 43.7 %all-gather.5.cloned.1.call-done = bf16[32,2176,128]{2,1,0:T(8,128)(2,1)} async-done(((bf16[32,272,128]{2,1,0:T(8,128)(2,1)}), bf16[32,2176,128]{2,1,0:T(8,128)(2,1)}) %all-gather.5.cloned.1.call-update) | async-done | bytes 17825808 | tf_op jit(solution)/shard_map/all_gather | solution.py:184
  396.5 11.9 fusion.246
  408.4 116.2 %while.30 = (s32[]{:T(128)}, bf16[16,704,128]{2,1,0:T(8,128)(2,1)}, f32[16,704,1]{1,2,0:T(1,128)}, f32[16,704,1]{1,2,0:T(1,128)}, bf16[16,704,128]{2,1,0:T(8,128...) while((s32[]{:T(128)}, bf16[16,704,128]{2,1,0:T(8,128)(2,1)}, ...), condition=%wide.region_11.12_spmd.clone, body=%wide.region_8.11_spmd.sunk.clone | while | flops 796588672 | bytes 21598036 | solution.py:225
  524.6 5.8 copy.61
  536.0 11.0 fusion.41
  556.0 124.0 %all-to-all-done.2 = f32[8,88,2048]{2,1,0:T(8,128)} async-done(((f32[8,88,2048]{2,1,0:T(8,128)}), f32[8,88,2048]{2,1,0:T(8,128)}, u32[]{:S(2)}, u32[]{:S(2)}) %all-to-all-start.2) | async-done | bytes 5767200 | tf_op jit(solution)/shard_map/all_to_all | solution.py:230
  680.0 8.1 multiply_reduce_fusion.5
  692.4 130.5 %all_to_all.49 = bf16[8,176,2048]{2,1,0:T(8,128)(2,1)S(1)} all-to-all(bf16[8,176,2048]{2,1,0:T(8,128)(2,1)S(1)} %bitcast.307), channel_id=1, replica_groups=mesh['dp'=4,'expert'=8] {'expert'}, dimensions={0} | all-to-all | bytes 11534336 | tf_op jit(solution)/shard_map/all_to_all | solution.py:245
  822.9 24.4 fusion.249
  847.3 25.5 multiply_convert_fusion.3
  872.8 22.5 convolution_convert_fusion.5
  903.9 124.3 %all-to-all-done.4 = bf16[8,176,2048]{2,1,0:T(8,128)(2,1)} async-done(((bf16[8,176,2048]{2,1,0:T(8,128)(2,1)}), bf16[8,176,2048]{2,1,0:T(8,128)(2,1)}, u32[]{:S(2)}, u32[]{:S(2)}) %all-to-all-start.4) | async-done | bytes 5767200 | tf_op jit(solution)/shard_map/all_to_all | solution.py:256
  1033.0 5.8 fusion.55
  1038.9 6.3 multiply_reduce_fusion.2
  1046.0 131.6 %all_to_all.50 = bf16[8,176,2048]{2,1,0:T(8,128)(2,1)} all-to-all(bf16[8,176,2048]{2,1,0:T(8,128)(2,1)S(1)} %bitcast.308), channel_id=1, replica_groups=mesh['dp'=4,'expert'=8] {'expert'}, dimensions={0} | all-to-all | bytes 11534336 | tf_op jit(solution)/shard_map/all_to_all | solution.py:279
  1177.7 30.6 multiply_convert_fusion.1
  1208.3 23.0 fusion.250
  1231.3 24.6 add_convert_fusion
  1262.3 126.2 %all-to-all-done.6 = bf16[8,176,2048]{2,1,0:T(8,128)(2,1)} async-done(((bf16[8,176,2048]{2,1,0:T(8,128)(2,1)}), bf16[8,176,2048]{2,1,0:T(8,128)(2,1)}, u32[]{:S(2)}, u32[]{:S(2)}) %all-to-all-start.6) | async-done | bytes 5767200 | tf_op jit(solution)/shard_map/all_to_all | solution.py:302
  1402.2 9.0 multiply_reduce_fusion.1
  1414.9 65.8 %all-to-all-done.7 = bf16[8,88,2048]{2,1,0:T(8,128)(2,1)S(1)} async-done(((bf16[8,88,2048]{2,1,0:T(8,128)(2,1)}), bf16[8,88,2048]{2,1,0:T(8,128)(2,1)S(1)}, u32[]{:S(2)}, u32[]{:S(2)}) %all-to-all-start.7) | async-done | bytes 2883616 | tf_op jit(solution)/shard_map/all_to_all | solution.py:320
  1482.3 8.9 fusion.69
  1493.5 250.8 %while.31 = (s32[]{:T(128)}, f32[16,704,128]{2,1,0:T(8,128)}, bf16[16,2176,128]{2,1,0:T(8,128)(2,1)}, bf16[16,2176,128]{2,1,0:T(8,128)(2,1)}, bf16[16,704,128]{2...) while((s32[]{:T(128)}, f32[16,704,128]{2,1,0:T(8,128)}, ...), condition=%wide.region_29.30_spmd.clone, body=%wide.region_27.29_spmd.sunk.clone | while | flops 1976524032 | bytes 52497520 | solution.py:362
  1744.3 16.0 pad_maximum_fusion
  1768.1 24.2 convolution_convert_fusion
  1792.3 24.3 convolution_convert_fusion.2
  1817.1 24.2 convolution_convert_fusion.1
  1842.4 5.7 multiply_subtract_fusion
  1850.7 11.2 convolution_convert_fusion.4
  1862.0 11.4 convolution_convert_fusion.3
  1873.5 63.9 %reduce-scatter.14.cloned.1.call-done = bf16[32,272,128]{2,1,0:T(8,128)(2,1)} async-done(((bf16[32,2176,128]{2,1,0:T(8,128)(2,1)}), bf16[32,272,128]{2,1,0:T(8,128)(2,1)}) %reduce-scatter.14.cloned.1.call-update) | async-done | bytes 2228240 | tf_op jit(solution)/shard_map/reduce_scatter | solution.py:388
  1940.7 15.6 fusion.238
  1969.6 10.6 fusion.48
  1984.8 91.4 %reduce-scatter.30.cloned.1.call-done = f32[64,4]{1,0:T(8,128)} async-done(((f32[2048,4]{1,0:T(8,128)}), f32[64,4]{1,0:T(8,128)}) %reduce-scatter.30.cloned.1.call-update) | async-done | bytes 1040
  2077.6 132.5 %reduce-scatter.28.cloned.1.call-done = f32[64,8]{1,0:T(8,128)} async-done(((f32[2048,8]{1,0:T(8,128)}), f32[64,8]{1,0:T(8,128)}) %reduce-scatter.28.cloned.1.call-update) | async-done | bytes 2064
  2211.5 110.0 %reduce-scatter.26.cloned.1.call-done = bf16[512,2816]{1,0:T(8,128)(2,1)} async-done(((bf16[2048,2816]{1,0:T(8,128)(2,1)}), bf16[512,2816]{1,0:T(8,128)(2,1)}) %reduce-scatter.26.cloned.1.call-update) | async-done | bytes 2883600 | tf_op jit(solution)/shard_map/reduce_scatter | solution.py:421
  2326.2 110.5 %reduce-scatter.22.cloned.1.call-done = bf16[512,2816]{1,0:T(8,128)(2,1)} async-done(((bf16[2048,2816]{1,0:T(8,128)(2,1)}), bf16[512,2816]{1,0:T(8,128)(2,1)}) %reduce-scatter.22.cloned.1.call-update) | async-done | bytes 2883600 | tf_op jit(solution)/shard_map/reduce_scatter | solution.py:415
  2441.5 110.5 %reduce-scatter.24.cloned.1.call-done = bf16[512,2816]{1,0:T(8,128)(2,1)} async-done(((bf16[2048,2816]{1,0:T(8,128)(2,1)}), bf16[512,2816]{1,0:T(8,128)(2,1)}) %reduce-scatter.24.cloned.1.call-update) | async-done | bytes 2883600 | tf_op jit(solution)/shard_map/reduce_scatter | solution.py:418
  2556.7 84.7 %reduce-scatter.18.cloned.1.call-done = bf16[512,2048]{1,0:T(8,128)(2,1)} async-done(((bf16[2048,2048]{1,0:T(8,128)(2,1)}), bf16[512,2048]{1,0:T(8,128)(2,1)}) %reduce-scatter.18.cloned.1.call-update) | async-done | bytes 2097168 | tf_op jit(solution)/shard_map/reduce_scatter | solution.py:409
  2645.6 85.5 %reduce-scatter.20.cloned.1.call-done = bf16[512,2048]{1,0:T(8,128)(2,1)} async-done(((bf16[2048,2048]{1,0:T(8,128)(2,1)}), bf16[512,2048]{1,0:T(8,128)(2,1)}) %reduce-scatter.20.cloned.1.call-update) | async-done | bytes 2097168 | tf_op jit(solution)/shard_map/reduce_scatter | solution.py:412
  2735.2 10.4 fusion.251
  2753.3 41.6 %all-reduce.4 = (f32[2048]{0:T(1024)S(1)}, f32[2048]{0:T(1024)S(1)}) all-reduce(f32[2048]{0:T(1024)S(1)} %get-tuple-element.123, f32[2048]{0:T(1024)S(1)} %copy-done.56), channel_id=3, replica_groups=mesh['dp'=4,'expert'=8] {'dp','expert'}, use_global_device_ids=true, to_apply=%region_37.38.clone | all-reduce | flops 4096 | bytes 32768
  2799.3 296.8 %reduce-scatter.16.cloned.1.call-done = f32[64,4096]{1,0:T(8,128)} async-done(((f32[2048,4096]{1,0:T(8,128)}), f32[64,4096]{1,0:T(8,128)}) %reduce-scatter.16.cloned.1.call-update) | async-done | bytes 1048592 | tf_op jit(solution)/shard_map/reduce_scatter | solution.py:427
  (484 shorter events, 534.4 us)
Async XLA Ops:
  7.2 545.1 %copy-start = (f32[2048,8]{0,1:T(8,128)S(1)}, f32[2048,8]{0,1:T(8,128)}, u32[]{:S(2)}) copy-start(f32[2048,8]{0,1:T(8,128)} %param.28) | copy-start | bytes 196612
  7.2 156.3 %copy-start.3 = (bf16[272,2048]{1,0:T(8,128)(2,1)S(1)}, bf16[272,2048]{1,0:T(8,128)(2,1)}, u32[]{:S(2)}) copy-start(bf16[272,2048]{1,0:T(8,128)(2,1)} %param.20) | copy-start | bytes 3342340
  7.2 156.3 %copy-start.25 = (f32[2048]{0:T(1024)S(1)}, f32[2048]{0:T(1024)}, u32[]{:S(2)}) copy-start(f32[2048]{0:T(1024)} %param.26) | copy-start | bytes 24580
  7.2 156.3 %all-gather.3.cloned.1.call-start = ((), (), s32[]{:S(2)}) async-start(), calls=%async_computation.18 | async-start | bytes 18874368 | tf_op jit(solution)/shard_map/all_gather | solution.py:177
  8.0 388.5 %all-gather.5.cloned.1.call-start = ((), (), s32[]{:S(2)}) async-start(), calls=%async_computation.19 | async-start | bytes 20054016 | tf_op jit(solution)/shard_map/all_gather | solution.py:184
  9.6 542.7 %copy-start.35 = (f32[272]{0:T(512)}, f32[272]{0:T(512)S(1)}, u32[]{:S(2)}) copy-start(f32[272]{0:T(512)S(1)} %add_rsqrt_fusion.1) | copy-start | bytes 3268
  10.8 162.6 %copy-start.22 = (f32[272,64]{1,0:T(8,128)}, f32[272,64]{1,0:T(8,128)S(1)}, u32[]{:S(2)}) copy-start(f32[272,64]{1,0:T(8,128)S(1)} %get-tuple-element.226) | copy-start | bytes 208900
  177.0 378.5 %copy-start.37 = (s32[272]{0:T(512)}, s32[272]{0:T(512)S(1)}, u32[]{:S(2)}) copy-start(s32[272]{0:T(512)S(1)} %get-tuple-element.143) | copy-start | bytes 3268
  177.0 378.5 %copy-start.41 = (s32[272]{0:T(512)}, s32[272]{0:T(512)S(1)}, u32[]{:S(2)}) copy-start(s32[272]{0:T(512)S(1)} %get-tuple-element.144) | copy-start | bytes 3268
  177.0 503.0 %copy-start.49 = (pred[8,272]{1,0:T(8,128)(4,1)}, pred[8,272]{1,0:T(8,128)(4,1)S(1)}, u32[]{:S(2)}) copy-start(pred[8,272]{1,0:T(8,128)(4,1)S(1)} %get-tuple-element.222) | copy-start | bytes 6532
  178.8 501.2 %copy-start.27 = (s32[8,272]{1,0:T(8,128)}, s32[8,272]{1,0:T(8,128)S(1)}, u32[]{:S(2)}) copy-start(s32[8,272]{1,0:T(8,128)S(1)} %fusion.147) | copy-start | bytes 26116
  179.7 8.7 all-to-all-start.1
  188.5 149.7 %all-to-all-start = ((bf16[8,88,2048]{2,1,0:T(8,128)(2,1)}), bf16[8,88,2048]{2,1,0:T(8,128)(2,1)}, u32[]{:S(2)}, u32[]{:S(2)}) async-start(bf16[8,88,2048]{2,1,0:T(8,128)(2,1)} %convolution_convert_fusion.8), calls=%async_computation | async-start | bytes 5767168 | tf_op jit(solution)/shard_map/all_to_all | solution.py:191
  193.1 12.4 copy-start.77
  211.5 136.1 %copy-start.18 = (f32[704,64]{1,0:T(8,128)}, f32[704,64]{1,0:T(8,128)S(1)}, u32[]{:S(2)}) copy-start(f32[704,64]{1,0:T(8,128)S(1)} %get-tuple-element.217) | copy-start | bytes 540676
  547.0 133.0 %all-to-all-start.2 = ((f32[8,88,2048]{2,1,0:T(8,128)}), f32[8,88,2048]{2,1,0:T(8,128)}, u32[]{:S(2)}, u32[]{:S(2)}) async-start(f32[8,88,2048]{2,1,0:T(8,128)} %fusion.41), calls=%async_computation.2 | async-start | bytes 11534336 | tf_op jit(solution)/shard_map/all_to_all | solution.py:230
  553.4 134.7 %copy-start.52 = (f32[272,1]{0,1:T(1,128)}, f32[272,1]{0,1:T(1,128)S(1)}, u32[]{:S(2)}) copy-start(f32[272,1]{0,1:T(1,128)S(1)} %stack.36) | copy-start | bytes 3268
  553.4 134.6 %copy-start.47 = (f32[272]{0:T(512)}, f32[272]{0:T(512)S(1)}, u32[]{:S(2)}) copy-start(f32[272]{0:T(512)S(1)} %reduce_max.29) | copy-start | bytes 3268
  553.5 134.6 %copy-start.54 = (f32[272,1]{0,1:T(1,128)}, f32[272,1]{0,1:T(1,128)S(1)}, u32[]{:S(2)}) copy-start(f32[272,1]{0,1:T(1,128)S(1)} %stack.37) | copy-start | bytes 3268
  553.5 134.6 %copy-start.31 = (s32[272]{0:T(512)}, s32[272]{0:T(512)S(1)}, u32[]{:S(2)}) copy-start(s32[272]{0:T(512)S(1)} %get-tuple-element.139) | copy-start | bytes 3268
  553.5 134.6 %copy-start.33 = (s32[272]{0:T(512)}, s32[272]{0:T(512)S(1)}, u32[]{:S(2)}) copy-start(s32[272]{0:T(512)S(1)} %get-tuple-element.140) | copy-start | bytes 3268
  553.5 134.9 %copy-start.72 = (pred[4,272]{1,0:T(4,128)(4,1)}, pred[4,272]{1,0:T(4,128)(4,1)S(1)}, u32[]{:S(2)}) copy-start(pred[4,272]{1,0:T(4,128)(4,1)S(1)} %get-tuple-element.218) | copy-start | bytes 3268
  555.4 132.7 %copy-start.69 = (f32[272]{0:T(512)}, f32[272]{0:T(512)S(1)}, u32[]{:S(2)}) copy-start(f32[272]{0:T(512)S(1)} %get-tuple-element.142) | copy-start | bytes 3268
  555.4 133.1 %copy-start.61 = (s32[4,272]{1,0:T(4,128)}, s32[4,272]{1,0:T(4,128)S(1)}, u32[]{:S(2)}) copy-start(s32[4,272]{1,0:T(4,128)S(1)} %fusion.162) | copy-start | bytes 13060
  556.0 132.2 %copy-start.45 = (f32[2048]{0:T(1024)S(1)}, f32[2048]{0:T(1024)}, u32[]{:S(2)}) copy-start(f32[2048]{0:T(1024)} %param.31) | copy-start | bytes 24580
  822.9 24.4 copy-start.16
  895.3 132.8 %all-to-all-start.4 = ((bf16[8,176,2048]{2,1,0:T(8,128)(2,1)}), bf16[8,176,2048]{2,1,0:T(8,128)(2,1)}, u32[]{:S(2)}, u32[]{:S(2)}) async-start(bf16[8,176,2048]{2,1,0:T(8,128)(2,1)} %bitcast.319), calls=%async_computation.4 | async-start | bytes 11534336 | tf_op jit(solution)/shard_map/all_to_all | solution.py:256
  903.8 129.2 %copy-start.8 = (f32[272,2048]{1,0:T(8,128)S(1)}, f32[272,2048]{1,0:T(8,128)}, u32[]{:S(2)}) copy-start(f32[272,2048]{1,0:T(8,128)} %copy-done.7) | copy-start | bytes 6684676
  1255.9 132.6 %all-to-all-start.6 = ((bf16[8,176,2048]{2,1,0:T(8,128)(2,1)}), bf16[8,176,2048]{2,1,0:T(8,128)(2,1)}, u32[]{:S(2)}, u32[]{:S(2)}) async-start(bf16[8,176,2048]{2,1,0:T(8,128)(2,1)} %bitcast.320), calls=%async_computation.6 | async-start | bytes 11534336 | tf_op jit(solution)/shard_map/all_to_all | solution.py:302
  1402.2 9.0 copy-start.5
  1411.2 69.5 %all-to-all-start.7 = ((bf16[8,88,2048]{2,1,0:T(8,128)(2,1)}), bf16[8,88,2048]{2,1,0:T(8,128)(2,1)S(1)}, u32[]{:S(2)}, u32[]{:S(2)}) async-start(bf16[8,88,2048]{2,1,0:T(8,128)(2,1)} %get-tuple-element.202), calls=%async_computation.7 | async-start | bytes 5767168 | tf_op jit(solution)/shard_map/all_to_all | solution.py:320
  1414.9 522.5 %reduce-scatter.14.cloned.1.call-start = ((), (), s32[]{:S(2)}) async-start(), calls=%async_computation.20 | async-start | bytes 20054016 | tf_op jit(solution)/shard_map/reduce_scatter | solution.py:388
  1760.4 315.8 %reduce-scatter.30.cloned.1.call-start = ((), (), s32[]{:S(2)}) async-start(), calls=%async_computation.28 | async-start | bytes 1081344
  1764.2 445.8 %reduce-scatter.28.cloned.1.call-start = ((), (), s32[]{:S(2)}) async-start(), calls=%async_computation.27 | async-start | bytes 1081344
  1765.2 27.0 copy-start.63
  1765.2 27.0 copy-start.65
  1768.0 553.5 %reduce-scatter.26.cloned.1.call-start = ((), (), s32[]{:S(2)}) async-start(), calls=%async_computation.26 | async-start | bytes 14417920 | tf_op jit(solution)/shard_map/reduce_scatter | solution.py:421
  1792.2 644.5 %reduce-scatter.22.cloned.1.call-start = ((), (), s32[]{:S(2)}) async-start(), calls=%async_computation.24 | async-start | bytes 14417920 | tf_op jit(solution)/shard_map/reduce_scatter | solution.py:415
  1816.6 735.3 %reduce-scatter.24.cloned.1.call-start = ((), (), s32[]{:S(2)}) async-start(), calls=%async_computation.25 | async-start | bytes 14417920 | tf_op jit(solution)/shard_map/reduce_scatter | solution.py:418
  1841.4 800.1 %reduce-scatter.18.cloned.1.call-start = ((), (), s32[]{:S(2)}) async-start(), calls=%async_computation.22 | async-start | bytes 10485760 | tf_op jit(solution)/shard_map/reduce_scatter | solution.py:409
  1861.9 869.2 %reduce-scatter.20.cloned.1.call-start = ((), (), s32[]{:S(2)}) async-start(), calls=%async_computation.23 | async-start | bytes 10485760 | tf_op jit(solution)/shard_map/reduce_scatter | solution.py:412
  1873.4 65.8 %copy-start.23 = (f32[272,64]{1,0:T(8,128)S(1)}, f32[272,64]{1,0:T(8,128)}, u32[]{:S(2)}) copy-start(f32[272,64]{1,0:T(8,128)} %copy-done.22) | copy-start | bytes 208900
  1873.4 65.8 %copy-start.24 = (f32[272,64]{1,0:T(8,128)S(1)}, f32[272,64]{1,0:T(8,128)}, u32[]{:S(2)}) copy-start(f32[272,64]{1,0:T(8,128)} %get-tuple-element.224) | copy-start | bytes 208900
  1873.4 1222.7 %reduce-scatter.16.cloned.1.call-start = ((), (), s32[]{:S(2)}) async-start(), calls=%async_computation.21 | async-start | bytes 34603008 | tf_op jit(solution)/shard_map/reduce_scatter | solution.py:427
  1980.2 765.5 %all-to-all-start.8 = ((bf16[8,88,2048]{2,1,0:T(8,128)(2,1)}), bf16[8,88,2048]{2,1,0:T(8,128)(2,1)}, u32[]{:S(2)}, u32[]{:S(2)}) async-start(bf16[8,88,2048]{2,1,0:T(8,128)(2,1)} %fusion.48), calls=%async_computation.8 | async-start | bytes 5767168 | tf_op jit(solution)/shard_map/all_to_all | solution.py:376
  2735.2 10.5 copy-start.29
  2735.2 10.5 copy-start.51
  2749.4 46.7 %copy-start.6 = (f32[272,2048]{1,0:T(8,128)S(1)}, f32[272,2048]{1,0:T(8,128)}, u32[]{:S(2)}) copy-start(f32[272,2048]{1,0:T(8,128)} %copy-done.5) | copy-start | bytes 6684676
  (48 other events, 197.9 us)
Sparse Core Ops, SparseCore 0:
  9.7 153.7 all-gather.2
  177.0 219.4 all-gather.4
  1760.4 176.9 reduce-scatter.13
  1940.0 136.0 reduce-scatter.29
  2078.9 131.0 reduce-scatter.27
  2213.0 108.4 reduce-scatter.25
  2324.6 112.0 reduce-scatter.21
  2439.8 112.0 reduce-scatter.23
  2555.0 86.3 reduce-scatter.17
  2644.6 86.4 reduce-scatter.19
  2734.0 362.1 reduce-scatter.15
where the time goes:
time: 3120 us; the launch traced here: 3100 us
  waiting for transfers between devices  1850 us (59%)
  matrix products  702 us (22%)
  blocking collectives  304 us (10%)
  other arithmetic  114 us (4%)
  local copies, waits for them, and re-layouts  84.8 us (3%)
  starting transfers between devices  32.4 us (1%)
    reduce_scatter x1, waiting for transfers between devices, body(): lax.psum_scatter(grad_kv, ('dp', 'expert'), scatter_dimension=0, tiled=True)  297 us
    unnamed x13, waiting for transfers between devices  225 us
    all_gather x1, waiting for transfers between devices, body(): kv_full = lax.all_gather(kv_weight, 'expert', axis=0, tiled=True)  153 us
    all_to_all x1, blocking collectives, body(): lax.all_to_all(ffn_grad_send, 'expert', split_axis=0, concat_axis=0, tile...  132 us
    all_to_all x1, blocking collectives, body(): lax.all_to_all(ffn_send, 'expert', split_axis=0, concat_axis=0, tiled=True)  131 us
    all_to_all x1, waiting for transfers between devices, body(): lax.all_to_all(grad_ffn_in.reshape(devices, ffn_capacity, D).astype(jnp.b...  126 us
    all_to_all x1, waiting for transfers between devices, body(): lax.all_to_all(ffn_partial.reshape(devices, ffn_capacity, D).astype(jnp.b...  124 us
    all_to_all x1, waiting for transfers between devices, body(): lax.all_to_all(send_rows, 'expert', split_axis=0, concat_axis=0, tiled=True)  124 us
  transfers between devices with their start and end apart: 18, of which 17 were waited for; matrix products, arithmetic and copies ran while one was open for 8% of the time, Pallas kernels for 0%

commit v1 on v0

v1 whole, which is shorter than its diff:
```python
import functools
import jax
import jax.numpy as jnp
from jax import lax
from jax.experimental import pallas as pl
from jax.experimental.pallas import tpu as pltpu
from jax.sharding import PartitionSpec as P

HEAD = 128
GROUPS = 4
LOG2E = 1.4426950408889634
VMEM_BYTES = 60 * 1024 * 1024


def dot_nt(left, right):
    return lax.dot_general(left, right, (((1,), (1,)), ((), ())), preferred_element_type=jnp.float32)


def dot_nn(left, right):
    return jnp.dot(left, right, preferred_element_type=jnp.float32)


def spin(values, cosine, sine):
    return values * cosine + pltpu.roll(values, HEAD // 2, 1) * sine


def fill_bias(bias_ref, key_ref, query_ref, keys):
    for group in range(GROUPS):
        place = query_ref[group, 0:1, :]
        own, parent, grand = (query_ref[group, 1 + n : 2 + n, :] for n in range(3))

        def one(block, carry, group=group, place=place, own=own, parent=parent, grand=grand):
            at = pl.multiple_of(block * keys, 16)
            key_place = key_ref[pl.ds(at, keys), 0:1]
            key_segment = key_ref[pl.ds(at, keys), 1:2]
            related = (key_segment == own) | (key_segment == parent) | (key_segment == grand)
            allowed = related & (key_place <= place)
            bias_ref[group * (group + 1) // 2 + block] = jnp.where(allowed, 0.0, -1e30)
            return carry

        lax.fori_loop(0, group + 1, one, 0)


def group_rows(refs, group, rows, lanes):
    parts = [ref[pl.ds(group * rows, rows), lanes] for ref in refs]
    return parts[0] if len(parts) == 1 else jnp.concatenate(parts, axis=0)


def attention_forward_body(sets, step_heads, rows, keys, scale, first_ref, *refs):
    query_refs = refs[:sets]
    key_ref, value_ref, key_info, query_info = refs[sets : sets + 4]
    out_refs = refs[sets + 4 : 2 * sets + 4]
    lse_ref, bias_ref, flipped_ref = refs[2 * sets + 4 :]
    wide = sets * rows

    @pl.when(pl.program_id(0) == 0)
    def _():
        fill_bias(bias_ref, key_info, query_info, keys)

    for head in range(step_heads):
        lanes = pl.ds(head * HEAD, HEAD)
        for block in range(GROUPS):
            values = value_ref[pl.ds(block * keys, keys), lanes].astype(jnp.float32)
            flipped_ref[head, block] = values.T.astype(jnp.bfloat16)
    for group in range(GROUPS):
        queries = [
            group_rows(query_refs, group, rows, pl.ds(head * HEAD, HEAD)) for head in range(step_heads)
        ]

        def one(block, carry, group=group, queries=queries):
            at = pl.multiple_of(block * keys, 16)
            bias = bias_ref[group * (group + 1) // 2 + block]
            result = []
            for head in range(step_heads):
                top, total, mixed = carry[3 * head : 3 * head + 3]
                scores = dot_nt(key_ref[pl.ds(at, keys), pl.ds(head * HEAD, HEAD)], queries[head])
                scores = scores * scale + bias
                new_top = jnp.maximum(top, jnp.max(scores, axis=0, keepdims=True))
                fade = jnp.exp2(top - new_top)
                parts = jnp.exp2(scores - new_top)
                total = total * fade + jnp.sum(parts, axis=0, keepdims=True)
                mixed = mixed * fade + dot_nn(flipped_ref[head, block], parts.astype(jnp.bfloat16))
                result += [new_top, total, mixed]
            return tuple(result)

        start = (
            jnp.full((1, wide), -1e30, jnp.float32),
            jnp.zeros((1, wide), jnp.float32),
            jnp.zeros((HEAD, wide), jnp.float32),
        ) * step_heads
        final = lax.fori_loop(0, group + 1, one, start)
        for head in range(step_heads):
            top, total, mixed = final[3 * head : 3 * head + 3]
            lse_ref[head, group : group + 1, :] = top + jnp.log2(total)
            rows_out = (mixed / total).T.astype(jnp.bfloat16)
            for n, ref in enumerate(out_refs):
                ref[pl.ds(group * rows, rows), pl.ds(head * HEAD, HEAD)] = rows_out[
                    n * rows : (n + 1) * rows
                ]


def attention_backward_body(sets, step_heads, rows, keys, scale, first_ref, *refs):
    query_refs, grad_refs, out_refs = (refs[n * sets : (n + 1) * sets] for n in range(3))
    key_ref, value_ref, lse_ref, key_info, query_info = refs[3 * sets : 3 * sets + 5]
    key_cos, key_sin = refs[3 * sets + 5 : 3 * sets + 7]
    table_refs = refs[3 * sets + 7 : 5 * sets + 7]
    rest = refs[5 * sets + 7 :]
    dq_refs = rest[:sets]
    dk_ref, dv_ref, bias_ref, flipped_ref, dk_acc, dv_acc = rest[sets:]
    softmax_scale = scale / LOG2E

    @pl.when(pl.program_id(0) == 0)
    def _():
        fill_bias(bias_ref, key_info, query_info, keys)

    dk_acc[...] = jnp.zeros_like(dk_acc)
    dv_acc[...] = jnp.zeros_like(dv_acc)
    for head in range(step_heads):
        lanes = pl.ds(head * HEAD, HEAD)
        for block in range(GROUPS):
            values = key_ref[pl.ds(block * keys, keys), lanes].astype(jnp.float32)
            flipped_ref[head, block] = values.T.astype(jnp.bfloat16)
    for group in range(GROUPS):
        queries, grads, centres, tops = [], [], [], []
        for head in range(step_heads):
            lanes = pl.ds(head * HEAD, HEAD)
            queries.append(group_rows(query_refs, group, rows, lanes))
            grad = group_rows(grad_refs, group, rows, lanes)
            out = group_rows(out_refs, group, rows, lanes)
            product = grad.astype(jnp.float32) * out.astype(jnp.float32)
            centres.append(jnp.sum(product.T, axis=0, keepdims=True))
            grads.append(grad)
            tops.append(lse_ref[head, group : group + 1, :])

        def one(block, carry, group=group, queries=queries, grads=grads, centres=centres, tops=tops):
            at = pl.multiple_of(block * keys, 16)
            bias = bias_ref[group * (group + 1) // 2 + block]
            result = []
            for head in range(step_heads):
                lanes = pl.ds(head * HEAD, HEAD)
                key_rows = key_ref[pl.ds(at, keys), lanes]
                scores = dot_nt(key_rows, queries[head])
                probs = jnp.exp2(scores * scale + (bias - tops[head]))
                grad_probs = dot_nt(value_ref[pl.ds(at, keys), lanes], grads[head])
                grad_scores = (probs * (grad_probs - centres[head])).astype(jnp.bfloat16)
                dv_acc[pl.ds(at, keys), lanes] += dot_nn(probs.astype(jnp.bfloat16), grads[head])
                dk_acc[pl.ds(at, keys), lanes] += dot_nn(grad_scores, queries[head])
                result.append(carry[head] + dot_nn(flipped_ref[head, block], grad_scores))
            return tuple(result)

        start = (jnp.zeros((HEAD, sets * rows), jnp.float32),) * step_heads
        final = lax.fori_loop(0, group + 1, one, start)
        for head in range(step_heads):
            dq = final[head].T * softmax_scale
            for n, ref in enumerate(dq_refs):
                span = pl.ds(group * rows, rows)
                turned = spin(
                    dq[n * rows : (n + 1) * rows], table_refs[2 * n][span, :], table_refs[2 * n + 1][span, :]
                )
                ref[span, pl.ds(head * HEAD, HEAD)] = turned.astype(jnp.bfloat16)
    for head in range(step_heads):
        lanes = pl.ds(head * HEAD, HEAD)
        for block in range(GROUPS):
            span = pl.ds(block * keys, keys)
            turned = spin(dk_acc[span, lanes] * softmax_scale, key_cos[span, :], key_sin[span, :])
            dk_ref[span, lanes] = turned.astype(jnp.bfloat16)
            dv_ref[span, lanes] = dv_acc[span, lanes].astype(jnp.bfloat16)


def whole_block(shape):
    return pl.BlockSpec(shape, lambda h, first: (0,) * len(shape))


def attention_forward(queries, starts, keys_all, values_all, key_info, query_info, heads):
    sets, total_rows, tokens = len(queries), queries[0].shape[0], keys_all.shape[0]
    rows, keys = total_rows // GROUPS, tokens // GROUPS
    step_heads = 2
    wide = step_heads * HEAD
    scale = HEAD ** (-0.5) * LOG2E
    query_specs = [
        pl.BlockSpec((total_rows, wide), lambda h, first, n=n: (0, first[n] + h)) for n in range(sets)
    ]
    plain = pl.BlockSpec((total_rows, wide), lambda h, first: (0, h))
    side = pl.BlockSpec((tokens, wide), lambda h, first: (0, h))
    return pl.pallas_call(
        functools.partial(attention_forward_body, sets, step_heads, rows, keys, scale),
        grid_spec=pltpu.PrefetchScalarGridSpec(
            num_scalar_prefetch=1,
            grid=(heads // step_heads,),
            in_specs=query_specs
            + [side, side, whole_block(key_info.shape), whole_block(query_info.shape)],
            out_specs=[plain] * sets
            + [pl.BlockSpec((step_heads, GROUPS, sets * rows), lambda h, first: (h, 0, 0))],
            scratch_shapes=[
                pltpu.VMEM((GROUPS * (GROUPS + 1) // 2, keys, sets * rows), jnp.float32),
                pltpu.VMEM((step_heads, GROUPS, HEAD, keys), jnp.bfloat16),
            ],
        ),
        out_shape=[jax.ShapeDtypeStruct((total_rows, heads * HEAD), jnp.bfloat16)] * sets
        + [jax.ShapeDtypeStruct((heads, GROUPS, sets * rows), jnp.float32)],
        compiler_params=pltpu.CompilerParams(vmem_limit_bytes=VMEM_BYTES),
        name="attention_forward",
    )(starts, *queries, keys_all, values_all, key_info, query_info)


def attention_backward(
    queries, starts, grads, outs, keys_all, values_all, lse, key_info, query_info, key_tables, row_tables, heads
):
    sets, total_rows, tokens = len(queries), queries[0].shape[0], keys_all.shape[0]
    rows, keys = total_rows // GROUPS, tokens // GROUPS
    step_heads = 1
    wide = step_heads * HEAD
    scale = HEAD ** (-0.5) * LOG2E
    shifted = [
        pl.BlockSpec((total_rows, wide), lambda h, first, n=n: (0, first[n] + h)) for n in range(sets)
    ]
    plain = pl.BlockSpec((total_rows, wide), lambda h, first: (0, h))
    side = pl.BlockSpec((tokens, wide), lambda h, first: (0, h))
    return pl.pallas_call(
        functools.partial(attention_backward_body, sets, step_heads, rows, keys, scale),
        grid_spec=pltpu.PrefetchScalarGridSpec(
            num_scalar_prefetch=1,
            grid=(heads // step_heads,),
            in_specs=shifted
            + shifted
            + [plain] * sets
            + [
                side,
                side,
                pl.BlockSpec((step_heads, GROUPS, sets * rows), lambda h, first: (h, 0, 0)),
                whole_block(key_info.shape),
                whole_block(query_info.shape),
                whole_block((tokens, HEAD)),
                whole_block((tokens, HEAD)),
            ]
            + [whole_block((total_rows, HEAD))] * (2 * sets),
            out_specs=[plain] * sets + [side, side],
            scratch_shapes=[
                pltpu.VMEM((GROUPS * (GROUPS + 1) // 2, keys, sets * rows), jnp.float32),
                pltpu.VMEM((step_heads, GROUPS, HEAD, keys), jnp.bfloat16),
                pltpu.VMEM((tokens, wide), jnp.float32),
                pltpu.VMEM((tokens, wide), jnp.float32),
            ],
        ),
        out_shape=[jax.ShapeDtypeStruct((total_rows, heads * HEAD), jnp.bfloat16)] * sets
        + [jax.ShapeDtypeStruct((tokens, heads * HEAD), jnp.bfloat16)] * 2,
        compiler_params=pltpu.CompilerParams(vmem_limit_bytes=VMEM_BYTES),
        name="attention_backward",
    )(
        starts,
        *queries,
        *grads,
        *outs,
        keys_all,
        values_all,
        lse,
        key_info,
        query_info,
        *key_tables,
        *[table for pair in row_tables for table in pair],
    )


def project_body(tile, x_ref, weight_ref, cos_ref, sin_ref, out_ref):
    for at in range(0, x_ref.shape[0], tile):
        span = pl.ds(at, tile)
        product = dot_nn(x_ref[span, :], weight_ref[...])
        for lane in range(0, out_ref.shape[1], HEAD):
            turned = spin(product[:, lane : lane + HEAD], cos_ref[span, :], sin_ref[span, :])
            out_ref[span, lane : lane + HEAD] = turned.astype(jnp.bfloat16)


def project_queries(rows_in, weight, tables):
    rows, depth = rows_in.shape
    columns = weight.shape[1]
    block = 512
    return pl.pallas_call(
        functools.partial(project_body, rows // GROUPS),
        grid=(columns // block,),
        in_specs=[
            pl.BlockSpec((rows, depth), lambda j: (0, 0)),
            pl.BlockSpec((depth, block), lambda j: (0, j)),
            pl.BlockSpec((rows, HEAD), lambda j: (0, 0)),
            pl.BlockSpec((rows, HEAD), lambda j: (0, 0)),
        ],
        out_specs=pl.BlockSpec((rows, block), lambda j: (0, j)),
        out_shape=jax.ShapeDtypeStruct((rows, columns), jnp.bfloat16),
        compiler_params=pltpu.CompilerParams(vmem_limit_bytes=VMEM_BYTES),
        name="project_queries",
    )(rows_in, weight, *tables)


def keys_values_body(half, x_ref, weight_ref, cos_ref, sin_ref, key_ref, value_ref):
    rows = x_ref.shape[1]
    for source in range(x_ref.shape[0]):
        span = pl.ds(source * rows, rows)
        product = dot_nn(x_ref[source], weight_ref[0])
        for lane in range(0, half, HEAD):
            turned = spin(product[:, lane : lane + HEAD], cos_ref[span, :], sin_ref[span, :])
            key_ref[span, lane : lane + HEAD] = turned.astype(jnp.bfloat16)
        value_ref[span, :] = product[:, half:].astype(jnp.bfloat16)


def project_keys_values(gathered, weights, tables):
    sources, rows, unused = gathered.shape
    parts, depth, columns = weights.shape
    half, tokens = columns // 2, sources * rows
    return pl.pallas_call(
        functools.partial(keys_values_body, half),
        grid=(parts,),
        in_specs=[
            pl.BlockSpec((sources, rows, depth), lambda j: (0, 0, 0)),
            pl.BlockSpec((1, depth, columns), lambda j: (j, 0, 0)),
            pl.BlockSpec((tokens, HEAD), lambda j: (0, 0)),
            pl.BlockSpec((tokens, HEAD), lambda j: (0, 0)),
        ],
        out_specs=[pl.BlockSpec((tokens, half), lambda j: (0, j))] * 2,
        out_shape=[jax.ShapeDtypeStruct((tokens, parts * half), jnp.bfloat16)] * 2,
        compiler_params=pltpu.CompilerParams(vmem_limit_bytes=VMEM_BYTES),
        name="project_keys_values",
    )(gathered, weights, *tables)


def merge_body(tile, plan_ref, slots_ref, dk_ref, dv_ref, weight_ref, out_ref, acc_ref):
    part = pl.program_id(1)
    sources, rows = plan_ref.shape[0], plan_ref.shape[1]
    ck = dk_ref.shape[1]

    @pl.when(part == 0)
    def _():
        for source in range(sources):
            acc_ref[pl.ds(source * rows, rows), :] = dot_nn(plan_ref[source], slots_ref[source])

    last = part == pl.num_programs(1) - 1
    for at in range(0, acc_ref.shape[0], tile):
        span = pl.ds(at, tile)
        acc_ref[span, :] += dot_nt(dk_ref[span, :], weight_ref[0, :, :ck]) + dot_nt(
            dv_ref[span, :], weight_ref[0, :, ck:]
        )

    @pl.when(last)
    def _():
        out_ref[...] = acc_ref[...].astype(jnp.bfloat16)


def merge_hidden_grads(plan, slots, grad_keys, grad_values, weights):
    sources, rows, capacity = plan.shape
    parts, depth, columns = weights.shape
    ck, tokens = columns // 2, sources * rows
    wide = depth // 2
    return pl.pallas_call(
        functools.partial(merge_body, tokens // GROUPS),
        grid=(2, parts),
        in_specs=[
            pl.BlockSpec((sources, rows, capacity), lambda i, j: (0, 0, 0)),
            pl.BlockSpec((sources, capacity, wide), lambda i, j: (0, 0, i)),
            pl.BlockSpec((tokens, ck), lambda i, j: (0, j)),
            pl.BlockSpec((tokens, ck), lambda i, j: (0, j)),
            pl.BlockSpec((1, wide, columns), lambda i, j: (j, i, 0)),
        ],
        out_specs=pl.BlockSpec((tokens, wide), lambda i, j: (0, i)),
        out_shape=jax.ShapeDtypeStruct((tokens, depth), jnp.bfloat16),
        scratch_shapes=[pltpu.VMEM((tokens, wide), jnp.float32)],
        compiler_params=pltpu.CompilerParams(vmem_limit_bytes=VMEM_BYTES),
        name="merge_hidden_grads",
    )(plan, slots, grad_keys, grad_values, weights)


D = 2048
HEADS = 16
ATT_EXPERTS = 8
FFN_EXPERTS = 4
TRUNK = 1024
SEG = 96
TREE_LEN = 2176
NODES = 13

epsilon = 1e-06
highest = lax.Precision.HIGHEST
bf16 = jnp.bfloat16
f32 = jnp.float32


def tree_layout(places):
    after_trunk = places - TRUNK
    after_branch = after_trunk - 4 * SEG
    segments = jnp.where(
        places < TRUNK,
        0,
        jnp.where(after_branch < 0, 1 + after_trunk // SEG, 5 + after_branch // SEG),
    )
    depths = jnp.where(
        places < TRUNK,
        places,
        jnp.where(after_branch < 0, TRUNK + after_trunk % SEG, TRUNK + SEG + after_branch % SEG),
    )
    return (segments.astype(jnp.int32), depths.astype(jnp.int32))


def rotation_tables(depths):
    half_size = HEAD // 2
    frequency = 10000.0 ** (-jnp.arange(half_size, dtype=f32) * 2.0 / HEAD)
    angles = depths.astype(f32)[:, None] * frequency[None, :]
    cosine, sine = jnp.cos(angles), jnp.sin(angles)
    cosines = jnp.concatenate([cosine, cosine], axis=1)
    forward = jnp.concatenate([-sine, sine], axis=1)
    return (cosines, forward), (cosines, -forward)


def lookup(table, indices):
    nodes = jnp.arange(NODES, dtype=jnp.int32)
    return jnp.sum(jnp.where(indices[:, None] == nodes[None, :], table[None, :], 0), axis=1)


def running_count(chosen):
    rows = chosen.shape[-1]
    index = jnp.arange(rows, dtype=jnp.int32)
    upto = (index[:, None] <= index[None, :]).astype(bf16)
    return jnp.dot(chosen.astype(bf16), upto, preferred_element_type=f32).astype(jnp.int32) - 1


def source_plan(routes, expert, capacity):
    chosen = jnp.any(routes == expert, axis=2)
    ranking = running_count(chosen)
    slots = jnp.arange(capacity, dtype=jnp.int32)
    return chosen[:, None, :] & (ranking[:, None, :] == slots[None, :, None])


def token_picks(routes, experts, capacity):
    labels = jnp.arange(experts, dtype=jnp.int32)
    hits = routes.T[:, None, :] == labels[None, :, None]
    ranking = running_count(hits[0] | hits[1])
    slots = jnp.arange(capacity, dtype=jnp.int32)
    picks = hits[:, :, None, :] & (ranking[None, :, None, :] == slots[None, None, :, None])
    return picks.astype(bf16), hits[0].T.astype(f32), hits[1].T.astype(f32)


def fill_slots(picks, pair):
    return jnp.einsum("kecr,krd->ecd", picks, pair, preferred_element_type=f32).astype(bf16)


def read_slots(picks, slots):
    return jnp.einsum("kecr,ecd->krd", picks, slots, preferred_element_type=f32)


def gate_values(hidden, router, first, second):
    logits = jnp.dot(hidden.astype(f32), router, precision=highest)
    picked = jnp.stack([jnp.sum(logits * first, axis=1), jnp.sum(logits * second, axis=1)], axis=1)
    return jax.nn.softmax(picked, axis=1)


def router_grads(hidden, router, gates, first, second, picked_grad):
    logit_pick = gates * (picked_grad - jnp.sum(gates * picked_grad, axis=1, keepdims=True))
    logit_grad = logit_pick[:, 0:1] * first + logit_pick[:, 1:2] * second
    router_grad = jnp.dot(hidden.astype(f32).T, logit_grad, precision=highest)
    hidden_grad = jnp.dot(logit_grad, router.T, precision=highest)
    return (router_grad, hidden_grad)


def rms_parts(values):
    inverse = lax.rsqrt(jnp.mean(values * values, axis=-1, keepdims=True) + epsilon)
    return (values * inverse, inverse)


def norm_back(grad_normed, normed, inverse):
    return inverse * (grad_normed - normed * jnp.mean(grad_normed * normed, axis=-1, keepdims=True))


def pair_grads(gates, branches, upstream):
    gate_grad = jnp.stack([jnp.sum(upstream * branches[k], axis=1) for k in range(2)], axis=1)
    scaled = jnp.stack([gates[:, k : k + 1] * upstream for k in range(2)]).astype(bf16)
    return gate_grad, scaled


def exchange(slots):
    return lax.all_to_all(slots, "expert", split_axis=0, concat_axis=0, tiled=True)


def shift(values, step, size, devices):
    moves = [(i, i // size * size + (i % size + step) % size) for i in range(devices)]
    return lax.ppermute(values, "expert", moves)


def group_gather(rows, size, devices):
    return jnp.concatenate([rows] + [shift(rows, step, size, devices) for step in range(1, size)])


def group_reduce(partial, size, devices):
    parts = partial.reshape(size, -1, partial.shape[1])
    total = parts[0].astype(f32)
    for step in range(1, size):
        total = total + shift(parts[step], -step, size, devices).astype(f32)
    return total.astype(bf16)


def dot_tn(left, right):
    return lax.dot_general(left, right, (((0,), (0,)), ((), ())), preferred_element_type=f32)


def body(
    tokens,
    teacher,
    att_routes,
    ffn_routes,
    parent,
    valid,
    gain_one,
    kv_weight,
    att_router,
    q_weight,
    o_weight,
    gain_two,
    ffn_router,
    gate_weight,
    up_weight,
    down_weight,
):
    row_count = tokens.shape[0]
    devices, replicas = lax.axis_size("expert"), lax.axis_size("dp")
    my_index, my_replica = lax.axis_index("expert"), lax.axis_index("dp")
    core = my_index % 2
    att_copies, ffn_copies = devices // ATT_EXPERTS, devices // FFN_EXPERTS
    att_capacity, ffn_capacity = row_count * 13 // 40, row_count * 13 // 20
    token_count = row_count * devices
    half = HEADS * HEAD // 2
    assert token_count == TREE_LEN * parent.shape[0] and parent.shape[0] == 1
    pair = [(i, i ^ 1) for i in range(devices)]
    own_places = my_index * row_count + jnp.arange(row_count, dtype=jnp.int32)

    x_in = tokens.astype(f32)
    normed_one, inverse_one = rms_parts(x_in)
    hidden = (normed_one * gain_one).astype(bf16)
    weight_rows = kv_weight.shape[0]
    piece = half // replicas
    kv_share = lax.dynamic_slice_in_dim(
        kv_weight.reshape(weight_rows, 4, replicas, piece), my_replica, 1, 2
    )
    kv_share = (
        kv_share.reshape(weight_rows, 2, 2, piece).transpose(0, 2, 1, 3).reshape(weight_rows, 4 * piece)
    )
    route_row = jnp.pad(att_routes.astype(bf16).reshape(1, -1), ((0, row_count - weight_rows - 1), (0, 4 * piece - 2 * row_count)))
    sending = jnp.concatenate([hidden, jnp.concatenate([kv_share, route_row])], axis=1)
    gathered = lax.all_gather(sending, "expert", axis=0)
    kv_half = lax.dynamic_slice_in_dim(gathered[:, :weight_rows], D + core * 2 * piece, 2 * piece, 2)
    kv_blocks = lax.all_gather(kv_half.reshape(D, 2 * piece), "dp", axis=0)
    all_routes = (
        gathered[:, weight_rows, D : D + 2 * row_count].astype(jnp.int32).reshape(devices, row_count, 2)
    )

    tree_places = jnp.arange(token_count, dtype=jnp.int32)
    tree_segments, tree_depths = tree_layout(tree_places)
    key_forward, key_backward = rotation_tables(tree_depths)
    key_info = jnp.pad(jnp.stack([tree_places, tree_segments], axis=1), ((0, 0), (0, 6)))
    experts_here = [my_index // att_copies]
    if att_copies == 1:
        experts_here.append(my_index ^ 1)
    plans = [source_plan(all_routes, expert, att_capacity) for expert in experts_here]
    slot_tables, query_parts = [], []
    for plan in plans:
        places = jnp.sum(
            jnp.where(plan, tree_places.reshape(devices, 1, row_count), 0), axis=2
        ).reshape(-1)
        segments, depths = tree_layout(places)
        parents = lookup(parent[0], segments)
        grands = lookup(parent[0], parents)
        query_parts.append(jnp.stack([places, segments, parents, grands]).reshape(4, GROUPS, -1))
        slot_tables.append(rotation_tables(depths))
    query_info = jnp.concatenate(query_parts, axis=2).transpose(1, 0, 2)
    own_plan = plans[0].astype(bf16)
    query_inputs = jnp.einsum(
        "scr,srd->scd", own_plan, gathered[:, :, :D], preferred_element_type=f32
    ).astype(bf16).reshape(-1, D)

    queries = project_queries(query_inputs, q_weight, slot_tables[0][0])
    keys_all, values_all = project_keys_values(gathered, kv_blocks, key_forward)

    def far_half(values):
        return lax.ppermute(
            lax.dynamic_slice_in_dim(values, (1 - core) * half, half, 1), "expert", pair
        )

    def join_halves(mine, sibling):
        other = lax.ppermute(sibling, "expert", pair)
        return jnp.where(
            core == 0,
            jnp.concatenate([mine, other], axis=1),
            jnp.concatenate([other, mine], axis=1),
        )

    heads = half // HEAD
    query_sets = [queries]
    starts = jnp.zeros((2,), jnp.int32)
    if att_copies == 1:
        query_sets.append(far_half(queries))
        starts = jnp.stack([core * heads, 0]).astype(jnp.int32)
    *att_outs, lse = attention_forward(
        query_sets, starts // 2, keys_all, values_all, key_info, query_info, heads
    )
    att_rows = join_halves(*att_outs) if att_copies == 1 else att_outs[0]
    att_partial = lax.dot_general(
        att_rows, o_weight, (((1,), (1,)), ((), ())), preferred_element_type=f32
    ).astype(bf16)
    att_back = exchange(att_partial.reshape(devices, att_capacity, D))
    att_picks, att_first, att_second = token_picks(att_routes, ATT_EXPERTS, att_capacity)
    att_gates = gate_values(hidden, att_router, att_first, att_second)
    if att_copies > 1:
        att_back = (
            att_back.astype(f32).reshape(ATT_EXPERTS, att_copies, att_capacity, D).sum(axis=1).astype(bf16)
        )
    att_branches = read_slots(att_picks, att_back)
    x_mid = x_in + att_gates[:, 0:1] * att_branches[0] + att_gates[:, 1:2] * att_branches[1]

    normed_two, inverse_two = rms_parts(x_mid)
    hidden_two = (normed_two * gain_two).astype(bf16)
    ffn_picks, ffn_first, ffn_second = token_picks(ffn_routes, FFN_EXPERTS, ffn_capacity)
    ffn_gates = gate_values(hidden_two, ffn_router, ffn_first, ffn_second)

    def to_experts(slots):
        rows = exchange(slots.reshape(devices, ffn_capacity // ffn_copies, D))
        return group_gather(rows.reshape(-1, D), ffn_copies, devices)

    def to_tokens(partial):
        rows = group_reduce(partial.astype(bf16), ffn_copies, devices)
        back = exchange(rows.reshape(devices, ffn_capacity // ffn_copies, D))
        return read_slots(ffn_picks, back.reshape(FFN_EXPERTS, ffn_capacity, D))

    ffn_inputs = to_experts(
        jnp.einsum(
            "ecr,rd->ecd", ffn_picks[0] + ffn_picks[1], hidden_two, preferred_element_type=f32
        ).astype(bf16)
    )
    gate_pre = jnp.dot(ffn_inputs, gate_weight, preferred_element_type=f32)
    up_pre = jnp.dot(ffn_inputs, up_weight, preferred_element_type=f32)
    sigmoid_gate = jax.nn.sigmoid(gate_pre)
    silu_gate = gate_pre * sigmoid_gate
    activated = (silu_gate * up_pre).astype(bf16)
    ffn_branches = to_tokens(
        lax.dot_general(activated, down_weight, (((1,), (1,)), ((), ())), preferred_element_type=f32)
    )
    result = x_mid + ffn_gates[:, 0:1] * ffn_branches[0] + ffn_gates[:, 1:2] * ffn_branches[1]

    tree_global = my_replica * parent.shape[0] + own_places // TREE_LEN
    tree_labels = jnp.arange(valid.shape[0], dtype=jnp.int32)
    limits = jnp.sum(
        jnp.where(tree_global[:, None] == tree_labels[None, :], valid[None, :], 0), axis=1
    )
    counted = own_places % TREE_LEN < limits
    loss_factor = valid.shape[0] * TREE_LEN / jnp.sum(valid).astype(f32)
    grad_result = jnp.where(counted[:, None], (result - teacher.astype(f32)) * loss_factor, 0.0)

    ffn_gate_grad, ffn_scaled = pair_grads(ffn_gates, ffn_branches, grad_result)
    grad_ffn_out = to_experts(fill_slots(ffn_picks, ffn_scaled))
    grad_down = dot_tn(grad_ffn_out, activated).astype(bf16)
    grad_ffn_out, grad_down = lax.optimization_barrier((grad_ffn_out, grad_down))
    summed_down = lax.psum_scatter(grad_down, "dp", scatter_dimension=0, tiled=True)
    grad_activated = jnp.dot(grad_ffn_out, down_weight, preferred_element_type=f32)
    grad_gate_pre = (
        grad_activated * up_pre * sigmoid_gate * (1.0 + gate_pre * (1.0 - sigmoid_gate))
    ).astype(bf16)
    grad_up_pre = (grad_activated * silu_gate).astype(bf16)
    grad_ffn_in = lax.dot_general(
        grad_gate_pre, gate_weight, (((1,), (1,)), ((), ())), preferred_element_type=f32
    ) + lax.dot_general(
        grad_up_pre, up_weight, (((1,), (1,)), ((), ())), preferred_element_type=f32
    )
    grad_gate = dot_tn(ffn_inputs, grad_gate_pre).astype(bf16)
    grad_up = dot_tn(ffn_inputs, grad_up_pre).astype(bf16)
    summed_gate = lax.psum_scatter(grad_gate, "dp", scatter_dimension=0, tiled=True)
    summed_up = lax.psum_scatter(grad_up, "dp", scatter_dimension=0, tiled=True)
    ffn_grad_pair = to_tokens(grad_ffn_in)
    grad_ffn_router, hidden_two_extra = router_grads(
        hidden_two, ffn_router, ffn_gates, ffn_first, ffn_second, ffn_gate_grad
    )
    grad_hidden_two = ffn_grad_pair[0] + ffn_grad_pair[1] + hidden_two_extra
    grad_gain_two = jnp.sum(grad_hidden_two * normed_two, axis=0)
    grad_mid = grad_result + norm_back(grad_hidden_two * gain_two, normed_two, inverse_two)

    att_gate_grad, att_scaled = pair_grads(att_gates, att_branches, grad_mid)
    att_slots = fill_slots(att_picks, att_scaled)
    if att_copies > 1:
        att_slots = jnp.repeat(att_slots, att_copies, axis=0)
    grad_att_out = exchange(att_slots).reshape(-1, D)
    grad_o = dot_tn(grad_att_out, att_rows).astype(bf16)
    grad_att_out, grad_o, grad_gate, grad_up = lax.optimization_barrier(
        (grad_att_out, grad_o, grad_gate, grad_up)
    )
    summed_o = lax.psum_scatter(grad_o, "dp", scatter_dimension=0, tiled=True)
    grad_heads = jnp.dot(grad_att_out, o_weight, preferred_element_type=f32).astype(bf16)
    grad_sets = [grad_heads]
    if att_copies == 1:
        grad_sets.append(far_half(grad_heads))
    *grad_queries, grad_keys, grad_values = attention_backward(
        query_sets,
        starts,
        grad_sets,
        att_outs,
        keys_all,
        values_all,
        lse,
        key_info,
        query_info,
        key_backward,
        [tables[1] for tables in slot_tables],
        heads,
    )
    grad_query_pre = join_halves(*grad_queries) if att_copies == 1 else grad_queries[0]
    grad_query_in = lax.dot_general(
        grad_query_pre, q_weight, (((1,), (1,)), ((), ())), preferred_element_type=f32
    ).astype(bf16)
    grad_q = dot_tn(query_inputs, grad_query_pre).astype(bf16)
    hidden_rows = gathered[:, :, :D].reshape(token_count, D)
    grad_kv = jnp.concatenate(
        [dot_tn(hidden_rows, grad_keys).astype(bf16), dot_tn(hidden_rows, grad_values).astype(bf16)], axis=1
    )
    summed_kv = lax.psum_scatter(grad_kv, "dp", scatter_dimension=0, tiled=True)
    summed_q = lax.psum_scatter(grad_q, "dp", scatter_dimension=0, tiled=True)

    merged = merge_hidden_grads(
        own_plan.transpose(0, 2, 1),
        grad_query_in.reshape(devices, att_capacity, D),
        grad_keys,
        grad_values,
        kv_blocks,
    ).reshape(devices // 2, 2, row_count, D)
    kept = lax.dynamic_index_in_dim(merged, core, 1, keepdims=False)
    passed = lax.ppermute(
        lax.dynamic_index_in_dim(merged, 1 - core, 1, keepdims=False), "expert", pair
    )
    chip_sum = (kept.astype(f32) + passed.astype(f32)).astype(bf16)
    same_core = [[2 * i + c for i in range(devices // 2)] for c in range(2)]
    arrived = lax.all_to_all(
        chip_sum, "expert", split_axis=0, concat_axis=0, axis_index_groups=same_core, tiled=True
    )
    grad_att_router, hidden_one_extra = router_grads(
        hidden, att_router, att_gates, att_first, att_second, att_gate_grad
    )
    grad_hidden_one = jnp.sum(arrived.astype(f32), axis=0) + hidden_one_extra
    grad_gain_one = jnp.sum(grad_hidden_one * normed_one, axis=0)
    grad_input = grad_mid + norm_back(grad_hidden_one * gain_one, normed_one, inverse_one)

    everyone = devices * replicas
    smalls = [grad_gain_one, grad_gain_two, grad_att_router, grad_ffn_router]
    packed = jnp.concatenate([small.reshape(everyone, -1) for small in smalls], axis=1)
    own_smalls = jnp.sum(
        lax.all_to_all(packed, ("dp", "expert"), split_axis=0, concat_axis=0, tiled=True), axis=0
    )
    share = D // everyone
    shared_gain_one = own_smalls[:share]
    shared_gain_two = own_smalls[share : 2 * share]
    shared_att_router = own_smalls[2 * share : (2 + ATT_EXPERTS) * share].reshape(share, ATT_EXPERTS)
    shared_ffn_router = own_smalls[(2 + ATT_EXPERTS) * share :].reshape(share, FFN_EXPERTS)

    kv_rows = exchange(summed_kv.reshape(devices, -1, 2 * half))
    kv_sum = jnp.sum(kv_rows.astype(f32).reshape(devices // 2, 2, -1, 2, half), axis=0)
    shared_kv = kv_sum.transpose(1, 2, 0, 3).reshape(-1, 4 * half)

    return (
        result.astype(bf16),
        grad_input.astype(bf16),
        shared_gain_one,
        shared_kv,
        shared_att_router,
        summed_q.astype(f32),
        summed_o.astype(f32),
        shared_gain_two,
        shared_ffn_router,
        summed_gate.astype(f32),
        summed_up.astype(f32),
        summed_down.astype(f32),
    )


def solution(mesh):
    in_specs = (
        P(("dp", "expert"), None),
        P(("dp", "expert"), None),
        P(("dp", "expert"), None),
        P(("dp", "expert"), None),
        P("dp", None),
        P(),
        P(),
        P("expert", None),
        P(),
        P(None, "expert"),
        P(None, "expert"),
        P(),
        P(),
        P(None, "expert"),
        P(None, "expert"),
        P(None, "expert"),
    )
    out_specs = (
        P(("dp", "expert"), None),
        P(("dp", "expert"), None),
        P(("dp", "expert")),
        P(("dp", "expert"), None),
        P(("dp", "expert"), None),
        P("dp", "expert"),
        P("dp", "expert"),
        P(("dp", "expert")),
        P(("dp", "expert"), None),
        P("dp", "expert"),
        P("dp", "expert"),
        P("dp", "expert"),
    )
    return jax.shard_map(body, mesh=mesh, in_specs=in_specs, out_specs=out_specs, check_vma=False)
```

time: 3120 us -> 1790 us (0.57)
  waiting for transfers between devices: 1850 us -> 877 us
  matrix products: 702 us -> 345 us
  Pallas kernels: 0 us -> 204 us
  blocking collectives: 304 us -> 138 us
    reduce_scatter x7 -> x6, waiting for transfers between devices: 862 us -> 377 us  [the longest x1 111 us: body(): lax.psum_scatter(grad_gate, 'dp', scatter_dimension=0, tiled=True)]
    dot_general x140 -> x26, matrix products: 598 us -> 245 us  [the longest x7 122 us: dot_tn(): lax.dot_general(left, right, (((0,), (0,)), ((), ())), preferred_element_...]
    all_to_all x7, waiting for transfers between devices: 566 us -> 307 us  [the longest x5 209 us: exchange(): lax.all_to_all(slots, 'expert', split_axis=0, concat_axis=0, tiled=True)]
    unnamed x13 -> x8, waiting for transfers between devices: 225 us -> 2.34 us
    pallas_call x0 -> x5, Pallas kernels: none -> 204 us  [the longest x1 80 us: attention_backward(): pl.pallas_call(functools.partial(attention_backward_body, sets, step_head...]
    all_to_all x2, blocking collectives: 262 us -> 138 us  [exchange(): lax.all_to_all(slots, 'expert', split_axis=0, concat_axis=0, tiled=True)]
    unnamed x1 -> x0, blocking collectives: 41.6 us -> none
    all_gather x2, waiting for transfers between devices: 196 us -> 157 us  [the longest x1 126 us: body(): gathered = lax.all_gather(sending, 'expert', axis=0)]
  transfers between devices with their start and end apart: 18 -> 24, of which waited for: 17 -> 19; matrix products, arithmetic and copies ran while one was open for 8% -> 11% of each run, Pallas kernels for 0% -> 4%
where the time goes in v1:
time: 1790 us; the launch traced here: 1780 us
  waiting for transfers between devices  877 us (49%)
  matrix products  345 us (19%)
  Pallas kernels  204 us (11%)
  blocking collectives  138 us (8%)
  other arithmetic  96.8 us (5%)
  local copies, waits for them, and re-layouts  70.9 us (4%)
  starting transfers between devices  32.8 us (2%)
    all_to_all x5, waiting for transfers between devices, exchange(): lax.all_to_all(slots, 'expert', split_axis=0, concat_axis=0, tiled=True)  209 us
    all_to_all x2, blocking collectives, exchange(): lax.all_to_all(slots, 'expert', split_axis=0, concat_axis=0, tiled=True)  138 us
    all_gather x1, waiting for transfers between devices, body(): gathered = lax.all_gather(sending, 'expert', axis=0)  126 us
    dot_general x7, matrix products, dot_tn(): lax.dot_general(left, right, (((0,), (0,)), ((), ())), preferred_element_...  122 us
    reduce_scatter x1, waiting for transfers between devices, body(): lax.psum_scatter(grad_gate, 'dp', scatter_dimension=0, tiled=True)  111 us
    reduce_scatter x1, waiting for transfers between devices, body(): summed_up = lax.psum_scatter(grad_up, 'dp', scatter_dimension=0, tiled=True)  100 us
    all_to_all x1, waiting for transfers between devices, body(): lax.all_to_all(chip_sum, 'expert', split_axis=0, concat_axis=0, axis_inde...  94.6 us
    reduce_scatter x1, waiting for transfers between devices, body(): summed_q = lax.psum_scatter(grad_q, 'dp', scatter_dimension=0, tiled=True)  85.3 us
  transfers between devices with their start and end apart: 24, of which 19 were waited for; matrix products, arithmetic and copies ran while one was open for 11% of the time, Pallas kernels for 4%

profile of v1, /device:TPU:0, one launch (start us, length us, event | category | flops | bytes accessed | tf_op | source)
XLA Modules:
  0.0 1780.9 jit_solution(66705179901543428)
XLA Ops:
  17.7 126.0 %all-gather.6.cloned.1.call-done = bf16[2176,3072]{1,0:T(8,128)(2,1)} async-done(((bf16[272,3072]{1,0:T(8,128)(2,1)}), bf16[2176,3072]{1,0:T(8,128)(2,1)}) %all-gather.6.cloned.1.call-update) | async-done | bytes 13369360 | tf_op jit(solution)/shard_map/all_gather | solution.py:543
  143.6 6.3 slice.162
  152.8 5.7 fusion.71
  176.5 7.6 convolution_convert_fusion.12
  184.1 11.3 project_queries.1.refs_0_
  206.8 30.7 %all-gather.4.cloned.1.call-done.weight_ref = bf16[4,2048,512]{2,1,0:T(8,128)(2,1)} async-done(((bf16[1,2048,512]{2,1,0:T(8,128)(2,1)}), bf16[4,2048,512]{2,1,0:T(8,128)(2,1)}) %all-gather.4.cloned.1.call-update) | async-done | bytes 8388624 | tf_op jit(solution)/shard_map/all_gather | solution.py:545
  237.5 26.0 %project_keys_values.1 = (bf16[2176,1024]{1,0:T(8,128)(2,1)}, bf16[2176,1024]{1,0:T(8,128)(2,1)}) custom-call(bf16[8,272,3072]{2,1,0:T(8,128)(2,1)} %bitcast.211, bf16[4,2048,512]{2,1,0:T(8,128)(2,1)} %all-gather.4.cloned.1.call-done.weight_ref, f32[2176,128]{1,0:T(8,128)} %get-tuple-element.176.cos_ref.refs_11_, f32[2176,128]{1,0:T(8,128)} %get-tuple-element.138.sin_ref), custom_call_target="tpu_custom_call" | custom-call | tf_op jit(solution)/shard_map/project_keys_values/pallas_call | solution.py:308
  263.5 57.1 %attention_forward.1 = (bf16[704,1024]{1,0:T(8,128)(2,1)}, bf16[704,1024]{1,0:T(8,128)(2,1)}, f32[8,4,352]{2,1,0:T(4,128)}) custom-call(s32[2]{0:T(128)} %and_select_fusion.6.first_ref, bf16[704,2048]{1,0:T(8,128)(2,1)} %project_queries.1.refs_0_, bf16[704,1024]{1,0:T(8,128)(2,1)} %collective-permute-done.refs_1_, ...), custom_call_target="tpu_custom_call" | custom-call | tf_op jit(solution)/shard_map/attention_forward/pallas_call | solution.py:185
  324.2 12.4 convolution_convert_fusion.10
  344.4 63.0 %all-to-all-done = bf16[8,88,2048]{2,1,0:T(8,128)(2,1)} async-done(((bf16[8,88,2048]{2,1,0:T(8,128)(2,1)}), bf16[8,88,2048]{2,1,0:T(8,128)(2,1)}, u32[]{:S(2)}, u32[]{:S(2)}) %all-to-all-start) | async-done | bytes 2883616 | tf_op jit(solution)/shard_map/all_to_all | solution.py:476
  416.0 68.8 %all_to_all.49 = bf16[8,88,2048]{2,1,0:T(8,128)(2,1)S(1)} all-to-all(bf16[8,88,2048]{2,1,0:T(8,128)(2,1)S(1)} %bitcast.237), channel_id=1, replica_groups=mesh['dp'=4,'expert'=8] {'expert'}, dimensions={0} | all-to-all | bytes 5767168 | tf_op jit(solution)/shard_map/all_to_all | solution.py:476
  484.8 5.3 collective-permute-done.2
  490.1 21.7 %fusion.181 = f32[1408,2816]{1,0:T(8,128)} fusion(bf16[2048,2816]{1,0:T(8,128)(2,1)S(1)} %bitcast.246, bf16[704,2048]{1,0:T(8,128)(2,1)S(1)} %collective-permute-done.2, bf16[704,2048]{1,0:T(8,128)(2,1)S(1)} %bitcast.230), kind=kOutput, calls=%fused_computation.363 | convolution fusion | flops 16251879424 | bytes 33161216 | tf_op jit(solution)/shard_map/dot_general | solution.py:632
  511.8 27.6 %multiply_convert_fusion.2 = (bf16[1408,2816]{1,0:T(8,128)(2,1)}, f32[1408,2816]{1,0:T(8,128)}) fusion(f32[1408,2816]{1,0:T(8,128)} %fusion.181, bf16[2048,2816]{1,0:T(8,128)(2,1)} %param.30, bf16[704,2048]{1,0:T(8,128)(2,1)S(1)} %collective-permute-done.2, bf16[704,2048]{1,0:T(8,128)(2,1)S(1)} %bitcast.231), kind=kOutput, calls=%fused_computation.2 | convolution fusion | flops 16275668992 | bytes 56950784 | tf_op jit(solution)/shard_map/dot_general | solution.py:633
  539.4 21.6 %convolution_convert_fusion.5 = bf16[1408,2048]{1,0:T(8,128)(2,1)S(1)} fusion(bf16[1408,2816]{1,0:T(8,128)(2,1)} %get-tuple-element.169, bf16[2048,2816]{1,0:T(8,128)(2,1)} %param.31), kind=kOutput, calls=%fused_computation.15 | convolution fusion | flops 16243228672 | bytes 25231360 | tf_op jit(solution)/shard_map/dot_general | solution.py:638
  561.5 5.2 collective-permute-done.3
  577.3 62.7 %all-to-all-done.2 = bf16[8,88,2048]{2,1,0:T(8,128)(2,1)} async-done(((bf16[8,88,2048]{2,1,0:T(8,128)(2,1)}), bf16[8,88,2048]{2,1,0:T(8,128)(2,1)}, u32[]{:S(2)}, u32[]{:S(2)}) %all-to-all-start.2) | async-done | bytes 2883616 | tf_op jit(solution)/shard_map/all_to_all | solution.py:476
  649.7 68.9 %all_to_all.50 = bf16[8,88,2048]{2,1,0:T(8,128)(2,1)S(1)} all-to-all(bf16[8,88,2048]{2,1,0:T(8,128)(2,1)S(1)} %bitcast.236), channel_id=1, replica_groups=mesh['dp'=4,'expert'=8] {'expert'}, dimensions={0} | all-to-all | bytes 5767168 | tf_op jit(solution)/shard_map/all_to_all | solution.py:476
  718.6 5.3 collective-permute-done.4
  725.5 21.4 %convolution_convert_fusion.2 = bf16[2048,2816]{1,0:T(8,128)(2,1)} fusion(bf16[1408,2816]{1,0:T(8,128)(2,1)S(1)} %bitcast.248, bf16[704,2048]{1,0:T(8,128)(2,1)S(1)} %collective-permute-done.4, bf16[704,2048]{1,0:T(8,128)(2,1)S(1)} %bitcast.218), kind=kOutput, calls=%fused_computation.8 | convolution fusion | flops 16257646592 | bytes 25231360 | tf_op jit(solution)/shard_map/dot_general | solution.py:497
  746.9 5.2 pad_maximum_fusion.2
  752.1 30.7 %multiply_convert_fusion = (bf16[1408,2816]{1,0:T(8,128)(2,1)}, bf16[1408,2816]{1,0:T(8,128)(2,1)}) fusion(f32[1408,2816]{1,0:T(8,128)} %fusion.181, f32[1408,2816]{1,0:T(8,128)} %get-tuple-element.170, bf16[1408,2048]{1,0:T(8,128)(2,1)} %pad_maximum_fusion.2, bf16[2048,2816]{1,0:T(8,128)(2,1)} %param.31), kind=kOutput, calls=%fused_computation | convolution fusion | flops 16291889152 | bytes 64880640 | tf_op jit(solution)/shard_map/dot_general | solution.py:656
  782.8 23.2 %fusion.187 = f32[1408,2048]{1,0:T(8,128)} fusion(bf16[1408,2816]{1,0:T(8,128)(2,1)} %get-tuple-element.144, bf16[2048,2816]{1,0:T(8,128)(2,1)} %param.29), kind=kOutput, calls=%fused_computation.368 | convolution fusion | flops 16240345088 | bytes 30998528 | tf_op jit(solution)/shard_map/dot_general | solution.py:661
  805.9 24.5 %add_convert_fusion = bf16[1408,2048]{1,0:T(8,128)(2,1)} fusion(f32[1408,2048]{1,0:T(8,128)} %fusion.187, bf16[1408,2816]{1,0:T(8,128)(2,1)} %get-tuple-element.143, bf16[2048,2816]{1,0:T(8,128)(2,1)} %param.30), kind=kOutput, calls=%fused_computation.5 | convolution fusion | flops 16246112256 | bytes 36765696 | tf_op jit(solution)/shard_map/dot_general | solution.py:663
  832.9 5.2 collective-permute-done.5
  845.1 65.6 %all-to-all-done.4 = bf16[8,88,2048]{2,1,0:T(8,128)(2,1)S(1)} async-done(((bf16[8,88,2048]{2,1,0:T(8,128)(2,1)}), bf16[8,88,2048]{2,1,0:T(8,128)(2,1)S(1)}, u32[]{:S(2)}, u32[]{:S(2)}) %all-to-all-start.4) | async-done | bytes 2883616 | tf_op jit(solution)/shard_map/all_to_all | solution.py:476
  928.5 24.3 %convolution_convert_fusion = bf16[2048,2816]{1,0:T(8,128)(2,1)} fusion(bf16[1408,2816]{1,0:T(8,128)(2,1)} %get-tuple-element.143, bf16[704,2048]{1,0:T(8,128)(2,1)} %copy-done.89, bf16[704,2048]{1,0:T(8,128)(2,1)S(1)} %bitcast.232), kind=kOutput, calls=%fused_computation.6 | convolution fusion | flops 16257646592 | bytes 25231360 | tf_op jit(solution)/shard_map/dot_general | solution.py:497
  952.8 24.0 %convolution_convert_fusion.1 = bf16[2048,2816]{1,0:T(8,128)(2,1)} fusion(bf16[1408,2816]{1,0:T(8,128)(2,1)} %get-tuple-element.144, bf16[704,2048]{1,0:T(8,128)(2,1)} %copy-done.89, bf16[704,2048]{1,0:T(8,128)(2,1)S(1)} %bitcast.233), kind=kOutput, calls=%fused_computation.7 | convolution fusion | flops 16257646592 | bytes 25231360 | tf_op jit(solution)/shard_map/dot_general | solution.py:497
  976.7 17.6 all-to-all-done.5
  994.4 13.2 convolution_convert_fusion.4
  1007.6 9.4 convolution_convert_fusion.9.refs_2_
  1019.0 8.8 slice.161
  1030.1 80.0 %attention_backward.1 = (bf16[704,1024]{1,0:T(8,128)(2,1)}, bf16[704,1024]{1,0:T(8,128)(2,1)}, bf16[2176,1024]{1,0:T(8,128)(2,1)}, bf16[2176,1024]{1,0:T(8,128)(2,1)}) custom-call(s32[2]{0:T(128)} %pad_add_fusion.1.first_ref, bf16[704,2048]{1,0:T(8,128)(2,1)} %project_queries.1.refs_0_, bf16[704,1024]{1,0:T(8,128)(2,1)} %collective-permute-done.refs_1_, ...), custom_call_target="tpu_custom_call" | custom-call | tf_op jit(solution)/shard_map/attention_backward/pallas_call | solution.py:219
  1110.2 15.3 convolution_convert_fusion.6
  1125.5 12.0 convolution_convert_fusion.7
  1137.6 8.4 pad_maximum_fusion
  1152.3 11.9 convolution_convert_fusion.3
  1165.6 11.6 convolution_convert_fusion.8
  1177.2 29.2 %merge_hidden_grads.1 = bf16[2176,2048]{1,0:T(8,128)(2,1)} custom-call(bf16[8,272,88]{2,1,0:T(8,128)(2,1)} %fusion.48.plan_ref, bf16[8,88,2048]{2,1,0:T(8,128)(2,1)} %bitcast.238, bf16[2176,1024]{1,0:T(8,128)(2,1)} %get-tuple-element.34.dk_ref, bf16[2176,1024]{1,0:T(8,128)(2,1)} %get-tuple-element.35.dv_ref, ...), custom_call_target="tpu_custom_call" | custom-call | tf_op jit(solution)/shard_map/merge_hidden_grads/pallas_call | solution.py:351
  1212.2 7.5 collective-permute-done.8
  1219.7 8.3 fusion.1
  1228.0 5.1 all-to-all-start.6
  1238.1 94.6 %all-to-all-done.6 = bf16[4,272,2048]{2,1,0:T(8,128)(2,1)} async-done(((bf16[4,272,2048]{2,1,0:T(8,128)(2,1)}), bf16[4,272,2048]{2,1,0:T(8,128)(2,1)}, u32[]{:S(2)}, u32[]{:S(2)}) %all-to-all-start.6) | async-done | bytes 4456480 | tf_op jit(solution)/shard_map/all_to_all | solution.py:731
  1361.2 100.2 %reduce-scatter.15.cloned.1.call-done = bf16[512,2816]{1,0:T(8,128)(2,1)} async-done(((bf16[2048,2816]{1,0:T(8,128)(2,1)}), bf16[512,2816]{1,0:T(8,128)(2,1)}) %reduce-scatter.15.cloned.1.call-update) | async-done | bytes 2883600 | tf_op jit(solution)/shard_map/reduce_scatter | solution.py:669
  1466.2 110.7 %reduce-scatter.13.cloned.1.call-done = bf16[512,2816]{1,0:T(8,128)(2,1)} async-done(((bf16[2048,2816]{1,0:T(8,128)(2,1)}), bf16[512,2816]{1,0:T(8,128)(2,1)}) %reduce-scatter.13.cloned.1.call-update) | async-done | bytes 2883600 | tf_op jit(solution)/shard_map/reduce_scatter | solution.py:668
  1585.6 81.1 %reduce-scatter.11.cloned.1.call-done = bf16[512,2048]{1,0:T(8,128)(2,1)} async-done(((bf16[2048,2048]{1,0:T(8,128)(2,1)}), bf16[512,2048]{1,0:T(8,128)(2,1)}) %reduce-scatter.11.cloned.1.call-update) | async-done | bytes 2097168 | tf_op jit(solution)/shard_map/reduce_scatter | solution.py:687
  1670.8 85.3 %reduce-scatter.9.cloned.1.call-done = bf16[512,2048]{1,0:T(8,128)(2,1)} async-done(((bf16[2048,2048]{1,0:T(8,128)(2,1)}), bf16[512,2048]{1,0:T(8,128)(2,1)}) %reduce-scatter.9.cloned.1.call-update) | async-done | bytes 2097168 | tf_op jit(solution)/shard_map/reduce_scatter | solution.py:716
  1760.2 6.6 reshape.734
  (386 shorter events, 190.3 us)
Async XLA Ops:
  7.2 334.2 %copy-start = (f32[2048,8]{0,1:T(8,128)S(1)}, f32[2048,8]{0,1:T(8,128)}, u32[]{:S(2)}) copy-start(f32[2048,8]{0,1:T(8,128)} %param.24) | copy-start | bytes 196612
  7.2 136.4 %all-gather.6.cloned.1.call-start = ((), (), s32[]{:S(2)}) async-start(), calls=%async_computation.22 | async-start | bytes 15040512 | tf_op jit(solution)/shard_map/all_gather | solution.py:543
  16.1 325.3 %copy-start.11 = (bf16[272,2048]{1,0:T(8,128)(2,1)}, bf16[272,2048]{1,0:T(8,128)(2,1)S(1)}, u32[]{:S(2)}) copy-start(bf16[272,2048]{1,0:T(8,128)(2,1)S(1)} %fusion.26) | copy-start | bytes 3342340
  17.6 219.9 %all-gather.4.cloned.1.call-start = ((), (), s32[]{:S(2)}) async-start(), calls=%async_computation.15 | async-start | bytes 10485760 | tf_op jit(solution)/shard_map/all_gather | solution.py:545
  198.0 65.5 %collective-permute-start = (bf16[704,1024]{1,0:T(8,128)(2,1)}, bf16[704,1024]{1,0:T(8,128)(2,1)}, u32[]{:S(2)}, u32[]{:S(2)}) collective-permute-start(bf16[704,1024]{1,0:T(8,128)(2,1)} %constant_dynamic-slice_fusion.2), channel_id=1, source_target_pairs={{0,1},{1,0},{2,3},{3,2},{4,5},{5,4},{6,7},{7,6},{8,9},{9,8},{10,11... | collective-permute-start | bytes 4325384 | tf_op jit(solution)/shard_map/ppermute | solution.py:578
  320.6 3.6 collective-permute-start.1
  336.6 70.8 %all-to-all-start = ((bf16[8,88,2048]{2,1,0:T(8,128)(2,1)}), bf16[8,88,2048]{2,1,0:T(8,128)(2,1)}, u32[]{:S(2)}, u32[]{:S(2)}) async-start(bf16[8,88,2048]{2,1,0:T(8,128)(2,1)} %bitcast.234), calls=%async_computation | async-start | bytes 5767168 | tf_op jit(solution)/shard_map/all_to_all | solution.py:476
  341.4 69.8 %copy-start.79 = (pred[2,8,272]{2,0,1:T(4,128)(4,1)}, pred[2,8,272]{2,0,1:T(4,128)(4,1)S(1)}, u32[]{:S(2)}) copy-start(pred[2,8,272]{2,0,1:T(4,128)(4,1)S(1)} %copy.109) | copy-start | bytes 13060
  342.6 68.6 %copy-start.75 = (f32[272]{0:T(512)}, f32[272]{0:T(512)S(1)}, u32[]{:S(2)}) copy-start(f32[272]{0:T(512)S(1)} %get-tuple-element.130) | copy-start | bytes 3268
  342.6 68.6 %copy-start.77 = (f32[272]{0:T(512)}, f32[272]{0:T(512)S(1)}, u32[]{:S(2)}) copy-start(f32[272]{0:T(512)S(1)} %get-tuple-element.131) | copy-start | bytes 3268
  344.2 67.0 %copy-start.31 = (pred[8,88,272]{2,1,0:T(8,128)(4,1)}, pred[8,88,272]{2,1,0:T(8,128)(4,1)S(1)}, u32[]{:S(2)}) copy-start(pred[8,88,272]{2,1,0:T(8,128)(4,1)S(1)} %iota_compare_fusion.6) | copy-start | bytes 574468
  411.2 78.9 %slice-start.5 = ((s8[11534336]{0:T(1024)(128)(4,1)}), s8[4194304]{0:T(1024)(128)(4,1)S(1)}, s32[]{:S(2)}) async-start(s8[11534336]{0:T(1024)(128)(4,1)} %bitcast.245), calls=%async_computation.28 | async-start | bytes 8388608
  411.3 78.9 %slice-start.6 = ((s8[11534336]{0:T(1024)(128)(4,1)}), s8[4194304]{0:T(1024)(128)(4,1)S(1)}, s32[]{:S(2)}) async-start(s8[11534336]{0:T(1024)(128)(4,1)} %bitcast.245), calls=%async_computation.29 | async-start | bytes 8388608
  414.3 75.8 %slice-start.7 = ((s8[11534336]{0:T(1024)(128)(4,1)}), s8[3145728]{0:T(1024)(128)(4,1)S(1)}, s32[]{:S(2)}) async-start(s8[11534336]{0:T(1024)(128)(4,1)} %bitcast.245), calls=%async_computation.30 | async-start | bytes 6291456
  484.8 27.0 %copy-start.23 = (bf16[8,88,2048]{2,1,0:T(8,128)(2,1)}, bf16[8,88,2048]{2,1,0:T(8,128)(2,1)S(1)}, u32[]{:S(2)}) copy-start(bf16[8,88,2048]{2,1,0:T(8,128)(2,1)S(1)} %all_to_all.49) | copy-start | bytes 8650756
  484.8 5.3 collective-permute-start.2
  490.1 21.7 %copy-start.89 = (bf16[704,2048]{1,0:T(8,128)(2,1)}, bf16[704,2048]{1,0:T(8,128)(2,1)S(1)}, u32[]{:S(2)}) copy-start(bf16[704,2048]{1,0:T(8,128)(2,1)S(1)} %collective-permute-done.2) | copy-start | bytes 8650756
  561.3 5.3 collective-permute-start.3
  569.5 70.5 %copy-start.29 = (pred[4,176,272]{2,1,0:T(8,128)(4,1)S(1)}, pred[4,176,272]{2,1,0:T(8,128)(4,1)}, u32[]{:S(2)}) copy-start(pred[4,176,272]{2,1,0:T(8,128)(4,1)} %copy-done.28) | copy-start | bytes 574468
  569.5 70.5 %all-to-all-start.2 = ((bf16[8,88,2048]{2,1,0:T(8,128)(2,1)}), bf16[8,88,2048]{2,1,0:T(8,128)(2,1)}, u32[]{:S(2)}, u32[]{:S(2)}) async-start(bf16[8,88,2048]{2,1,0:T(8,128)(2,1)} %bitcast.30), calls=%async_computation.2 | async-start | bytes 5767168 | tf_op jit(solution)/shard_map/all_to_all | solution.py:476
  577.2 66.8 %copy-start.65 = (f32[272]{0:T(512)}, f32[272]{0:T(512)S(1)}, u32[]{:S(2)}) copy-start(f32[272]{0:T(512)S(1)} %fusion.172) | copy-start | bytes 3268
  646.9 78.5 %slice-start.8 = ((s8[7929856]{0:T(1024)(128)(4,1)}), s8[4194304]{0:T(1024)(128)(4,1)S(1)}, s32[]{:S(2)}) async-start(s8[7929856]{0:T(1024)(128)(4,1)} %bitcast.247), calls=%async_computation.31 | async-start | bytes 8388608
  647.2 78.2 %slice-start.9 = ((s8[7929856]{0:T(1024)(128)(4,1)}), s8[3735552]{0:T(1024)(128)(4,1)S(1)}, s32[]{:S(2)}) async-start(s8[7929856]{0:T(1024)(128)(4,1)} %bitcast.247), calls=%async_computation.32 | async-start | bytes 7471104
  718.6 5.3 collective-permute-start.4
  832.7 5.3 collective-permute-start.5
  840.9 69.9 %copy-start.30 = (pred[4,176,272]{2,1,0:T(8,128)(4,1)S(1)}, pred[4,176,272]{2,1,0:T(8,128)(4,1)}, u32[]{:S(2)}) copy-start(pred[4,176,272]{2,1,0:T(8,128)(4,1)} %copy-done.28) | copy-start | bytes 574468
  840.9 69.8 %copy-start.57 = (pred[2,4,272]{2,1,0:T(4,128)(4,1)S(1)}, pred[2,4,272]{2,1,0:T(4,128)(4,1)}, u32[]{:S(2)}) copy-start(pred[2,4,272]{2,1,0:T(4,128)(4,1)} %copy-done.55) | copy-start | bytes 6532
  840.9 69.8 %all-to-all-start.4 = ((bf16[8,88,2048]{2,1,0:T(8,128)(2,1)}), bf16[8,88,2048]{2,1,0:T(8,128)(2,1)S(1)}, u32[]{:S(2)}, u32[]{:S(2)}) async-start(bf16[8,88,2048]{2,1,0:T(8,128)(2,1)} %bitcast.44), calls=%async_computation.4 | async-start | bytes 5767168 | tf_op jit(solution)/shard_map/all_to_all | solution.py:476
  845.1 67.8 %copy-start.71 = (f32[272]{0:T(512)}, f32[272]{0:T(512)S(1)}, u32[]{:S(2)}) copy-start(f32[272]{0:T(512)S(1)} %get-tuple-element.126) | copy-start | bytes 3268
  845.1 67.8 %copy-start.73 = (f32[272]{0:T(512)}, f32[272]{0:T(512)S(1)}, u32[]{:S(2)}) copy-start(f32[272]{0:T(512)S(1)} %get-tuple-element.127) | copy-start | bytes 3268
  923.7 70.6 %all-to-all-start.5 = ((bf16[8,88,2048]{2,1,0:T(8,128)(2,1)}), bf16[8,88,2048]{2,1,0:T(8,128)(2,1)}, u32[]{:S(2)}, u32[]{:S(2)}) async-start(bf16[8,88,2048]{2,1,0:T(8,128)(2,1)} %bitcast_convert_fusion), calls=%async_computation.5 | async-start | bytes 5767168 | tf_op jit(solution)/shard_map/all_to_all | solution.py:476
  928.4 415.4 %reduce-scatter.7.cloned.1.call-start = ((), (), s32[]{:S(2)}) async-start(), calls=%async_computation.16 | async-start | bytes 10485760 | tf_op jit(solution)/shard_map/reduce_scatter | solution.py:715
  1018.4 11.7 collective-permute-start.6
  1030.1 95.4 %slice-start.2 = ((s8[8912896]{0:T(1024)(128)(4,1)}), s8[524288]{0:T(1024)(128)(4,1)S(1)}, s32[]{:S(2)}) async-start(s8[8912896]{0:T(1024)(128)(4,1)} %bitcast.221), calls=%async_computation.25 | async-start | bytes 1048576
  1146.0 210.5 %reduce-scatter.17.cloned.1.call-start = ((), (), s32[]{:S(2)}) async-start(), calls=%async_computation.21 | async-start | bytes 14417920 | tf_op jit(solution)/shard_map/reduce_scatter | solution.py:655
  1146.5 314.9 %reduce-scatter.15.cloned.1.call-start = ((), (), s32[]{:S(2)}) async-start(), calls=%async_computation.20 | async-start | bytes 14417920 | tf_op jit(solution)/shard_map/reduce_scatter | solution.py:669
  1147.1 429.7 %reduce-scatter.13.cloned.1.call-start = ((), (), s32[]{:S(2)}) async-start(), calls=%async_computation.19 | async-start | bytes 14417920 | tf_op jit(solution)/shard_map/reduce_scatter | solution.py:668
  1147.7 518.9 %reduce-scatter.11.cloned.1.call-start = ((), (), s32[]{:S(2)}) async-start(), calls=%async_computation.18 | async-start | bytes 10485760 | tf_op jit(solution)/shard_map/reduce_scatter | solution.py:687
  1148.5 607.6 %reduce-scatter.9.cloned.1.call-start = ((), (), s32[]{:S(2)}) async-start(), calls=%async_computation.17 | async-start | bytes 10485760 | tf_op jit(solution)/shard_map/reduce_scatter | solution.py:716
  1148.5 3.8 collective-permute-start.7
  1211.5 8.2 collective-permute-start.8
  1228.0 104.7 %all-to-all-start.6 = ((bf16[4,272,2048]{2,1,0:T(8,128)(2,1)}), bf16[4,272,2048]{2,1,0:T(8,128)(2,1)}, u32[]{:S(2)}, u32[]{:S(2)}) async-start(bf16[4,272,2048]{2,1,0:T(8,128)(2,1)} %fusion.1), calls=%async_computation.6 | async-start | bytes 8912896 | tf_op jit(solution)/shard_map/all_to_all | solution.py:731
  1238.1 98.1 %copy-start.5 = (bf16[272,2048]{1,0:T(8,128)(2,1)S(1)}, bf16[272,2048]{1,0:T(8,128)(2,1)}, u32[]{:S(2)}) copy-start(bf16[272,2048]{1,0:T(8,128)(2,1)} %param.16) | copy-start | bytes 3342340
  1238.1 98.1 %copy-start.40 = (f32[2048]{0:T(1024)S(1)}, f32[2048]{0:T(1024)}, u32[]{:S(2)}) copy-start(f32[2048]{0:T(1024)} %param.22) | copy-start | bytes 24580
  1238.1 98.1 %copy-start.61 = (f32[272]{0:T(512)S(1)}, f32[272]{0:T(512)}, u32[]{:S(2)}) copy-start(f32[272]{0:T(512)} %copy-done.60) | copy-start | bytes 3268
  1341.1 10.7 all-to-all-start.7
  1351.8 408.4 %all-to-all-start.8 = ((bf16[8,64,2048]{2,1,0:T(8,128)(2,1)}), bf16[8,64,2048]{2,1,0:T(8,128)(2,1)}, u32[]{:S(2)}, u32[]{:S(2)}) async-start(bf16[8,64,2048]{2,1,0:T(8,128)(2,1)} %bitcast.66), calls=%async_computation.9 | async-start | bytes 4194304 | tf_op jit(solution)/shard_map/all_to_all | solution.py:476
  1466.2 115.6 %copy-start.9 = (f32[272,2048]{1,0:T(8,128)S(1)}, f32[272,2048]{1,0:T(8,128)}, u32[]{:S(2)}) copy-start(f32[272,2048]{1,0:T(8,128)} %copy-done.8) | copy-start | bytes 6684676
  (77 other events, 319.8 us)
Sparse Core Ops, SparseCore 0:
  17.7 125.8 all-gather.5
  151.6 85.8 all-gather.3
  1146.1 84.4 reduce-scatter.6
  1233.8 112.0 reduce-scatter.16
  1349.2 112.1 reduce-scatter.14
  1464.7 112.1 reduce-scatter.12
  1580.2 86.4 reduce-scatter.10
  1669.7 86.3 reduce-scatter.8

commit v2 on v1

--- a/solution.py
+++ b/solution.py
@@ -668,6 +668,7 @@
     summed_gate = lax.psum_scatter(grad_gate, "dp", scatter_dimension=0, tiled=True)
     summed_up = lax.psum_scatter(grad_up, "dp", scatter_dimension=0, tiled=True)
     ffn_grad_pair = to_tokens(grad_ffn_in)
+    ffn_grad_pair, grad_gate, grad_up = lax.optimization_barrier((ffn_grad_pair, grad_gate, grad_up))
     grad_ffn_router, hidden_two_extra = router_grads(
         hidden_two, ffn_router, ffn_gates, ffn_first, ffn_second, ffn_gate_grad
     )
@@ -677,18 +678,18 @@
 
     att_gate_grad, att_scaled = pair_grads(att_gates, att_branches, grad_mid)
     att_slots = fill_slots(att_picks, att_scaled)
+    att_slots, summed_down = lax.optimization_barrier((att_slots, summed_down))
     if att_copies > 1:
         att_slots = jnp.repeat(att_slots, att_copies, axis=0)
     grad_att_out = exchange(att_slots).reshape(-1, D)
     grad_o = dot_tn(grad_att_out, att_rows).astype(bf16)
-    grad_att_out, grad_o, grad_gate, grad_up = lax.optimization_barrier(
-        (grad_att_out, grad_o, grad_gate, grad_up)
-    )
+    grad_att_out, grad_o = lax.optimization_barrier((grad_att_out, grad_o))
     summed_o = lax.psum_scatter(grad_o, "dp", scatter_dimension=0, tiled=True)
     grad_heads = jnp.dot(grad_att_out, o_weight, preferred_element_type=f32).astype(bf16)
     grad_sets = [grad_heads]
     if att_copies == 1:
         grad_sets.append(far_half(grad_heads))
+    grad_sets[-1], summed_gate = lax.optimization_barrier((grad_sets[-1], summed_gate))
     *grad_queries, grad_keys, grad_values = attention_backward(
         query_sets,
         starts,
@@ -708,6 +709,7 @@
         grad_query_pre, q_weight, (((1,), (1,)), ((), ())), preferred_element_type=f32
     ).astype(bf16)
     grad_q = dot_tn(query_inputs, grad_query_pre).astype(bf16)
+    grad_query_in, summed_up = lax.optimization_barrier((grad_query_in, summed_up))
     hidden_rows = gathered[:, :, :D].reshape(token_count, D)
     grad_kv = jnp.concatenate(
         [dot_tn(hidden_rows, grad_keys).astype(bf16), dot_tn(hidden_rows, grad_values).astype(bf16)], axis=1
@@ -731,6 +733,7 @@
     arrived = lax.all_to_all(
         chip_sum, "expert", split_axis=0, concat_axis=0, axis_index_groups=same_core, tiled=True
     )
+    arrived, summed_kv = lax.optimization_barrier((arrived, summed_kv))
     grad_att_router, hidden_one_extra = router_grads(
         hidden, att_router, att_gates, att_first, att_second, att_gate_grad
     )

time: 1790 us -> 1490 us (0.83)
  waiting for transfers between devices: 877 us -> 505 us
  blocking collectives: 138 us -> 208 us
    reduce_scatter x1, waiting for transfers between devices: 111 us -> 0.01 us  [body(): lax.psum_scatter(grad_gate, 'dp', scatter_dimension=0, tiled=True)]
    reduce_scatter x1, waiting for transfers between devices: 100 us -> 0.01 us  [body(): summed_up = lax.psum_scatter(grad_up, 'dp', scatter_dimension=0, tiled=True)]
    reduce_scatter x1, waiting for transfers between devices: 81.1 us -> 0.01 us  [body(): summed_o = lax.psum_scatter(grad_o, 'dp', scatter_dimension=0, tiled=True)]
    all_to_all x2 -> x3, blocking collectives: 138 us -> 208 us  [exchange(): lax.all_to_all(slots, 'expert', split_axis=0, concat_axis=0, tiled=True)]
    reduce_scatter x1, waiting for transfers between devices: 85.3 us -> 35 us  [body(): summed_q = lax.psum_scatter(grad_q, 'dp', scatter_dimension=0, tiled=True)]
    all_to_all x5 -> x4, waiting for transfers between devices: 209 us -> 191 us  [exchange(): lax.all_to_all(slots, 'expert', split_axis=0, concat_axis=0, tiled=True)]
  transfers between devices with their start and end apart: 24 -> 23, of which waited for: 19 -> 14; matrix products, arithmetic and copies ran while one was open for 11% -> 24% of each run, Pallas kernels for 4% -> 10%
where the time goes in v2:
time: 1490 us; the launch traced here: 1480 us
  waiting for transfers between devices  505 us (34%)
  matrix products  349 us (23%)
  blocking collectives  208 us (14%)
  Pallas kernels  204 us (14%)
  other arithmetic  94.6 us (6%)
  local copies, waits for them, and re-layouts  77.4 us (5%)
  starting transfers between devices  28.8 us (2%)
  between operations  16.6 us (1%)
    all_to_all x3, blocking collectives, exchange(): lax.all_to_all(slots, 'expert', split_axis=0, concat_axis=0, tiled=True)  208 us
    all_to_all x4, waiting for transfers between devices, exchange(): lax.all_to_all(slots, 'expert', split_axis=0, concat_axis=0, tiled=True)  191 us
    all_gather x1, waiting for transfers between devices, body(): gathered = lax.all_gather(sending, 'expert', axis=0)  126 us
    dot_general x7, matrix products, dot_tn(): lax.dot_general(left, right, (((0,), (0,)), ((), ())), preferred_element_...  120 us
    all_to_all x1, waiting for transfers between devices, body(): lax.all_to_all(chip_sum, 'expert', split_axis=0, concat_axis=0, axis_inde...  88.7 us
    pallas_call x1, Pallas kernels, attention_backward(): pl.pallas_call(functools.partial(attention_backward_body, sets, step_head...  80.1 us
    pallas_call x1, Pallas kernels, attention_forward(): pl.pallas_call(functools.partial(attention_forward_body, sets, step_heads...  57.2 us
    reduce_scatter x1, waiting for transfers between devices, body(): summed_q = lax.psum_scatter(grad_q, 'dp', scatter_dimension=0, tiled=True)  35 us
  transfers between devices with their start and end apart: 23, of which 14 were waited for; matrix products, arithmetic and copies ran while one was open for 24% of the time, Pallas kernels for 10%

profile of v2, /device:TPU:0, one launch (start us, length us, event | category | flops | bytes accessed | tf_op | source)
XLA Modules:
  0.0 1482.5 jit_solution(2324810522439214845)
XLA Ops:
  17.6 126.0 %all-gather.6.cloned.1.call-done = bf16[2176,3072]{1,0:T(8,128)(2,1)} async-done(((bf16[272,3072]{1,0:T(8,128)(2,1)}), bf16[2176,3072]{1,0:T(8,128)(2,1)}) %all-gather.6.cloned.1.call-update) | async-done | bytes 13369360 | tf_op jit(solution)/shard_map/all_gather | solution.py:543
  143.6 6.3 slice.162
  152.8 5.7 fusion.70
  176.5 7.7 convolution_convert_fusion.12
  184.2 11.3 project_queries.1.refs_0_
  206.9 30.6 %all-gather.4.cloned.1.call-done.weight_ref = bf16[4,2048,512]{2,1,0:T(8,128)(2,1)} async-done(((bf16[1,2048,512]{2,1,0:T(8,128)(2,1)}), bf16[4,2048,512]{2,1,0:T(8,128)(2,1)}) %all-gather.4.cloned.1.call-update) | async-done | bytes 8388624 | tf_op jit(solution)/shard_map/all_gather | solution.py:545
  237.5 25.6 %project_keys_values.1 = (bf16[2176,1024]{1,0:T(8,128)(2,1)}, bf16[2176,1024]{1,0:T(8,128)(2,1)}) custom-call(bf16[8,272,3072]{2,1,0:T(8,128)(2,1)} %bitcast.209, bf16[4,2048,512]{2,1,0:T(8,128)(2,1)} %all-gather.4.cloned.1.call-done.weight_ref, f32[2176,128]{1,0:T(8,128)} %get-tuple-element.196.cos_ref.refs_11_, f32[2176,128]{1,0:T(8,128)} %get-tuple-element.156.sin_ref), custom_call_target="tpu_custom_call" | custom-call | tf_op jit(solution)/shard_map/project_keys_values/pallas_call | solution.py:308
  263.1 57.2 %attention_forward.1 = (bf16[704,1024]{1,0:T(8,128)(2,1)}, bf16[704,1024]{1,0:T(8,128)(2,1)}, f32[8,4,352]{2,1,0:T(4,128)}) custom-call(s32[2]{0:T(128)} %get-tuple-element.191.first_ref, bf16[704,2048]{1,0:T(8,128)(2,1)} %project_queries.1.refs_0_, bf16[704,1024]{1,0:T(8,128)(2,1)} %collective-permute-done.refs_1_, ...), custom_call_target="tpu_custom_call" | custom-call | tf_op jit(solution)/shard_map/attention_forward/pallas_call | solution.py:185
  323.9 12.0 convolution_convert_fusion.10
  335.9 4.8 all-to-all-start
  343.7 63.0 %all-to-all-done = bf16[8,88,2048]{2,1,0:T(8,128)(2,1)} async-done(((bf16[8,88,2048]{2,1,0:T(8,128)(2,1)}), bf16[8,88,2048]{2,1,0:T(8,128)(2,1)}, u32[]{:S(2)}, u32[]{:S(2)}) %all-to-all-start) | async-done | bytes 2883616 | tf_op jit(solution)/shard_map/all_to_all | solution.py:476
  415.3 69.0 %all_to_all.49 = bf16[8,88,2048]{2,1,0:T(8,128)(2,1)S(1)} all-to-all(bf16[8,88,2048]{2,1,0:T(8,128)(2,1)S(1)} %bitcast.238), channel_id=1, replica_groups=mesh['dp'=4,'expert'=8] {'expert'}, dimensions={0} | all-to-all | bytes 5767168 | tf_op jit(solution)/shard_map/all_to_all | solution.py:476
  484.4 5.3 collective-permute-done.2
  489.7 21.7 %fusion.180 = f32[1408,2816]{1,0:T(8,128)} fusion(bf16[2048,2816]{1,0:T(8,128)(2,1)S(1)} %bitcast.247, bf16[704,2048]{1,0:T(8,128)(2,1)S(1)} %collective-permute-done.2, bf16[704,2048]{1,0:T(8,128)(2,1)S(1)} %bitcast.229), kind=kOutput, calls=%fused_computation.361 | convolution fusion | flops 16251879424 | bytes 33161216 | tf_op jit(solution)/shard_map/dot_general | solution.py:632
  511.4 27.6 %multiply_convert_fusion.2 = (bf16[1408,2816]{1,0:T(8,128)(2,1)}, f32[1408,2816]{1,0:T(8,128)}) fusion(f32[1408,2816]{1,0:T(8,128)} %fusion.180, bf16[2048,2816]{1,0:T(8,128)(2,1)} %param.30, bf16[704,2048]{1,0:T(8,128)(2,1)S(1)} %collective-permute-done.2, bf16[704,2048]{1,0:T(8,128)(2,1)S(1)} %bitcast.230), kind=kOutput, calls=%fused_computation.2 | convolution fusion | flops 16275668992 | bytes 56950784 | tf_op jit(solution)/shard_map/dot_general | solution.py:633
  539.0 21.6 %convolution_convert_fusion.5 = bf16[1408,2048]{1,0:T(8,128)(2,1)S(1)} fusion(bf16[1408,2816]{1,0:T(8,128)(2,1)} %get-tuple-element.187, bf16[2048,2816]{1,0:T(8,128)(2,1)} %param.31), kind=kOutput, calls=%fused_computation.15 | convolution fusion | flops 16243228672 | bytes 25231360 | tf_op jit(solution)/shard_map/dot_general | solution.py:638
  561.1 5.2 collective-permute-done.3
  576.9 62.7 %all-to-all-done.2 = bf16[8,88,2048]{2,1,0:T(8,128)(2,1)} async-done(((bf16[8,88,2048]{2,1,0:T(8,128)(2,1)}), bf16[8,88,2048]{2,1,0:T(8,128)(2,1)}, u32[]{:S(2)}, u32[]{:S(2)}) %all-to-all-start.2) | async-done | bytes 2883616 | tf_op jit(solution)/shard_map/all_to_all | solution.py:476
  649.2 68.9 %all_to_all.50 = bf16[8,88,2048]{2,1,0:T(8,128)(2,1)S(1)} all-to-all(bf16[8,88,2048]{2,1,0:T(8,128)(2,1)S(1)} %bitcast.237), channel_id=1, replica_groups=mesh['dp'=4,'expert'=8] {'expert'}, dimensions={0} | all-to-all | bytes 5767168 | tf_op jit(solution)/shard_map/all_to_all | solution.py:476
  718.1 5.3 collective-permute-done.4
  725.0 21.4 %convolution_convert_fusion.2 = bf16[2048,2816]{1,0:T(8,128)(2,1)} fusion(bf16[1408,2816]{1,0:T(8,128)(2,1)S(1)} %bitcast.249, bf16[704,2048]{1,0:T(8,128)(2,1)S(1)} %collective-permute-done.4, bf16[704,2048]{1,0:T(8,128)(2,1)S(1)} %bitcast.216), kind=kOutput, calls=%fused_computation.8 | convolution fusion | flops 16257646592 | bytes 25231360 | tf_op jit(solution)/shard_map/dot_general | solution.py:497
  746.4 5.2 pad_maximum_fusion.2
  751.7 32.0 %multiply_convert_fusion = (bf16[1408,2816]{1,0:T(8,128)(2,1)}, bf16[1408,2816]{1,0:T(8,128)(2,1)}) fusion(f32[1408,2816]{1,0:T(8,128)} %fusion.180, f32[1408,2816]{1,0:T(8,128)} %get-tuple-element.188, bf16[1408,2048]{1,0:T(8,128)(2,1)} %pad_maximum_fusion.2, bf16[2048,2816]{1,0:T(8,128)(2,1)} %param.31), kind=kOutput, calls=%fused_computation | convolution fusion | flops 16291889152 | bytes 64880640 | tf_op jit(solution)/shard_map/dot_general | solution.py:656
  783.7 24.0 %convolution_convert_fusion.1 = bf16[2048,2816]{1,0:T(8,128)(2,1)} fusion(bf16[1408,2816]{1,0:T(8,128)(2,1)} %get-tuple-element.162, bf16[704,2048]{1,0:T(8,128)(2,1)} %copy-done.85, bf16[704,2048]{1,0:T(8,128)(2,1)S(1)} %bitcast.231), kind=kOutput, calls=%fused_computation.7 | convolution fusion | flops 16257646592 | bytes 25231360 | tf_op jit(solution)/shard_map/dot_general | solution.py:497
  807.8 23.3 %fusion.186 = f32[1408,2048]{1,0:T(8,128)} fusion(bf16[1408,2816]{1,0:T(8,128)(2,1)} %get-tuple-element.162, bf16[2048,2816]{1,0:T(8,128)(2,1)} %param.29), kind=kOutput, calls=%fused_computation.366 | convolution fusion | flops 16240345088 | bytes 30998528 | tf_op jit(solution)/shard_map/dot_general | solution.py:661
  831.1 24.9 %add_convert_fusion = bf16[1408,2048]{1,0:T(8,128)(2,1)} fusion(f32[1408,2048]{1,0:T(8,128)} %fusion.186, bf16[1408,2816]{1,0:T(8,128)(2,1)} %get-tuple-element.161, bf16[2048,2816]{1,0:T(8,128)(2,1)} %param.30), kind=kOutput, calls=%fused_computation.5 | convolution fusion | flops 16246112256 | bytes 36765696 | tf_op jit(solution)/shard_map/dot_general | solution.py:663
  860.4 24.2 %convolution_convert_fusion = bf16[2048,2816]{1,0:T(8,128)(2,1)} fusion(bf16[1408,2816]{1,0:T(8,128)(2,1)} %get-tuple-element.161, bf16[704,2048]{1,0:T(8,128)(2,1)S(1)} %copy-done.86, bf16[704,2048]{1,0:T(8,128)(2,1)S(1)} %bitcast.232), kind=kOutput, calls=%fused_computation.6 | convolution fusion | flops 16257646592 | bytes 25231360 | tf_op jit(solution)/shard_map/dot_general | solution.py:497
  884.6 5.9 add_convert_fusion.1
  894.5 65.6 %all-to-all-done.4 = bf16[8,88,2048]{2,1,0:T(8,128)(2,1)S(1)} async-done(((bf16[8,88,2048]{2,1,0:T(8,128)(2,1)}), bf16[8,88,2048]{2,1,0:T(8,128)(2,1)S(1)}, u32[]{:S(2)}, u32[]{:S(2)}) %all-to-all-start.4) | async-done | bytes 2883616 | tf_op jit(solution)/shard_map/all_to_all | solution.py:476
  971.2 70.0 %all_to_all.51 = bf16[8,88,2048]{2,1,0:T(8,128)(2,1)S(1)} all-to-all(bf16[8,88,2048]{2,1,0:T(8,128)(2,1)} %bitcast_convert_fusion), channel_id=1, replica_groups=mesh['dp'=4,'expert'=8] {'expert'}, dimensions={0} | all-to-all | bytes 5767168 | tf_op jit(solution)/shard_map/all_to_all | solution.py:476
  1042.8 10.9 convolution_convert_fusion.4
  1053.8 9.4 convolution_convert_fusion.9.refs_2_
  1066.0 9.2 slice.161
  1076.3 80.1 %attention_backward.1 = (bf16[704,1024]{1,0:T(8,128)(2,1)}, bf16[704,1024]{1,0:T(8,128)(2,1)}, bf16[2176,1024]{1,0:T(8,128)(2,1)}, bf16[2176,1024]{1,0:T(8,128)(2,1)}) custom-call(s32[2]{0:T(128)} %get-tuple-element.192.first_ref, bf16[704,2048]{1,0:T(8,128)(2,1)} %project_queries.1.refs_0_, bf16[704,1024]{1,0:T(8,128)(2,1)} %collective-permute-done.refs_1_, ...), custom_call_target="tpu_custom_call" | custom-call | tf_op jit(solution)/shard_map/attention_backward/pallas_call | solution.py:219
  1156.5 15.3 %convolution_convert_fusion.6 = bf16[2048,1024]{0,1:T(8,128)(2,1)} fusion(bf16[2176,2048]{1,0:T(8,128)(2,1)} %bitcast.218, bf16[2176,1024]{1,0:T(8,128)(2,1)} %get-tuple-element.49.dv_ref), kind=kOutput, calls=%fused_computation.30 | convolution fusion | flops 9128902656 | bytes 17563648 | tf_op jit(solution)/shard_map/dot_general | solution.py:497
  1171.8 12.0 convolution_convert_fusion.7
  1183.9 8.4 pad_maximum_fusion
  1196.8 12.1 convolution_convert_fusion.8
  1209.0 12.6 convolution_convert_fusion.3
  1221.6 29.4 %merge_hidden_grads.1 = bf16[2176,2048]{1,0:T(8,128)(2,1)} custom-call(bf16[8,272,88]{2,1,0:T(8,128)(2,1)} %fusion.47.plan_ref, bf16[8,88,2048]{2,1,0:T(8,128)(2,1)} %bitcast.239, bf16[2176,1024]{1,0:T(8,128)(2,1)} %get-tuple-element.48.dk_ref, bf16[2176,1024]{1,0:T(8,128)(2,1)} %get-tuple-element.49.dv_ref, ...), custom_call_target="tpu_custom_call" | custom-call | tf_op jit(solution)/shard_map/merge_hidden_grads/pallas_call | solution.py:351
  1251.0 5.1 dynamic-slice_bitcast_fusion
  1256.5 7.5 collective-permute-done.8
  1264.0 8.5 fusion.1
  1272.5 4.9 all-to-all-start.6
  1288.3 88.7 %all-to-all-done.6 = bf16[4,272,2048]{2,1,0:T(8,128)(2,1)} async-done(((bf16[4,272,2048]{2,1,0:T(8,128)(2,1)}), bf16[4,272,2048]{2,1,0:T(8,128)(2,1)}, u32[]{:S(2)}, u32[]{:S(2)}) %all-to-all-start.6) | async-done | bytes 4456480 | tf_op jit(solution)/shard_map/all_to_all | solution.py:733
  1403.2 5.1 convert_element_type.262
  1422.7 35.0 %reduce-scatter.15.cloned.1.call-done = bf16[512,2048]{1,0:T(8,128)(2,1)} async-done(((bf16[2048,2048]{1,0:T(8,128)(2,1)}), bf16[512,2048]{1,0:T(8,128)(2,1)}) %reduce-scatter.15.cloned.1.call-update) | async-done | bytes 2097168 | tf_op jit(solution)/shard_map/reduce_scatter | solution.py:718
  1461.9 6.6 reshape.734
  (376 shorter events, 171.3 us)
Async XLA Ops:
  7.2 333.5 %copy-start = (f32[2048,8]{0,1:T(8,128)S(1)}, f32[2048,8]{0,1:T(8,128)}, u32[]{:S(2)}) copy-start(f32[2048,8]{0,1:T(8,128)} %param.24) | copy-start | bytes 196612
  7.2 136.4 %all-gather.6.cloned.1.call-start = ((), (), s32[]{:S(2)}) async-start(), calls=%async_computation.22 | async-start | bytes 15040512 | tf_op jit(solution)/shard_map/all_gather | solution.py:543
  16.1 324.6 %copy-start.9 = (bf16[272,2048]{1,0:T(8,128)(2,1)}, bf16[272,2048]{1,0:T(8,128)(2,1)S(1)}, u32[]{:S(2)}) copy-start(bf16[272,2048]{1,0:T(8,128)(2,1)S(1)} %fusion.26) | copy-start | bytes 3342340
  17.6 219.9 %all-gather.4.cloned.1.call-start = ((), (), s32[]{:S(2)}) async-start(), calls=%async_computation.15 | async-start | bytes 10485760 | tf_op jit(solution)/shard_map/all_gather | solution.py:545
  168.2 16.0 %copy-start.68 = (pred[8,272]{1,0:T(8,128)(4,1)}, pred[8,272]{1,0:T(8,128)(4,1)S(1)}, u32[]{:S(2)}) copy-start(pred[8,272]{1,0:T(8,128)(4,1)S(1)} %copy.115) | copy-start | bytes 6532
  198.1 65.0 %collective-permute-start = (bf16[704,1024]{1,0:T(8,128)(2,1)}, bf16[704,1024]{1,0:T(8,128)(2,1)}, u32[]{:S(2)}, u32[]{:S(2)}) collective-permute-start(bf16[704,1024]{1,0:T(8,128)(2,1)} %constant_dynamic-slice_fusion.2), channel_id=1, source_target_pairs={{0,1},{1,0},{2,3},{3,2},{4,5},{5,4},{6,7},{7,6},{8,9},{9,8},{10,11... | collective-permute-start | bytes 4325384 | tf_op jit(solution)/shard_map/ppermute | solution.py:578
  320.3 3.6 collective-permute-start.1
  335.9 70.8 %all-to-all-start = ((bf16[8,88,2048]{2,1,0:T(8,128)(2,1)}), bf16[8,88,2048]{2,1,0:T(8,128)(2,1)}, u32[]{:S(2)}, u32[]{:S(2)}) async-start(bf16[8,88,2048]{2,1,0:T(8,128)(2,1)} %bitcast.233), calls=%async_computation | async-start | bytes 5767168 | tf_op jit(solution)/shard_map/all_to_all | solution.py:476
  340.7 69.8 %copy-start.76 = (pred[2,8,272]{2,0,1:T(4,128)(4,1)}, pred[2,8,272]{2,0,1:T(4,128)(4,1)S(1)}, u32[]{:S(2)}) copy-start(pred[2,8,272]{2,0,1:T(4,128)(4,1)S(1)} %copy.109) | copy-start | bytes 13060
  341.9 68.6 %copy-start.72 = (f32[272]{0:T(512)}, f32[272]{0:T(512)S(1)}, u32[]{:S(2)}) copy-start(f32[272]{0:T(512)S(1)} %get-tuple-element.148) | copy-start | bytes 3268
  341.9 68.6 %copy-start.74 = (f32[272]{0:T(512)}, f32[272]{0:T(512)S(1)}, u32[]{:S(2)}) copy-start(f32[272]{0:T(512)S(1)} %get-tuple-element.149) | copy-start | bytes 3268
  343.4 67.1 %copy-start.32 = (pred[8,88,272]{2,1,0:T(8,128)(4,1)}, pred[8,88,272]{2,1,0:T(8,128)(4,1)S(1)}, u32[]{:S(2)}) copy-start(pred[8,88,272]{2,1,0:T(8,128)(4,1)S(1)} %iota_compare_fusion.6) | copy-start | bytes 574468
  410.6 79.1 %slice-start.5 = ((s8[11534336]{0:T(1024)(128)(4,1)}), s8[4194304]{0:T(1024)(128)(4,1)S(1)}, s32[]{:S(2)}) async-start(s8[11534336]{0:T(1024)(128)(4,1)} %bitcast.246), calls=%async_computation.28 | async-start | bytes 8388608
  410.6 79.1 %slice-start.6 = ((s8[11534336]{0:T(1024)(128)(4,1)}), s8[4194304]{0:T(1024)(128)(4,1)S(1)}, s32[]{:S(2)}) async-start(s8[11534336]{0:T(1024)(128)(4,1)} %bitcast.246), calls=%async_computation.29 | async-start | bytes 8388608
  413.6 76.0 %slice-start.7 = ((s8[11534336]{0:T(1024)(128)(4,1)}), s8[3145728]{0:T(1024)(128)(4,1)S(1)}, s32[]{:S(2)}) async-start(s8[11534336]{0:T(1024)(128)(4,1)} %bitcast.246), calls=%async_computation.30 | async-start | bytes 6291456
  484.4 27.0 %copy-start.20 = (bf16[8,88,2048]{2,1,0:T(8,128)(2,1)}, bf16[8,88,2048]{2,1,0:T(8,128)(2,1)S(1)}, u32[]{:S(2)}) copy-start(bf16[8,88,2048]{2,1,0:T(8,128)(2,1)S(1)} %all_to_all.49) | copy-start | bytes 8650756
  484.4 5.3 collective-permute-start.2
  489.7 21.7 %copy-start.85 = (bf16[704,2048]{1,0:T(8,128)(2,1)}, bf16[704,2048]{1,0:T(8,128)(2,1)S(1)}, u32[]{:S(2)}) copy-start(bf16[704,2048]{1,0:T(8,128)(2,1)S(1)} %collective-permute-done.2) | copy-start | bytes 8650756
  560.9 5.3 collective-permute-start.3
  569.0 70.5 %copy-start.30 = (pred[4,176,272]{2,1,0:T(8,128)(4,1)S(1)}, pred[4,176,272]{2,1,0:T(8,128)(4,1)}, u32[]{:S(2)}) copy-start(pred[4,176,272]{2,1,0:T(8,128)(4,1)} %copy-done.29) | copy-start | bytes 574468
  569.0 70.5 %all-to-all-start.2 = ((bf16[8,88,2048]{2,1,0:T(8,128)(2,1)}), bf16[8,88,2048]{2,1,0:T(8,128)(2,1)}, u32[]{:S(2)}, u32[]{:S(2)}) async-start(bf16[8,88,2048]{2,1,0:T(8,128)(2,1)} %bitcast.30), calls=%async_computation.2 | async-start | bytes 5767168 | tf_op jit(solution)/shard_map/all_to_all | solution.py:476
  573.6 397.6 %reduce-scatter.7.cloned.1.call-start = ((), (), s32[]{:S(2)}) async-start(), calls=%async_computation.16 | async-start | bytes 14417920 | tf_op jit(solution)/shard_map/reduce_scatter | solution.py:655
  576.8 66.8 %copy-start.64 = (f32[272]{0:T(512)}, f32[272]{0:T(512)S(1)}, u32[]{:S(2)}) copy-start(f32[272]{0:T(512)S(1)} %fusion.171) | copy-start | bytes 3268
  646.4 78.5 %slice-start.8 = ((s8[7929856]{0:T(1024)(128)(4,1)}), s8[4194304]{0:T(1024)(128)(4,1)S(1)}, s32[]{:S(2)}) async-start(s8[7929856]{0:T(1024)(128)(4,1)} %bitcast.248), calls=%async_computation.31 | async-start | bytes 8388608
  646.7 78.2 %slice-start.9 = ((s8[7929856]{0:T(1024)(128)(4,1)}), s8[3735552]{0:T(1024)(128)(4,1)S(1)}, s32[]{:S(2)}) async-start(s8[7929856]{0:T(1024)(128)(4,1)} %bitcast.248), calls=%async_computation.32 | async-start | bytes 7471104
  718.1 5.3 collective-permute-start.4
  751.6 324.7 %reduce-scatter.9.cloned.1.call-start = ((), (), s32[]{:S(2)}) async-start(), calls=%async_computation.17 | async-start | bytes 14417920 | tf_op jit(solution)/shard_map/reduce_scatter | solution.py:668
  751.7 32.0 %copy-start.21 = (bf16[8,88,2048]{2,1,0:T(8,128)(2,1)S(1)}, bf16[8,88,2048]{2,1,0:T(8,128)(2,1)}, u32[]{:S(2)}) copy-start(bf16[8,88,2048]{2,1,0:T(8,128)(2,1)} %copy-done.20) | copy-start | bytes 8650756
  807.7 401.3 %reduce-scatter.11.cloned.1.call-start = ((), (), s32[]{:S(2)}) async-start(), calls=%async_computation.18 | async-start | bytes 14417920 | tf_op jit(solution)/shard_map/reduce_scatter | solution.py:669
  859.9 24.7 %collective-permute-start.5 = (bf16[704,2048]{1,0:T(8,128)(2,1)}, bf16[704,2048]{1,0:T(8,128)(2,1)}, u32[]{:S(2)}, u32[]{:S(2)}) collective-permute-start(bf16[704,2048]{1,0:T(8,128)(2,1)} %slice.177), channel_id=1, source_target_pairs={{0,1},{1,0},{2,3},{3,2},{4,5},{5,4},{6,7},{7,6},{8,9},{9,8},{10,11... | collective-permute-start | bytes 8650760 | tf_op jit(solution)/shard_map/ppermute | solution.py:481
  890.5 69.7 %copy-start.31 = (pred[4,176,272]{2,1,0:T(8,128)(4,1)S(1)}, pred[4,176,272]{2,1,0:T(8,128)(4,1)}, u32[]{:S(2)}) copy-start(pred[4,176,272]{2,1,0:T(8,128)(4,1)} %copy-done.29) | copy-start | bytes 574468
  890.5 69.6 %copy-start.58 = (pred[2,4,272]{2,1,0:T(4,128)(4,1)S(1)}, pred[2,4,272]{2,1,0:T(4,128)(4,1)}, u32[]{:S(2)}) copy-start(pred[2,4,272]{2,1,0:T(4,128)(4,1)} %copy-done.56) | copy-start | bytes 6532
  890.5 69.6 %all-to-all-start.4 = ((bf16[8,88,2048]{2,1,0:T(8,128)(2,1)}), bf16[8,88,2048]{2,1,0:T(8,128)(2,1)S(1)}, u32[]{:S(2)}, u32[]{:S(2)}) async-start(bf16[8,88,2048]{2,1,0:T(8,128)(2,1)} %bitcast.44), calls=%async_computation.4 | async-start | bytes 5767168 | tf_op jit(solution)/shard_map/all_to_all | solution.py:476
  894.3 482.7 %reduce-scatter.13.cloned.1.call-start = ((), (), s32[]{:S(2)}) async-start(), calls=%async_computation.19 | async-start | bytes 10485760 | tf_op jit(solution)/shard_map/reduce_scatter | solution.py:717
  971.2 71.6 %copy-start.27 = (bf16[704,1024]{1,0:T(8,128)(2,1)S(1)}, bf16[704,1024]{1,0:T(8,128)(2,1)}, u32[]{:S(2)}) copy-start(bf16[704,1024]{1,0:T(8,128)(2,1)} %get-tuple-element.36.refs_4_) | copy-start | bytes 4325380
  1066.0 10.3 collective-permute-start.6
  1076.3 95.4 %slice-start.2 = ((s8[8912896]{0:T(1024)(128)(4,1)}), s8[524288]{0:T(1024)(128)(4,1)S(1)}, s32[]{:S(2)}) async-start(s8[8912896]{0:T(1024)(128)(4,1)} %bitcast.219), calls=%async_computation.25 | async-start | bytes 1048576
  1192.3 222.1 %reduce-scatter.17.cloned.1.call-start = ((), (), s32[]{:S(2)}) async-start(), calls=%async_computation.21 | async-start | bytes 10485760 | tf_op jit(solution)/shard_map/reduce_scatter | solution.py:687
  1193.0 264.7 %reduce-scatter.15.cloned.1.call-start = ((), (), s32[]{:S(2)}) async-start(), calls=%async_computation.20 | async-start | bytes 10485760 | tf_op jit(solution)/shard_map/reduce_scatter | solution.py:718
  1193.1 3.8 collective-permute-start.7
  1256.2 7.9 collective-permute-start.8
  1272.5 104.5 %all-to-all-start.6 = ((bf16[4,272,2048]{2,1,0:T(8,128)(2,1)}), bf16[4,272,2048]{2,1,0:T(8,128)(2,1)}, u32[]{:S(2)}, u32[]{:S(2)}) async-start(bf16[4,272,2048]{2,1,0:T(8,128)(2,1)} %fusion.1), calls=%async_computation.9 | async-start | bytes 8912896 | tf_op jit(solution)/shard_map/all_to_all | solution.py:733
  1288.3 92.1 %copy-start.5 = (bf16[272,2048]{1,0:T(8,128)(2,1)S(1)}, bf16[272,2048]{1,0:T(8,128)(2,1)}, u32[]{:S(2)}) copy-start(bf16[272,2048]{1,0:T(8,128)(2,1)} %param.16) | copy-start | bytes 3342340
  1288.3 92.1 %copy-start.41 = (f32[2048]{0:T(1024)S(1)}, f32[2048]{0:T(1024)}, u32[]{:S(2)}) copy-start(f32[2048]{0:T(1024)} %param.22) | copy-start | bytes 24580
  1288.3 92.1 %copy-start.61 = (f32[272]{0:T(512)S(1)}, f32[272]{0:T(512)}, u32[]{:S(2)}) copy-start(f32[272]{0:T(512)} %copy-done.60) | copy-start | bytes 3268
  1288.3 92.1 %copy-start.71 = (f32[272]{0:T(512)S(1)}, f32[272]{0:T(512)}, u32[]{:S(2)}) copy-start(f32[272]{0:T(512)} %copy-done.70) | copy-start | bytes 3268
  1386.6 12.1 all-to-all-start.7
  1398.6 63.2 %all-to-all-start.8 = ((bf16[8,64,2048]{2,1,0:T(8,128)(2,1)}), bf16[8,64,2048]{2,1,0:T(8,128)(2,1)}, u32[]{:S(2)}, u32[]{:S(2)}) async-start(bf16[8,64,2048]{2,1,0:T(8,128)(2,1)} %bitcast.223), calls=%async_computation.12 | async-start | bytes 4194304 | tf_op jit(solution)/shard_map/all_to_all | solution.py:476
  (72 other events, 299.1 us)
Sparse Core Ops, SparseCore 0:
  17.7 125.8 all-gather.5
  151.6 85.8 all-gather.3
  751.7 110.0 reduce-scatter.6
  864.8 112.0 reduce-scatter.8
  979.9 112.1 reduce-scatter.10
  1192.4 84.7 reduce-scatter.12
  1280.6 86.4 reduce-scatter.16
  1370.1 87.6 reduce-scatter.14

commit v3 on v2

--- a/solution.py
+++ b/solution.py
@@ -261,7 +261,19 @@
     )
 
 
-def project_body(tile, x_ref, weight_ref, cos_ref, sin_ref, out_ref):
+def project_body(plan_ref, hidden_ref, weight_ref, cos_ref, sin_ref, out_ref, x_ref):
+    sources, capacity = plan_ref.shape[0], plan_ref.shape[1]
+    bundle = max(1, sources * capacity // GROUPS // capacity)
+    tile = bundle * capacity
+
+    @pl.when(pl.program_id(0) == 0)
+    def _():
+        for group in range(sources // bundle):
+            parts = [
+                dot_nn(plan_ref[group * bundle + n], hidden_ref[group * bundle + n]) for n in range(bundle)
+            ]
+            x_ref[pl.ds(group * tile, tile), :] = jnp.concatenate(parts, axis=0).astype(jnp.bfloat16)
+
     for at in range(0, x_ref.shape[0], tile):
         span = pl.ds(at, tile)
         product = dot_nn(x_ref[span, :], weight_ref[...])
@@ -270,27 +282,35 @@
             out_ref[span, lane : lane + HEAD] = turned.astype(jnp.bfloat16)
 
 
-def project_queries(rows_in, weight, tables):
-    rows, depth = rows_in.shape
-    columns = weight.shape[1]
+def project_queries(plan, hidden, weight, tables):
+    sources, capacity, row_count = plan.shape
+    depth, columns = weight.shape
+    rows = sources * capacity
     block = 512
     return pl.pallas_call(
-        functools.partial(project_body, rows // GROUPS),
+        project_body,
         grid=(columns // block,),
         in_specs=[
-            pl.BlockSpec((rows, depth), lambda j: (0, 0)),
+            pl.BlockSpec((sources, capacity, row_count), lambda j: (0, 0, 0)),
+            pl.BlockSpec((sources, row_count, depth), lambda j: (0, 0, 0)),
             pl.BlockSpec((depth, block), lambda j: (0, j)),
             pl.BlockSpec((rows, HEAD), lambda j: (0, 0)),
             pl.BlockSpec((rows, HEAD), lambda j: (0, 0)),
         ],
-        out_specs=pl.BlockSpec((rows, block), lambda j: (0, j)),
-        out_shape=jax.ShapeDtypeStruct((rows, columns), jnp.bfloat16),
+        out_specs=[
+            pl.BlockSpec((rows, block), lambda j: (0, j)),
+            pl.BlockSpec((rows, depth), lambda j: (0, 0)),
+        ],
+        out_shape=[
+            jax.ShapeDtypeStruct((rows, columns), jnp.bfloat16),
+            jax.ShapeDtypeStruct((rows, depth), jnp.bfloat16),
+        ],
         compiler_params=pltpu.CompilerParams(vmem_limit_bytes=VMEM_BYTES),
         name="project_queries",
-    )(rows_in, weight, *tables)
-
-
-def keys_values_body(half, x_ref, weight_ref, cos_ref, sin_ref, key_ref, value_ref):
+    )(plan, hidden, weight, *tables)
+
+
+def keys_values_body(half, order_ref, x_ref, weight_ref, cos_ref, sin_ref, key_ref, value_ref):
     rows = x_ref.shape[1]
     for source in range(x_ref.shape[0]):
         span = pl.ds(source * rows, rows)
@@ -301,27 +321,30 @@
         value_ref[span, :] = product[:, half:].astype(jnp.bfloat16)
 
 
-def project_keys_values(gathered, weights, tables):
-    sources, rows, unused = gathered.shape
+def project_keys_values(hidden, weights, tables, order):
+    sources, rows, unused = hidden.shape
     parts, depth, columns = weights.shape
     half, tokens = columns // 2, sources * rows
     return pl.pallas_call(
         functools.partial(keys_values_body, half),
-        grid=(parts,),
-        in_specs=[
-            pl.BlockSpec((sources, rows, depth), lambda j: (0, 0, 0)),
-            pl.BlockSpec((1, depth, columns), lambda j: (j, 0, 0)),
-            pl.BlockSpec((tokens, HEAD), lambda j: (0, 0)),
-            pl.BlockSpec((tokens, HEAD), lambda j: (0, 0)),
-        ],
-        out_specs=[pl.BlockSpec((tokens, half), lambda j: (0, j))] * 2,
+        grid_spec=pltpu.PrefetchScalarGridSpec(
+            num_scalar_prefetch=1,
+            grid=(parts,),
+            in_specs=[
+                pl.BlockSpec((sources, rows, depth), lambda j, order: (0, 0, 0)),
+                pl.BlockSpec((1, depth, columns), lambda j, order: (j, 0, 0)),
+                pl.BlockSpec((tokens, HEAD), lambda j, order: (0, 0)),
+                pl.BlockSpec((tokens, HEAD), lambda j, order: (0, 0)),
+            ],
+            out_specs=[pl.BlockSpec((tokens, half), lambda j, order: (0, order[j]))] * 2,
+        ),
         out_shape=[jax.ShapeDtypeStruct((tokens, parts * half), jnp.bfloat16)] * 2,
         compiler_params=pltpu.CompilerParams(vmem_limit_bytes=VMEM_BYTES),
         name="project_keys_values",
-    )(gathered, weights, *tables)
-
-
-def merge_body(tile, plan_ref, slots_ref, dk_ref, dv_ref, weight_ref, out_ref, acc_ref):
+    )(order, hidden, weights, *tables)
+
+
+def merge_body(tile, order_ref, plan_ref, slots_ref, dk_ref, dv_ref, weight_ref, out_ref, acc_ref):
     part = pl.program_id(1)
     sources, rows = plan_ref.shape[0], plan_ref.shape[1]
     ck = dk_ref.shape[1]
@@ -343,27 +366,631 @@
         out_ref[...] = acc_ref[...].astype(jnp.bfloat16)
 
 
-def merge_hidden_grads(plan, slots, grad_keys, grad_values, weights):
+def merge_hidden_grads(plan, slots, grad_keys, grad_values, weights, order):
     sources, rows, capacity = plan.shape
     parts, depth, columns = weights.shape
     ck, tokens = columns // 2, sources * rows
     wide = depth // 2
     return pl.pallas_call(
         functools.partial(merge_body, tokens // GROUPS),
-        grid=(2, parts),
-        in_specs=[
-            pl.BlockSpec((sources, rows, capacity), lambda i, j: (0, 0, 0)),
-            pl.BlockSpec((sources, capacity, wide), lambda i, j: (0, 0, i)),
-            pl.BlockSpec((tokens, ck), lambda i, j: (0, j)),
-            pl.BlockSpec((tokens, ck), lambda i, j: (0, j)),
-            pl.BlockSpec((1, wide, columns), lambda i, j: (j, i, 0)),
-        ],
-        out_specs=pl.BlockSpec((tokens, wide), lambda i, j: (0, i)),
+        grid_spec=pltpu.PrefetchScalarGridSpec(
+            num_scalar_prefetch=1,
+            grid=(2, parts),
+            in_specs=[
+                pl.BlockSpec((sources, rows, capacity), lambda i, j, order: (0, 0, 0)),
+                pl.BlockSpec((sources, capacity, wide), lambda i, j, order: (0, 0, i)),
+                pl.BlockSpec((tokens, ck), lambda i, j, order: (0, order[j])),
+                pl.BlockSpec((tokens, ck), lambda i, j, order: (0, order[j])),
+                pl.BlockSpec((1, wide, columns), lambda i, j, order: (j, i, 0)),
+            ],
+            out_specs=pl.BlockSpec((tokens, wide), lambda i, j, order: (0, i)),
+            scratch_shapes=[pltpu.VMEM((tokens, wide), jnp.float32)],
+        ),
         out_shape=jax.ShapeDtypeStruct((tokens, depth), jnp.bfloat16),
-        scratch_shapes=[pltpu.VMEM((tokens, wide), jnp.float32)],
         compiler_params=pltpu.CompilerParams(vmem_limit_bytes=VMEM_BYTES),
         name="merge_hidden_grads",
-    )(plan, slots, grad_keys, grad_values, weights)
+    )(order, plan, slots, grad_keys, grad_values, weights)
+
+
+def mesh_device(index):
+    return {"expert": index}
+
+
+def chip_order(chip, step):
+    flip = chip // 2
+    near = chip + flip * (3 - 2 * chip)
+    place = step + near * (1 - 2 * step) if step < 2 else step
+    return place + flip * (3 - 2 * place)
+
+
+def enter(devices, me):
+    barrier = pltpu.get_barrier_semaphore()
+    for step in range(1, devices):
+        pl.semaphore_signal(
+            barrier,
+            inc=1,
+            device_id=mesh_device(lax.rem(me + step, devices)),
+            device_id_type=pl.DeviceIdType.MESH,
+        )
+    pl.semaphore_wait(barrier, devices - 1)
+
+
+def remote(source, target, send, recv, device):
+    return pltpu.make_async_remote_copy(
+        src_ref=source,
+        dst_ref=target,
+        send_sem=send,
+        recv_sem=recv,
+        device_id=mesh_device(device),
+        device_id_type=pl.DeviceIdType.MESH,
+    )
+
+
+class Dispatch:
+    def __init__(self, me, slots, landing, local_sem, send, recv, pass_send, pass_recv):
+        self.me, self.chip, self.core = me, me // 2, lax.rem(me, 2)
+        self.slots, self.landing = slots, landing
+        self.local_sem, self.send, self.recv = local_sem, send, recv
+        self.pass_send, self.pass_recv = pass_send, pass_recv
+        self.rows, self.half = slots.shape[1], slots.shape[2] // 2
+
+    def columns(self, core):
+        return pl.ds(pl.multiple_of(core * self.half, 128), self.half)
+
+    def place(self, source, core):
+        rows = pl.ds(pl.multiple_of(lax.rem(source, 2) * self.rows, 16), self.rows)
+        return self.landing.at[source // 2, rows, self.columns(core)]
+
+    def direct(self, step):
+        target = lax.rem(self.me + step, 8)
+        core = lax.rem(target, 2)
+        return remote(
+            self.slots.at[target // 2, :, self.columns(core)],
+            self.place(self.me, core),
+            self.send.at[step],
+            self.recv.at[step],
+            target,
+        )
+
+    def local(self):
+        return pltpu.make_async_copy(
+            self.slots.at[self.chip, :, self.columns(self.core)],
+            self.place(self.me, self.core),
+            self.local_sem,
+        )
+
+    def start(self):
+        self.local().start()
+        for step in range(1, 8):
+            self.direct(step).start()
+
+    def pass_on(self, source):
+        place = self.place(source, self.core)
+        return remote(
+            place, place, self.pass_send.at[source], self.pass_recv.at[source], self.me + 1 - 2 * self.core
+        )
+
+    def arrive(self, step):
+        chip = chip_order(self.chip, step)
+        for source in (2 * chip, 2 * chip + 1):
+            offset = lax.rem(self.me - source + 8, 8)
+
+            @pl.when(offset == 0)
+            def _():
+                self.local().wait()
+
+            @pl.when(offset != 0)
+            def _(source=source, offset=offset):
+                place = self.place(source, self.core)
+                remote(place, place, self.send.at[offset], self.recv.at[offset], self.me).wait_recv()
+
+            self.pass_on(source).start()
+
+    def ready(self, step):
+        chip = chip_order(self.chip, step)
+        for source in (2 * chip, 2 * chip + 1):
+            place = self.place(source, 1 - self.core)
+            remote(
+                place, place, self.pass_send.at[source], self.pass_recv.at[source], self.me
+            ).wait_recv()
+        return chip
+
+    def finish(self):
+        for step in range(1, 8):
+            self.direct(step).wait_send()
+        for source in range(8):
+            self.pass_on(source).wait_send()
+
+
+class Collect:
+    def __init__(
+        self, me, far_first, kept, passing, passed, total, back, local_sem, pass_send, pass_recv, send, recv
+    ):
+        self.me, self.chip, self.core, self.far_first = me, me // 2, lax.rem(me, 2), far_first
+        self.kept, self.passing, self.passed, self.total, self.back = kept, passing, passed, total, back
+        self.local_sem, self.pass_send, self.pass_recv = local_sem, pass_send, pass_recv
+        self.send, self.recv = send, recv
+        self.rows, self.half = back.shape[1], back.shape[2] // 2
+
+    def swap(self, step):
+        return remote(
+            self.passing.at[step],
+            self.passed.at[step],
+            self.pass_send.at[step],
+            self.pass_recv.at[step],
+            self.me + 1 - 2 * self.core,
+        )
+
+    def place(self, chip, core):
+        return self.back.at[chip, :, pl.ds(pl.multiple_of(core * self.half, 128), self.half)]
+
+    def local(self, step, source_core):
+        return pltpu.make_async_copy(
+            self.total.at[step, pl.ds(pl.multiple_of(source_core * self.rows, 16), self.rows), :],
+            self.place(self.chip, self.core),
+            self.local_sem,
+        )
+
+    def outgoing(self, step, source):
+        rows = pl.ds(pl.multiple_of(lax.rem(source, 2) * self.rows, 16), self.rows)
+        offset = lax.rem(source - self.me + 8, 8)
+        return remote(
+            self.total.at[step, rows, :],
+            self.place(self.chip, self.core),
+            self.send.at[offset],
+            self.recv.at[offset],
+            source,
+        )
+
+    def block(self, step):
+        return chip_order(self.chip, 3 - step if self.far_first else step)
+
+    def each(self, step, own, other):
+        chip = self.block(step)
+        for source in (2 * chip, 2 * chip + 1):
+            if step != (3 if self.far_first else 0):
+                other(source)
+                continue
+
+            @pl.when(source == self.me)
+            def _():
+                own()
+
+            @pl.when(source != self.me)
+            def _(source=source):
+                other(source)
+
+    def settle(self, step):
+        self.swap(step).wait_recv()
+        tile = 2 * self.rows // 4
+        for at in range(0, 2 * self.rows, tile):
+            span = pl.ds(at, tile)
+            summed = self.kept[step % 2, span, :] + self.passed[step, span, :].astype(jnp.float32)
+            self.total[step, span, :] = summed.astype(jnp.bfloat16)
+        self.each(
+            step,
+            lambda: self.local(step, self.core).start(),
+            lambda source: self.outgoing(step, source).start(),
+        )
+
+    def finish(self):
+        for step in range(4):
+            self.swap(step).wait_send()
+            self.each(
+                step,
+                lambda step=step: self.local(step, self.core).wait(),
+                lambda source, step=step: self.outgoing(step, source).wait_send(),
+            )
+        for offset in range(1, 8):
+            source = lax.rem(self.me + 8 - offset, 8)
+            place = self.place(source // 2, lax.rem(source, 2))
+            remote(place, place, self.send.at[offset], self.recv.at[offset], self.me).wait_recv()
+
+
+def ffn_forward_body(
+    chunk,
+    slots,
+    gate_hbm,
+    up_hbm,
+    down_hbm,
+    rows_out,
+    gate_out,
+    up_out,
+    act_out,
+    back,
+    gate,
+    up,
+    down,
+    landing,
+    pre_stage,
+    act,
+    kept,
+    passing,
+    passed,
+    total,
+    weight_sem,
+    stage_sem,
+    act_sem,
+    rows_sem,
+    local_sem,
+    send,
+    recv,
+    pass_send,
+    pass_recv,
+    swap_send,
+    swap_recv,
+    out_send,
+    out_recv,
+):
+    me = lax.axis_index("expert")
+    enter(8, me)
+    loads = [
+        pltpu.make_async_copy(source, target, weight_sem.at[n])
+        for n, (source, target) in enumerate(((gate_hbm, gate), (up_hbm, up), (down_hbm, down)))
+    ]
+    dispatch = Dispatch(me, slots, landing, local_sem.at[0], send, recv, pass_send, pass_recv)
+    collect = Collect(
+        me, False, kept, passing, passed, total, back, local_sem.at[1], swap_send, swap_recv, out_send, out_recv
+    )
+    dispatch.start()
+    for load in loads:
+        load.start()
+    block = landing.shape[1]
+    hidden_units = gate.shape[1]
+    chunks = hidden_units // chunk
+    half = back.shape[2] // 2
+
+    def stage_copies(chip, part, slot):
+        span = pl.ds(pl.multiple_of(chip * block, 16), block)
+        columns = pl.ds(pl.multiple_of(part * chunk, 128), chunk)
+        return [
+            pltpu.make_async_copy(
+                pre_stage.at[slot, n], out.at[span, columns], stage_sem.at[slot, n]
+            )
+            for n, out in enumerate((gate_out, up_out))
+        ]
+
+    def act_copy(chip, step):
+        span = pl.ds(pl.multiple_of(chip * block, 16), block)
+        return pltpu.make_async_copy(act.at[step % 2], act_out.at[span, :], act_sem.at[step % 2])
+
+    def rows_copy(chip, step):
+        span = pl.ds(pl.multiple_of(chip * block, 16), block)
+        return pltpu.make_async_copy(landing.at[chip], rows_out.at[span, :], rows_sem.at[step])
+
+    for step in range(4):
+        if step == 0:
+            dispatch.arrive(0)
+        chip = dispatch.ready(step)
+        rows_copy(chip, step).start()
+        if step == 0:
+            loads[0].wait()
+            loads[1].wait()
+        if step >= 2:
+            act_copy(chip_order(me // 2, step - 2), step - 2).wait()
+
+        def hidden_part(part, carry, chip=chip, step=step):
+            slot = lax.rem(part + step * chunks, 2)
+            columns = pl.ds(pl.multiple_of(part * chunk, 128), chunk)
+
+            @pl.when(part + step * chunks >= 2)
+            def _():
+                for copy in stage_copies(chip, part, slot):
+                    copy.wait()
+
+            gated = dot_nn(landing[chip], gate[:, columns])
+            raised = dot_nn(landing[chip], up[:, columns])
+            pre_stage[slot, 0] = gated.astype(jnp.bfloat16)
+            pre_stage[slot, 1] = raised.astype(jnp.bfloat16)
+            act[step % 2, :, columns] = (gated * jax.nn.sigmoid(gated) * raised).astype(jnp.bfloat16)
+            for copy in stage_copies(chip, part, slot):
+                copy.start()
+            return carry
+
+        lax.fori_loop(0, chunks, hidden_part, 0)
+        act_copy(chip, step).start()
+        if step < 3:
+            dispatch.arrive(step + 1)
+        if step == 0:
+            loads[2].wait()
+        else:
+            collect.settle(step - 1)
+        core = collect.core
+        width = min(256, half)
+
+        def far_part(part, carry, step=step):
+            at = pl.multiple_of((1 - core) * half + part * width, 128)
+            product = dot_nt(act[step % 2], down[pl.ds(at, width), :])
+            passing[step, :, pl.ds(pl.multiple_of(part * width, 128), width)] = product.astype(jnp.bfloat16)
+            return carry
+
+        def near_part(part, carry, step=step):
+            at = pl.multiple_of(core * half + part * width, 128)
+            product = dot_nt(act[step % 2], down[pl.ds(at, width), :])
+            kept[step % 2, :, pl.ds(pl.multiple_of(part * width, 128), width)] = product
+            return carry
+
+        lax.fori_loop(0, half // width, far_part, 0)
+        collect.swap(step).start()
+        lax.fori_loop(0, half // width, near_part, 0)
+    collect.settle(3)
+    for step in (2, 3):
+        act_copy(chip_order(me // 2, step), step).wait()
+    for step in range(4):
+        rows_copy(chip_order(me // 2, step), step).wait()
+    for slot in range(2):
+        for copy in stage_copies(0, 0, slot):
+            copy.wait()
+    dispatch.finish()
+    collect.finish()
+
+
+def ffn_forward(slots, gate_weight, up_weight, down_weight):
+    chips, capacity, depth = slots.shape
+    hidden_units = gate_weight.shape[1]
+    block = 2 * capacity
+    chunk = 256 if hidden_units % 256 == 0 else 128
+    half = depth // 2
+    rows = chips * block
+    any_space = pl.BlockSpec(memory_space=pl.ANY)
+    bf = jnp.bfloat16
+    dma = pltpu.SemaphoreType.DMA
+    return pl.pallas_call(
+        functools.partial(ffn_forward_body, chunk),
+        in_specs=[any_space] * 4,
+        out_specs=[any_space] * 5,
+        out_shape=[
+            jax.ShapeDtypeStruct((rows, depth), bf),
+            jax.ShapeDtypeStruct((rows, hidden_units), bf),
+            jax.ShapeDtypeStruct((rows, hidden_units), bf),
+            jax.ShapeDtypeStruct((rows, hidden_units), bf),
+            jax.ShapeDtypeStruct((chips, capacity, depth), bf),
+        ],
+        scratch_shapes=[
+            pltpu.VMEM((depth, hidden_units), bf),
+            pltpu.VMEM((depth, hidden_units), bf),
+            pltpu.VMEM((depth, hidden_units), bf),
+            pltpu.VMEM((chips, block, depth), bf),
+            pltpu.VMEM((2, 2, block, chunk), bf),
+            pltpu.VMEM((2, block, hidden_units), bf),
+            pltpu.VMEM((2, block, half), jnp.float32),
+            pltpu.VMEM((chips, block, half), bf),
+            pltpu.VMEM((chips, block, half), bf),
+            pltpu.VMEM((chips, block, half), bf),
+            dma((3,)),
+            dma((2, 2)),
+            dma((2,)),
+            dma((4,)),
+            dma((2,)),
+            dma((8,)),
+            dma((8,)),
+            dma((8,)),
+            dma((8,)),
+            dma((4,)),
+            dma((4,)),
+            dma((8,)),
+            dma((8,)),
+        ],
+        compiler_params=pltpu.CompilerParams(
+            collective_id=1, has_side_effects=True, vmem_limit_bytes=VMEM_BYTES
+        ),
+        name="ffn_forward",
+    )(slots, gate_weight, up_weight, down_weight)
+
+
+def send_rows_body(slots, rows_out, local_sem, send, recv, pass_send, pass_recv):
+    me = lax.axis_index("expert")
+    enter(8, me)
+    dispatch = Dispatch(me, slots, rows_out, local_sem.at[0], send, recv, pass_send, pass_recv)
+    dispatch.start()
+    for step in range(4):
+        dispatch.arrive(step)
+    for step in range(4):
+        dispatch.ready(step)
+    dispatch.finish()
+
+
+def send_rows(slots, collective):
+    chips, capacity, depth = slots.shape
+    any_space = pl.BlockSpec(memory_space=pl.ANY)
+    dma = pltpu.SemaphoreType.DMA
+    return pl.pallas_call(
+        send_rows_body,
+        in_specs=[any_space],
+        out_specs=any_space,
+        out_shape=jax.ShapeDtypeStruct((chips, 2 * capacity, depth), jnp.bfloat16),
+        scratch_shapes=[dma((1,)), dma((8,)), dma((8,)), dma((8,)), dma((8,))],
+        compiler_params=pltpu.CompilerParams(collective_id=collective, has_side_effects=True),
+        name="send_rows",
+    )(slots)
+
+
+def ffn_backward_body(
+    chunk,
+    grad_rows,
+    gate_in,
+    up_in,
+    gate_hbm,
+    up_hbm,
+    down_hbm,
+    dgate_out,
+    dup_out,
+    back,
+    gate,
+    up,
+    down,
+    grad,
+    pre_stage,
+    pair,
+    kept,
+    passing,
+    passed,
+    total,
+    weight_sem,
+    grad_sem,
+    stage_sem,
+    pair_sem,
+    local_sem,
+    swap_send,
+    swap_recv,
+    out_send,
+    out_recv,
+):
+    me = lax.axis_index("expert")
+    enter(8, me)
+    collect = Collect(
+        me, True, kept, passing, passed, total, back, local_sem.at[0], swap_send, swap_recv, out_send, out_recv
+    )
+    loads = [
+        pltpu.make_async_copy(source, target, weight_sem.at[n])
+        for n, (source, target) in enumerate(((down_hbm, down), (gate_hbm, gate), (up_hbm, up)))
+    ]
+    block = grad.shape[1]
+    hidden_units = gate.shape[1]
+    chunks = hidden_units // chunk
+    half = back.shape[2] // 2
+    width = min(256, half)
+
+    def span_of(chip):
+        return pl.ds(pl.multiple_of(chip * block, 16), block)
+
+    def grad_copy(step):
+        return pltpu.make_async_copy(
+            grad_rows.at[span_of(collect.block(step)), :], grad.at[step % 2], grad_sem.at[step % 2]
+        )
+
+    def stage_copies(chip, part, slot):
+        columns = pl.ds(pl.multiple_of(part * chunk, 128), chunk)
+        return [
+            pltpu.make_async_copy(
+                source.at[span_of(chip), columns], pre_stage.at[slot, n], stage_sem.at[slot, n]
+            )
+            for n, source in enumerate((gate_in, up_in))
+        ]
+
+    def pair_copies(chip):
+        return [
+            pltpu.make_async_copy(pair.at[n], out.at[span_of(chip), :], pair_sem.at[n])
+            for n, out in enumerate((dgate_out, dup_out))
+        ]
+
+    grad_copy(0).start()
+    loads[0].start()
+    for copy in stage_copies(collect.block(0), 0, 0):
+        copy.start()
+    loads[1].start()
+    loads[2].start()
+    loads[0].wait()
+    for step in range(4):
+        chip = collect.block(step)
+        grad_copy(step).wait()
+        if step < 3:
+            grad_copy(step + 1).start()
+        if step > 0:
+            for copy in pair_copies(collect.block(step - 1)):
+                copy.wait()
+
+        def hidden_part(part, carry, chip=chip, step=step):
+            slot = lax.rem(part, 2)
+            columns = pl.ds(pl.multiple_of(part * chunk, 128), chunk)
+            for copy in stage_copies(chip, part, slot):
+                copy.wait()
+
+            @pl.when(part + 1 < chunks)
+            def _():
+                for copy in stage_copies(chip, part + 1, 1 - slot):
+                    copy.start()
+
+            upstream = dot_nn(grad[step % 2], down[:, columns])
+            gated = pre_stage[slot, 0].astype(jnp.float32)
+            raised = pre_stage[slot, 1].astype(jnp.float32)
+            sigmoid = jax.nn.sigmoid(gated)
+            scaled = upstream * sigmoid
+            pair[0, :, columns] = (scaled * raised * (1.0 + gated * (1.0 - sigmoid))).astype(jnp.bfloat16)
+            pair[1, :, columns] = (scaled * gated).astype(jnp.bfloat16)
+            return carry
+
+        lax.fori_loop(0, chunks, hidden_part, 0)
+        for copy in pair_copies(chip):
+            copy.start()
+        if step < 3:
+            for copy in stage_copies(collect.block(step + 1), 0, 0):
+                copy.start()
+        if step == 0:
+            loads[1].wait()
+            loads[2].wait()
+        else:
+            collect.settle(step - 1)
+        core = collect.core
+
+        def product(at):
+            return dot_nt(pair[0], gate[pl.ds(at, width), :]) + dot_nt(pair[1], up[pl.ds(at, width), :])
+
+        def far_part(part, carry, step=step):
+            at = pl.multiple_of((1 - core) * half + part * width, 128)
+            columns = pl.ds(pl.multiple_of(part * width, 128), width)
+            passing[step, :, columns] = product(at).astype(jnp.bfloat16)
+            return carry
+
+        def near_part(part, carry, step=step):
+            at = pl.multiple_of(core * half + part * width, 128)
+            kept[step % 2, :, pl.ds(pl.multiple_of(part * width, 128), width)] = product(at)
+            return carry
+
+        lax.fori_loop(0, half // width, far_part, 0)
+        collect.swap(step).start()
+        lax.fori_loop(0, half // width, near_part, 0)
+    collect.settle(3)
+    for copy in pair_copies(collect.block(3)):
+        copy.wait()
+    collect.finish()
+
+
+def ffn_backward(grad_rows, gate_pre, up_pre, gate_weight, up_weight, down_weight, capacity):
+    rows, depth = grad_rows.shape
+    hidden_units = gate_weight.shape[1]
+    block = 2 * capacity
+    chips = rows // block
+    chunk = 256 if hidden_units % 256 == 0 else 128
+    half = depth // 2
+    any_space = pl.BlockSpec(memory_space=pl.ANY)
+    bf = jnp.bfloat16
+    dma = pltpu.SemaphoreType.DMA
+    return pl.pallas_call(
+        functools.partial(ffn_backward_body, chunk),
+        in_specs=[any_space] * 6,
+        out_specs=[any_space] * 3,
+        out_shape=[
+            jax.ShapeDtypeStruct((rows, hidden_units), bf),
+            jax.ShapeDtypeStruct((rows, hidden_units), bf),
+            jax.ShapeDtypeStruct((chips, capacity, depth), bf),
+        ],
+        scratch_shapes=[
+            pltpu.VMEM((depth, hidden_units), bf),
+            pltpu.VMEM((depth, hidden_units), bf),
+            pltpu.VMEM((depth, hidden_units), bf),
+            pltpu.VMEM((2, block, depth), bf),
+            pltpu.VMEM((2, 2, block, chunk), bf),
+            pltpu.VMEM((2, block, hidden_units), bf),
+            pltpu.VMEM((2, block, half), jnp.float32),
+            pltpu.VMEM((chips, block, half), bf),
+            pltpu.VMEM((chips, block, half), bf),
+            pltpu.VMEM((chips, block, half), bf),
+            dma((3,)),
+            dma((2,)),
+            dma((2, 2)),
+            dma((2,)),
+            dma((1,)),
+            dma((4,)),
+            dma((4,)),
+            dma((8,)),
+            dma((8,)),
+        ],
+        compiler_params=pltpu.CompilerParams(
+            collective_id=3, has_side_effects=True, vmem_limit_bytes=VMEM_BYTES
+        ),
+        name="ffn_backward",
+    )(grad_rows, gate_pre, up_pre, gate_weight, up_weight, down_weight)
 
 
 D = 2048
@@ -491,6 +1118,17 @@
     for step in range(1, size):
         total = total + shift(parts[step], -step, size, devices).astype(f32)
     return total.astype(bf16)
+
+
+def spread_over_replicas(block, my_replica, replicas):
+    if replicas != 4:
+        return lax.all_gather(block, "dp", axis=0), jnp.arange(replicas, dtype=jnp.int32)
+    across, along = ([(i, i ^ n) for i in range(4)] for n in (1, 2))
+    first, second = lax.ppermute(block, "dp", across), lax.ppermute(block, "dp", along)
+    cut = block.shape[0] // 2
+    upper, lower = lax.ppermute(second[:cut], "dp", across), lax.ppermute(first[cut:], "dp", along)
+    blocks = jnp.stack([block, first, second, jnp.concatenate([upper, lower])])
+    return blocks, my_replica ^ jnp.arange(4, dtype=jnp.int32)
 
 
 def dot_tn(left, right):
@@ -538,14 +1176,12 @@
     kv_share = (
         kv_share.reshape(weight_rows, 2, 2, piece).transpose(0, 2, 1, 3).reshape(weight_rows, 4 * piece)
     )
-    route_row = jnp.pad(att_routes.astype(bf16).reshape(1, -1), ((0, row_count - weight_rows - 1), (0, 4 * piece - 2 * row_count)))
-    sending = jnp.concatenate([hidden, jnp.concatenate([kv_share, route_row])], axis=1)
-    gathered = lax.all_gather(sending, "expert", axis=0)
-    kv_half = lax.dynamic_slice_in_dim(gathered[:, :weight_rows], D + core * 2 * piece, 2 * piece, 2)
-    kv_blocks = lax.all_gather(kv_half.reshape(D, 2 * piece), "dp", axis=0)
-    all_routes = (
-        gathered[:, weight_rows, D : D + 2 * row_count].astype(jnp.int32).reshape(devices, row_count, 2)
-    )
+    all_routes = lax.all_gather(att_routes, "expert", axis=0)
+    kv_gathered = lax.all_gather(kv_share, "expert", axis=0)
+    kv_gathered, hidden_sent = lax.optimization_barrier((kv_gathered, hidden))
+    hidden_all = lax.all_gather(hidden_sent, "expert", axis=0)
+    kv_half = lax.dynamic_slice_in_dim(kv_gathered, core * 2 * piece, 2 * piece, 2).reshape(D, 2 * piece)
+    kv_blocks, block_order = spread_over_replicas(kv_half, my_replica, replicas)
 
     tree_places = jnp.arange(token_count, dtype=jnp.int32)
     tree_segments, tree_depths = tree_layout(tree_places)
@@ -567,12 +1203,15 @@
         slot_tables.append(rotation_tables(depths))
     query_info = jnp.concatenate(query_parts, axis=2).transpose(1, 0, 2)
     own_plan = plans[0].astype(bf16)
-    query_inputs = jnp.einsum(
-        "scr,srd->scd", own_plan, gathered[:, :, :D], preferred_element_type=f32
-    ).astype(bf16).reshape(-1, D)
-
-    queries = project_queries(query_inputs, q_weight, slot_tables[0][0])
-    keys_all, values_all = project_keys_values(gathered, kv_blocks, key_forward)
+    att_picks, att_first, att_second = token_picks(att_routes, ATT_EXPERTS, att_capacity)
+    att_gates = gate_values(hidden, att_router, att_first, att_second)
+    ffn_picks, ffn_first, ffn_second = token_picks(ffn_routes, FFN_EXPERTS, ffn_capacity)
+    prepared = (key_forward, key_backward, key_info, slot_tables, query_info, own_plan, att_picks, att_gates, ffn_picks)
+    hidden_all, prepared = lax.optimization_barrier((hidden_all, prepared))
+    key_forward, key_backward, key_info, slot_tables, query_info, own_plan, att_picks, att_gates, ffn_picks = prepared
+
+    queries, query_inputs = project_queries(own_plan, hidden_all, q_weight, slot_tables[0][0])
+    keys_all, values_all = project_keys_values(hidden_all, kv_blocks, key_forward, block_order)
 
     def far_half(values):
         return lax.ppermute(
@@ -601,8 +1240,6 @@
         att_rows, o_weight, (((1,), (1,)), ((), ())), preferred_element_type=f32
     ).astype(bf16)
     att_back = exchange(att_partial.reshape(devices, att_capacity, D))
-    att_picks, att_first, att_second = token_picks(att_routes, ATT_EXPERTS, att_capacity)
-    att_gates = gate_values(hidden, att_router, att_first, att_second)
     if att_copies > 1:
         att_back = (
             att_back.astype(f32).reshape(ATT_EXPERTS, att_copies, att_capacity, D).sum(axis=1).astype(bf16)
@@ -612,7 +1249,6 @@
 
     normed_two, inverse_two = rms_parts(x_mid)
     hidden_two = (normed_two * gain_two).astype(bf16)
-    ffn_picks, ffn_first, ffn_second = token_picks(ffn_routes, FFN_EXPERTS, ffn_capacity)
     ffn_gates = gate_values(hidden_two, ffn_router, ffn_first, ffn_second)
 
     def to_experts(slots):
@@ -624,19 +1260,27 @@
         back = exchange(rows.reshape(devices, ffn_capacity // ffn_copies, D))
         return read_slots(ffn_picks, back.reshape(FFN_EXPERTS, ffn_capacity, D))
 
-    ffn_inputs = to_experts(
-        jnp.einsum(
-            "ecr,rd->ecd", ffn_picks[0] + ffn_picks[1], hidden_two, preferred_element_type=f32
-        ).astype(bf16)
-    )
-    gate_pre = jnp.dot(ffn_inputs, gate_weight, preferred_element_type=f32)
-    up_pre = jnp.dot(ffn_inputs, up_weight, preferred_element_type=f32)
-    sigmoid_gate = jax.nn.sigmoid(gate_pre)
-    silu_gate = gate_pre * sigmoid_gate
-    activated = (silu_gate * up_pre).astype(bf16)
-    ffn_branches = to_tokens(
-        lax.dot_general(activated, down_weight, (((1,), (1,)), ((), ())), preferred_element_type=f32)
-    )
+    ffn_slots = jnp.einsum(
+        "ecr,rd->ecd", ffn_picks[0] + ffn_picks[1], hidden_two, preferred_element_type=f32
+    ).astype(bf16)
+    fused = devices == 8 and ffn_copies == 2 and ffn_capacity % 16 == 0
+    if fused:
+        ffn_inputs, gate_pre, up_pre, activated, ffn_back = ffn_forward(
+            ffn_slots, gate_weight, up_weight, down_weight
+        )
+        ffn_branches = read_slots(ffn_picks, ffn_back)
+    else:
+        ffn_inputs = to_experts(ffn_slots)
+        gate_pre = jnp.dot(ffn_inputs, gate_weight, preferred_element_type=f32)
+        up_pre = jnp.dot(ffn_inputs, up_weight, preferred_element_type=f32)
+        sigmoid_gate = jax.nn.sigmoid(gate_pre)
+        silu_gate = gate_pre * sigmoid_gate
+        activated = (silu_gate * up_pre).astype(bf16)
+        ffn_branches = to_tokens(
+            lax.dot_general(
+                activated, down_weight, (((1,), (1,)), ((), ())), preferred_element_type=f32
+            )
+        )
     result = x_mid + ffn_gates[:, 0:1] * ffn_branches[0] + ffn_gates[:, 1:2] * ffn_branches[1]
 
     tree_global = my_replica * parent.shape[0] + own_places // TREE_LEN
@@ -649,26 +1293,37 @@
     grad_result = jnp.where(counted[:, None], (result - teacher.astype(f32)) * loss_factor, 0.0)
 
     ffn_gate_grad, ffn_scaled = pair_grads(ffn_gates, ffn_branches, grad_result)
-    grad_ffn_out = to_experts(fill_slots(ffn_picks, ffn_scaled))
+    ffn_grad_slots = fill_slots(ffn_picks, ffn_scaled)
+    if fused:
+        grad_ffn_out = send_rows(ffn_grad_slots, 2).reshape(-1, D)
+    else:
+        grad_ffn_out = to_experts(ffn_grad_slots)
     grad_down = dot_tn(grad_ffn_out, activated).astype(bf16)
     grad_ffn_out, grad_down = lax.optimization_barrier((grad_ffn_out, grad_down))
     summed_down = lax.psum_scatter(grad_down, "dp", scatter_dimension=0, tiled=True)
-    grad_activated = jnp.dot(grad_ffn_out, down_weight, preferred_element_type=f32)
-    grad_gate_pre = (
-        grad_activated * up_pre * sigmoid_gate * (1.0 + gate_pre * (1.0 - sigmoid_gate))
-    ).astype(bf16)
-    grad_up_pre = (grad_activated * silu_gate).astype(bf16)
-    grad_ffn_in = lax.dot_general(
-        grad_gate_pre, gate_weight, (((1,), (1,)), ((), ())), preferred_element_type=f32
-    ) + lax.dot_general(
-        grad_up_pre, up_weight, (((1,), (1,)), ((), ())), preferred_element_type=f32
-    )
-    grad_gate = dot_tn(ffn_inputs, grad_gate_pre).astype(bf16)
+    if fused:
+        grad_gate_pre, grad_up_pre, ffn_grad_back = ffn_backward(
+            grad_ffn_out, gate_pre, up_pre, gate_weight, up_weight, down_weight, ffn_capacity
+        )
+        grad_gate = dot_tn(ffn_inputs, grad_gate_pre).astype(bf16)
+        ffn_grad_back, grad_gate = lax.optimization_barrier((ffn_grad_back, grad_gate))
+        ffn_grad_pair = read_slots(ffn_picks, ffn_grad_back)
+    else:
+        grad_activated = jnp.dot(grad_ffn_out, down_weight, preferred_element_type=f32)
+        grad_gate_pre = (
+            grad_activated * up_pre * sigmoid_gate * (1.0 + gate_pre * (1.0 - sigmoid_gate))
+        ).astype(bf16)
+        grad_up_pre = (grad_activated * silu_gate).astype(bf16)
+        grad_ffn_in = lax.dot_general(
+            grad_gate_pre, gate_weight, (((1,), (1,)), ((), ())), preferred_element_type=f32
+        ) + lax.dot_general(
+            grad_up_pre, up_weight, (((1,), (1,)), ((), ())), preferred_element_type=f32
+        )
+        grad_gate = dot_tn(ffn_inputs, grad_gate_pre).astype(bf16)
+        ffn_grad_pair = to_tokens(grad_ffn_in)
     grad_up = dot_tn(ffn_inputs, grad_up_pre).astype(bf16)
     summed_gate = lax.psum_scatter(grad_gate, "dp", scatter_dimension=0, tiled=True)
     summed_up = lax.psum_scatter(grad_up, "dp", scatter_dimension=0, tiled=True)
-    ffn_grad_pair = to_tokens(grad_ffn_in)
-    ffn_grad_pair, grad_gate, grad_up = lax.optimization_barrier((ffn_grad_pair, grad_gate, grad_up))
     grad_ffn_router, hidden_two_extra = router_grads(
         hidden_two, ffn_router, ffn_gates, ffn_first, ffn_second, ffn_gate_grad
     )
@@ -689,7 +1344,7 @@
     grad_sets = [grad_heads]
     if att_copies == 1:
         grad_sets.append(far_half(grad_heads))
-    grad_sets[-1], summed_gate = lax.optimization_barrier((grad_sets[-1], summed_gate))
+    grad_sets[-1], summed_gate, grad_up = lax.optimization_barrier((grad_sets[-1], summed_gate, grad_up))
     *grad_queries, grad_keys, grad_values = attention_backward(
         query_sets,
         starts,
@@ -709,8 +1364,8 @@
         grad_query_pre, q_weight, (((1,), (1,)), ((), ())), preferred_element_type=f32
     ).astype(bf16)
     grad_q = dot_tn(query_inputs, grad_query_pre).astype(bf16)
-    grad_query_in, summed_up = lax.optimization_barrier((grad_query_in, summed_up))
-    hidden_rows = gathered[:, :, :D].reshape(token_count, D)
+    grad_query_in, summed_up, summed_o = lax.optimization_barrier((grad_query_in, summed_up, summed_o))
+    hidden_rows = hidden_all.reshape(token_count, D)
     grad_kv = jnp.concatenate(
         [dot_tn(hidden_rows, grad_keys).astype(bf16), dot_tn(hidden_rows, grad_values).astype(bf16)], axis=1
     )
@@ -723,6 +1378,7 @@
         grad_keys,
         grad_values,
         kv_blocks,
+        block_order,
     ).reshape(devices // 2, 2, row_count, D)
     kept = lax.dynamic_index_in_dim(merged, core, 1, keepdims=False)
     passed = lax.ppermute(

time: 1490 us -> 1340 us (0.90)
  Pallas kernels: 204 us -> 552 us
  waiting for transfers between devices: 505 us -> 319 us
  matrix products: 349 us -> 191 us
  blocking collectives: 208 us -> 83.6 us
  local copies, waits for them, and re-layouts: 77.4 us -> 55.5 us
    pallas_call x3 -> x6, Pallas kernels: 66.4 us -> 415 us  [the longest x1 152 us: ffn_forward(): pl.pallas_call(functools.partial(ffn_forward_body, chunk), in_specs=[any_...]
    dot_general x7 -> x0, matrix products: 159 us -> none  [the longest x1 32 us: body(): jnp.dot(grad_ffn_out, down_weight, preferred_element_type=f32)]
    all_to_all x3 -> x1, blocking collectives: 208 us -> 69.7 us  [exchange(): lax.all_to_all(slots, 'expert', split_axis=0, concat_axis=0, tiled=True)]
    all_gather x2, waiting for transfers between devices: 157 us -> 48.5 us  [the longest x1 48.2 us: body(): kv_gathered = lax.all_gather(kv_share, 'expert', axis=0)]
    all_to_all x4 -> x2, waiting for transfers between devices: 191 us -> 91.9 us  [exchange(): lax.all_to_all(slots, 'expert', split_axis=0, concat_axis=0, tiled=True)]
    reduce_scatter x1, waiting for transfers between devices: 0.01 us -> 38.4 us  [body(): summed_o = lax.psum_scatter(grad_o, 'dp', scatter_dimension=0, tiled=True)]
    reduce_scatter x1, waiting for transfers between devices: 35 us -> 0.01 us  [body(): summed_q = lax.psum_scatter(grad_q, 'dp', scatter_dimension=0, tiled=True)]
    reduce_scatter x1, waiting for transfers between devices: 0.01 us -> 28.3 us  [body(): summed_kv = lax.psum_scatter(grad_kv, 'dp', scatter_dimension=0, tiled=True)]
  transfers between devices with their start and end apart: 23 -> 21, of which waited for: 14 -> 13; matrix products, arithmetic and copies ran while one was open for 24% -> 19% of each run, Pallas kernels for 10% -> 21%
where the time goes in v3:
time: 1340 us; the launch traced here: 1330 us
  Pallas kernels  552 us (41%)
  waiting for transfers between devices  319 us (24%)
  matrix products  191 us (14%)
  other arithmetic  86.8 us (6%)
  blocking collectives  83.6 us (6%)
  local copies, waits for them, and re-layouts  55.5 us (4%)
  starting transfers between devices  24.9 us (2%)
  between operations  16.4 us (1%)
    pallas_call x1, Pallas kernels, ffn_forward(): pl.pallas_call(functools.partial(ffn_forward_body, chunk), in_specs=[any_...  152 us
    pallas_call x1, Pallas kernels, ffn_backward(): pl.pallas_call(functools.partial(ffn_backward_body, chunk), in_specs=[any...  130 us
    dot_general x7, matrix products, dot_tn(): lax.dot_general(left, right, (((0,), (0,)), ((), ())), preferred_element_...  122 us
    all_to_all x2, waiting for transfers between devices, exchange(): lax.all_to_all(slots, 'expert', split_axis=0, concat_axis=0, tiled=True)  91.9 us
    pallas_call x1, Pallas kernels, attention_backward(): pl.pallas_call(functools.partial(attention_backward_body, sets, step_head...  79.8 us
    all_to_all x1, blocking collectives, exchange(): lax.all_to_all(slots, 'expert', split_axis=0, concat_axis=0, tiled=True)  69.7 us
    all_to_all x1, waiting for transfers between devices, body(): lax.all_to_all(chip_sum, 'expert', split_axis=0, concat_axis=0, axis_inde...  66.2 us
    pallas_call x1, Pallas kernels, send_rows(): pl.pallas_call(send_rows_body, in_specs=[any_space], out_specs=any_space,...  61.4 us
  transfers between devices with their start and end apart: 21, of which 13 were waited for; matrix products, arithmetic and copies ran while one was open for 19% of the time, Pallas kernels for 21%

profile of v3, /device:TPU:0, one launch (start us, length us, event | category | flops | bytes accessed | tf_op | source)
XLA Modules:
  0.0 1329.2 jit_solution(4494394808711293026)
XLA Ops:
  13.4 48.2 %all-gather.6.cloned.1.call-done = bf16[8,256,1024]{2,1,0:T(8,128)(2,1)} async-done(((bf16[1,256,1024]{2,1,0:T(8,128)(2,1)}), bf16[8,256,1024]{2,1,0:T(8,128)(2,1)}) %all-gather.6.cloned.1.call-update) | async-done | bytes 4194320 | tf_op jit(solution)/shard_map/all_gather | solution.py:1180
  61.7 13.9 %all-gather.2 = s32[8,272,2]{1,2,0:T(2,128)S(1)} all-gather(s32[1,272,2]{1,2,0:T(2,128)S(1)} %bitcast.224), channel_id=3, replica_groups=mesh['dp'=4,'expert'=8] {'expert'}, dimensions={0}, use_global_device_ids=true | all-gather | bytes 19584 | tf_op jit(solution)/shard_map/all_gather | solution.py:1179
  82.4 3.6 multiply_cosine_fusion.1
  111.5 3.9 fusion.38
  116.9 21.9 %collective-permute-done.2 = bf16[2048,512]{1,0:T(8,128)(2,1)} collective-permute-done((bf16[2048,512]{1,0:T(8,128)(2,1)S(1)}, bf16[2048,512]{1,0:T(8,128)(2,1)}, u32[]{:S(2)}, u32[]{:S(2)}) %collective-permute-start.2) | collective-permute-done | bytes 2097184 | tf_op jit(solution)/shard_map/ppermute | solution.py:1127
  151.2 15.4 %project_queries.1 = (bf16[704,2048]{1,0:T(8,128)(2,1)}, bf16[704,2048]{1,0:T(8,128)(2,1)}) custom-call(bf16[8,88,272]{2,1,0:T(8,128)(2,1)} %copy.86.plan_ref, bf16[8,272,2048]{2,1,0:T(8,128)(2,1)} %bitcast.204, bf16[2048,2048]{1,0:T(8,128)(2,1)} %weight_ref.1, f32[704,128]{1,0:T(8,128)} %get-tuple-element.101.cos_ref.refs_13_, ...), custom_call_target="tpu_custom_call" | custom-call | tf_op jit(solution)/shard_map/project_queries/pallas_call | solution.py:290
  172.2 6.2 pad_maximum_fusion.weight_ref
  178.4 26.2 %project_keys_values.1 = (bf16[2176,1024]{1,0:T(8,128)(2,1)}, bf16[2176,1024]{1,0:T(8,128)(2,1)}) custom-call(s32[4]{0:T(128)} %iota_xor_fusion.order_ref, bf16[8,272,2048]{2,1,0:T(8,128)(2,1)} %bitcast.205, bf16[4,2048,512]{2,1,0:T(8,128)(2,1)} %pad_maximum_fusion.weight_ref, f32[2176,128]{1,0:T(8,128)} %pad_maximum_fusion.2.cos_ref.refs_11_, ...), custom_call_target="tpu_custom_call" | custom-call | tf_op jit(solution)/shard_map/project_keys_values/pallas_call | solution.py:328
  204.5 57.2 %attention_forward.1 = (bf16[704,1024]{1,0:T(8,128)(2,1)}, bf16[704,1024]{1,0:T(8,128)(2,1)}, f32[8,4,352]{2,1,0:T(4,128)}) custom-call(s32[2]{0:T(128)} %get-tuple-element.239.first_ref, bf16[704,2048]{1,0:T(8,128)(2,1)} %get-tuple-element.72.refs_0_, bf16[704,1024]{1,0:T(8,128)(2,1)} %collective-permute-done.refs_1_, ...), custom_call_target="tpu_custom_call" | custom-call | tf_op jit(solution)/shard_map/attention_forward/pallas_call | solution.py:185
  265.2 11.8 convolution_convert_fusion.9
  277.1 4.6 all-to-all-start
  283.2 64.4 %all-to-all-done = bf16[8,88,2048]{2,1,0:T(8,128)(2,1)} async-done(((bf16[8,88,2048]{2,1,0:T(8,128)(2,1)}), bf16[8,88,2048]{2,1,0:T(8,128)(2,1)}, u32[]{:S(2)}, u32[]{:S(2)}) %all-to-all-start) | async-done | bytes 2883616 | tf_op jit(solution)/shard_map/all_to_all | solution.py:1103
  347.6 3.8 convolution_bitcast_fusion.2
  358.6 152.5 %ffn_forward.1 = (bf16[1408,2048]{1,0:T(8,128)(2,1)}, bf16[1408,2816]{1,0:T(8,128)(2,1)}, bf16[1408,2816]{1,0:T(8,128)(2,1)}, bf16[1408,2816]{1,0:T(8,128)(2,1)}, bf16[4,176,2048]{2,1,0:T(8,128)(2,1)}) custom-call(bf16[4,176,2048]{2,1,0:T(8,128)(2,1)} %convolution_convert_fusion.10.slots, bf16[2048,2816]{1,0:T(8,128)(2,1)} %gate_hbm.3, ...), custom_call_target="tpu_custom_call" | custom-call | tf_op jit(solution)/shard_map/ffn_forward/pallas_call | solution.py:738
  511.1 3.9 convolution_bitcast_fusion.1
  518.7 4.0 bitcast_convert_fusion.1.slots
  522.6 61.4 %send_rows.1 = bf16[4,352,2048]{2,1,0:T(8,128)(2,1)} custom-call(bf16[4,176,2048]{2,1,0:T(8,128)(2,1)} %bitcast_convert_fusion.1.slots), custom_call_target="tpu_custom_call" | custom-call | tf_op jit(solution)/shard_map/send_rows/pallas_call | solution.py:797
  584.0 24.4 %convolution_convert_fusion.2 = bf16[2048,2816]{1,0:T(8,128)(2,1)} fusion(bf16[1408,2048]{1,0:T(8,128)(2,1)} %bitcast.208, bf16[1408,2816]{1,0:T(8,128)(2,1)} %get-tuple-element.84), kind=kOutput, calls=%fused_computation.2 | convolution fusion | flops 16246112256 | bytes 25231360 | tf_op jit(solution)/shard_map/dot_general | solution.py:1135
  608.4 129.5 %ffn_backward.1 = (bf16[1408,2816]{1,0:T(8,128)(2,1)}, bf16[1408,2816]{1,0:T(8,128)(2,1)}, bf16[4,176,2048]{2,1,0:T(8,128)(2,1)}) custom-call(bf16[1408,2048]{1,0:T(8,128)(2,1)} %bitcast.209, bf16[1408,2816]{1,0:T(8,128)(2,1)} %get-tuple-element.86.gate_in, bf16[1408,2816]{1,0:T(8,128)(2,1)} %get-tuple-element.87.up_in, bf16[2048,2816]{1,0:T(8,128)(2,1)} %gate_hbm.3, ...), custom_call_target="tpu_custom_call" | custom-call | tf_op jit(solution)/shard_map/ffn_backward/pallas_call | solution.py:959
  738.0 24.5 %convolution_convert_fusion.1 = bf16[2048,2816]{1,0:T(8,128)(2,1)} fusion(bf16[1408,2048]{1,0:T(8,128)(2,1)} %get-tuple-element.89, bf16[1408,2816]{1,0:T(8,128)(2,1)} %get-tuple-element.90), kind=kOutput, calls=%fused_computation.1 | convolution fusion | flops 16246112256 | bytes 25231360 | tf_op jit(solution)/shard_map/dot_general | solution.py:1135
  762.6 24.2 %convolution_convert_fusion = bf16[2048,2816]{1,0:T(8,128)(2,1)} fusion(bf16[1408,2048]{1,0:T(8,128)(2,1)} %get-tuple-element.89, bf16[1408,2816]{1,0:T(8,128)(2,1)} %get-tuple-element.96), kind=kOutput, calls=%fused_computation | convolution fusion | flops 16246112256 | bytes 25231360 | tf_op jit(solution)/shard_map/dot_general | solution.py:1135
  787.2 4.2 convolution_bitcast_fusion
  800.0 69.7 %all_to_all.29 = bf16[8,88,2048]{2,1,0:T(8,128)(2,1)S(1)} all-to-all(bf16[8,88,2048]{2,1,0:T(8,128)(2,1)S(1)} %bitcast_convert_fusion), channel_id=1, replica_groups=mesh['dp'=4,'expert'=8] {'expert'}, dimensions={0} | all-to-all | bytes 5767168 | tf_op jit(solution)/shard_map/all_to_all | solution.py:1103
  871.3 9.4 convolution_convert_fusion.4
  881.0 9.4 convolution_convert_fusion.8.refs_2_
  891.9 3.6 collective-permute-done.6.refs_3_
  895.4 79.8 %attention_backward.1 = (bf16[704,1024]{1,0:T(8,128)(2,1)}, bf16[704,1024]{1,0:T(8,128)(2,1)}, bf16[2176,1024]{1,0:T(8,128)(2,1)}, bf16[2176,1024]{1,0:T(8,128)(2,1)}) custom-call(s32[2]{0:T(128)} %get-tuple-element.240.first_ref, bf16[704,2048]{1,0:T(8,128)(2,1)} %get-tuple-element.72.refs_0_, bf16[704,1024]{1,0:T(8,128)(2,1)} %collective-permute-done.refs_1_, ...), custom_call_target="tpu_custom_call" | custom-call | tf_op jit(solution)/shard_map/attention_backward/pallas_call | solution.py:219
  975.3 15.9 %convolution_convert_fusion.5 = bf16[2048,1024]{0,1:T(8,128)(2,1)} fusion(bf16[2176,2048]{1,0:T(8,128)(2,1)} %all-gather.8.cloned.1.call-done, bf16[2176,1024]{1,0:T(8,128)(2,1)} %get-tuple-element.110.dv_ref), kind=kOutput, calls=%fused_computation.13 | convolution fusion | flops 9128902656 | bytes 17563648 | tf_op jit(solution)/shard_map/dot_general | solution.py:1135
  991.3 11.8 convolution_convert_fusion.6
  1003.1 8.6 pad_maximum_fusion.1
  1015.4 12.2 convolution_convert_fusion.3
  1029.2 11.7 convolution_convert_fusion.7
  1040.9 38.4 %reduce-scatter.13.cloned.1.call-done = bf16[512,2048]{1,0:T(8,128)(2,1)} async-done(((bf16[2048,2048]{1,0:T(8,128)(2,1)}), bf16[512,2048]{1,0:T(8,128)(2,1)}) %reduce-scatter.13.cloned.1.call-update) | async-done | bytes 2097168 | tf_op jit(solution)/shard_map/reduce_scatter | solution.py:1342
  1079.3 30.1 %merge_hidden_grads.1 = bf16[2176,2048]{1,0:T(8,128)(2,1)} custom-call(s32[4]{0:T(128)} %iota_xor_fusion.order_ref, bf16[8,272,88]{2,1,0:T(8,128)(2,1)} %bitcast.215, bf16[8,88,2048]{2,1,0:T(8,128)(2,1)} %bitcast.218, bf16[2176,1024]{1,0:T(8,128)(2,1)} %get-tuple-element.109.dk_ref, bf16[2176,1024]{1,0:T(8,128)(2,1)} %get-tuple-element.110.dv_ref, ...), custom_call_target="tpu_custom_call" | custom-call | tf_op jit(solution)/shard_map/merge_hidden_grads/pallas_call | solution.py:374
  1109.4 5.1 dynamic-slice_bitcast_fusion
  1114.5 7.9 collective-permute-done.8
  1122.4 8.5 fusion
  1130.9 5.0 all-to-all-start.2
  1140.7 28.3 %reduce-scatter.15.cloned.1.call-done = bf16[512,2048]{0,1:T(8,128)(2,1)} async-done(((bf16[2048,2048]{0,1:T(8,128)(2,1)}), bf16[512,2048]{0,1:T(8,128)(2,1)}) %reduce-scatter.15.cloned.1.call-update) | async-done | bytes 2097168 | tf_op jit(solution)/shard_map/reduce_scatter | solution.py:1372
  1169.1 66.2 %all-to-all-done.2 = bf16[4,272,2048]{2,1,0:T(8,128)(2,1)} async-done(((bf16[4,272,2048]{2,1,0:T(8,128)(2,1)}), bf16[4,272,2048]{2,1,0:T(8,128)(2,1)}, u32[]{:S(2)}, u32[]{:S(2)}) %all-to-all-start.2) | async-done | bytes 4456480 | tf_op jit(solution)/shard_map/all_to_all | solution.py:1389
  1238.7 4.0 fusion.14
  1249.0 5.6 all-to-all-done.3
  1254.7 4.6 all-to-all-start.4
  1259.3 4.9 convert_element_type.196
  1272.7 4.3 convert_element_type.192
  1280.8 27.5 %all-to-all-done.4 = bf16[8,64,2048]{2,1,0:T(8,128)(2,1)} async-done(((bf16[8,64,2048]{2,1,0:T(8,128)(2,1)}), bf16[8,64,2048]{2,1,0:T(8,128)(2,1)}, u32[]{:S(2)}, u32[]{:S(2)}) %all-to-all-start.4) | async-done | bytes 2097184 | tf_op jit(solution)/shard_map/all_to_all | solution.py:1103
  1308.3 6.6 reshape.681
  1314.9 4.3 reduce_sum.289
  (302 shorter events, 119.6 us)
Async XLA Ops:
  7.2 71.3 %copy-start = (f32[2048,8]{0,1:T(8,128)S(1)}, f32[2048,8]{0,1:T(8,128)}, u32[]{:S(2)}) copy-start(f32[2048,8]{0,1:T(8,128)} %param.24) | copy-start | bytes 196612
  7.2 54.5 %all-gather.6.cloned.1.call-start = ((), (), s32[]{:S(2)}) async-start(), calls=%async_computation.11 | async-start | bytes 4718592 | tf_op jit(solution)/shard_map/all_gather | solution.py:1180
  11.7 50.0 %copy-start.56 = (s32[272,2]{0,1:T(2,128)S(1)}, s32[272,2]{0,1:T(2,128)}, u32[]{:S(2)}) copy-start(s32[272,2]{0,1:T(2,128)} %param.18) | copy-start | bytes 6532
  11.7 137.4 %all-gather.8.cloned.1.call-start = ((), (), s32[]{:S(2)}) async-start(), calls=%async_computation.18 | async-start | bytes 10027008 | tf_op jit(solution)/shard_map/all_gather | solution.py:1182
  12.1 63.8 %copy-start.46 = (f32[272]{0:T(512)}, f32[272]{0:T(512)S(1)}, u32[]{:S(2)}) copy-start(f32[272]{0:T(512)S(1)} %add_rsqrt_fusion.1) | copy-start | bytes 3268
  12.1 68.8 %copy-start.57 = (s32[1,13]{1,0:T(1,128)S(1)}, s32[1,13]{1,0:T(1,128)}, u32[]{:S(2)}) copy-start(s32[1,13]{1,0:T(1,128)} %param.20) | copy-start | bytes 160
  78.2 9.9 copy-start.40
  78.4 9.8 copy-start.42
  78.5 15.9 %copy-start.27 = (pred[2,8,272]{2,1,0:T(8,128)(4,1)}, pred[2,8,272]{2,1,0:T(8,128)(4,1)S(1)}, u32[]{:S(2)}) copy-start(pred[2,8,272]{2,1,0:T(8,128)(4,1)S(1)} %iota_compare_fusion.13) | copy-start | bytes 13060
  78.5 8.7 copy-start.58
  90.8 48.0 %collective-permute-start.2 = (bf16[2048,512]{1,0:T(8,128)(2,1)S(1)}, bf16[2048,512]{1,0:T(8,128)(2,1)}, u32[]{:S(2)}, u32[]{:S(2)}) collective-permute-start(bf16[2048,512]{1,0:T(8,128)(2,1)S(1)} %bitcast.212), channel_id=1, source_target_pairs={{0,16},{8,24},{16,0},{24,8},{1,17},{9,25},{17,1},{25,9},{2,18},{10... | collective-permute-start | bytes 6291464 | tf_op jit(solution)/shard_map/ppermute | solution.py:1127
  92.3 50.2 %collective-permute-start.1 = (bf16[2048,512]{1,0:T(8,128)(2,1)S(1)}, bf16[2048,512]{1,0:T(8,128)(2,1)}, u32[]{:S(2)}, u32[]{:S(2)}) collective-permute-start(bf16[2048,512]{1,0:T(8,128)(2,1)S(1)} %bitcast.213), channel_id=1, source_target_pairs={{0,8},{8,0},{16,24},{24,16},{1,9},{9,1},{17,25},{25,17},{2,10},{10... | collective-permute-start | bytes 6291464 | tf_op jit(solution)/shard_map/ppermute | solution.py:1127
  116.8 29.5 %copy-start.41 = (s32[1,4,176]{2,0,1:T(1,128)S(1)}, s32[1,4,176]{2,0,1:T(1,128)}, u32[]{:S(2)}) copy-start(s32[1,4,176]{2,0,1:T(1,128)} %copy-done.40) | copy-start | bytes 8452
  116.8 29.5 %copy-start.43 = (s32[1,4,176]{2,0,1:T(1,128)S(1)}, s32[1,4,176]{2,0,1:T(1,128)}, u32[]{:S(2)}) copy-start(s32[1,4,176]{2,0,1:T(1,128)} %copy-done.42) | copy-start | bytes 8452
  116.8 29.5 %copy-start.50 = (s32[1,4,176]{2,0,1:T(1,128)S(1)}, s32[1,4,176]{2,0,1:T(1,128)}, u32[]{:S(2)}) copy-start(s32[1,4,176]{2,0,1:T(1,128)} %stack.109) | copy-start | bytes 8452
  116.8 29.5 %copy-start.51 = (s32[1,4,176]{2,0,1:T(1,128)S(1)}, s32[1,4,176]{2,0,1:T(1,128)}, u32[]{:S(2)}) copy-start(s32[1,4,176]{2,0,1:T(1,128)} %stack.113) | copy-start | bytes 8452
  116.8 29.5 %copy-start.52 = (s32[1,4,176]{2,0,1:T(1,128)S(1)}, s32[1,4,176]{2,0,1:T(1,128)}, u32[]{:S(2)}) copy-start(s32[1,4,176]{2,0,1:T(1,128)} %stack.110) | copy-start | bytes 8452
  116.8 29.5 %copy-start.53 = (s32[1,4,176]{2,0,1:T(1,128)S(1)}, s32[1,4,176]{2,0,1:T(1,128)}, u32[]{:S(2)}) copy-start(s32[1,4,176]{2,0,1:T(1,128)} %stack.114) | copy-start | bytes 8452
  116.8 29.5 %copy-start.54 = (s32[1,4,176]{2,0,1:T(1,128)S(1)}, s32[1,4,176]{2,0,1:T(1,128)}, u32[]{:S(2)}) copy-start(s32[1,4,176]{2,0,1:T(1,128)} %get-tuple-element.245) | copy-start | bytes 8452
  116.9 29.5 %copy-start.55 = (s32[1,4,176]{2,0,1:T(1,128)S(1)}, s32[1,4,176]{2,0,1:T(1,128)}, u32[]{:S(2)}) copy-start(s32[1,4,176]{2,0,1:T(1,128)} %get-tuple-element.246) | copy-start | bytes 8452
  141.1 29.4 %collective-permute-start.3 = (bf16[1024,512]{1,0:T(8,128)(2,1)}, bf16[1024,512]{1,0:T(8,128)(2,1)}, u32[]{:S(2)}, u32[]{:S(2)}) collective-permute-start(bf16[1024,512]{1,0:T(8,128)(2,1)} %slice.136), channel_id=1, source_target_pairs={{0,8},{8,0},{16,24},{24,16},{1,9},{9,1},{17,25},{25,17},{2,10},{10... | collective-permute-start | bytes 3145736 | tf_op jit(solution)/shard_map/ppermute | solution.py:1129
  144.8 25.7 %collective-permute-start.4 = (bf16[1024,512]{1,0:T(8,128)(2,1)}, bf16[1024,512]{1,0:T(8,128)(2,1)}, u32[]{:S(2)}, u32[]{:S(2)}) collective-permute-start(bf16[1024,512]{1,0:T(8,128)(2,1)} %slice.137), channel_id=1, source_target_pairs={{0,16},{8,24},{16,0},{24,8},{1,17},{9,25},{17,1},{25,9},{2,18},{10... | collective-permute-start | bytes 3145736 | tf_op jit(solution)/shard_map/ppermute | solution.py:1129
  169.1 35.5 %collective-permute-start = (bf16[704,1024]{1,0:T(8,128)(2,1)}, bf16[704,1024]{1,0:T(8,128)(2,1)}, u32[]{:S(2)}, u32[]{:S(2)}) collective-permute-start(bf16[704,1024]{1,0:T(8,128)(2,1)} %constant_dynamic-slice_fusion.2), channel_id=1, source_target_pairs={{0,1},{1,0},{2,3},{3,2},{4,5},{5,4},{6,7},{7,6},{8,9},{9,8},{10,11... | collective-permute-start | bytes 4325384 | tf_op jit(solution)/shard_map/ppermute | solution.py:1217
  261.7 3.5 collective-permute-start.5
  265.2 11.8 copy-start.63
  277.1 70.5 %copy-start.21 = (bf16[2,8,88,272]{3,2,0,1:T(8,128)(2,1)S(1)}, bf16[2,8,88,272]{3,2,0,1:T(8,128)(2,1)}, u32[]{:S(2)}) copy-start(bf16[2,8,88,272]{3,2,0,1:T(8,128)(2,1)} %and_convert_fusion.1) | copy-start | bytes 2297860
  277.1 70.5 %all-to-all-start = ((bf16[8,88,2048]{2,1,0:T(8,128)(2,1)}), bf16[8,88,2048]{2,1,0:T(8,128)(2,1)}, u32[]{:S(2)}, u32[]{:S(2)}) async-start(bf16[8,88,2048]{2,1,0:T(8,128)(2,1)} %bitcast.219), calls=%async_computation | async-start | bytes 5767168 | tf_op jit(solution)/shard_map/all_to_all | solution.py:1103
  281.6 518.3 %reduce-scatter.7.cloned.1.call-start = ((), (), s32[]{:S(2)}) async-start(), calls=%async_computation.12 | async-start | bytes 14417920 | tf_op jit(solution)/shard_map/reduce_scatter | solution.py:1303
  608.4 283.5 %reduce-scatter.9.cloned.1.call-start = ((), (), s32[]{:S(2)}) async-start(), calls=%async_computation.13 | async-start | bytes 14417920 | tf_op jit(solution)/shard_map/reduce_scatter | solution.py:1325
  762.5 278.4 %reduce-scatter.11.cloned.1.call-start = ((), (), s32[]{:S(2)}) async-start(), calls=%async_computation.14 | async-start | bytes 14417920 | tf_op jit(solution)/shard_map/reduce_scatter | solution.py:1326
  786.8 292.5 %reduce-scatter.13.cloned.1.call-start = ((), (), s32[]{:S(2)}) async-start(), calls=%async_computation.15 | async-start | bytes 10485760 | tf_op jit(solution)/shard_map/reduce_scatter | solution.py:1342
  799.9 71.3 %copy-start.19 = (bf16[704,1024]{1,0:T(8,128)(2,1)S(1)}, bf16[704,1024]{1,0:T(8,128)(2,1)}, u32[]{:S(2)}) copy-start(bf16[704,1024]{1,0:T(8,128)(2,1)} %get-tuple-element.80.refs_4_) | copy-start | bytes 4325380
  800.0 71.3 %copy-start.64 = (bf16[704,1024]{1,0:T(8,128)(2,1)S(1)}, bf16[704,1024]{1,0:T(8,128)(2,1)}, u32[]{:S(2)}) copy-start(bf16[704,1024]{1,0:T(8,128)(2,1)} %copy-done.63) | copy-start | bytes 4325380
  880.7 288.3 %reduce-scatter.15.cloned.1.call-start = ((), (), s32[]{:S(2)}) async-start(), calls=%async_computation.16 | async-start | bytes 10485760 | tf_op jit(solution)/shard_map/reduce_scatter | solution.py:1372
  891.9 3.6 collective-permute-start.6
  895.4 95.8 %slice-start = ((s8[8912896]{0:T(1024)(128)(4,1)}), s8[524288]{0:T(1024)(128)(4,1)S(1)}, s32[]{:S(2)}) async-start(s8[8912896]{0:T(1024)(128)(4,1)} %bitcast.206), calls=%async_computation.19 | async-start | bytes 1048576
  975.3 15.9 %slice-start.1 = ((s8[8912896]{0:T(1024)(128)(4,1)}), s8[4194304]{0:T(1024)(128)(4,1)S(1)}, s32[]{:S(2)}) async-start(s8[8912896]{0:T(1024)(128)(4,1)} %bitcast.206), calls=%async_computation.20 | async-start | bytes 8388608
  975.3 15.9 %slice-start.2 = ((s8[8912896]{0:T(1024)(128)(4,1)}), s8[4194304]{0:T(1024)(128)(4,1)S(1)}, s32[]{:S(2)}) async-start(s8[8912896]{0:T(1024)(128)(4,1)} %bitcast.206), calls=%async_computation.21 | async-start | bytes 8388608
  975.3 15.9 %copy-start.13 = (bf16[2176,1024]{1,0:T(8,128)(2,1)S(1)}, bf16[2176,1024]{1,0:T(8,128)(2,1)}, u32[]{:S(2)}) copy-start(bf16[2176,1024]{1,0:T(8,128)(2,1)} %get-tuple-element.109.dk_ref) | copy-start | bytes 13369348
  1011.7 261.0 %reduce-scatter.17.cloned.1.call-start = ((), (), s32[]{:S(2)}) async-start(), calls=%async_computation.17 | async-start | bytes 10485760 | tf_op jit(solution)/shard_map/reduce_scatter | solution.py:1373
  1011.8 3.7 collective-permute-start.7
  1114.5 7.9 collective-permute-start.8
  1130.9 104.4 %all-to-all-start.2 = ((bf16[4,272,2048]{2,1,0:T(8,128)(2,1)}), bf16[4,272,2048]{2,1,0:T(8,128)(2,1)}, u32[]{:S(2)}, u32[]{:S(2)}) async-start(bf16[4,272,2048]{2,1,0:T(8,128)(2,1)} %fusion), calls=%async_computation.6 | async-start | bytes 8912896 | tf_op jit(solution)/shard_map/all_to_all | solution.py:1389
  1140.7 98.0 %copy-start.2 = (bf16[272,2048]{1,0:T(8,128)(2,1)S(1)}, bf16[272,2048]{1,0:T(8,128)(2,1)}, u32[]{:S(2)}) copy-start(bf16[272,2048]{1,0:T(8,128)(2,1)} %param.16) | copy-start | bytes 3342340
  1140.7 98.0 %copy-start.31 = (f32[2048]{0:T(1024)S(1)}, f32[2048]{0:T(1024)}, u32[]{:S(2)}) copy-start(f32[2048]{0:T(1024)} %param.22) | copy-start | bytes 24580
  1140.7 98.0 %copy-start.47 = (f32[272]{0:T(512)S(1)}, f32[272]{0:T(512)}, u32[]{:S(2)}) copy-start(f32[272]{0:T(512)} %copy-done.46) | copy-start | bytes 3268
  1243.6 11.0 all-to-all-start.3
  1254.7 53.7 %all-to-all-start.4 = ((bf16[8,64,2048]{2,1,0:T(8,128)(2,1)}), bf16[8,64,2048]{2,1,0:T(8,128)(2,1)}, u32[]{:S(2)}, u32[]{:S(2)}) async-start(bf16[8,64,2048]{2,1,0:T(8,128)(2,1)} %bitcast.65), calls=%async_computation.9 | async-start | bytes 4194304 | tf_op jit(solution)/shard_map/all_to_all | solution.py:1103
  (44 other events, 168.5 us)
Sparse Core Ops, SparseCore 0:
  11.8 49.8 all-gather.5
  63.9 85.1 all-gather.7
  608.5 126.1 reduce-scatter.6
  762.7 112.1 reduce-scatter.8
  877.8 112.0 reduce-scatter.10
  992.9 86.3 reduce-scatter.12
  1082.6 86.3 reduce-scatter.14
  1172.1 87.6 reduce-scatter.16

commit v4 on v3

--- a/solution.py
+++ b/solution.py
@@ -91,7 +91,7 @@
         final = lax.fori_loop(0, group + 1, one, start)
         for head in range(step_heads):
             top, total, mixed = final[3 * head : 3 * head + 3]
-            lse_ref[head, group : group + 1, :] = top + jnp.log2(total)
+            lse_ref[head, group] = top + jnp.log2(total)
             rows_out = (mixed / total).T.astype(jnp.bfloat16)
             for n, ref in enumerate(out_refs):
                 ref[pl.ds(group * rows, rows), pl.ds(head * HEAD, HEAD)] = rows_out[
@@ -130,7 +130,7 @@
             product = grad.astype(jnp.float32) * out.astype(jnp.float32)
             centres.append(jnp.sum(product.T, axis=0, keepdims=True))
             grads.append(grad)
-            tops.append(lse_ref[head, group : group + 1, :])
+            tops.append(lse_ref[head, group])
 
         def one(block, carry, group=group, queries=queries, grads=grads, centres=centres, tops=tops):
             at = pl.multiple_of(block * keys, 16)
@@ -190,14 +190,14 @@
             in_specs=query_specs
             + [side, side, whole_block(key_info.shape), whole_block(query_info.shape)],
             out_specs=[plain] * sets
-            + [pl.BlockSpec((step_heads, GROUPS, sets * rows), lambda h, first: (h, 0, 0))],
+            + [pl.BlockSpec((step_heads, GROUPS, 1, sets * rows), lambda h, first: (h, 0, 0, 0))],
             scratch_shapes=[
                 pltpu.VMEM((GROUPS * (GROUPS + 1) // 2, keys, sets * rows), jnp.float32),
                 pltpu.VMEM((step_heads, GROUPS, HEAD, keys), jnp.bfloat16),
             ],
         ),
         out_shape=[jax.ShapeDtypeStruct((total_rows, heads * HEAD), jnp.bfloat16)] * sets
-        + [jax.ShapeDtypeStruct((heads, GROUPS, sets * rows), jnp.float32)],
+        + [jax.ShapeDtypeStruct((heads, GROUPS, 1, sets * rows), jnp.float32)],
         compiler_params=pltpu.CompilerParams(vmem_limit_bytes=VMEM_BYTES),
         name="attention_forward",
     )(starts, *queries, keys_all, values_all, key_info, query_info)
@@ -227,7 +227,7 @@
             + [
                 side,
                 side,
-                pl.BlockSpec((step_heads, GROUPS, sets * rows), lambda h, first: (h, 0, 0)),
+                pl.BlockSpec((step_heads, GROUPS, 1, sets * rows), lambda h, first: (h, 0, 0, 0)),
                 whole_block(key_info.shape),
                 whole_block(query_info.shape),
                 whole_block((tokens, HEAD)),
@@ -441,16 +441,21 @@
         rows = pl.ds(pl.multiple_of(lax.rem(source, 2) * self.rows, 16), self.rows)
         return self.landing.at[source // 2, rows, self.columns(core)]
 
-    def direct(self, step):
-        target = lax.rem(self.me + step, 8)
+    def direct(self, target):
         core = lax.rem(target, 2)
+        offset = lax.rem(target - self.me + 8, 8)
         return remote(
             self.slots.at[target // 2, :, self.columns(core)],
             self.place(self.me, core),
-            self.send.at[step],
-            self.recv.at[step],
+            self.send.at[offset],
+            self.recv.at[offset],
             target,
         )
+
+    def sends(self, step):
+        chip = chip_order(self.chip, step)
+        targets = [2 * chip, 2 * chip + 1] if step else [self.me + 1 - 2 * self.core]
+        return [self.direct(target) for target in targets]
 
     def local(self):
         return pltpu.make_async_copy(
@@ -459,10 +464,17 @@
             self.local_sem,
         )
 
-    def start(self):
-        self.local().start()
-        for step in range(1, 8):
-            self.direct(step).start()
+    def start(self, steps):
+        for step in steps:
+            if step == 0:
+                self.local().start()
+            for copy in self.sends(step):
+                copy.start()
+
+    def sent(self, steps):
+        for step in steps:
+            for copy in self.sends(step):
+                copy.wait_send()
 
     def pass_on(self, source):
         place = self.place(source, self.core)
@@ -495,9 +507,7 @@
             ).wait_recv()
         return chip
 
-    def finish(self):
-        for step in range(1, 8):
-            self.direct(step).wait_send()
+    def passed_on(self):
         for source in range(8):
             self.pass_on(source).wait_send()
 
@@ -514,7 +524,7 @@
 
     def swap(self, step):
         return remote(
-            self.passing.at[step],
+            self.passing.at[step % 2],
             self.passed.at[step],
             self.pass_send.at[step],
             self.pass_recv.at[step],
@@ -565,7 +575,7 @@
         tile = 2 * self.rows // 4
         for at in range(0, 2 * self.rows, tile):
             span = pl.ds(at, tile)
-            summed = self.kept[step % 2, span, :] + self.passed[step, span, :].astype(jnp.float32)
+            summed = self.kept[span, :] + self.passed[step, span, :].astype(jnp.float32)
             self.total[step, span, :] = summed.astype(jnp.bfloat16)
         self.each(
             step,
@@ -575,7 +585,8 @@
 
     def finish(self):
         for step in range(4):
-            self.swap(step).wait_send()
+            if step >= 2:
+                self.swap(step).wait_send()
             self.each(
                 step,
                 lambda step=step: self.local(step, self.core).wait(),
@@ -632,7 +643,7 @@
     collect = Collect(
         me, False, kept, passing, passed, total, back, local_sem.at[1], swap_send, swap_recv, out_send, out_recv
     )
-    dispatch.start()
+    dispatch.start((0, 1, 2))
     for load in loads:
         load.start()
     block = landing.shape[1]
@@ -689,30 +700,36 @@
 
         lax.fori_loop(0, chunks, hidden_part, 0)
         act_copy(chip, step).start()
-        if step < 3:
-            dispatch.arrive(step + 1)
         if step == 0:
             loads[2].wait()
         else:
             collect.settle(step - 1)
         core = collect.core
-        width = min(256, half)
+        width = min(512, half)
 
         def far_part(part, carry, step=step):
             at = pl.multiple_of((1 - core) * half + part * width, 128)
             product = dot_nt(act[step % 2], down[pl.ds(at, width), :])
-            passing[step, :, pl.ds(pl.multiple_of(part * width, 128), width)] = product.astype(jnp.bfloat16)
+            passing[step % 2, :, pl.ds(pl.multiple_of(part * width, 128), width)] = product.astype(jnp.bfloat16)
             return carry
 
         def near_part(part, carry, step=step):
             at = pl.multiple_of(core * half + part * width, 128)
             product = dot_nt(act[step % 2], down[pl.ds(at, width), :])
-            kept[step % 2, :, pl.ds(pl.multiple_of(part * width, 128), width)] = product
+            kept[:, pl.ds(pl.multiple_of(part * width, 128), width)] = product
             return carry
 
+        if step >= 2:
+            collect.swap(step - 2).wait_send()
         lax.fori_loop(0, half // width, far_part, 0)
         collect.swap(step).start()
+        if step in (1, 2):
+            dispatch.arrive(step + 1)
         lax.fori_loop(0, half // width, near_part, 0)
+        if step == 0:
+            dispatch.sent((1, 2))
+            dispatch.start((3,))
+            dispatch.arrive(1)
     collect.settle(3)
     for step in (2, 3):
         act_copy(chip_order(me // 2, step), step).wait()
@@ -721,7 +738,8 @@
     for slot in range(2):
         for copy in stage_copies(0, 0, slot):
             copy.wait()
-    dispatch.finish()
+    dispatch.sent((0, 3))
+    dispatch.passed_on()
     collect.finish()
 
 
@@ -753,8 +771,8 @@
             pltpu.VMEM((chips, block, depth), bf),
             pltpu.VMEM((2, 2, block, chunk), bf),
             pltpu.VMEM((2, block, hidden_units), bf),
-            pltpu.VMEM((2, block, half), jnp.float32),
-            pltpu.VMEM((chips, block, half), bf),
+            pltpu.VMEM((block, half), jnp.float32),
+            pltpu.VMEM((2, block, half), bf),
             pltpu.VMEM((chips, block, half), bf),
             pltpu.VMEM((chips, block, half), bf),
             dma((3,)),
@@ -782,12 +800,13 @@
     me = lax.axis_index("expert")
     enter(8, me)
     dispatch = Dispatch(me, slots, rows_out, local_sem.at[0], send, recv, pass_send, pass_recv)
-    dispatch.start()
+    dispatch.start((0, 1, 2, 3))
     for step in range(4):
         dispatch.arrive(step)
     for step in range(4):
         dispatch.ready(step)
-    dispatch.finish()
+    dispatch.sent((0, 1, 2, 3))
+    dispatch.passed_on()
 
 
 def send_rows(slots, collective):
@@ -849,7 +868,7 @@
     hidden_units = gate.shape[1]
     chunks = hidden_units // chunk
     half = back.shape[2] // 2
-    width = min(256, half)
+    width = min(512, half)
 
     def span_of(chip):
         return pl.ds(pl.multiple_of(chip * block, 16), block)
@@ -929,14 +948,16 @@
         def far_part(part, carry, step=step):
             at = pl.multiple_of((1 - core) * half + part * width, 128)
             columns = pl.ds(pl.multiple_of(part * width, 128), width)
-            passing[step, :, columns] = product(at).astype(jnp.bfloat16)
+            passing[step % 2, :, columns] = product(at).astype(jnp.bfloat16)
             return carry
 
         def near_part(part, carry, step=step):
             at = pl.multiple_of(core * half + part * width, 128)
-            kept[step % 2, :, pl.ds(pl.multiple_of(part * width, 128), width)] = product(at)
+            kept[:, pl.ds(pl.multiple_of(part * width, 128), width)] = product(at)
             return carry
 
+        if step >= 2:
+            collect.swap(step - 2).wait_send()
         lax.fori_loop(0, half // width, far_part, 0)
         collect.swap(step).start()
         lax.fori_loop(0, half // width, near_part, 0)
@@ -951,7 +972,7 @@
     hidden_units = gate_weight.shape[1]
     block = 2 * capacity
     chips = rows // block
-    chunk = 256 if hidden_units % 256 == 0 else 128
+    chunk = hidden_units // 2 if hidden_units % 256 == 0 else 128
     half = depth // 2
     any_space = pl.BlockSpec(memory_space=pl.ANY)
     bf = jnp.bfloat16
@@ -972,8 +993,8 @@
             pltpu.VMEM((2, block, depth), bf),
             pltpu.VMEM((2, 2, block, chunk), bf),
             pltpu.VMEM((2, block, hidden_units), bf),
-            pltpu.VMEM((2, block, half), jnp.float32),
-            pltpu.VMEM((chips, block, half), bf),
+            pltpu.VMEM((block, half), jnp.float32),
+            pltpu.VMEM((2, block, half), bf),
             pltpu.VMEM((chips, block, half), bf),
             pltpu.VMEM((chips, block, half), bf),
             dma((3,)),
@@ -991,6 +1012,251 @@
         ),
         name="ffn_backward",
     )(grad_rows, gate_pre, up_pre, gate_weight, up_weight, down_weight)
+
+
+def attention_send_body(
+    scale,
+    query_hbm,
+    sibling_hbm,
+    key_hbm,
+    value_hbm,
+    out_weight_hbm,
+    key_info,
+    query_info,
+    own_out,
+    sibling_out,
+    rows_out,
+    back,
+    lse_ref,
+    queries,
+    siblings,
+    keys_v,
+    values_v,
+    out_weight,
+    bias_ref,
+    flipped,
+    own_stage,
+    sibling_stage,
+    arrived,
+    rows_stage,
+    sending,
+    load_sem,
+    own_sem,
+    sibling_sem,
+    rows_sem,
+    local_sem,
+    swap_send,
+    swap_recv,
+    out_send,
+    out_recv,
+):
+    me = lax.axis_index("expert")
+    chip, core = me // 2, lax.rem(me, 2)
+    enter(8, me)
+    half = keys_v.shape[1]
+    rows = own_stage.shape[1]
+    keys = keys_v.shape[0] // GROUPS
+    heads = half // HEAD
+    capacity = back.shape[1]
+    own_columns = pl.ds(pl.multiple_of(core * half, 128), half)
+    far_columns = pl.ds(pl.multiple_of((1 - core) * half, 128), half)
+    loads = [
+        pltpu.make_async_copy(source, target, load_sem.at[n])
+        for n, (source, target) in enumerate(
+            (
+                (value_hbm, values_v),
+                (key_hbm, keys_v),
+                (query_hbm.at[:, own_columns], queries),
+                (sibling_hbm, siblings),
+                (out_weight_hbm, out_weight),
+            )
+        )
+    ]
+    for load in loads:
+        load.start()
+    fill_bias(bias_ref, key_info, query_info, keys)
+    loads[0].wait()
+
+    def flip(head, carry):
+        lanes = pl.ds(pl.multiple_of(head * HEAD, HEAD), HEAD)
+        for block in range(GROUPS):
+            values = values_v[pl.ds(block * keys, keys), lanes].astype(jnp.float32)
+            flipped[head, block] = values.T.astype(jnp.bfloat16)
+        return carry
+
+    lax.fori_loop(0, heads, flip, 0)
+    for load in loads[1:4]:
+        load.wait()
+
+    def group_of(step):
+        return chip_order(chip, 3 - step)
+
+    def span_of(step):
+        return pl.ds(pl.multiple_of(group_of(step) * rows, 16), rows)
+
+    def own_copy(step):
+        return pltpu.make_async_copy(own_stage.at[step], own_out.at[span_of(step), :], own_sem.at[step])
+
+    def sibling_copy(step):
+        return pltpu.make_async_copy(
+            sibling_stage.at[step], sibling_out.at[span_of(step), :], sibling_sem.at[step]
+        )
+
+    def rows_copy(step):
+        return pltpu.make_async_copy(
+            rows_stage.at[step], rows_out.at[span_of(step), :], rows_sem.at[step]
+        )
+
+    def swap(step):
+        return remote(
+            sibling_stage.at[step], arrived.at[step], swap_send.at[step], swap_recv.at[step], me + 1 - 2 * core
+        )
+
+    def outgoing(step, n):
+        source = 2 * group_of(step) + n
+        offset = lax.rem(source - me + 8, 8)
+        return remote(sending.at[step, n], back.at[me], out_send.at[offset], out_recv.at[offset], source)
+
+    def local(step, n):
+        return pltpu.make_async_copy(sending.at[step, n], back.at[me], local_sem)
+
+    def each(step, own, other):
+        for n in range(2):
+            if step < 3:
+                other(n)
+                continue
+
+            @pl.when(core == n)
+            def _(n=n):
+                own(n)
+
+            @pl.when(core != n)
+            def _(n=n):
+                other(n)
+
+    def attend(step):
+        group = group_of(step)
+        first_block = group * (group + 1) // 2
+        span = span_of(step)
+
+        def head_pair(pair, carry):
+            lanes = [pl.ds(pl.multiple_of((2 * pair + n) * HEAD, HEAD), HEAD) for n in range(2)]
+            parts = [jnp.concatenate([queries[span, lane], siblings[span, lane]], axis=0) for lane in lanes]
+
+            def one(block, state):
+                at = pl.multiple_of(block * keys, 16)
+                bias = bias_ref[first_block + block]
+                result = []
+                for n in range(2):
+                    top, total, mixed = state[3 * n : 3 * n + 3]
+                    scores = dot_nt(keys_v[pl.ds(at, keys), lanes[n]], parts[n]) * scale + bias
+                    new_top = jnp.maximum(top, jnp.max(scores, axis=0, keepdims=True))
+                    fade = jnp.exp2(top - new_top)
+                    probs = jnp.exp2(scores - new_top)
+                    total = total * fade + jnp.sum(probs, axis=0, keepdims=True)
+                    mixed = mixed * fade + dot_nn(flipped[2 * pair + n, block], probs.astype(jnp.bfloat16))
+                    result += [new_top, total, mixed]
+                return tuple(result)
+
+            start = (
+                jnp.full((1, 2 * rows), -1e30, jnp.float32),
+                jnp.zeros((1, 2 * rows), jnp.float32),
+                jnp.zeros((HEAD, 2 * rows), jnp.float32),
+            ) * 2
+            final = lax.fori_loop(0, group + 1, one, start)
+            for n in range(2):
+                top, total, mixed = final[3 * n : 3 * n + 3]
+                lse_ref[2 * pair + n, group] = top + jnp.log2(total)
+                result = (mixed / total).T.astype(jnp.bfloat16)
+                own_stage[step, :, lanes[n]] = result[:rows]
+                sibling_stage[step, :, lanes[n]] = result[rows:]
+            return carry
+
+        lax.fori_loop(0, heads // 2, head_pair, 0)
+        swap(step).start()
+        own_copy(step).start()
+        sibling_copy(step).start()
+
+    def settle(step):
+        swap(step).wait_recv()
+        rows_stage[step, :, own_columns] = own_stage[step]
+        rows_stage[step, :, far_columns] = arrived[step]
+        rows_copy(step).start()
+        width = 512
+        for at in range(0, back.shape[2], min(width, back.shape[2])):
+            columns = pl.ds(at, min(width, back.shape[2]))
+            product = dot_nt(rows_stage[step], out_weight[columns, :])
+            for n in range(2):
+                part = product[n * capacity : (n + 1) * capacity]
+                sending[step, n, :, columns] = part.astype(jnp.bfloat16)
+        each(step, lambda n: local(step, n).start(), lambda n: outgoing(step, n).start())
+
+    for step in range(4):
+        attend(step)
+        if step == 1:
+            loads[4].wait()
+        if step > 0:
+            settle(step - 1)
+    settle(3)
+    for step in range(4):
+        swap(step).wait_send()
+        own_copy(step).wait()
+        sibling_copy(step).wait()
+        rows_copy(step).wait()
+        each(step, lambda n, step=step: local(step, n).wait(), lambda n, step=step: outgoing(step, n).wait_send())
+    for offset in range(1, 8):
+        place = back.at[lax.rem(me + 8 - offset, 8)]
+        remote(place, place, out_send.at[offset], out_recv.at[offset], me).wait_recv()
+
+
+def attention_send(queries, siblings, keys_all, values_all, out_weight, key_info, query_info, capacity):
+    total_rows, width = queries.shape
+    tokens, half = keys_all.shape
+    depth = out_weight.shape[0]
+    rows, keys, heads = total_rows // GROUPS, tokens // GROUPS, half // HEAD
+    any_space = pl.BlockSpec(memory_space=pl.ANY)
+    here = pl.BlockSpec(memory_space=pltpu.VMEM)
+    bf = jnp.bfloat16
+    dma = pltpu.SemaphoreType.DMA
+    return pl.pallas_call(
+        functools.partial(attention_send_body, HEAD ** (-0.5) * LOG2E),
+        in_specs=[any_space] * 5 + [here] * 2,
+        out_specs=[any_space] * 4 + [here],
+        out_shape=[
+            jax.ShapeDtypeStruct((total_rows, half), bf),
+            jax.ShapeDtypeStruct((total_rows, half), bf),
+            jax.ShapeDtypeStruct((total_rows, width), bf),
+            jax.ShapeDtypeStruct((8, capacity, depth), bf),
+            jax.ShapeDtypeStruct((heads, GROUPS, 1, 2 * rows), jnp.float32),
+        ],
+        scratch_shapes=[
+            pltpu.VMEM((total_rows, half), bf),
+            pltpu.VMEM((total_rows, half), bf),
+            pltpu.VMEM((tokens, half), bf),
+            pltpu.VMEM((tokens, half), bf),
+            pltpu.VMEM(out_weight.shape, bf),
+            pltpu.VMEM((GROUPS * (GROUPS + 1) // 2, keys, 2 * rows), jnp.float32),
+            pltpu.VMEM((heads, GROUPS, HEAD, keys), bf),
+            pltpu.VMEM((GROUPS, rows, half), bf),
+            pltpu.VMEM((GROUPS, rows, half), bf),
+            pltpu.VMEM((GROUPS, rows, half), bf),
+            pltpu.VMEM((GROUPS, rows, width), bf),
+            pltpu.VMEM((GROUPS, 2, capacity, depth), bf),
+            dma((5,)),
+            dma((GROUPS,)),
+            dma((GROUPS,)),
+            dma((GROUPS,)),
+            dma,
+            dma((GROUPS,)),
+            dma((GROUPS,)),
+            dma((8,)),
+            dma((8,)),
+        ],
+        compiler_params=pltpu.CompilerParams(
+            collective_id=4, has_side_effects=True, vmem_limit_bytes=VMEM_BYTES
+        ),
+        name="attention_send",
+    )(queries, siblings, keys_all, values_all, out_weight, key_info, query_info)
 
 
 D = 2048
@@ -1176,12 +1442,13 @@
     kv_share = (
         kv_share.reshape(weight_rows, 2, 2, piece).transpose(0, 2, 1, 3).reshape(weight_rows, 4 * piece)
     )
-    all_routes = lax.all_gather(att_routes, "expert", axis=0)
     kv_gathered = lax.all_gather(kv_share, "expert", axis=0)
     kv_gathered, hidden_sent = lax.optimization_barrier((kv_gathered, hidden))
     hidden_all = lax.all_gather(hidden_sent, "expert", axis=0)
     kv_half = lax.dynamic_slice_in_dim(kv_gathered, core * 2 * piece, 2 * piece, 2).reshape(D, 2 * piece)
+    kv_half, routes_sent = lax.optimization_barrier((kv_half, att_routes))
     kv_blocks, block_order = spread_over_replicas(kv_half, my_replica, replicas)
+    all_routes = lax.all_gather(routes_sent, "expert", axis=0)
 
     tree_places = jnp.arange(token_count, dtype=jnp.int32)
     tree_segments, tree_depths = tree_layout(tree_places)
@@ -1232,14 +1499,20 @@
     if att_copies == 1:
         query_sets.append(far_half(queries))
         starts = jnp.stack([core * heads, 0]).astype(jnp.int32)
-    *att_outs, lse = attention_forward(
-        query_sets, starts // 2, keys_all, values_all, key_info, query_info, heads
-    )
-    att_rows = join_halves(*att_outs) if att_copies == 1 else att_outs[0]
-    att_partial = lax.dot_general(
-        att_rows, o_weight, (((1,), (1,)), ((), ())), preferred_element_type=f32
-    ).astype(bf16)
-    att_back = exchange(att_partial.reshape(devices, att_capacity, D))
+    fused = devices == 8 and att_copies == 1 and ffn_copies == 2 and ffn_capacity % 16 == 0
+    if fused:
+        *att_outs, att_rows, att_back, lse = attention_send(
+            *query_sets, keys_all, values_all, o_weight, key_info, query_info, att_capacity
+        )
+    else:
+        *att_outs, lse = attention_forward(
+            query_sets, starts // 2, keys_all, values_all, key_info, query_info, heads
+        )
+        att_rows = join_halves(*att_outs) if att_copies == 1 else att_outs[0]
+        att_partial = lax.dot_general(
+            att_rows, o_weight, (((1,), (1,)), ((), ())), preferred_element_type=f32
+        ).astype(bf16)
+        att_back = exchange(att_partial.reshape(devices, att_capacity, D))
     if att_copies > 1:
         att_back = (
             att_back.astype(f32).reshape(ATT_EXPERTS, att_copies, att_capacity, D).sum(axis=1).astype(bf16)
@@ -1263,7 +1536,6 @@
     ffn_slots = jnp.einsum(
         "ecr,rd->ecd", ffn_picks[0] + ffn_picks[1], hidden_two, preferred_element_type=f32
     ).astype(bf16)
-    fused = devices == 8 and ffn_copies == 2 and ffn_capacity % 16 == 0
     if fused:
         ffn_inputs, gate_pre, up_pre, activated, ffn_back = ffn_forward(
             ffn_slots, gate_weight, up_weight, down_weight
@@ -1321,9 +1593,7 @@
         )
         grad_gate = dot_tn(ffn_inputs, grad_gate_pre).astype(bf16)
         ffn_grad_pair = to_tokens(grad_ffn_in)
-    grad_up = dot_tn(ffn_inputs, grad_up_pre).astype(bf16)
     summed_gate = lax.psum_scatter(grad_gate, "dp", scatter_dimension=0, tiled=True)
-    summed_up = lax.psum_scatter(grad_up, "dp", scatter_dimension=0, tiled=True)
     grad_ffn_router, hidden_two_extra = router_grads(
         hidden_two, ffn_router, ffn_gates, ffn_first, ffn_second, ffn_gate_grad
     )
@@ -1333,18 +1603,21 @@
 
     att_gate_grad, att_scaled = pair_grads(att_gates, att_branches, grad_mid)
     att_slots = fill_slots(att_picks, att_scaled)
-    att_slots, summed_down = lax.optimization_barrier((att_slots, summed_down))
     if att_copies > 1:
         att_slots = jnp.repeat(att_slots, att_copies, axis=0)
+    att_slots, summed_down, ffn_inputs = lax.optimization_barrier((att_slots, summed_down, ffn_inputs))
+    grad_up = dot_tn(ffn_inputs, grad_up_pre).astype(bf16)
+    summed_up = lax.psum_scatter(grad_up, "dp", scatter_dimension=0, tiled=True)
     grad_att_out = exchange(att_slots).reshape(-1, D)
-    grad_o = dot_tn(grad_att_out, att_rows).astype(bf16)
-    grad_att_out, grad_o = lax.optimization_barrier((grad_att_out, grad_o))
-    summed_o = lax.psum_scatter(grad_o, "dp", scatter_dimension=0, tiled=True)
+    grad_att_out, grad_up = lax.optimization_barrier((grad_att_out, grad_up))
     grad_heads = jnp.dot(grad_att_out, o_weight, preferred_element_type=f32).astype(bf16)
+    grad_heads, grad_att_out = lax.optimization_barrier((grad_heads, grad_att_out))
     grad_sets = [grad_heads]
     if att_copies == 1:
         grad_sets.append(far_half(grad_heads))
-    grad_sets[-1], summed_gate, grad_up = lax.optimization_barrier((grad_sets[-1], summed_gate, grad_up))
+    grad_o = dot_tn(grad_att_out, att_rows).astype(bf16)
+    summed_o = lax.psum_scatter(grad_o, "dp", scatter_dimension=0, tiled=True)
+    grad_sets[-1], summed_gate, grad_o = lax.optimization_barrier((grad_sets[-1], summed_gate, grad_o))
     *grad_queries, grad_keys, grad_values = attention_backward(
         query_sets,
         starts,
@@ -1363,15 +1636,6 @@
     grad_query_in = lax.dot_general(
         grad_query_pre, q_weight, (((1,), (1,)), ((), ())), preferred_element_type=f32
     ).astype(bf16)
-    grad_q = dot_tn(query_inputs, grad_query_pre).astype(bf16)
-    grad_query_in, summed_up, summed_o = lax.optimization_barrier((grad_query_in, summed_up, summed_o))
-    hidden_rows = hidden_all.reshape(token_count, D)
-    grad_kv = jnp.concatenate(
-        [dot_tn(hidden_rows, grad_keys).astype(bf16), dot_tn(hidden_rows, grad_values).astype(bf16)], axis=1
-    )
-    summed_kv = lax.psum_scatter(grad_kv, "dp", scatter_dimension=0, tiled=True)
-    summed_q = lax.psum_scatter(grad_q, "dp", scatter_dimension=0, tiled=True)
-
     merged = merge_hidden_grads(
         own_plan.transpose(0, 2, 1),
         grad_query_in.reshape(devices, att_capacity, D),
@@ -1385,11 +1649,20 @@
         lax.dynamic_index_in_dim(merged, 1 - core, 1, keepdims=False), "expert", pair
     )
     chip_sum = (kept.astype(f32) + passed.astype(f32)).astype(bf16)
+    chip_sum, hidden_rows, query_inputs, summed_up = lax.optimization_barrier(
+        (chip_sum, hidden_all.reshape(token_count, D), query_inputs, summed_up)
+    )
+    grad_kv = jnp.concatenate(
+        [dot_tn(hidden_rows, grad_keys).astype(bf16), dot_tn(hidden_rows, grad_values).astype(bf16)], axis=1
+    )
+    summed_kv = lax.psum_scatter(grad_kv, "dp", scatter_dimension=0, tiled=True)
+    grad_q = dot_tn(query_inputs, grad_query_pre).astype(bf16)
+    summed_q = lax.psum_scatter(grad_q, "dp", scatter_dimension=0, tiled=True)
     same_core = [[2 * i + c for i in range(devices // 2)] for c in range(2)]
     arrived = lax.all_to_all(
         chip_sum, "expert", split_axis=0, concat_axis=0, axis_index_groups=same_core, tiled=True
     )
-    arrived, summed_kv = lax.optimization_barrier((arrived, summed_kv))
+    arrived, grad_kv, grad_q, summed_o = lax.optimization_barrier((arrived, grad_kv, grad_q, summed_o))
     grad_att_router, hidden_one_extra = router_grads(
         hidden, att_router, att_gates, att_first, att_second, att_gate_grad
     )
@@ -1410,8 +1683,10 @@
     shared_ffn_router = own_smalls[(2 + ATT_EXPERTS) * share :].reshape(share, FFN_EXPERTS)
 
     kv_rows = exchange(summed_kv.reshape(devices, -1, 2 * half))
-    kv_sum = jnp.sum(kv_rows.astype(f32).reshape(devices // 2, 2, -1, 2, half), axis=0)
-    shared_kv = kv_sum.transpose(1, 2, 0, 3).reshape(-1, 4 * half)
+    kv_sum = jnp.sum(kv_rows.astype(f32).reshape(devices // 2, 2, -1, 2 * half), axis=0)
+    shared_kv = jnp.concatenate(
+        [kv_sum[n, :, m * half : (m + 1) * half] for m in range(2) for n in range(2)], axis=1
+    )
 
     return (
         result.astype(bf16),

time: 1340 us -> 1210 us (0.903)
  waiting for transfers between devices: 319 us -> 221 us
    all_to_all x2 -> x1, waiting for transfers between devices: 91.9 us -> 6.78 us  [exchange(): lax.all_to_all(slots, 'expert', split_axis=0, concat_axis=0, tiled=True)]
    pallas_call x1, Pallas kernels: 130 us -> 88.5 us  [ffn_backward(): pl.pallas_call(functools.partial(ffn_backward_body, chunk), in_specs=[any...]
    reduce_scatter x1, waiting for transfers between devices: 38.4 us -> 0.02 us  [body(): summed_o = lax.psum_scatter(grad_o, 'dp', scatter_dimension=0, tiled=True)]
    pallas_call x1, Pallas kernels: 57.2 us -> 94.1 us  [attention_send(): pl.pallas_call(functools.partial(attention_send_body, HEAD ** (-0.5) * LO...]
    reduce_scatter x1, waiting for transfers between devices: 28.3 us -> 0.02 us  [body(): summed_kv = lax.psum_scatter(grad_kv, 'dp', scatter_dimension=0, tiled=True)]
    all_to_all x1, waiting for transfers between devices: 66.2 us -> 94.3 us  [body(): lax.all_to_all(chip_sum, 'expert', split_axis=0, concat_axis=0, axis_inde...]
    reduce_scatter x1, waiting for transfers between devices: 0.01 us -> 20.8 us  [body(): summed_q = lax.psum_scatter(grad_q, 'dp', scatter_dimension=0, tiled=True)]
    pallas_call x1, Pallas kernels: 61.4 us -> 76.2 us  [send_rows(): pl.pallas_call(send_rows_body, in_specs=[any_space], out_specs=any_space,...]
  transfers between devices with their start and end apart: 21 -> 19, of which waited for: 13 -> 10; matrix products, arithmetic and copies ran while one was open for 19% -> 20% of each run, Pallas kernels for 21% -> 20%
where the time goes in v4:
time: 1210 us
  Pallas kernels  553 us (46%)
  waiting for transfers between devices  221 us (18%)
  matrix products  180 us (15%)
  blocking collectives  91.7 us (8%)
  other arithmetic  79.6 us (7%)
  local copies, waits for them, and re-layouts  43.1 us (4%)
  starting transfers between devices  20.6 us (2%)
  between operations  16.3 us (1%)
    pallas_call x1, Pallas kernels, ffn_forward(): pl.pallas_call(functools.partial(ffn_forward_body, chunk), in_specs=[any_...  143 us
    dot_general x7, matrix products, dot_tn(): lax.dot_general(left, right, (((0,), (0,)), ((), ())), preferred_element_...  124 us
    all_to_all x1, waiting for transfers between devices, body(): lax.all_to_all(chip_sum, 'expert', split_axis=0, concat_axis=0, axis_inde...  94.3 us
    pallas_call x1, Pallas kernels, attention_send(): pl.pallas_call(functools.partial(attention_send_body, HEAD ** (-0.5) * LO...  94.1 us
    pallas_call x1, Pallas kernels, ffn_backward(): pl.pallas_call(functools.partial(ffn_backward_body, chunk), in_specs=[any...  88.5 us
    pallas_call x1, Pallas kernels, attention_backward(): pl.pallas_call(functools.partial(attention_backward_body, sets, step_head...  80.3 us
    all_to_all x1, blocking collectives, exchange(): lax.all_to_all(slots, 'expert', split_axis=0, concat_axis=0, tiled=True)  77.6 us
    pallas_call x1, Pallas kernels, send_rows(): pl.pallas_call(send_rows_body, in_specs=[any_space], out_specs=any_space,...  76.2 us
  transfers between devices with their start and end apart: 19, of which 10 were waited for; matrix products, arithmetic and copies ran while one was open for 20% of the time, Pallas kernels for 20%

profile of v4, /device:TPU:0, one launch (start us, length us, event | category | flops | bytes accessed | tf_op | source)
XLA Modules:
  0.0 1205.2 jit_solution(15668873508554958880)
XLA Ops:
  7.2 3.3 copy.65
  13.4 48.2 %all-gather.6.cloned.1.call-done = bf16[8,256,1024]{2,1,0:T(8,128)(2,1)} async-done(((bf16[1,256,1024]{2,1,0:T(8,128)(2,1)}), bf16[8,256,1024]{2,1,0:T(8,128)(2,1)}) %all-gather.6.cloned.1.call-update) | async-done | bytes 4194320 | tf_op jit(solution)/shard_map/all_gather | solution.py:1445
  67.6 3.9 fusion.38
  84.4 14.1 %all-gather.2 = s32[8,272,2]{1,2,0:T(2,128)S(1)} all-gather(s32[1,272,2]{1,2,0:T(2,128)S(1)} %bitcast.232), channel_id=3, replica_groups=mesh['dp'=4,'expert'=8] {'expert'}, dimensions={0}, use_global_device_ids=true | all-gather | bytes 19584 | tf_op jit(solution)/shard_map/all_gather | solution.py:1451
  104.8 19.3 %collective-permute-done.2 = bf16[2048,512]{1,0:T(8,128)(2,1)} collective-permute-done((bf16[2048,512]{1,0:T(8,128)(2,1)S(1)}, bf16[2048,512]{1,0:T(8,128)(2,1)}, u32[]{:S(2)}, u32[]{:S(2)}) %collective-permute-start.2) | collective-permute-done | bytes 2097184 | tf_op jit(solution)/shard_map/ppermute | solution.py:1393
  136.3 12.9 %all-gather.8.cloned.1.call-done = bf16[2176,2048]{1,0:T(8,128)(2,1)} async-done(((bf16[272,2048]{1,0:T(8,128)(2,1)}), bf16[2176,2048]{1,0:T(8,128)(2,1)}) %all-gather.8.cloned.1.call-update) | async-done | bytes 8912912 | tf_op jit(solution)/shard_map/all_gather | solution.py:1447
  151.3 15.1 %project_queries.1 = (bf16[704,2048]{1,0:T(8,128)(2,1)}, bf16[704,2048]{1,0:T(8,128)(2,1)}) custom-call(bf16[8,88,272]{2,1,0:T(8,128)(2,1)} %copy.71.plan_ref, bf16[8,272,2048]{2,1,0:T(8,128)(2,1)} %bitcast.212, bf16[2048,2048]{1,0:T(8,128)(2,1)} %weight_ref.1, f32[704,128]{1,0:T(8,128)} %get-tuple-element.115.cos_ref.refs_13_, ...), custom_call_target="tpu_custom_call" | custom-call | tf_op jit(solution)/shard_map/project_queries/pallas_call | solution.py:290
  171.5 6.1 pad_maximum_fusion.weight_ref
  177.6 26.6 %project_keys_values.1 = (bf16[2176,1024]{1,0:T(8,128)(2,1)}, bf16[2176,1024]{1,0:T(8,128)(2,1)}) custom-call(s32[4]{0:T(128)} %iota_xor_fusion.order_ref, bf16[8,272,2048]{2,1,0:T(8,128)(2,1)} %bitcast.213, bf16[4,2048,512]{2,1,0:T(8,128)(2,1)} %pad_maximum_fusion.weight_ref, f32[2176,128]{1,0:T(8,128)} %pad_maximum_fusion.2.cos_ref.refs_11_, ...), custom_call_target="tpu_custom_call" | custom-call | tf_op jit(solution)/shard_map/project_keys_values/pallas_call | solution.py:328
  204.2 94.1 %attention_send.1 = (bf16[704,1024]{1,0:T(8,128)(2,1)}, bf16[704,1024]{1,0:T(8,128)(2,1)}, bf16[704,2048]{1,0:T(8,128)(2,1)}, bf16[8,88,2048]{2,1,0:T(8,128)(2,1)}, f32[8,4,1,352]{3,2,1,0:T(1,128)}) custom-call(bf16[704,2048]{1,0:T(8,128)(2,1)} %get-tuple-element.81.query_hbm.refs_0_, bf16[704,1024]{1,0:T(8,128)(2,1)} %collective-permute-done.sibling_hbm.refs_1_, ...), custom_call_target="tpu_custom_call" | custom-call | tf_op jit(solution)/shard_map/attention_send/pallas_call | solution.py:1221
  298.3 3.8 convolution_bitcast_fusion.2
  306.1 3.2 convolution_convert_fusion.9.slots
  309.4 142.6 %ffn_forward.1 = (bf16[1408,2048]{1,0:T(8,128)(2,1)}, bf16[1408,2816]{1,0:T(8,128)(2,1)}, bf16[1408,2816]{1,0:T(8,128)(2,1)}, bf16[1408,2816]{1,0:T(8,128)(2,1)}, bf16[4,176,2048]{2,1,0:T(8,128)(2,1)}) custom-call(bf16[4,176,2048]{2,1,0:T(8,128)(2,1)} %convolution_convert_fusion.9.slots, bf16[2048,2816]{1,0:T(8,128)(2,1)} %gate_hbm.3, ...), custom_call_target="tpu_custom_call" | custom-call | tf_op jit(solution)/shard_map/ffn_forward/pallas_call | solution.py:756
  452.0 3.9 convolution_bitcast_fusion.1
  459.6 4.0 bitcast_convert_fusion.1.slots
  463.6 76.2 %send_rows.1 = bf16[4,352,2048]{2,1,0:T(8,128)(2,1)} custom-call(bf16[4,176,2048]{2,1,0:T(8,128)(2,1)} %bitcast_convert_fusion.1.slots), custom_call_target="tpu_custom_call" | custom-call | tf_op jit(solution)/shard_map/send_rows/pallas_call | solution.py:816
  539.8 24.2 %convolution_convert_fusion.2 = bf16[2048,2816]{1,0:T(8,128)(2,1)} fusion(bf16[1408,2048]{1,0:T(8,128)(2,1)} %bitcast.216, bf16[1408,2816]{1,0:T(8,128)(2,1)} %get-tuple-element.92), kind=kOutput, calls=%fused_computation.2 | convolution fusion | flops 16246112256 | bytes 25231360 | tf_op jit(solution)/shard_map/dot_general | solution.py:1401
  564.1 88.5 %ffn_backward.1 = (bf16[1408,2816]{1,0:T(8,128)(2,1)}, bf16[1408,2816]{1,0:T(8,128)(2,1)}, bf16[4,176,2048]{2,1,0:T(8,128)(2,1)}) custom-call(bf16[1408,2048]{1,0:T(8,128)(2,1)} %bitcast.217, bf16[1408,2816]{1,0:T(8,128)(2,1)} %get-tuple-element.94.gate_in, bf16[1408,2816]{1,0:T(8,128)(2,1)} %get-tuple-element.95.up_in, bf16[2048,2816]{1,0:T(8,128)(2,1)} %gate_hbm.3, ...), custom_call_target="tpu_custom_call" | custom-call | tf_op jit(solution)/shard_map/ffn_backward/pallas_call | solution.py:980
  652.6 24.7 %convolution_convert_fusion.1 = bf16[2048,2816]{1,0:T(8,128)(2,1)} fusion(bf16[1408,2048]{1,0:T(8,128)(2,1)} %get-tuple-element.102, bf16[1408,2816]{1,0:T(8,128)(2,1)} %get-tuple-element.98), kind=kOutput, calls=%fused_computation.1 | convolution fusion | flops 16246112256 | bytes 25231360 | tf_op jit(solution)/shard_map/dot_general | solution.py:1401
  677.5 3.9 convolution_bitcast_fusion
  681.5 3.4 multiply_reduce_fusion
  691.0 25.4 %convolution_convert_fusion = bf16[2048,2816]{1,0:T(8,128)(2,1)} fusion(bf16[1408,2048]{1,0:T(8,128)(2,1)} %get-tuple-element.102, bf16[1408,2816]{1,0:T(8,128)(2,1)} %get-tuple-element.103), kind=kOutput, calls=%fused_computation | convolution fusion | flops 16246112256 | bytes 25231360 | tf_op jit(solution)/shard_map/dot_general | solution.py:1401
  716.5 77.6 %all_to_all.24 = bf16[8,88,2048]{2,1,0:T(8,128)(2,1)S(1)} all-to-all(bf16[8,88,2048]{2,1,0:T(8,128)(2,1)S(1)} %bitcast_convert_fusion), channel_id=1, replica_groups=mesh['dp'=4,'expert'=8] {'expert'}, dimensions={0} | all-to-all | bytes 5767168 | tf_op jit(solution)/shard_map/all_to_all | solution.py:1369
  794.1 8.8 convolution_convert_fusion.8.refs_2_
  802.9 9.1 convolution_convert_fusion.4
  817.9 80.3 %attention_backward.1 = (bf16[704,1024]{1,0:T(8,128)(2,1)}, bf16[704,1024]{1,0:T(8,128)(2,1)}, bf16[2176,1024]{1,0:T(8,128)(2,1)}, bf16[2176,1024]{1,0:T(8,128)(2,1)}) custom-call(s32[2]{0:T(128)} %pad_add_fusion.1.first_ref, bf16[704,2048]{1,0:T(8,128)(2,1)} %get-tuple-element.81.query_hbm.refs_0_, ...), custom_call_target="tpu_custom_call" | custom-call | tf_op jit(solution)/shard_map/attention_backward/pallas_call | solution.py:219
  898.4 3.4 collective-permute-done.6
  901.7 11.6 convolution_convert_fusion.7
  913.4 30.1 %merge_hidden_grads.1 = bf16[2176,2048]{1,0:T(8,128)(2,1)} custom-call(s32[4]{0:T(128)} %iota_xor_fusion.order_ref, bf16[8,272,88]{2,1,0:T(8,128)(2,1)} %bitcast.224, bf16[8,88,2048]{2,1,0:T(8,128)(2,1)} %bitcast.226, bf16[2176,1024]{1,0:T(8,128)(2,1)} %get-tuple-element.121.dk_ref, bf16[2176,1024]{1,0:T(8,128)(2,1)} %get-tuple-element.122.dv_ref, ...), custom_call_target="tpu_custom_call" | custom-call | tf_op jit(solution)/shard_map/merge_hidden_grads/pallas_call | solution.py:374
  943.5 5.2 dynamic-slice_bitcast_fusion
  948.7 7.9 collective-permute-done.7
  956.6 8.5 fusion
  965.1 15.4 %convolution_convert_fusion.5 = bf16[2048,1024]{0,1:T(8,128)(2,1)} fusion(bf16[2176,2048]{1,0:T(8,128)(2,1)} %all-gather.8.cloned.1.call-done, bf16[2176,1024]{1,0:T(8,128)(2,1)} %get-tuple-element.122.dv_ref), kind=kOutput, calls=%fused_computation.14 | convolution fusion | flops 9128902656 | bytes 17563648 | tf_op jit(solution)/shard_map/dot_general | solution.py:1401
  980.5 13.4 %convolution_convert_fusion.6 = bf16[2048,1024]{0,1:T(8,128)(2,1)} fusion(bf16[2176,2048]{1,0:T(8,128)(2,1)S(1)} %bitcast.215, bf16[2176,1024]{1,0:T(8,128)(2,1)} %get-tuple-element.121.dk_ref), kind=kOutput, calls=%fused_computation.15 | convolution fusion | flops 9128902656 | bytes 17563648 | tf_op jit(solution)/shard_map/dot_general | solution.py:1401
  994.0 8.4 pad_maximum_fusion.1
  1004.3 11.8 convolution_convert_fusion.3
  1016.2 5.2 all-to-all-start.1
  1026.4 94.3 %all-to-all-done.1 = bf16[4,272,2048]{2,1,0:T(8,128)(2,1)} async-done(((bf16[4,272,2048]{2,1,0:T(8,128)(2,1)}), bf16[4,272,2048]{2,1,0:T(8,128)(2,1)}, u32[]{:S(2)}, u32[]{:S(2)}) %all-to-all-start.1) | async-done | bytes 4456480 | tf_op jit(solution)/shard_map/all_to_all | solution.py:1662
  1120.8 3.4 convert_reduce_fusion
  1124.2 3.2 fusion.14
  1129.0 4.0 all-to-all-start.2
  1133.1 4.0 copy.75
  1137.0 4.1 all-to-all-done.2
  1141.1 4.6 all-to-all-start.3
  1145.7 5.0 convert_element_type.192
  1163.1 20.8 %reduce-scatter.17.cloned.1.call-done = bf16[512,2048]{1,0:T(8,128)(2,1)} async-done(((bf16[2048,2048]{1,0:T(8,128)(2,1)}), bf16[512,2048]{1,0:T(8,128)(2,1)}) %reduce-scatter.17.cloned.1.call-update) | async-done | bytes 2097168 | tf_op jit(solution)/shard_map/reduce_scatter | solution.py:1660
  1183.9 4.1 convert_element_type.188
  1188.0 6.8 all-to-all-done.3
  (264 shorter events, 90.2 us)
Async XLA Ops:
  7.2 54.7 %copy-start = (f32[2048,8]{0,1:T(8,128)S(1)}, f32[2048,8]{0,1:T(8,128)}, u32[]{:S(2)}) copy-start(f32[2048,8]{0,1:T(8,128)} %param.24) | copy-start | bytes 196612
  7.2 54.5 %all-gather.6.cloned.1.call-start = ((), (), s32[]{:S(2)}) async-start(), calls=%async_computation.10 | async-start | bytes 4718592 | tf_op jit(solution)/shard_map/all_gather | solution.py:1445
  11.7 50.1 %copy-start.40 = (s32[272,2]{0,1:T(2,128)S(1)}, s32[272,2]{0,1:T(2,128)}, u32[]{:S(2)}) copy-start(s32[272,2]{0,1:T(2,128)} %param.18) | copy-start | bytes 6532
  11.7 137.5 %all-gather.8.cloned.1.call-start = ((), (), s32[]{:S(2)}) async-start(), calls=%async_computation.17 | async-start | bytes 10027008 | tf_op jit(solution)/shard_map/all_gather | solution.py:1447
  12.1 49.7 %copy-start.31 = (f32[272]{0:T(512)}, f32[272]{0:T(512)S(1)}, u32[]{:S(2)}) copy-start(f32[272]{0:T(512)S(1)} %add_rsqrt_fusion.1) | copy-start | bytes 3268
  12.1 52.2 %copy-start.46 = (s32[4]{0:T(128)S(1)}, s32[4]{0:T(128)}, u32[]{:S(2)}) copy-start(s32[4]{0:T(128)} %param.21) | copy-start | bytes 52
  12.1 52.2 %copy-start.45 = (s32[272,2]{0,1:T(2,128)S(1)}, s32[272,2]{0,1:T(2,128)}, u32[]{:S(2)}) copy-start(s32[272,2]{0,1:T(2,128)} %param.19) | copy-start | bytes 6532
  61.7 629.3 %reduce-scatter.7.cloned.1.call-start = ((), (), s32[]{:S(2)}) async-start(), calls=%async_computation.11 | async-start | bytes 14417920 | tf_op jit(solution)/shard_map/reduce_scatter | solution.py:1575
  61.8 5.8 copy-start.22
  64.4 617.1 %copy-start.29 = (pred[2,4,272]{2,1,0:T(4,128)(4,1)}, pred[2,4,272]{2,1,0:T(4,128)(4,1)S(1)}, u32[]{:S(2)}) copy-start(pred[2,4,272]{2,1,0:T(4,128)(4,1)S(1)} %iota_compare_fusion.14) | copy-start | bytes 6532
  64.4 139.7 %copy-start.27 = (f32[272,2]{0,1:T(2,128)}, f32[272,2]{0,1:T(2,128)S(1)}, u32[]{:S(2)}) copy-start(f32[272,2]{0,1:T(2,128)S(1)} %broadcast_divide_fusion.1) | copy-start | bytes 6532
  76.2 25.3 %copy-start.44 = (s32[1,13]{1,0:T(1,128)S(1)}, s32[1,13]{1,0:T(1,128)}, u32[]{:S(2)}) copy-start(s32[1,13]{1,0:T(1,128)} %param.20) | copy-start | bytes 160
  76.2 48.0 %collective-permute-start.2 = (bf16[2048,512]{1,0:T(8,128)(2,1)S(1)}, bf16[2048,512]{1,0:T(8,128)(2,1)}, u32[]{:S(2)}, u32[]{:S(2)}) collective-permute-start(bf16[2048,512]{1,0:T(8,128)(2,1)S(1)} %bitcast.221), channel_id=1, source_target_pairs={{0,16},{8,24},{16,0},{24,8},{1,17},{9,25},{17,1},{25,9},{2,18},{10... | collective-permute-start | bytes 6291464 | tf_op jit(solution)/shard_map/ppermute | solution.py:1393
  77.8 50.2 %collective-permute-start.1 = (bf16[2048,512]{1,0:T(8,128)(2,1)S(1)}, bf16[2048,512]{1,0:T(8,128)(2,1)}, u32[]{:S(2)}, u32[]{:S(2)}) collective-permute-start(bf16[2048,512]{1,0:T(8,128)(2,1)S(1)} %bitcast.222), channel_id=1, source_target_pairs={{0,8},{8,0},{16,24},{24,16},{1,9},{9,1},{17,25},{25,17},{2,10},{10... | collective-permute-start | bytes 6291464 | tf_op jit(solution)/shard_map/ppermute | solution.py:1393
  126.5 43.3 %collective-permute-start.3 = (bf16[1024,512]{1,0:T(8,128)(2,1)}, bf16[1024,512]{1,0:T(8,128)(2,1)}, u32[]{:S(2)}, u32[]{:S(2)}) collective-permute-start(bf16[1024,512]{1,0:T(8,128)(2,1)} %slice.152), channel_id=1, source_target_pairs={{0,8},{8,0},{16,24},{24,16},{1,9},{9,1},{17,25},{25,17},{2,10},{10... | collective-permute-start | bytes 3145736 | tf_op jit(solution)/shard_map/ppermute | solution.py:1395
  130.3 39.5 %collective-permute-start.4 = (bf16[1024,512]{1,0:T(8,128)(2,1)}, bf16[1024,512]{1,0:T(8,128)(2,1)}, u32[]{:S(2)}, u32[]{:S(2)}) collective-permute-start(bf16[1024,512]{1,0:T(8,128)(2,1)} %slice.153), channel_id=1, source_target_pairs={{0,16},{8,24},{16,0},{24,8},{1,17},{9,25},{17,1},{25,9},{2,18},{10... | collective-permute-start | bytes 3145736 | tf_op jit(solution)/shard_map/ppermute | solution.py:1395
  169.0 35.2 %collective-permute-start = (bf16[704,1024]{1,0:T(8,128)(2,1)}, bf16[704,1024]{1,0:T(8,128)(2,1)}, u32[]{:S(2)}, u32[]{:S(2)}) collective-permute-start(bf16[704,1024]{1,0:T(8,128)(2,1)} %constant_dynamic-slice_fusion.1), channel_id=1, source_target_pairs={{0,1},{1,0},{2,3},{3,2},{4,5},{5,4},{6,7},{7,6},{8,9},{9,8},{10,11... | collective-permute-start | bytes 4325384 | tf_op jit(solution)/shard_map/ppermute | solution.py:1484
  204.2 94.1 %copy-start.17 = (bf16[2,8,88,272]{3,2,0,1:T(8,128)(2,1)S(1)}, bf16[2,8,88,272]{3,2,0,1:T(8,128)(2,1)}, u32[]{:S(2)}) copy-start(bf16[2,8,88,272]{3,2,0,1:T(8,128)(2,1)} %and_convert_fusion.1) | copy-start | bytes 2297860
  564.0 250.0 %reduce-scatter.9.cloned.1.call-start = ((), (), s32[]{:S(2)}) async-start(), calls=%async_computation.12 | async-start | bytes 14417920 | tf_op jit(solution)/shard_map/reduce_scatter | solution.py:1596
  677.3 287.8 %reduce-scatter.11.cloned.1.call-start = ((), (), s32[]{:S(2)}) async-start(), calls=%async_computation.13 | async-start | bytes 14417920 | tf_op jit(solution)/shard_map/reduce_scatter | solution.py:1610
  677.4 7.5 slice-start.3
  677.5 4.0 copy-start.36
  677.5 4.0 copy-start.38
  677.5 7.4 slice-start.4
  716.4 310.0 %reduce-scatter.13.cloned.1.call-start = ((), (), s32[]{:S(2)}) async-start(), calls=%async_computation.14 | async-start | bytes 10485760 | tf_op jit(solution)/shard_map/reduce_scatter | solution.py:1619
  794.1 8.9 copy-start.48
  802.9 9.2 copy-start.11
  812.1 321.0 %reduce-scatter.15.cloned.1.call-start = ((), (), s32[]{:S(2)}) async-start(), calls=%async_computation.15 | async-start | bytes 10485760 | tf_op jit(solution)/shard_map/reduce_scatter | solution.py:1658
  813.4 3.4 collective-permute-start.5
  898.2 3.5 collective-permute-start.6
  901.7 11.6 copy-start.49
  948.7 7.9 collective-permute-start.7
  956.6 23.9 %slice-start = ((s8[8912896]{0:T(1024)(128)(4,1)}), s8[524288]{0:T(1024)(128)(4,1)S(1)}, s32[]{:S(2)}) async-start(s8[8912896]{0:T(1024)(128)(4,1)} %bitcast.214), calls=%async_computation.18 | async-start | bytes 1048576
  965.1 15.4 %slice-start.1 = ((s8[8912896]{0:T(1024)(128)(4,1)}), s8[4194304]{0:T(1024)(128)(4,1)S(1)}, s32[]{:S(2)}) async-start(s8[8912896]{0:T(1024)(128)(4,1)} %bitcast.214), calls=%async_computation.19 | async-start | bytes 8388608
  965.1 15.4 %slice-start.2 = ((s8[8912896]{0:T(1024)(128)(4,1)}), s8[4194304]{0:T(1024)(128)(4,1)S(1)}, s32[]{:S(2)}) async-start(s8[8912896]{0:T(1024)(128)(4,1)} %bitcast.214), calls=%async_computation.20 | async-start | bytes 8388608
  1002.4 181.4 %reduce-scatter.17.cloned.1.call-start = ((), (), s32[]{:S(2)}) async-start(), calls=%async_computation.16 | async-start | bytes 10485760 | tf_op jit(solution)/shard_map/reduce_scatter | solution.py:1660
  1016.1 5.3 copy-start.10
  1016.2 5.3 copy-start.30
  1016.2 5.3 copy-start.37
  1016.2 5.3 copy-start.39
  1016.2 104.6 %all-to-all-start.1 = ((bf16[4,272,2048]{2,1,0:T(8,128)(2,1)}), bf16[4,272,2048]{2,1,0:T(8,128)(2,1)}, u32[]{:S(2)}, u32[]{:S(2)}) async-start(bf16[4,272,2048]{2,1,0:T(8,128)(2,1)} %fusion), calls=%async_computation.4 | async-start | bytes 8912896 | tf_op jit(solution)/shard_map/all_to_all | solution.py:1662
  1026.4 97.8 %copy-start.2 = (bf16[272,2048]{1,0:T(8,128)(2,1)S(1)}, bf16[272,2048]{1,0:T(8,128)(2,1)}, u32[]{:S(2)}) copy-start(bf16[272,2048]{1,0:T(8,128)(2,1)} %param.16) | copy-start | bytes 3342340
  1026.4 97.8 %copy-start.26 = (f32[2048]{0:T(1024)S(1)}, f32[2048]{0:T(1024)}, u32[]{:S(2)}) copy-start(f32[2048]{0:T(1024)} %param.22) | copy-start | bytes 24580
  1026.4 97.8 %copy-start.32 = (f32[272]{0:T(512)S(1)}, f32[272]{0:T(512)}, u32[]{:S(2)}) copy-start(f32[272]{0:T(512)} %copy-done.31) | copy-start | bytes 3268
  1026.4 97.8 %copy-start.35 = (f32[272]{0:T(512)S(1)}, f32[272]{0:T(512)}, u32[]{:S(2)}) copy-start(f32[272]{0:T(512)} %copy-done.34) | copy-start | bytes 3268
  1129.0 12.1 %all-to-all-start.2 = ((f32[32,1,896]{2,1,0:T(1,128)}), f32[32,1,896]{2,1,0:T(1,128)S(1)}, u32[]{:S(2)}, u32[]{:S(2)}) async-start(f32[32,1,896]{2,1,0:T(1,128)} %copy.74), calls=%async_computation.6 | async-start | bytes 229376 | tf_op jit(solution)/shard_map/all_to_all | solution.py:1677
  1141.1 53.7 %all-to-all-start.3 = ((bf16[8,64,2048]{2,1,0:T(8,128)(2,1)}), bf16[8,64,2048]{2,1,0:T(8,128)(2,1)}, u32[]{:S(2)}, u32[]{:S(2)}) async-start(bf16[8,64,2048]{2,1,0:T(8,128)(2,1)} %bitcast.220), calls=%async_computation.8 | async-start | bytes 4194304 | tf_op jit(solution)/shard_map/all_to_all | solution.py:1369
  1145.7 5.0 copy-start.12
  (26 other events, 57.8 us)
Sparse Core Ops, SparseCore 0:
  11.8 49.8 all-gather.5
  63.9 85.2 all-gather.7
  564.1 112.1 reduce-scatter.6
  679.3 119.6 reduce-scatter.8
  801.9 112.0 reduce-scatter.10
  917.0 86.3 reduce-scatter.12
  1006.8 86.3 reduce-scatter.14
  1096.2 87.5 reduce-scatter.16

commit v5 on v4

--- a/solution.py
+++ b/solution.py
@@ -106,7 +106,8 @@
     table_refs = refs[3 * sets + 7 : 5 * sets + 7]
     rest = refs[5 * sets + 7 :]
     dq_refs = rest[:sets]
-    dk_ref, dv_ref, bias_ref, flipped_ref, dk_acc, dv_acc = rest[sets:]
+    dkv_ref, bias_ref, flipped_ref, dk_acc, dv_acc = rest[sets:]
+    half = dkv_ref.shape[1] // 2
     softmax_scale = scale / LOG2E
 
     @pl.when(pl.program_id(0) == 0)
@@ -160,11 +161,12 @@
                 ref[span, pl.ds(head * HEAD, HEAD)] = turned.astype(jnp.bfloat16)
     for head in range(step_heads):
         lanes = pl.ds(head * HEAD, HEAD)
+        first_lane = pl.multiple_of((pl.program_id(0) * step_heads + head) * HEAD, HEAD)
         for block in range(GROUPS):
             span = pl.ds(block * keys, keys)
             turned = spin(dk_acc[span, lanes] * softmax_scale, key_cos[span, :], key_sin[span, :])
-            dk_ref[span, lanes] = turned.astype(jnp.bfloat16)
-            dv_ref[span, lanes] = dv_acc[span, lanes].astype(jnp.bfloat16)
+            dkv_ref[span, pl.ds(first_lane, HEAD)] = turned.astype(jnp.bfloat16)
+            dkv_ref[span, pl.ds(half + first_lane, HEAD)] = dv_acc[span, lanes].astype(jnp.bfloat16)
 
 
 def whole_block(shape):
@@ -234,7 +236,7 @@
                 whole_block((tokens, HEAD)),
             ]
             + [whole_block((total_rows, HEAD))] * (2 * sets),
-            out_specs=[plain] * sets + [side, side],
+            out_specs=[plain] * sets + [whole_block((tokens, 2 * heads * HEAD))],
             scratch_shapes=[
                 pltpu.VMEM((GROUPS * (GROUPS + 1) // 2, keys, sets * rows), jnp.float32),
                 pltpu.VMEM((step_heads, GROUPS, HEAD, keys), jnp.bfloat16),
@@ -243,7 +245,7 @@
             ],
         ),
         out_shape=[jax.ShapeDtypeStruct((total_rows, heads * HEAD), jnp.bfloat16)] * sets
-        + [jax.ShapeDtypeStruct((tokens, heads * HEAD), jnp.bfloat16)] * 2,
+        + [jax.ShapeDtypeStruct((tokens, 2 * heads * HEAD), jnp.bfloat16)],
         compiler_params=pltpu.CompilerParams(vmem_limit_bytes=VMEM_BYTES),
         name="attention_backward",
     )(
@@ -366,7 +368,7 @@
         out_ref[...] = acc_ref[...].astype(jnp.bfloat16)
 
 
-def merge_hidden_grads(plan, slots, grad_keys, grad_values, weights, order):
+def merge_hidden_grads(plan, slots, grads, weights, order):
     sources, rows, capacity = plan.shape
     parts, depth, columns = weights.shape
     ck, tokens = columns // 2, sources * rows
@@ -380,7 +382,7 @@
                 pl.BlockSpec((sources, rows, capacity), lambda i, j, order: (0, 0, 0)),
                 pl.BlockSpec((sources, capacity, wide), lambda i, j, order: (0, 0, i)),
                 pl.BlockSpec((tokens, ck), lambda i, j, order: (0, order[j])),
-                pl.BlockSpec((tokens, ck), lambda i, j, order: (0, order[j])),
+                pl.BlockSpec((tokens, ck), lambda i, j, order: (0, parts + order[j])),
                 pl.BlockSpec((1, wide, columns), lambda i, j, order: (j, i, 0)),
             ],
             out_specs=pl.BlockSpec((tokens, wide), lambda i, j, order: (0, i)),
@@ -389,7 +391,7 @@
         out_shape=jax.ShapeDtypeStruct((tokens, depth), jnp.bfloat16),
         compiler_params=pltpu.CompilerParams(vmem_limit_bytes=VMEM_BYTES),
         name="merge_hidden_grads",
-    )(order, plan, slots, grad_keys, grad_values, weights)
+    )(order, plan, slots, grads, grads, weights)
 
 
 def mesh_device(index):
@@ -401,6 +403,20 @@
     near = chip + flip * (3 - 2 * chip)
     place = step + near * (1 - 2 * step) if step < 2 else step
     return place + flip * (3 - 2 * place)
+
+
+def far_order(chip, step):
+    return chip_order(chip, 3 - step)
+
+
+def is_middle(chip):
+    flip = chip // 2
+    return chip + flip * (3 - 2 * chip)
+
+
+def crossing_order(chip, step):
+    end, middle = chip_order(chip, step), chip_order(chip, (2, 3, 1, 0)[step])
+    return end + is_middle(chip) * (middle - end)
 
 
 def enter(devices, me):
@@ -427,8 +443,8 @@
 
 
 class Dispatch:
-    def __init__(self, me, slots, landing, local_sem, send, recv, pass_send, pass_recv):
-        self.me, self.chip, self.core = me, me // 2, lax.rem(me, 2)
+    def __init__(self, me, order, slots, landing, local_sem, send, recv, pass_send, pass_recv):
+        self.me, self.chip, self.core, self.order = me, me // 2, lax.rem(me, 2), order
         self.slots, self.landing = slots, landing
         self.local_sem, self.send, self.recv = local_sem, send, recv
         self.pass_send, self.pass_recv = pass_send, pass_recv
@@ -464,10 +480,11 @@
             self.local_sem,
         )
 
+    def start_local(self):
+        self.local().start()
+
     def start(self, steps):
         for step in steps:
-            if step == 0:
-                self.local().start()
             for copy in self.sends(step):
                 copy.start()
 
@@ -483,7 +500,7 @@
         )
 
     def arrive(self, step):
-        chip = chip_order(self.chip, step)
+        chip = self.order(self.chip, step)
         for source in (2 * chip, 2 * chip + 1):
             offset = lax.rem(self.me - source + 8, 8)
 
@@ -499,7 +516,7 @@
             self.pass_on(source).start()
 
     def ready(self, step):
-        chip = chip_order(self.chip, step)
+        chip = self.order(self.chip, step)
         for source in (2 * chip, 2 * chip + 1):
             place = self.place(source, 1 - self.core)
             remote(
@@ -514,9 +531,10 @@
 
 class Collect:
     def __init__(
-        self, me, far_first, kept, passing, passed, total, back, local_sem, pass_send, pass_recv, send, recv
+        self, me, order, own_steps, kept, passing, passed, total, back, local_sem, pass_send, pass_recv, send, recv
     ):
-        self.me, self.chip, self.core, self.far_first = me, me // 2, lax.rem(me, 2), far_first
+        self.me, self.chip, self.core = me, me // 2, lax.rem(me, 2)
+        self.order, self.own_steps = order, own_steps
         self.kept, self.passing, self.passed, self.total, self.back = kept, passing, passed, total, back
         self.local_sem, self.pass_send, self.pass_recv = local_sem, pass_send, pass_recv
         self.send, self.recv = send, recv
@@ -553,12 +571,12 @@
         )
 
     def block(self, step):
-        return chip_order(self.chip, 3 - step if self.far_first else step)
+        return self.order(self.chip, step)
 
     def each(self, step, own, other):
         chip = self.block(step)
         for source in (2 * chip, 2 * chip + 1):
-            if step != (3 if self.far_first else 0):
+            if step not in self.own_steps:
                 other(source)
                 continue
 
@@ -639,11 +657,18 @@
         pltpu.make_async_copy(source, target, weight_sem.at[n])
         for n, (source, target) in enumerate(((gate_hbm, gate), (up_hbm, up), (down_hbm, down)))
     ]
-    dispatch = Dispatch(me, slots, landing, local_sem.at[0], send, recv, pass_send, pass_recv)
+    dispatch = Dispatch(me, crossing_order, slots, landing, local_sem.at[0], send, recv, pass_send, pass_recv)
     collect = Collect(
-        me, False, kept, passing, passed, total, back, local_sem.at[1], swap_send, swap_recv, out_send, out_recv
+        me, crossing_order, (0, 3), kept, passing, passed, total, back, local_sem.at[1], swap_send, swap_recv, out_send, out_recv
     )
-    dispatch.start((0, 1, 2))
+    middle = is_middle(me // 2)
+    dispatch.start_local()
+    dispatch.start((0, 1))
+
+    @pl.when(middle == 1)
+    def _():
+        dispatch.start((2,))
+
     for load in loads:
         load.start()
     block = landing.shape[1]
@@ -678,7 +703,7 @@
             loads[0].wait()
             loads[1].wait()
         if step >= 2:
-            act_copy(chip_order(me // 2, step - 2), step - 2).wait()
+            act_copy(crossing_order(me // 2, step - 2), step - 2).wait()
 
         def hidden_part(part, carry, chip=chip, step=step):
             slot = lax.rem(part + step * chunks, 2)
@@ -696,6 +721,17 @@
             act[step % 2, :, columns] = (gated * jax.nn.sigmoid(gated) * raised).astype(jnp.bfloat16)
             for copy in stage_copies(chip, part, slot):
                 copy.start()
+            if step == 0:
+                @pl.when((part == chunks // 3) & (middle == 0))
+                def _():
+                    dispatch.sent((1,))
+                    dispatch.start((2,))
+
+                @pl.when((part == chunks // 2) & (middle == 1))
+                def _():
+                    dispatch.sent((1, 2))
+                    dispatch.start((3,))
+
             return carry
 
         lax.fori_loop(0, chunks, hidden_part, 0)
@@ -723,18 +759,21 @@
             collect.swap(step - 2).wait_send()
         lax.fori_loop(0, half // width, far_part, 0)
         collect.swap(step).start()
-        if step in (1, 2):
+        if step == 0:
+
+            @pl.when(middle == 0)
+            def _():
+                dispatch.sent((2,))
+                dispatch.start((3,))
+
+        if step < 3:
             dispatch.arrive(step + 1)
         lax.fori_loop(0, half // width, near_part, 0)
-        if step == 0:
-            dispatch.sent((1, 2))
-            dispatch.start((3,))
-            dispatch.arrive(1)
     collect.settle(3)
     for step in (2, 3):
-        act_copy(chip_order(me // 2, step), step).wait()
+        act_copy(crossing_order(me // 2, step), step).wait()
     for step in range(4):
-        rows_copy(chip_order(me // 2, step), step).wait()
+        rows_copy(crossing_order(me // 2, step), step).wait()
     for slot in range(2):
         for copy in stage_copies(0, 0, slot):
             copy.wait()
@@ -799,7 +838,8 @@
 def send_rows_body(slots, rows_out, local_sem, send, recv, pass_send, pass_recv):
     me = lax.axis_index("expert")
     enter(8, me)
-    dispatch = Dispatch(me, slots, rows_out, local_sem.at[0], send, recv, pass_send, pass_recv)
+    dispatch = Dispatch(me, chip_order, slots, rows_out, local_sem.at[0], send, recv, pass_send, pass_recv)
+    dispatch.start_local()
     dispatch.start((0, 1, 2, 3))
     for step in range(4):
         dispatch.arrive(step)
@@ -858,7 +898,7 @@
     me = lax.axis_index("expert")
     enter(8, me)
     collect = Collect(
-        me, True, kept, passing, passed, total, back, local_sem.at[0], swap_send, swap_recv, out_send, out_recv
+        me, far_order, (3,), kept, passing, passed, total, back, local_sem.at[0], swap_send, swap_recv, out_send, out_recv
     )
     loads = [
         pltpu.make_async_copy(source, target, weight_sem.at[n])
@@ -1012,6 +1052,206 @@
         ),
         name="ffn_backward",
     )(grad_rows, gate_pre, up_pre, gate_weight, up_weight, down_weight)
+
+
+def send_slots_body(
+    slots, rows_hbm, grads_hbm, landing, grad_out, rows_v, grads_v, stage, load_sem, stage_sem, local_sem, send, recv
+):
+    me = lax.axis_index("expert")
+    enter(8, me)
+
+    def outgoing(offset):
+        target = lax.rem(me + offset, 8)
+        return remote(slots.at[target], landing.at[me], send.at[offset], recv.at[offset], target)
+
+    local = pltpu.make_async_copy(slots.at[me], landing.at[me], local_sem)
+    for offset in range(1, 8):
+        outgoing(offset).start()
+    local.start()
+    loads = [
+        pltpu.make_async_copy(source, target, load_sem.at[n])
+        for n, (source, target) in enumerate(((rows_hbm, rows_v), (grads_hbm, grads_v)))
+    ]
+    for load in loads:
+        load.start()
+    for load in loads:
+        load.wait()
+    width = stage.shape[1]
+    blocks = rows_v.shape[1] // width
+
+    def stage_copy(block):
+        slot = lax.rem(block, 2)
+        span = pl.ds(pl.multiple_of(block * width, 16), width)
+        return pltpu.make_async_copy(stage.at[slot], grad_out.at[span, :], stage_sem.at[slot])
+
+    def one(block, carry):
+        @pl.when(block >= 2)
+        def _():
+            stage_copy(block - 2).wait()
+
+        columns = pl.ds(pl.multiple_of(block * width, 128), width)
+        turned = rows_v[:, columns].astype(jnp.float32).T.astype(jnp.bfloat16)
+        stage[lax.rem(block, 2)] = dot_nn(turned, grads_v[...]).astype(jnp.bfloat16)
+        stage_copy(block).start()
+        return carry
+
+    lax.fori_loop(0, blocks, one, 0)
+    for block in (blocks - 2, blocks - 1):
+        stage_copy(block).wait()
+    local.wait()
+    for offset in range(1, 8):
+        outgoing(offset).wait_send()
+        place = landing.at[lax.rem(me + 8 - offset, 8)]
+        remote(place, place, send.at[offset], recv.at[offset], me).wait_recv()
+
+
+def send_slots(slots, rows, grads):
+    total, depth = rows.shape
+    hidden_units = grads.shape[1]
+    width = min(256, depth // 2)
+    any_space = pl.BlockSpec(memory_space=pl.ANY)
+    bf = jnp.bfloat16
+    dma = pltpu.SemaphoreType.DMA
+    return pl.pallas_call(
+        send_slots_body,
+        in_specs=[any_space] * 3,
+        out_specs=[any_space] * 2,
+        out_shape=[
+            jax.ShapeDtypeStruct(slots.shape, bf),
+            jax.ShapeDtypeStruct((depth, hidden_units), bf),
+        ],
+        scratch_shapes=[
+            pltpu.VMEM((total, depth), bf),
+            pltpu.VMEM((total, hidden_units), bf),
+            pltpu.VMEM((2, width, hidden_units), bf),
+            dma((2,)),
+            dma((2,)),
+            dma,
+            dma((8,)),
+            dma((8,)),
+        ],
+        compiler_params=pltpu.CompilerParams(
+            collective_id=5, has_side_effects=True, vmem_limit_bytes=VMEM_BYTES
+        ),
+        name="send_slots",
+    )(slots, rows, grads)
+
+
+def merge_return_body(
+    dp_axis,
+    plan_hbm,
+    slots_hbm,
+    grads_hbm,
+    weight_hbm,
+    back,
+    plan,
+    slots,
+    grads,
+    weight,
+    kept,
+    passing,
+    passed,
+    total,
+    load_sem,
+    local_sem,
+    swap_send,
+    swap_recv,
+    out_send,
+    out_recv,
+):
+    me = lax.axis_index("expert")
+    replica = lax.axis_index(dp_axis)
+    enter(8, me)
+    loads = [
+        pltpu.make_async_copy(source, target, load_sem.at[n])
+        for n, (source, target) in enumerate(
+            ((plan_hbm, plan), (slots_hbm, slots), (grads_hbm, grads), (weight_hbm, weight))
+        )
+    ]
+    for load in loads:
+        load.start()
+    collect = Collect(
+        me, far_order, (3,), kept, passing, passed, total, back, local_sem.at[0], swap_send, swap_recv, out_send, out_recv
+    )
+    rows, half = collect.rows, collect.half
+    parts, ck = weight.shape[0], weight.shape[2] // 2
+    values_at = grads.shape[1] // 2
+    width = min(512, half)
+    for load in loads:
+        load.wait()
+    for step in range(4):
+        chip = collect.block(step)
+        span = pl.ds(pl.multiple_of(chip * 2 * rows, 16), 2 * rows)
+
+        def product(at, chip=chip, span=span):
+            columns = pl.ds(at, width)
+            result = jnp.concatenate(
+                [dot_nn(plan[2 * chip + n], slots[2 * chip + n, :, columns]) for n in range(2)], axis=0
+            )
+            for part in range(parts):
+                low = lax.rem(replica, 2) + (part % 2) * (1 - 2 * lax.rem(replica, 2))
+                high = replica // 2 + (part // 2) * (1 - 2 * (replica // 2))
+                at_keys = pl.multiple_of((2 * high + low) * ck, 128)
+                result += dot_nt(grads[span, pl.ds(at_keys, ck)], weight[part, columns, :ck])
+                result += dot_nt(grads[span, pl.ds(values_at + at_keys, ck)], weight[part, columns, ck:])
+            return result
+
+        def far_part(part, carry, step=step, product=product):
+            at = pl.multiple_of((1 - collect.core) * half + part * width, 128)
+            columns = pl.ds(pl.multiple_of(part * width, 128), width)
+            passing[step % 2, :, columns] = product(at).astype(jnp.bfloat16)
+            return carry
+
+        def near_part(part, carry, product=product):
+            at = pl.multiple_of(collect.core * half + part * width, 128)
+            kept[:, pl.ds(pl.multiple_of(part * width, 128), width)] = product(at)
+            return carry
+
+        if step >= 2:
+            collect.swap(step - 2).wait_send()
+        lax.fori_loop(0, half // width, far_part, 0)
+        collect.swap(step).start()
+        if step > 0:
+            collect.settle(step - 1)
+        lax.fori_loop(0, half // width, near_part, 0)
+    collect.settle(3)
+    collect.finish()
+
+
+def merge_return(plan, slots, grads, weights):
+    sources, rows, capacity = plan.shape
+    parts, depth, columns = weights.shape
+    tokens = sources * rows
+    half = depth // 2
+    any_space = pl.BlockSpec(memory_space=pl.ANY)
+    bf = jnp.bfloat16
+    dma = pltpu.SemaphoreType.DMA
+    return pl.pallas_call(
+        functools.partial(merge_return_body, "dp"),
+        in_specs=[any_space] * 4,
+        out_specs=any_space,
+        out_shape=jax.ShapeDtypeStruct((sources // 2, rows, depth), bf),
+        scratch_shapes=[
+            pltpu.VMEM(plan.shape, bf),
+            pltpu.VMEM(slots.shape, bf),
+            pltpu.VMEM(grads.shape, bf),
+            pltpu.VMEM(weights.shape, bf),
+            pltpu.VMEM((2 * rows, half), jnp.float32),
+            pltpu.VMEM((2, 2 * rows, half), bf),
+            pltpu.VMEM((sources // 2, 2 * rows, half), bf),
+            pltpu.VMEM((sources // 2, 2 * rows, half), bf),
+            dma((4,)),
+            dma((1,)),
+            dma((4,)),
+            dma((4,)),
+            dma((8,)),
+            dma((8,)),
+        ],
+        compiler_params=pltpu.CompilerParams(
+            collective_id=6, has_side_effects=True, vmem_limit_bytes=VMEM_BYTES
+        ),
+        name="merge_return",
+    )(plan, slots, grads, weights)
 
 
 def attention_send_body(
@@ -1474,7 +1714,7 @@
     att_gates = gate_values(hidden, att_router, att_first, att_second)
     ffn_picks, ffn_first, ffn_second = token_picks(ffn_routes, FFN_EXPERTS, ffn_capacity)
     prepared = (key_forward, key_backward, key_info, slot_tables, query_info, own_plan, att_picks, att_gates, ffn_picks)
-    hidden_all, prepared = lax.optimization_barrier((hidden_all, prepared))
+    hidden_all, kv_blocks, prepared = lax.optimization_barrier((hidden_all, kv_blocks, prepared))
     key_forward, key_backward, key_info, slot_tables, query_info, own_plan, att_picks, att_gates, ffn_picks = prepared
 
     queries, query_inputs = project_queries(own_plan, hidden_all, q_weight, slot_tables[0][0])
@@ -1499,11 +1739,14 @@
     if att_copies == 1:
         query_sets.append(far_half(queries))
         starts = jnp.stack([core * heads, 0]).astype(jnp.int32)
-    fused = devices == 8 and att_copies == 1 and ffn_copies == 2 and ffn_capacity % 16 == 0
+    fused = devices == 8 and replicas == 4 and att_copies == 1 and ffn_copies == 2 and ffn_capacity % 16 == 0
     if fused:
         *att_outs, att_rows, att_back, lse = attention_send(
             *query_sets, keys_all, values_all, o_weight, key_info, query_info, att_capacity
         )
+        att_elsewhere = [
+            lax.ppermute(att_rows, "dp", [(i, i ^ n) for i in range(replicas)]) for n in range(1, replicas)
+        ]
     else:
         *att_outs, lse = attention_forward(
             query_sets, starts // 2, keys_all, values_all, key_info, query_info, heads
@@ -1567,6 +1810,7 @@
     ffn_gate_grad, ffn_scaled = pair_grads(ffn_gates, ffn_branches, grad_result)
     ffn_grad_slots = fill_slots(ffn_picks, ffn_scaled)
     if fused:
+        ffn_grad_slots, att_elsewhere = lax.optimization_barrier((ffn_grad_slots, att_elsewhere))
         grad_ffn_out = send_rows(ffn_grad_slots, 2).reshape(-1, D)
     else:
         grad_ffn_out = to_experts(ffn_grad_slots)
@@ -1605,20 +1849,35 @@
     att_slots = fill_slots(att_picks, att_scaled)
     if att_copies > 1:
         att_slots = jnp.repeat(att_slots, att_copies, axis=0)
-    att_slots, summed_down, ffn_inputs = lax.optimization_barrier((att_slots, summed_down, ffn_inputs))
-    grad_up = dot_tn(ffn_inputs, grad_up_pre).astype(bf16)
+    att_slots, summed_down = lax.optimization_barrier((att_slots, summed_down))
+    if fused:
+        grad_att_out, grad_up = send_slots(att_slots, ffn_inputs, grad_up_pre)
+        grad_att_out = grad_att_out.reshape(-1, D)
+    else:
+        grad_att_out = exchange(att_slots).reshape(-1, D)
+        grad_up = dot_tn(ffn_inputs, grad_up_pre).astype(bf16)
+        grad_att_out, grad_up = lax.optimization_barrier((grad_att_out, grad_up))
     summed_up = lax.psum_scatter(grad_up, "dp", scatter_dimension=0, tiled=True)
-    grad_att_out = exchange(att_slots).reshape(-1, D)
-    grad_att_out, grad_up = lax.optimization_barrier((grad_att_out, grad_up))
     grad_heads = jnp.dot(grad_att_out, o_weight, preferred_element_type=f32).astype(bf16)
     grad_heads, grad_att_out = lax.optimization_barrier((grad_heads, grad_att_out))
     grad_sets = [grad_heads]
     if att_copies == 1:
         grad_sets.append(far_half(grad_heads))
-    grad_o = dot_tn(grad_att_out, att_rows).astype(bf16)
-    summed_o = lax.psum_scatter(grad_o, "dp", scatter_dimension=0, tiled=True)
-    grad_sets[-1], summed_gate, grad_o = lax.optimization_barrier((grad_sets[-1], summed_gate, grad_o))
-    *grad_queries, grad_keys, grad_values = attention_backward(
+    if fused:
+        share = D // replicas
+
+        def columns_of(replica):
+            return lax.dynamic_slice_in_dim(grad_att_out, replica * share, share, 1)
+
+        grad_columns = [columns_of(my_replica)] + [
+            lax.ppermute(columns_of(my_replica ^ n), "dp", [(i, i ^ n) for i in range(replicas)])
+            for n in range(1, replicas)
+        ]
+    else:
+        grad_o = dot_tn(grad_att_out, att_rows).astype(bf16)
+        summed_o = lax.psum_scatter(grad_o, "dp", scatter_dimension=0, tiled=True).astype(f32)
+    grad_sets[-1], summed_gate = lax.optimization_barrier((grad_sets[-1], summed_gate))
+    *grad_queries, grad_keys_values = attention_backward(
         query_sets,
         starts,
         grad_sets,
@@ -1633,36 +1892,40 @@
         heads,
     )
     grad_query_pre = join_halves(*grad_queries) if att_copies == 1 else grad_queries[0]
+    grad_kv = dot_tn(hidden_all.reshape(token_count, D), grad_keys_values).astype(bf16)
+    grad_q = dot_tn(query_inputs, grad_query_pre).astype(bf16)
+    summed_kv = lax.psum_scatter(grad_kv, "dp", scatter_dimension=0, tiled=True)
+    summed_q = lax.psum_scatter(grad_q, "dp", scatter_dimension=0, tiled=True)
     grad_query_in = lax.dot_general(
         grad_query_pre, q_weight, (((1,), (1,)), ((), ())), preferred_element_type=f32
     ).astype(bf16)
-    merged = merge_hidden_grads(
+    grad_query_in, grad_kv, grad_q, summed_up = lax.optimization_barrier(
+        (grad_query_in, grad_kv, grad_q, summed_up)
+    )
+
+    merge_args = (
         own_plan.transpose(0, 2, 1),
         grad_query_in.reshape(devices, att_capacity, D),
-        grad_keys,
-        grad_values,
+        grad_keys_values,
         kv_blocks,
-        block_order,
-    ).reshape(devices // 2, 2, row_count, D)
-    kept = lax.dynamic_index_in_dim(merged, core, 1, keepdims=False)
-    passed = lax.ppermute(
-        lax.dynamic_index_in_dim(merged, 1 - core, 1, keepdims=False), "expert", pair
     )
-    chip_sum = (kept.astype(f32) + passed.astype(f32)).astype(bf16)
-    chip_sum, hidden_rows, query_inputs, summed_up = lax.optimization_barrier(
-        (chip_sum, hidden_all.reshape(token_count, D), query_inputs, summed_up)
-    )
-    grad_kv = jnp.concatenate(
-        [dot_tn(hidden_rows, grad_keys).astype(bf16), dot_tn(hidden_rows, grad_values).astype(bf16)], axis=1
-    )
-    summed_kv = lax.psum_scatter(grad_kv, "dp", scatter_dimension=0, tiled=True)
-    grad_q = dot_tn(query_inputs, grad_query_pre).astype(bf16)
-    summed_q = lax.psum_scatter(grad_q, "dp", scatter_dimension=0, tiled=True)
-    same_core = [[2 * i + c for i in range(devices // 2)] for c in range(2)]
-    arrived = lax.all_to_all(
-        chip_sum, "expert", split_axis=0, concat_axis=0, axis_index_groups=same_core, tiled=True
-    )
-    arrived, grad_kv, grad_q, summed_o = lax.optimization_barrier((arrived, grad_kv, grad_q, summed_o))
+    if fused:
+        arrived = merge_return(*merge_args)
+        arrived, grad_columns, summed_kv = lax.optimization_barrier((arrived, grad_columns, summed_kv))
+        summed_o = sum(
+            dot_tn(grad, rows) for grad, rows in zip(grad_columns, [att_rows] + att_elsewhere)
+        )
+    else:
+        merged = merge_hidden_grads(*merge_args, block_order).reshape(devices // 2, 2, row_count, D)
+        kept = lax.dynamic_index_in_dim(merged, core, 1, keepdims=False)
+        passed = lax.ppermute(
+            lax.dynamic_index_in_dim(merged, 1 - core, 1, keepdims=False), "expert", pair
+        )
+        chip_sum = (kept.astype(f32) + passed.astype(f32)).astype(bf16)
+        same_core = [[2 * i + c for i in range(devices // 2)] for c in range(2)]
+        arrived = lax.all_to_all(
+            chip_sum, "expert", split_axis=0, concat_axis=0, axis_index_groups=same_core, tiled=True
+        )
     grad_att_router, hidden_one_extra = router_grads(
         hidden, att_router, att_gates, att_first, att_second, att_gate_grad
     )
@@ -1695,7 +1958,7 @@
         shared_kv,
         shared_att_router,
         summed_q.astype(f32),
-        summed_o.astype(f32),
+        summed_o,
         shared_gain_two,
         shared_ffn_router,
         summed_gate.astype(f32),

time: 1210 us -> 1170 us (0.967)
  Pallas kernels: 553 us -> 672 us
  waiting for transfers between devices: 221 us -> 149 us
  blocking collectives: 91.7 us -> 49.4 us
  matrix products: 180 us -> 162 us
  other arithmetic: 79.6 us -> 61.9 us
    pallas_call x1 -> x2, Pallas kernels: 30.1 us -> 151 us  [the longest x1 92.3 us: merge_return(): pl.pallas_call(functools.partial(merge_return_body, 'dp'), in_specs=[any_...]
    all_to_all x2 -> x0, waiting for transfers between devices: 98.4 us -> none  [the longest x1 94.3 us: body(): lax.all_to_all(chip_sum, 'expert', split_axis=0, concat_axis=0, axis_inde...]
    all_to_all x1, blocking collectives: 77.6 us -> 35.1 us  [body(): lax.all_to_all(packed, ('dp', 'expert'), split_axis=0, concat_axis=0, til...]
    reduce_scatter x1, waiting for transfers between devices: 0.01 us -> 34.2 us  [body(): lax.psum_scatter(grad_gate, 'dp', scatter_dimension=0, tiled=True)]
    dot_general x7 -> x8, matrix products: 124 us -> 104 us  [dot_tn(): lax.dot_general(left, right, (((0,), (0,)), ((), ())), preferred_element_...]
    all_gather x1, waiting for transfers between devices: 12.9 us -> 0.01 us  [body(): hidden_all = lax.all_gather(hidden_sent, 'expert', axis=0)]
    ppermute x1, waiting for transfers between devices: 0.01 us -> 12.9 us  [spread_over_replicas(): lax.ppermute(second[:cut], 'dp', across)]
  transfers between devices with their start and end apart: 19 -> 21, of which waited for: 10 -> 7; matrix products, arithmetic and copies ran while one was open for 20% -> 18% of each run, Pallas kernels for 20% -> 42%
where the time goes in v5:
time: 1170 us; the launch traced here: 1160 us
  Pallas kernels  672 us (57%)
  matrix products  162 us (14%)
  waiting for transfers between devices  149 us (13%)
  other arithmetic  61.9 us (5%)
  blocking collectives  49.4 us (4%)
  local copies, waits for them, and re-layouts  33.5 us (3%)
  starting transfers between devices  20 us (2%)
  between operations  16.1 us (1%)
    pallas_call x1, Pallas kernels, ffn_forward(): pl.pallas_call(functools.partial(ffn_forward_body, chunk), in_specs=[any_...  142 us
    dot_general x8, matrix products, dot_tn(): lax.dot_general(left, right, (((0,), (0,)), ((), ())), preferred_element_...  104 us
    pallas_call x1, Pallas kernels, attention_send(): pl.pallas_call(functools.partial(attention_send_body, HEAD ** (-0.5) * LO...  94.3 us
    pallas_call x1, Pallas kernels, merge_return(): pl.pallas_call(functools.partial(merge_return_body, 'dp'), in_specs=[any_...  92.3 us
    pallas_call x1, Pallas kernels, ffn_backward(): pl.pallas_call(functools.partial(ffn_backward_body, chunk), in_specs=[any...  88.4 us
    pallas_call x1, Pallas kernels, attention_backward(): pl.pallas_call(functools.partial(attention_backward_body, sets, step_head...  83.5 us
    pallas_call x1, Pallas kernels, send_rows(): pl.pallas_call(send_rows_body, in_specs=[any_space], out_specs=any_space,...  71.6 us
    pallas_call x1, Pallas kernels, send_slots(): pl.pallas_call(send_slots_body, in_specs=[any_space] * 3, out_specs=[any_...  58.6 us
  transfers between devices with their start and end apart: 21, of which 7 were waited for; matrix products, arithmetic and copies ran while one was open for 18% of the time, Pallas kernels for 42%

profile of v5, /device:TPU:0, one launch (start us, length us, event | category | flops | bytes accessed | tf_op | source)
XLA Modules:
  0.0 1163.8 jit_solution(10790965523017697899)
XLA Ops:
  7.2 3.3 copy.62
  13.4 48.2 %all-gather.6.cloned.1.call-done = bf16[8,256,1024]{2,1,0:T(8,128)(2,1)} async-done(((bf16[1,256,1024]{2,1,0:T(8,128)(2,1)}), bf16[8,256,1024]{2,1,0:T(8,128)(2,1)}) %all-gather.6.cloned.1.call-update) | async-done | bytes 4194320 | tf_op jit(solution)/shard_map/all_gather | solution.py:1685
  67.4 5.7 fusion.37
  81.5 3.3 fusion.145
  84.8 14.3 %all-gather.2 = s32[8,272,2]{1,2,0:T(2,128)S(1)} all-gather(s32[1,272,2]{1,2,0:T(2,128)S(1)} %bitcast.224), channel_id=3, replica_groups=mesh['dp'=4,'expert'=8] {'expert'}, dimensions={0}, use_global_device_ids=true | all-gather | bytes 19584 | tf_op jit(solution)/shard_map/all_gather | solution.py:1691
  102.6 20.1 %collective-permute-done.1 = bf16[2048,512]{1,0:T(8,128)(2,1)} collective-permute-done((bf16[2048,512]{1,0:T(8,128)(2,1)S(1)}, bf16[2048,512]{1,0:T(8,128)(2,1)}, u32[]{:S(2)}, u32[]{:S(2)}) %collective-permute-start.1) | collective-permute-done | bytes 2097184 | tf_op jit(solution)/shard_map/ppermute | solution.py:1633
  129.2 2.6 multiply_cosine_fusion.1
  135.7 12.9 %collective-permute-done.2 = bf16[1024,512]{1,0:T(8,128)(2,1)S(1)} collective-permute-done((bf16[1024,512]{1,0:T(8,128)(2,1)S(1)}, bf16[1024,512]{1,0:T(8,128)(2,1)S(1)}, u32[]{:S(2)}, u32[]{:S(2)}) %collective-permute-start.2) | collective-permute-done | bytes 1048608 | tf_op jit(solution)/shard_map/ppermute | solution.py:1635
  148.5 2.6 collective-permute-done.3
  151.2 6.1 pad_maximum_fusion.weight_ref.weight_hbm
  159.5 15.0 %project_queries.1 = (bf16[704,2048]{1,0:T(8,128)(2,1)}, bf16[704,2048]{1,0:T(8,128)(2,1)}) custom-call(bf16[8,88,272]{2,1,0:T(8,128)(2,1)} %copy.68.plan_ref, bf16[8,272,2048]{2,1,0:T(8,128)(2,1)} %bitcast.206, bf16[2048,2048]{1,0:T(8,128)(2,1)} %weight_ref.1, f32[704,128]{1,0:T(8,128)} %get-tuple-element.121.cos_ref.refs_13_, ...), custom_call_target="tpu_custom_call" | custom-call | tf_op jit(solution)/shard_map/project_queries/pallas_call | solution.py:292
  174.5 2.6 constant_dynamic-slice_fusion.5
  179.1 26.6 %project_keys_values.1 = (bf16[2176,1024]{1,0:T(8,128)(2,1)}, bf16[2176,1024]{1,0:T(8,128)(2,1)}) custom-call(s32[4]{0:T(128)} %iota_xor_fusion.order_ref, bf16[8,272,2048]{2,1,0:T(8,128)(2,1)} %bitcast.207, bf16[4,2048,512]{2,1,0:T(8,128)(2,1)} %pad_maximum_fusion.weight_ref.weight_hbm, f32[2176,128]{1,0:T(8,128)} %pad_maximum_fusion.1.cos_ref.refs_11_, ...), custom_call_target="tpu_custom_call" | custom-call | tf_op jit(solution)/shard_map/project_keys_values/pallas_call | solution.py:330
  206.8 94.3 %attention_send.1 = (bf16[704,1024]{1,0:T(8,128)(2,1)}, bf16[704,1024]{1,0:T(8,128)(2,1)}, bf16[704,2048]{1,0:T(8,128)(2,1)}, bf16[8,88,2048]{2,1,0:T(8,128)(2,1)}, f32[8,4,1,352]{3,2,1,0:T(1,128)}) custom-call(bf16[704,2048]{1,0:T(8,128)(2,1)} %get-tuple-element.88.query_hbm.refs_0_, bf16[704,1024]{1,0:T(8,128)(2,1)} %copy-done.12, ...), custom_call_target="tpu_custom_call" | custom-call | tf_op jit(solution)/shard_map/attention_send/pallas_call | solution.py:1461
  304.7 4.1 convolution_bitcast_fusion.2
  312.8 3.3 convolution_convert_fusion.6.slots
  316.1 142.2 %ffn_forward.1 = (bf16[1408,2048]{1,0:T(8,128)(2,1)}, bf16[1408,2816]{1,0:T(8,128)(2,1)}, bf16[1408,2816]{1,0:T(8,128)(2,1)}, bf16[1408,2816]{1,0:T(8,128)(2,1)}, bf16[4,176,2048]{2,1,0:T(8,128)(2,1)}) custom-call(bf16[4,176,2048]{2,1,0:T(8,128)(2,1)} %convolution_convert_fusion.6.slots, bf16[2048,2816]{1,0:T(8,128)(2,1)} %gate_hbm.3, ...), custom_call_target="tpu_custom_call" | custom-call | tf_op jit(solution)/shard_map/ffn_forward/pallas_call | solution.py:795
  458.4 3.9 convolution_bitcast_fusion.1
  465.9 4.0 bitcast_convert_fusion.1.slots
  469.9 71.6 %send_rows.1 = bf16[4,352,2048]{2,1,0:T(8,128)(2,1)} custom-call(bf16[4,176,2048]{2,1,0:T(8,128)(2,1)} %bitcast_convert_fusion.1.slots), custom_call_target="tpu_custom_call" | custom-call | tf_op jit(solution)/shard_map/send_rows/pallas_call | solution.py:856
  541.5 24.2 %convolution_convert_fusion.1 = bf16[2048,2816]{1,0:T(8,128)(2,1)} fusion(bf16[1408,2048]{1,0:T(8,128)(2,1)} %bitcast.208, bf16[1408,2816]{1,0:T(8,128)(2,1)} %get-tuple-element.101), kind=kOutput, calls=%fused_computation.1 | convolution fusion | flops 16246112256 | bytes 25231360 | tf_op jit(solution)/shard_map/dot_general | solution.py:1641
  565.8 88.4 %ffn_backward.1 = (bf16[1408,2816]{1,0:T(8,128)(2,1)}, bf16[1408,2816]{1,0:T(8,128)(2,1)}, bf16[4,176,2048]{2,1,0:T(8,128)(2,1)}) custom-call(bf16[1408,2048]{1,0:T(8,128)(2,1)} %bitcast.209, bf16[1408,2816]{1,0:T(8,128)(2,1)} %get-tuple-element.103.gate_in, bf16[1408,2816]{1,0:T(8,128)(2,1)} %get-tuple-element.104.up_in, bf16[2048,2816]{1,0:T(8,128)(2,1)} %gate_hbm.3, ...), custom_call_target="tpu_custom_call" | custom-call | tf_op jit(solution)/shard_map/ffn_backward/pallas_call | solution.py:1020
  654.2 24.9 %convolution_convert_fusion = bf16[2048,2816]{1,0:T(8,128)(2,1)} fusion(bf16[1408,2048]{1,0:T(8,128)(2,1)} %get-tuple-element.106.rows_hbm, bf16[1408,2816]{1,0:T(8,128)(2,1)} %get-tuple-element.107), kind=kOutput, calls=%fused_computation | convolution fusion | flops 16246112256 | bytes 25231360 | tf_op jit(solution)/shard_map/dot_general | solution.py:1641
  679.3 3.9 convolution_bitcast_fusion
  683.3 2.9 multiply_reduce_fusion
  689.2 4.0 bitcast_convert_fusion.slots
  693.3 58.6 %send_slots.1 = (bf16[8,88,2048]{2,1,0:T(8,128)(2,1)}, bf16[2048,2816]{1,0:T(8,128)(2,1)}) custom-call(bf16[8,88,2048]{2,1,0:T(8,128)(2,1)} %bitcast_convert_fusion.slots, bf16[1408,2048]{1,0:T(8,128)(2,1)} %get-tuple-element.106.rows_hbm, bf16[1408,2816]{1,0:T(8,128)(2,1)} %get-tuple-element.111.grads_hbm), custom_call_target="tpu_custom_call" | custom-call | tf_op jit(solution)/shard_map/send_slots/pallas_call | solution.py:1115
  751.9 9.4 convolution_convert_fusion.5.refs_2_
  765.1 34.2 %reduce-scatter.8.cloned.1.call-done = bf16[512,2816]{1,0:T(8,128)(2,1)} async-done(((bf16[2048,2816]{1,0:T(8,128)(2,1)}), bf16[512,2816]{1,0:T(8,128)(2,1)}) %reduce-scatter.8.cloned.1.call-update) | async-done | bytes 2883600 | tf_op jit(solution)/shard_map/reduce_scatter | solution.py:1840
  799.3 83.5 %attention_backward.1 = (bf16[704,1024]{1,0:T(8,128)(2,1)}, bf16[704,1024]{1,0:T(8,128)(2,1)}, bf16[2176,2048]{1,0:T(8,128)(2,1)}) custom-call(s32[2]{0:T(128)} %pad_add_fusion.1.first_ref, bf16[704,2048]{1,0:T(8,128)(2,1)} %get-tuple-element.88.query_hbm.refs_0_, bf16[704,1024]{1,0:T(8,128)(2,1)} %copy-done.12, bf16[704,2048]{1,0:T(8,128)(2,1)} %copy-done.11, ...), custom_call_target="tpu_custom_call" | custom-call | tf_op jit(solution)/shard_map/attention_backward/pallas_call | solution.py:221
  882.8 26.1 %convolution_convert_fusion.3 = bf16[2048,2048]{1,0:T(8,128)(2,1)} fusion(bf16[2176,2048]{1,0:T(8,128)(2,1)} %all-gather.8.cloned.1.call-done, bf16[2176,2048]{1,0:T(8,128)(2,1)} %get-tuple-element.127.grads_hbm), kind=kOutput, calls=%fused_computation.5 | convolution fusion | flops 18257805312 | bytes 26214400 | tf_op jit(solution)/shard_map/dot_general | solution.py:1641
  909.2 3.4 collective-permute-done.9
  912.6 12.3 %convolution_convert_fusion.2 = bf16[2048,2048]{1,0:T(8,128)(2,1)} fusion(bf16[704,2048]{1,0:T(8,128)(2,1)S(1)} %copy-done.40, bf16[704,1024]{1,0:T(8,128)(2,1)} %collective-permute-done.9, bf16[704,1024]{1,0:T(8,128)(2,1)} %get-tuple-element.125, pred[]{:T(512)S(6)} %eq.225), kind=kOutput, calls=%fused_computation.4 | convolution fusion | flops 5922750464 | bytes 14155777 | tf_op jit(solution)/shard_map/dot_general | solution.py:1641
  931.0 2.9 constant_dynamic-slice_fusion
  937.4 11.9 %convolution_convert_fusion.4 = bf16[704,2048]{1,0:T(8,128)(2,1)} fusion(bf16[2048,2048]{1,0:T(8,128)(2,1)} %weight_ref.1, bf16[704,1024]{1,0:T(8,128)(2,1)} %collective-permute-done.9, bf16[704,1024]{1,0:T(8,128)(2,1)S(1)} %copy-done.41, pred[]{:T(512)S(6)} %eq.225), kind=kOutput, calls=%fused_computation.20 | convolution fusion | flops 5919997952 | bytes 14155777 | tf_op jit(solution)/shard_map/dot_general | solution.py:1899
  949.3 92.3 %merge_return.1 = bf16[4,272,2048]{2,1,0:T(8,128)(2,1)} custom-call(bf16[8,272,88]{2,1,0:T(8,128)(2,1)} %bitcast.215, bf16[8,88,2048]{2,1,0:T(8,128)(2,1)} %bitcast.217, bf16[2176,2048]{1,0:T(8,128)(2,1)} %get-tuple-element.127.grads_hbm, bf16[4,2048,512]{2,1,0:T(8,128)(2,1)} %pad_maximum_fusion.weight_ref.weight_hbm), custom_call_target="tpu_custom_call" | custom-call | tf_op jit(solution)/shard_map/merge_return/pallas_call | solution.py:1229
  1042.5 3.9 convert_reduce_fusion
  1046.5 3.2 fusion.13
  1050.7 35.1 %all_to_all.14 = f32[32,1,896]{2,1,0:T(1,128)S(1)} all-to-all(f32[32,1,896]{2,1,0:T(1,128)S(1)} %copy.71), channel_id=1, replica_groups=mesh['dp'=4,'expert'=8] {'dp','expert'}, dimensions={0} | all-to-all | bytes 229376 | tf_op jit(solution)/shard_map/all_to_all | solution.py:1940
  1085.8 4.6 all-to-all-start.1
  1090.4 5.0 convert_element_type.160
  1095.4 2.9 convert_element_type.158
  1098.3 27.4 %reduce-scatter.14.cloned.1.call-done = bf16[512,2048]{1,0:T(8,128)(2,1)} async-done(((bf16[2048,2048]{1,0:T(8,128)(2,1)}), bf16[512,2048]{1,0:T(8,128)(2,1)}) %reduce-scatter.14.cloned.1.call-update) | async-done | bytes 2097168 | tf_op jit(solution)/shard_map/reduce_scatter | solution.py:1898
  1125.7 4.3 convert_element_type.157
  1130.0 3.1 convert_element_type.159
  1135.5 3.9 fusion.148
  1139.4 4.0 fusion.149
  1145.1 6.2 add_add_fusion
  (242 shorter events, 74.3 us)
Async XLA Ops:
  7.2 54.7 %copy-start = (f32[2048,8]{0,1:T(8,128)S(1)}, f32[2048,8]{0,1:T(8,128)}, u32[]{:S(2)}) copy-start(f32[2048,8]{0,1:T(8,128)} %param.24) | copy-start | bytes 196612
  7.2 54.5 %all-gather.6.cloned.1.call-start = ((), (), s32[]{:S(2)}) async-start(), calls=%async_computation.7 | async-start | bytes 4718592 | tf_op jit(solution)/shard_map/all_gather | solution.py:1685
  11.7 50.1 %copy-start.35 = (s32[272,2]{0,1:T(2,128)S(1)}, s32[272,2]{0,1:T(2,128)}, u32[]{:S(2)}) copy-start(s32[272,2]{0,1:T(2,128)} %param.18) | copy-start | bytes 6532
  11.7 145.7 %all-gather.8.cloned.1.call-start = ((), (), s32[]{:S(2)}) async-start(), calls=%async_computation.13 | async-start | bytes 10027008 | tf_op jit(solution)/shard_map/all_gather | solution.py:1687
  12.1 49.7 %copy-start.31 = (f32[272]{0:T(512)}, f32[272]{0:T(512)S(1)}, u32[]{:S(2)}) copy-start(f32[272]{0:T(512)S(1)} %add_rsqrt_fusion.1) | copy-start | bytes 3268
  12.1 52.1 %copy-start.38 = (s32[272,2]{0,1:T(2,128)S(1)}, s32[272,2]{0,1:T(2,128)}, u32[]{:S(2)}) copy-start(s32[272,2]{0,1:T(2,128)} %param.19) | copy-start | bytes 6532
  61.7 631.6 %reduce-scatter.6.cloned.1.call-start = ((), (), s32[]{:S(2)}) async-start(), calls=%async_computation.8 | async-start | bytes 14417920 | tf_op jit(solution)/shard_map/reduce_scatter | solution.py:1819
  61.8 5.6 copy-start.24
  67.4 7.1 copy-start.20
  74.8 47.9 %collective-permute-start.1 = (bf16[2048,512]{1,0:T(8,128)(2,1)S(1)}, bf16[2048,512]{1,0:T(8,128)(2,1)}, u32[]{:S(2)}, u32[]{:S(2)}) collective-permute-start(bf16[2048,512]{1,0:T(8,128)(2,1)S(1)} %bitcast.212), channel_id=1, source_target_pairs={{0,16},{8,24},{16,0},{24,8},{1,17},{9,25},{17,1},{25,9},{2,18},{10... | collective-permute-start | bytes 6291464 | tf_op jit(solution)/shard_map/ppermute | solution.py:1633
  76.3 49.2 %collective-permute-start = (bf16[2048,512]{1,0:T(8,128)(2,1)S(1)}, bf16[2048,512]{1,0:T(8,128)(2,1)}, u32[]{:S(2)}, u32[]{:S(2)}) collective-permute-start(bf16[2048,512]{1,0:T(8,128)(2,1)S(1)} %bitcast.213), channel_id=1, source_target_pairs={{0,8},{8,0},{16,24},{24,16},{1,9},{9,1},{17,25},{25,17},{2,10},{10... | collective-permute-start | bytes 6291464 | tf_op jit(solution)/shard_map/ppermute | solution.py:1633
  77.8 127.9 %copy-start.29 = (f32[272,2]{0,1:T(2,128)}, f32[272,2]{0,1:T(2,128)S(1)}, u32[]{:S(2)}) copy-start(f32[272,2]{0,1:T(2,128)S(1)} %broadcast_divide_fusion.1) | copy-start | bytes 6532
  81.5 20.5 %copy-start.37 = (s32[1,13]{1,0:T(1,128)S(1)}, s32[1,13]{1,0:T(1,128)}, u32[]{:S(2)}) copy-start(s32[1,13]{1,0:T(1,128)} %param.20) | copy-start | bytes 160
  124.0 24.5 %collective-permute-start.2 = (bf16[1024,512]{1,0:T(8,128)(2,1)S(1)}, bf16[1024,512]{1,0:T(8,128)(2,1)S(1)}, u32[]{:S(2)}, u32[]{:S(2)}) collective-permute-start(bf16[1024,512]{1,0:T(8,128)(2,1)S(1)} %slice.148), channel_id=1, source_target_pairs={{0,8},{8,0},{16,24},{24,16},{1,9},{9,1},{17,25},{25,17},{2,10},{10... | collective-permute-start | bytes 3145736 | tf_op jit(solution)/shard_map/ppermute | solution.py:1635
  126.9 24.2 %collective-permute-start.3 = (bf16[1024,512]{1,0:T(8,128)(2,1)S(1)}, bf16[1024,512]{1,0:T(8,128)(2,1)S(1)}, u32[]{:S(2)}, u32[]{:S(2)}) collective-permute-start(bf16[1024,512]{1,0:T(8,128)(2,1)S(1)} %slice.149), channel_id=1, source_target_pairs={{0,16},{8,24},{16,0},{24,8},{1,17},{9,25},{17,1},{25,9},{2,18},{10... | collective-permute-start | bytes 3145736 | tf_op jit(solution)/shard_map/ppermute | solution.py:1635
  177.1 28.6 %collective-permute-start.4 = (bf16[704,1024]{1,0:T(8,128)(2,1)}, bf16[704,1024]{1,0:T(8,128)(2,1)S(1)}, u32[]{:S(2)}, u32[]{:S(2)}) collective-permute-start(bf16[704,1024]{1,0:T(8,128)(2,1)} %constant_dynamic-slice_fusion.5), channel_id=1, source_target_pairs={{0,1},{1,0},{2,3},{3,2},{4,5},{5,4},{6,7},{7,6},{8,9},{9,8},{10,11... | collective-permute-start | bytes 4325384 | tf_op jit(solution)/shard_map/ppermute | solution.py:1724
  301.2 168.7 %collective-permute-start.7 = (bf16[704,2048]{1,0:T(8,128)(2,1)}, bf16[704,2048]{1,0:T(8,128)(2,1)}, u32[]{:S(2)}, u32[]{:S(2)}) collective-permute-start(bf16[704,2048]{1,0:T(8,128)(2,1)} %get-tuple-element.99), channel_id=1, source_target_pairs={{0,24},{8,16},{16,8},{24,0},{1,25},{9,17},{17,9},{25,1},{2,26},{10... | collective-permute-start | bytes 8650760 | tf_op jit(solution)/shard_map/ppermute | solution.py:1748
  302.8 167.1 %collective-permute-start.6 = (bf16[704,2048]{1,0:T(8,128)(2,1)}, bf16[704,2048]{1,0:T(8,128)(2,1)}, u32[]{:S(2)}, u32[]{:S(2)}) collective-permute-start(bf16[704,2048]{1,0:T(8,128)(2,1)} %get-tuple-element.99), channel_id=1, source_target_pairs={{0,16},{8,24},{16,0},{24,8},{1,17},{9,25},{17,1},{25,9},{2,18},{10... | collective-permute-start | bytes 8650760 | tf_op jit(solution)/shard_map/ppermute | solution.py:1748
  303.3 166.6 %collective-permute-start.5 = (bf16[704,2048]{1,0:T(8,128)(2,1)}, bf16[704,2048]{1,0:T(8,128)(2,1)}, u32[]{:S(2)}, u32[]{:S(2)}) collective-permute-start(bf16[704,2048]{1,0:T(8,128)(2,1)} %get-tuple-element.99), channel_id=1, source_target_pairs={{0,8},{8,0},{16,24},{24,16},{1,9},{9,1},{17,25},{25,17},{2,10},{10... | collective-permute-start | bytes 8650760 | tf_op jit(solution)/shard_map/ppermute | solution.py:1748
  458.4 3.9 copy-start.17
  565.7 233.6 %reduce-scatter.8.cloned.1.call-start = ((), (), s32[]{:S(2)}) async-start(), calls=%async_computation.9 | async-start | bytes 14417920 | tf_op jit(solution)/shard_map/reduce_scatter | solution.py:1840
  679.1 270.2 %reduce-scatter.10.cloned.1.call-start = ((), (), s32[]{:S(2)}) async-start(), calls=%async_computation.10 | async-start | bytes 14417920 | tf_op jit(solution)/shard_map/reduce_scatter | solution.py:1860
  679.3 6.9 slice-start
  679.3 6.9 slice-start.1
  751.9 289.8 %reduce-scatter.12.cloned.1.call-start = ((), (), s32[]{:S(2)}) async-start(), calls=%async_computation.11 | async-start | bytes 10485760 | tf_op jit(solution)/shard_map/reduce_scatter | solution.py:1897
  761.4 38.0 %copy-start.11 = (bf16[704,2048]{1,0:T(8,128)(2,1)}, bf16[704,2048]{1,0:T(8,128)(2,1)S(1)}, u32[]{:S(2)}) copy-start(bf16[704,2048]{1,0:T(8,128)(2,1)S(1)} %convolution_convert_fusion.5.refs_2_) | copy-start | bytes 8650756
  762.8 36.6 %collective-permute-start.8 = (bf16[704,1024]{1,0:T(8,128)(2,1)}, bf16[704,1024]{1,0:T(8,128)(2,1)}, u32[]{:S(2)}, u32[]{:S(2)}) collective-permute-start(bf16[704,1024]{1,0:T(8,128)(2,1)} %constant_dynamic-slice_fusion.4), channel_id=1, source_target_pairs={{0,1},{1,0},{2,3},{3,2},{4,5},{5,4},{6,7},{7,6},{8,9},{9,8},{10,11... | collective-permute-start | bytes 4325384 | tf_op jit(solution)/shard_map/ppermute | solution.py:1724
  908.9 3.7 copy-start.40
  909.0 216.7 %reduce-scatter.14.cloned.1.call-start = ((), (), s32[]{:S(2)}) async-start(), calls=%async_computation.12 | async-start | bytes 10485760 | tf_op jit(solution)/shard_map/reduce_scatter | solution.py:1898
  909.0 3.6 collective-permute-start.9
  925.0 3.6 copy-start.30
  925.0 3.7 copy-start.8
  925.0 3.7 copy-start.25
  928.6 5.3 copy-start.33
  931.0 6.4 copy-start.41
  933.9 107.7 %collective-permute-start.12 = (bf16[704,512]{1,0:T(8,128)(2,1)S(1)}, bf16[704,512]{1,0:T(8,128)(2,1)S(1)}, u32[]{:S(2)}, u32[]{:S(2)}) collective-permute-start(bf16[704,512]{1,0:T(8,128)(2,1)S(1)} %get-tuple-element.229), channel_id=1, source_target_pairs={{0,24},{8,16},{16,8},{24,0},{1,25},{9,17},{17,9},{25,1},{2,26},{10... | collective-permute-start | bytes 2162696 | tf_op jit(solution)/shard_map/ppermute | solution.py:1873
  935.7 106.0 %collective-permute-start.11 = (bf16[704,512]{1,0:T(8,128)(2,1)S(1)}, bf16[704,512]{1,0:T(8,128)(2,1)}, u32[]{:S(2)}, u32[]{:S(2)}) collective-permute-start(bf16[704,512]{1,0:T(8,128)(2,1)S(1)} %get-tuple-element.230), channel_id=1, source_target_pairs={{0,16},{8,24},{16,0},{24,8},{1,17},{9,25},{17,1},{25,9},{2,18},{10... | collective-permute-start | bytes 2162696 | tf_op jit(solution)/shard_map/ppermute | solution.py:1873
  937.0 104.6 %collective-permute-start.10 = (bf16[704,512]{1,0:T(8,128)(2,1)S(1)}, bf16[704,512]{1,0:T(8,128)(2,1)}, u32[]{:S(2)}, u32[]{:S(2)}) collective-permute-start(bf16[704,512]{1,0:T(8,128)(2,1)S(1)} %get-tuple-element.231), channel_id=1, source_target_pairs={{0,8},{8,0},{16,24},{24,16},{1,9},{9,1},{17,25},{25,17},{2,10},{10... | collective-permute-start | bytes 2162696 | tf_op jit(solution)/shard_map/ppermute | solution.py:1873
  1042.5 3.9 copy-start.2
  1042.5 3.9 copy-start.28
  1042.5 4.0 copy-start.32
  1042.5 4.0 copy-start.34
  1085.8 67.7 %all-to-all-start.1 = ((bf16[8,64,2048]{2,1,0:T(8,128)(2,1)}), bf16[8,64,2048]{2,1,0:T(8,128)(2,1)}, u32[]{:S(2)}, u32[]{:S(2)}) async-start(bf16[8,64,2048]{2,1,0:T(8,128)(2,1)} %bitcast.220), calls=%async_computation.5 | async-start | bytes 4194304 | tf_op jit(solution)/shard_map/all_to_all | solution.py:1609
  1090.4 5.0 copy-start.13
  1125.7 4.3 copy-start.14
  1130.0 3.2 copy-start.15
  1130.0 3.6 copy-start.16
  1139.4 4.1 copy-start.6
  (17 other events, 29.0 us)
Sparse Core Ops, SparseCore 0:
  11.8 49.8 all-gather.5
  63.9 85.2 all-gather.7
  565.9 110.7 reduce-scatter.5
  679.6 119.6 reduce-scatter.7
  802.3 112.0 reduce-scatter.9
  917.3 117.2 reduce-scatter.11
  1038.0 87.6 reduce-scatter.13

commit v6 on v5

--- a/solution.py
+++ b/solution.py
@@ -835,33 +835,125 @@
     )(slots, gate_weight, up_weight, down_weight)
 
 
-def send_rows_body(slots, rows_out, local_sem, send, recv, pass_send, pass_recv):
+def send_rows_body(
+    slots,
+    act_hbm,
+    rows_out,
+    grad_out,
+    landing,
+    act,
+    total,
+    stage,
+    act_sem,
+    rows_sem,
+    stage_sem,
+    local_sem,
+    send,
+    recv,
+    pass_send,
+    pass_recv,
+):
     me = lax.axis_index("expert")
     enter(8, me)
-    dispatch = Dispatch(me, chip_order, slots, rows_out, local_sem.at[0], send, recv, pass_send, pass_recv)
+    dispatch = Dispatch(me, chip_order, slots, landing, local_sem.at[0], send, recv, pass_send, pass_recv)
     dispatch.start_local()
     dispatch.start((0, 1, 2, 3))
+    block = landing.shape[1]
+    width = stage.shape[1]
+    parts = landing.shape[2] // width
+
+    def span_of(step):
+        return pl.ds(pl.multiple_of(chip_order(me // 2, step) * block, 16), block)
+
+    def act_copy(step):
+        return pltpu.make_async_copy(
+            act_hbm.at[span_of(step), :],
+            act.at[step // 2, pl.ds(step % 2 * block, block), :],
+            act_sem.at[step],
+        )
+
+    def rows_copy(step):
+        chip = chip_order(me // 2, step)
+        return pltpu.make_async_copy(landing.at[chip], rows_out.at[chip], rows_sem.at[step])
+
+    def stage_copy(part):
+        slot = lax.rem(part, 2)
+        span = pl.ds(pl.multiple_of(part * width, 16), width)
+        return pltpu.make_async_copy(stage.at[slot], grad_out.at[span, :], stage_sem.at[slot])
+
     for step in range(4):
-        dispatch.arrive(step)
+        act_copy(step).start()
+    for pair in range(2):
+        steps = (2 * pair, 2 * pair + 1)
+        for step in steps:
+            dispatch.arrive(step)
+        chips = [dispatch.ready(step) for step in steps]
+        for step in steps:
+            rows_copy(step).start()
+            act_copy(step).wait()
+
+        def one(part, carry, pair=pair, chips=chips):
+            columns = pl.ds(pl.multiple_of(part * width, 128), width)
+            rows = jnp.concatenate([landing[chip, :, columns] for chip in chips], axis=0)
+            turned = rows.astype(jnp.float32).T.astype(jnp.bfloat16)
+            product = dot_nn(turned, act[pair])
+            span = pl.ds(pl.multiple_of(part * width, 16), width)
+            if pair == 0:
+                total[span, :] = product
+                return carry
+
+            @pl.when(part >= 2)
+            def _():
+                stage_copy(part - 2).wait()
+
+            stage[lax.rem(part, 2)] = (total[span, :] + product).astype(jnp.bfloat16)
+            stage_copy(part).start()
+            return carry
+
+        lax.fori_loop(0, parts, one, 0)
+    for part in (parts - 2, parts - 1):
+        stage_copy(part).wait()
     for step in range(4):
-        dispatch.ready(step)
+        rows_copy(step).wait()
     dispatch.sent((0, 1, 2, 3))
     dispatch.passed_on()
 
 
-def send_rows(slots, collective):
+def send_rows(slots, act):
     chips, capacity, depth = slots.shape
+    rows, hidden_units = act.shape
+    block = 2 * capacity
+    width = min(256, depth // 2)
     any_space = pl.BlockSpec(memory_space=pl.ANY)
+    bf = jnp.bfloat16
     dma = pltpu.SemaphoreType.DMA
     return pl.pallas_call(
         send_rows_body,
-        in_specs=[any_space],
-        out_specs=any_space,
-        out_shape=jax.ShapeDtypeStruct((chips, 2 * capacity, depth), jnp.bfloat16),
-        scratch_shapes=[dma((1,)), dma((8,)), dma((8,)), dma((8,)), dma((8,))],
-        compiler_params=pltpu.CompilerParams(collective_id=collective, has_side_effects=True),
+        in_specs=[any_space] * 2,
+        out_specs=[any_space] * 2,
+        out_shape=[
+            jax.ShapeDtypeStruct((chips, block, depth), bf),
+            jax.ShapeDtypeStruct((depth, hidden_units), bf),
+        ],
+        scratch_shapes=[
+            pltpu.VMEM((chips, block, depth), bf),
+            pltpu.VMEM((2, 2 * block, hidden_units), bf),
+            pltpu.VMEM((depth, hidden_units), jnp.float32),
+            pltpu.VMEM((2, width, hidden_units), bf),
+            dma((4,)),
+            dma((4,)),
+            dma((2,)),
+            dma((1,)),
+            dma((8,)),
+            dma((8,)),
+            dma((8,)),
+            dma((8,)),
+        ],
+        compiler_params=pltpu.CompilerParams(
+            collective_id=2, has_side_effects=True, vmem_limit_bytes=VMEM_BYTES
+        ),
         name="send_rows",
-    )(slots)
+    )(slots, act)
 
 
 def ffn_backward_body(
@@ -1744,9 +1836,7 @@
         *att_outs, att_rows, att_back, lse = attention_send(
             *query_sets, keys_all, values_all, o_weight, key_info, query_info, att_capacity
         )
-        att_elsewhere = [
-            lax.ppermute(att_rows, "dp", [(i, i ^ n) for i in range(replicas)]) for n in range(1, replicas)
-        ]
+        att_everywhere = lax.all_gather(att_rows, "dp", axis=0, tiled=True)
     else:
         *att_outs, lse = attention_forward(
             query_sets, starts // 2, keys_all, values_all, key_info, query_info, heads
@@ -1810,11 +1900,12 @@
     ffn_gate_grad, ffn_scaled = pair_grads(ffn_gates, ffn_branches, grad_result)
     ffn_grad_slots = fill_slots(ffn_picks, ffn_scaled)
     if fused:
-        ffn_grad_slots, att_elsewhere = lax.optimization_barrier((ffn_grad_slots, att_elsewhere))
-        grad_ffn_out = send_rows(ffn_grad_slots, 2).reshape(-1, D)
+        ffn_grad_slots, att_everywhere = lax.optimization_barrier((ffn_grad_slots, att_everywhere))
+        grad_ffn_out, grad_down = send_rows(ffn_grad_slots, activated)
+        grad_ffn_out = grad_ffn_out.reshape(-1, D)
     else:
         grad_ffn_out = to_experts(ffn_grad_slots)
-    grad_down = dot_tn(grad_ffn_out, activated).astype(bf16)
+        grad_down = dot_tn(grad_ffn_out, activated).astype(bf16)
     grad_ffn_out, grad_down = lax.optimization_barrier((grad_ffn_out, grad_down))
     summed_down = lax.psum_scatter(grad_down, "dp", scatter_dimension=0, tiled=True)
     if fused:
@@ -1876,7 +1967,6 @@
     else:
         grad_o = dot_tn(grad_att_out, att_rows).astype(bf16)
         summed_o = lax.psum_scatter(grad_o, "dp", scatter_dimension=0, tiled=True).astype(f32)
-    grad_sets[-1], summed_gate = lax.optimization_barrier((grad_sets[-1], summed_gate))
     *grad_queries, grad_keys_values = attention_backward(
         query_sets,
         starts,
@@ -1891,6 +1981,7 @@
         [tables[1] for tables in slot_tables],
         heads,
     )
+    grad_keys_values, summed_gate = lax.optimization_barrier((grad_keys_values, summed_gate))
     grad_query_pre = join_halves(*grad_queries) if att_copies == 1 else grad_queries[0]
     grad_kv = dot_tn(hidden_all.reshape(token_count, D), grad_keys_values).astype(bf16)
     grad_q = dot_tn(query_inputs, grad_query_pre).astype(bf16)
@@ -1912,8 +2003,12 @@
     if fused:
         arrived = merge_return(*merge_args)
         arrived, grad_columns, summed_kv = lax.optimization_barrier((arrived, grad_columns, summed_kv))
-        summed_o = sum(
-            dot_tn(grad, rows) for grad, rows in zip(grad_columns, [att_rows] + att_elsewhere)
+        column_stack = jnp.stack(grad_columns)
+        summed_o = dot_tn(
+            jnp.concatenate(
+                [lax.dynamic_index_in_dim(column_stack, my_replica ^ n, 0, False) for n in range(replicas)]
+            ),
+            att_everywhere,
         )
     else:
         merged = merge_hidden_grads(*merge_args, block_order).reshape(devices // 2, 2, row_count, D)
@@ -1936,6 +2031,7 @@
     everyone = devices * replicas
     smalls = [grad_gain_one, grad_gain_two, grad_att_router, grad_ffn_router]
     packed = jnp.concatenate([small.reshape(everyone, -1) for small in smalls], axis=1)
+    packed, summed_o = lax.optimization_barrier((packed, summed_o))
     own_smalls = jnp.sum(
         lax.all_to_all(packed, ("dp", "expert"), split_axis=0, concat_axis=0, tiled=True), axis=0
     )

time: 1170 us -> 1140 us (0.974)
  matrix products: 162 us -> 132 us
  Pallas kernels: 672 us -> 685 us
    reduce_scatter x1, waiting for transfers between devices: 34.2 us -> 0.02 us  [body(): lax.psum_scatter(grad_gate, 'dp', scatter_dimension=0, tiled=True)]
    dot_general x8 -> x4, matrix products: 104 us -> 74.2 us  [dot_tn(): lax.dot_general(left, right, (((0,), (0,)), ((), ())), preferred_element_...]
    reduce_scatter x1, waiting for transfers between devices: 0.01 us -> 15.6 us  [body(): summed_up = lax.psum_scatter(grad_up, 'dp', scatter_dimension=0, tiled=True)]
    pallas_call x1, Pallas kernels: 71.6 us -> 85.4 us  [send_rows(): pl.pallas_call(send_rows_body, in_specs=[any_space] * 2, out_specs=[any_s...]
  transfers between devices with their start and end apart: 21 -> 19, of which waited for: 7 -> 10; matrix products, arithmetic and copies ran while one was open for 18% -> 19% of each run, Pallas kernels for 42% -> 43%
where the time goes in v6:
time: 1140 us; the launch traced here: 1130 us
  Pallas kernels  685 us (60%)
  waiting for transfers between devices  139 us (12%)
  matrix products  132 us (12%)
  other arithmetic  64.6 us (6%)
  blocking collectives  46.8 us (4%)
  local copies, waits for them, and re-layouts  33.4 us (3%)
  starting transfers between devices  16.9 us (1%)
  between operations  16.2 us (1%)
    pallas_call x1, Pallas kernels, ffn_forward(): pl.pallas_call(functools.partial(ffn_forward_body, chunk), in_specs=[any_...  143 us
    pallas_call x1, Pallas kernels, attention_send(): pl.pallas_call(functools.partial(attention_send_body, HEAD ** (-0.5) * LO...  94.3 us
    pallas_call x1, Pallas kernels, merge_return(): pl.pallas_call(functools.partial(merge_return_body, 'dp'), in_specs=[any_...  90 us
    pallas_call x1, Pallas kernels, ffn_backward(): pl.pallas_call(functools.partial(ffn_backward_body, chunk), in_specs=[any...  88.3 us
    pallas_call x1, Pallas kernels, send_rows(): pl.pallas_call(send_rows_body, in_specs=[any_space] * 2, out_specs=[any_s...  85.4 us
    pallas_call x1, Pallas kernels, attention_backward(): pl.pallas_call(functools.partial(attention_backward_body, sets, step_head...  83.3 us
    dot_general x4, matrix products, dot_tn(): lax.dot_general(left, right, (((0,), (0,)), ((), ())), preferred_element_...  74.2 us
    pallas_call x1, Pallas kernels, send_slots(): pl.pallas_call(send_slots_body, in_specs=[any_space] * 3, out_specs=[any_...  58.7 us
  transfers between devices with their start and end apart: 19, of which 10 were waited for; matrix products, arithmetic and copies ran while one was open for 19% of the time, Pallas kernels for 43%

profile of v6, /device:TPU:0, one launch (start us, length us, event | category | flops | bytes accessed | tf_op | source)
XLA Modules:
  0.0 1133.7 jit_solution(9415034302727240534)
XLA Ops:
  7.2 3.3 copy.62
  13.4 48.2 %all-gather.7.cloned.1.call-done = bf16[8,256,1024]{2,1,0:T(8,128)(2,1)} async-done(((bf16[1,256,1024]{2,1,0:T(8,128)(2,1)}), bf16[8,256,1024]{2,1,0:T(8,128)(2,1)}) %all-gather.7.cloned.1.call-update) | async-done | bytes 4194320 | tf_op jit(solution)/shard_map/all_gather | solution.py:1777
  67.4 5.7 fusion.45
  81.5 3.4 fusion.154
  84.8 14.2 %all-gather.2 = s32[8,272,2]{1,2,0:T(2,128)S(1)} all-gather(s32[1,272,2]{1,2,0:T(2,128)S(1)} %bitcast.230), channel_id=3, replica_groups=mesh['dp'=4,'expert'=8] {'expert'}, dimensions={0}, use_global_device_ids=true | all-gather | bytes 19584 | tf_op jit(solution)/shard_map/all_gather | solution.py:1783
  102.7 20.0 %collective-permute-done.1 = bf16[2048,512]{1,0:T(8,128)(2,1)} collective-permute-done((bf16[2048,512]{1,0:T(8,128)(2,1)S(1)}, bf16[2048,512]{1,0:T(8,128)(2,1)}, u32[]{:S(2)}, u32[]{:S(2)}) %collective-permute-start.1) | collective-permute-done | bytes 2097184 | tf_op jit(solution)/shard_map/ppermute | solution.py:1725
  129.1 2.6 multiply_cosine_fusion.1
  136.9 11.6 %collective-permute-done.2 = bf16[1024,512]{1,0:T(8,128)(2,1)S(1)} collective-permute-done((bf16[1024,512]{1,0:T(8,128)(2,1)S(1)}, bf16[1024,512]{1,0:T(8,128)(2,1)S(1)}, u32[]{:S(2)}, u32[]{:S(2)}) %collective-permute-start.2) | collective-permute-done | bytes 1048608 | tf_op jit(solution)/shard_map/ppermute | solution.py:1727
  148.5 2.6 collective-permute-done.3
  151.2 6.1 pad_maximum_fusion.weight_ref.weight_hbm
  159.5 15.1 %project_queries.1 = (bf16[704,2048]{1,0:T(8,128)(2,1)}, bf16[704,2048]{1,0:T(8,128)(2,1)}) custom-call(bf16[8,88,272]{2,1,0:T(8,128)(2,1)} %copy.68.plan_ref, bf16[8,272,2048]{2,1,0:T(8,128)(2,1)} %bitcast.208, bf16[2048,2048]{1,0:T(8,128)(2,1)} %weight_ref.1, f32[704,128]{1,0:T(8,128)} %pad_maximum_fusion.5.cos_ref.refs_13_, ...), custom_call_target="tpu_custom_call" | custom-call | tf_op jit(solution)/shard_map/project_queries/pallas_call | solution.py:292
  174.5 2.6 constant_dynamic-slice_fusion.5
  177.6 26.5 %project_keys_values.1 = (bf16[2176,1024]{1,0:T(8,128)(2,1)}, bf16[2176,1024]{1,0:T(8,128)(2,1)}) custom-call(s32[4]{0:T(128)} %iota_xor_fusion.order_ref, bf16[8,272,2048]{2,1,0:T(8,128)(2,1)} %bitcast.209, bf16[4,2048,512]{2,1,0:T(8,128)(2,1)} %pad_maximum_fusion.weight_ref.weight_hbm, f32[2176,128]{1,0:T(8,128)} %pad_maximum_fusion.2.cos_ref.refs_11_, ...), custom_call_target="tpu_custom_call" | custom-call | tf_op jit(solution)/shard_map/project_keys_values/pallas_call | solution.py:330
  205.3 94.3 %attention_send.1 = (bf16[704,1024]{1,0:T(8,128)(2,1)}, bf16[704,1024]{1,0:T(8,128)(2,1)}, bf16[704,2048]{1,0:T(8,128)(2,1)}, bf16[8,88,2048]{2,1,0:T(8,128)(2,1)}, f32[8,4,1,352]{3,2,1,0:T(1,128)}) custom-call(bf16[704,2048]{1,0:T(8,128)(2,1)} %get-tuple-element.90.query_hbm.refs_0_, bf16[704,1024]{1,0:T(8,128)(2,1)} %copy-done.12, ...), custom_call_target="tpu_custom_call" | custom-call | tf_op jit(solution)/shard_map/attention_send/pallas_call | solution.py:1553
  301.7 3.8 convolution_bitcast_fusion.2
  309.5 3.3 convolution_convert_fusion.5.slots
  312.8 143.2 %ffn_forward.1 = (bf16[1408,2048]{1,0:T(8,128)(2,1)}, bf16[1408,2816]{1,0:T(8,128)(2,1)}, bf16[1408,2816]{1,0:T(8,128)(2,1)}, bf16[1408,2816]{1,0:T(8,128)(2,1)}, bf16[4,176,2048]{2,1,0:T(8,128)(2,1)}) custom-call(bf16[4,176,2048]{2,1,0:T(8,128)(2,1)} %convolution_convert_fusion.5.slots, bf16[2048,2816]{1,0:T(8,128)(2,1)} %gate_hbm.3, ...), custom_call_target="tpu_custom_call" | custom-call | tf_op jit(solution)/shard_map/ffn_forward/pallas_call | solution.py:795
  456.1 3.9 convolution_bitcast_fusion.1
  463.6 4.0 bitcast_convert_fusion.1.slots
  467.6 85.4 %send_rows.1 = (bf16[4,352,2048]{2,1,0:T(8,128)(2,1)}, bf16[2048,2816]{1,0:T(8,128)(2,1)}) custom-call(bf16[4,176,2048]{2,1,0:T(8,128)(2,1)} %bitcast_convert_fusion.1.slots, bf16[1408,2816]{1,0:T(8,128)(2,1)} %get-tuple-element.103.act_hbm), custom_call_target="tpu_custom_call" | custom-call | tf_op jit(solution)/shard_map/send_rows/pallas_call | solution.py:930
  553.1 88.3 %ffn_backward.1 = (bf16[1408,2816]{1,0:T(8,128)(2,1)}, bf16[1408,2816]{1,0:T(8,128)(2,1)}, bf16[4,176,2048]{2,1,0:T(8,128)(2,1)}) custom-call(bf16[1408,2048]{1,0:T(8,128)(2,1)} %bitcast.215, bf16[1408,2816]{1,0:T(8,128)(2,1)} %get-tuple-element.107.gate_in, bf16[1408,2816]{1,0:T(8,128)(2,1)} %get-tuple-element.108.up_in, bf16[2048,2816]{1,0:T(8,128)(2,1)} %gate_hbm.3, ...), custom_call_target="tpu_custom_call" | custom-call | tf_op jit(solution)/shard_map/ffn_backward/pallas_call | solution.py:1112
  641.4 24.6 %convolution_convert_fusion = bf16[2048,2816]{1,0:T(8,128)(2,1)} fusion(bf16[1408,2048]{1,0:T(8,128)(2,1)} %get-tuple-element.110.rows_hbm, bf16[1408,2816]{1,0:T(8,128)(2,1)} %get-tuple-element.111), kind=kOutput, calls=%fused_computation | convolution fusion | flops 16246112256 | bytes 25231360 | tf_op jit(solution)/shard_map/dot_general | solution.py:1733
  666.2 3.9 convolution_bitcast_fusion
  670.1 2.9 multiply_reduce_fusion
  676.1 4.0 bitcast_convert_fusion.slots
  680.1 58.7 %send_slots.1 = (bf16[8,88,2048]{2,1,0:T(8,128)(2,1)}, bf16[2048,2816]{1,0:T(8,128)(2,1)}) custom-call(bf16[8,88,2048]{2,1,0:T(8,128)(2,1)} %bitcast_convert_fusion.slots, bf16[1408,2048]{1,0:T(8,128)(2,1)} %get-tuple-element.110.rows_hbm, bf16[1408,2816]{1,0:T(8,128)(2,1)} %get-tuple-element.115.grads_hbm), custom_call_target="tpu_custom_call" | custom-call | tf_op jit(solution)/shard_map/send_slots/pallas_call | solution.py:1207
  738.9 9.4 convolution_convert_fusion.4.refs_2_
  752.2 2.6 collective-permute-done.5.refs_3_
  754.8 83.3 %attention_backward.1 = (bf16[704,1024]{1,0:T(8,128)(2,1)}, bf16[704,1024]{1,0:T(8,128)(2,1)}, bf16[2176,2048]{1,0:T(8,128)(2,1)}) custom-call(s32[2]{0:T(128)} %pad_add_fusion.1.first_ref, bf16[704,2048]{1,0:T(8,128)(2,1)} %get-tuple-element.90.query_hbm.refs_0_, bf16[704,1024]{1,0:T(8,128)(2,1)} %copy-done.12, bf16[704,2048]{1,0:T(8,128)(2,1)} %copy-done.11, ...), custom_call_target="tpu_custom_call" | custom-call | tf_op jit(solution)/shard_map/attention_backward/pallas_call | solution.py:221
  838.2 26.4 %convolution_convert_fusion.2 = bf16[2048,2048]{1,0:T(8,128)(2,1)} fusion(bf16[2176,2048]{1,0:T(8,128)(2,1)} %all-gather.11.cloned.1.call-done, bf16[2176,2048]{1,0:T(8,128)(2,1)} %get-tuple-element.131.grads_hbm), kind=kOutput, calls=%fused_computation.4 | convolution fusion | flops 18257805312 | bytes 26214400 | tf_op jit(solution)/shard_map/dot_general | solution.py:1733
  865.5 3.2 collective-permute-done.6
  868.7 12.4 %convolution_convert_fusion.1 = bf16[2048,2048]{1,0:T(8,128)(2,1)} fusion(bf16[704,2048]{1,0:T(8,128)(2,1)S(1)} %copy-done.40, bf16[704,1024]{1,0:T(8,128)(2,1)} %collective-permute-done.6, bf16[704,1024]{1,0:T(8,128)(2,1)} %get-tuple-element.127, pred[]{:T(512)S(6)} %eq.225), kind=kOutput, calls=%fused_computation.3 | convolution fusion | flops 5922750464 | bytes 14155777 | tf_op jit(solution)/shard_map/dot_general | solution.py:1733
  887.3 3.3 constant_dynamic-slice_fusion
  894.0 11.9 %convolution_convert_fusion.3 = bf16[704,2048]{1,0:T(8,128)(2,1)} fusion(bf16[2048,2048]{1,0:T(8,128)(2,1)} %weight_ref.1, bf16[704,1024]{1,0:T(8,128)(2,1)} %collective-permute-done.6, bf16[704,1024]{1,0:T(8,128)(2,1)S(1)} %copy-done.41, pred[]{:T(512)S(6)} %eq.225), kind=kOutput, calls=%fused_computation.18 | convolution fusion | flops 5919997952 | bytes 14155777 | tf_op jit(solution)/shard_map/dot_general | solution.py:1990
  906.0 15.6 %reduce-scatter.10.cloned.1.call-done = bf16[512,2816]{1,0:T(8,128)(2,1)} async-done(((bf16[2048,2816]{1,0:T(8,128)(2,1)}), bf16[512,2816]{1,0:T(8,128)(2,1)}) %reduce-scatter.10.cloned.1.call-update) | async-done | bytes 2883600 | tf_op jit(solution)/shard_map/reduce_scatter | solution.py:1951
  921.5 90.0 %merge_return.1 = bf16[4,272,2048]{2,1,0:T(8,128)(2,1)} custom-call(bf16[8,272,88]{2,1,0:T(8,128)(2,1)} %bitcast.216, bf16[8,88,2048]{2,1,0:T(8,128)(2,1)} %bitcast.218, bf16[2176,2048]{1,0:T(8,128)(2,1)} %get-tuple-element.131.grads_hbm, bf16[4,2048,512]{2,1,0:T(8,128)(2,1)} %pad_maximum_fusion.weight_ref.weight_hbm), custom_call_target="tpu_custom_call" | custom-call | tf_op jit(solution)/shard_map/merge_return/pallas_call | solution.py:1321
  1011.6 4.9 reduce-scatter.12.cloned.1.call-done
  1016.6 3.5 convert_reduce_fusion
  1020.1 3.2 fusion.21
  1026.4 10.8 fusion.4
  1037.3 32.6 %all_to_all.14 = f32[32,1,896]{2,1,0:T(1,128)S(1)} all-to-all(f32[32,1,896]{2,1,0:T(1,128)S(1)} %copy.71), channel_id=1, replica_groups=mesh['dp'=4,'expert'=8] {'dp','expert'}, dimensions={0} | all-to-all | bytes 229376 | tf_op jit(solution)/shard_map/all_to_all | solution.py:2036
  1069.9 4.4 all-to-all-start.1
  1074.2 4.9 convert_element_type.156
  1079.1 3.0 convert_element_type.154
  1082.2 25.4 %reduce-scatter.14.cloned.1.call-done = bf16[512,2048]{1,0:T(8,128)(2,1)} async-done(((bf16[2048,2048]{1,0:T(8,128)(2,1)}), bf16[512,2048]{1,0:T(8,128)(2,1)}) %reduce-scatter.14.cloned.1.call-update) | async-done | bytes 2097168 | tf_op jit(solution)/shard_map/reduce_scatter | solution.py:1989
  1107.6 4.3 convert_element_type.153
  1111.9 2.9 convert_element_type.155
  1118.7 4.6 all-to-all-done.1
  (238 shorter events, 72.6 us)
Async XLA Ops:
  7.2 54.7 %copy-start = (f32[2048,8]{0,1:T(8,128)S(1)}, f32[2048,8]{0,1:T(8,128)}, u32[]{:S(2)}) copy-start(f32[2048,8]{0,1:T(8,128)} %param.24) | copy-start | bytes 196612
  7.2 54.5 %all-gather.7.cloned.1.call-start = ((), (), s32[]{:S(2)}) async-start(), calls=%async_computation.7 | async-start | bytes 4718592 | tf_op jit(solution)/shard_map/all_gather | solution.py:1777
  11.7 50.1 %copy-start.35 = (s32[272,2]{0,1:T(2,128)S(1)}, s32[272,2]{0,1:T(2,128)}, u32[]{:S(2)}) copy-start(s32[272,2]{0,1:T(2,128)} %param.18) | copy-start | bytes 6532
  11.7 145.7 %all-gather.11.cloned.1.call-start = ((), (), s32[]{:S(2)}) async-start(), calls=%async_computation.14 | async-start | bytes 10027008 | tf_op jit(solution)/shard_map/all_gather | solution.py:1779
  12.1 49.7 %copy-start.31 = (f32[272]{0:T(512)}, f32[272]{0:T(512)S(1)}, u32[]{:S(2)}) copy-start(f32[272]{0:T(512)S(1)} %add_rsqrt_fusion.1) | copy-start | bytes 3268
  12.1 52.1 %copy-start.38 = (s32[272,2]{0,1:T(2,128)S(1)}, s32[272,2]{0,1:T(2,128)}, u32[]{:S(2)}) copy-start(s32[272,2]{0,1:T(2,128)} %param.19) | copy-start | bytes 6532
  61.7 405.9 %all-gather.9.cloned.1.call-start = ((), (), s32[]{:S(2)}) async-start(), calls=%async_computation.8 | async-start | bytes 14417920 | tf_op jit(solution)/shard_map/all_gather | solution.py:1839
  61.8 5.6 copy-start.24
  67.4 7.1 copy-start.19
  74.7 47.9 %collective-permute-start.1 = (bf16[2048,512]{1,0:T(8,128)(2,1)S(1)}, bf16[2048,512]{1,0:T(8,128)(2,1)}, u32[]{:S(2)}, u32[]{:S(2)}) collective-permute-start(bf16[2048,512]{1,0:T(8,128)(2,1)S(1)} %bitcast.212), channel_id=1, source_target_pairs={{0,16},{8,24},{16,0},{24,8},{1,17},{9,25},{17,1},{25,9},{2,18},{10... | collective-permute-start | bytes 6291464 | tf_op jit(solution)/shard_map/ppermute | solution.py:1725
  76.3 49.2 %collective-permute-start = (bf16[2048,512]{1,0:T(8,128)(2,1)S(1)}, bf16[2048,512]{1,0:T(8,128)(2,1)}, u32[]{:S(2)}, u32[]{:S(2)}) collective-permute-start(bf16[2048,512]{1,0:T(8,128)(2,1)S(1)} %bitcast.213), channel_id=1, source_target_pairs={{0,8},{8,0},{16,24},{24,16},{1,9},{9,1},{17,25},{25,17},{2,10},{10... | collective-permute-start | bytes 6291464 | tf_op jit(solution)/shard_map/ppermute | solution.py:1725
  77.8 223.9 %copy-start.29 = (f32[272,2]{0,1:T(2,128)}, f32[272,2]{0,1:T(2,128)S(1)}, u32[]{:S(2)}) copy-start(f32[272,2]{0,1:T(2,128)S(1)} %broadcast_divide_fusion.1) | copy-start | bytes 6532
  81.5 20.5 %copy-start.37 = (s32[1,13]{1,0:T(1,128)S(1)}, s32[1,13]{1,0:T(1,128)}, u32[]{:S(2)}) copy-start(s32[1,13]{1,0:T(1,128)} %param.20) | copy-start | bytes 160
  124.0 24.5 %collective-permute-start.2 = (bf16[1024,512]{1,0:T(8,128)(2,1)S(1)}, bf16[1024,512]{1,0:T(8,128)(2,1)S(1)}, u32[]{:S(2)}, u32[]{:S(2)}) collective-permute-start(bf16[1024,512]{1,0:T(8,128)(2,1)S(1)} %slice.148), channel_id=1, source_target_pairs={{0,8},{8,0},{16,24},{24,16},{1,9},{9,1},{17,25},{25,17},{2,10},{10... | collective-permute-start | bytes 3145736 | tf_op jit(solution)/shard_map/ppermute | solution.py:1727
  126.9 24.2 %collective-permute-start.3 = (bf16[1024,512]{1,0:T(8,128)(2,1)S(1)}, bf16[1024,512]{1,0:T(8,128)(2,1)S(1)}, u32[]{:S(2)}, u32[]{:S(2)}) collective-permute-start(bf16[1024,512]{1,0:T(8,128)(2,1)S(1)} %slice.149), channel_id=1, source_target_pairs={{0,16},{8,24},{16,0},{24,8},{1,17},{9,25},{17,1},{25,9},{2,18},{10... | collective-permute-start | bytes 3145736 | tf_op jit(solution)/shard_map/ppermute | solution.py:1727
  177.1 27.0 %collective-permute-start.4 = (bf16[704,1024]{1,0:T(8,128)(2,1)}, bf16[704,1024]{1,0:T(8,128)(2,1)S(1)}, u32[]{:S(2)}, u32[]{:S(2)}) collective-permute-start(bf16[704,1024]{1,0:T(8,128)(2,1)} %constant_dynamic-slice_fusion.5), channel_id=1, source_target_pairs={{0,1},{1,0},{2,3},{3,2},{4,5},{5,4},{6,7},{7,6},{8,9},{9,8},{10,11... | collective-permute-start | bytes 4325384 | tf_op jit(solution)/shard_map/ppermute | solution.py:1816
  299.6 380.5 %reduce-scatter.6.cloned.1.call-start = ((), (), s32[]{:S(2)}) async-start(), calls=%async_computation.9 | async-start | bytes 14417920 | tf_op jit(solution)/shard_map/reduce_scatter | solution.py:1910
  456.1 3.9 copy-start.15
  553.0 285.2 %reduce-scatter.8.cloned.1.call-start = ((), (), s32[]{:S(2)}) async-start(), calls=%async_computation.10 | async-start | bytes 14417920 | tf_op jit(solution)/shard_map/reduce_scatter | solution.py:1931
  666.0 255.5 %reduce-scatter.10.cloned.1.call-start = ((), (), s32[]{:S(2)}) async-start(), calls=%async_computation.11 | async-start | bytes 14417920 | tf_op jit(solution)/shard_map/reduce_scatter | solution.py:1951
  666.1 6.9 slice-start
  666.2 6.9 slice-start.1
  738.9 277.7 %reduce-scatter.12.cloned.1.call-start = ((), (), s32[]{:S(2)}) async-start(), calls=%async_computation.12 | async-start | bytes 10485760 | tf_op jit(solution)/shard_map/reduce_scatter | solution.py:1988
  748.4 6.5 copy-start.11
  749.8 5.0 collective-permute-start.5
  864.6 4.1 copy-start.40
  864.6 243.0 %reduce-scatter.14.cloned.1.call-start = ((), (), s32[]{:S(2)}) async-start(), calls=%async_computation.13 | async-start | bytes 10485760 | tf_op jit(solution)/shard_map/reduce_scatter | solution.py:1989
  864.7 4.1 collective-permute-start.6
  881.2 3.7 copy-start.30
  881.2 3.8 copy-start.8
  881.2 3.8 copy-start.25
  884.9 5.6 copy-start.33
  887.3 6.8 copy-start.41
  890.5 121.0 %collective-permute-start.9 = (bf16[704,512]{1,0:T(8,128)(2,1)}, bf16[704,512]{1,0:T(8,128)(2,1)S(1)}, u32[]{:S(2)}, u32[]{:S(2)}) collective-permute-start(bf16[704,512]{1,0:T(8,128)(2,1)} %get-tuple-element.237), channel_id=1, source_target_pairs={{0,24},{8,16},{16,8},{24,0},{1,25},{9,17},{17,9},{25,1},{2,26},{10... | collective-permute-start | bytes 2162696 | tf_op jit(solution)/shard_map/ppermute | solution.py:1964
  892.1 119.5 %collective-permute-start.8 = (bf16[704,512]{1,0:T(8,128)(2,1)}, bf16[704,512]{1,0:T(8,128)(2,1)S(1)}, u32[]{:S(2)}, u32[]{:S(2)}) collective-permute-start(bf16[704,512]{1,0:T(8,128)(2,1)} %get-tuple-element.238), channel_id=1, source_target_pairs={{0,16},{8,24},{16,0},{24,8},{1,17},{9,25},{17,1},{25,9},{2,18},{10... | collective-permute-start | bytes 2162696 | tf_op jit(solution)/shard_map/ppermute | solution.py:1964
  892.2 119.3 %collective-permute-start.7 = (bf16[704,512]{1,0:T(8,128)(2,1)S(1)}, bf16[704,512]{1,0:T(8,128)(2,1)S(1)}, u32[]{:S(2)}, u32[]{:S(2)}) collective-permute-start(bf16[704,512]{1,0:T(8,128)(2,1)S(1)} %get-tuple-element.239), channel_id=1, source_target_pairs={{0,8},{8,0},{16,24},{24,16},{1,9},{9,1},{17,25},{25,17},{2,10},{10... | collective-permute-start | bytes 2162696 | tf_op jit(solution)/shard_map/ppermute | solution.py:1964
  1011.6 5.0 copy-start.20
  1011.6 5.0 copy-start.21
  1011.6 5.0 copy-start.22
  1016.6 3.5 copy-start.2
  1016.6 3.5 copy-start.28
  1016.6 3.5 copy-start.32
  1016.6 3.5 copy-start.34
  1069.9 53.4 %all-to-all-start.1 = ((bf16[8,64,2048]{2,1,0:T(8,128)(2,1)}), bf16[8,64,2048]{2,1,0:T(8,128)(2,1)}, u32[]{:S(2)}, u32[]{:S(2)}) async-start(bf16[8,64,2048]{2,1,0:T(8,128)(2,1)} %bitcast.222), calls=%async_computation.5 | async-start | bytes 4194304 | tf_op jit(solution)/shard_map/all_to_all | solution.py:1701
  1074.2 4.9 copy-start.13
  1107.6 4.3 copy-start.14
  1111.9 2.9 copy-start.36
  1111.9 3.0 copy-start.6
  (15 other events, 23.6 us)
Sparse Core Ops, SparseCore 0:
  11.8 49.8 all-gather.6
  63.9 85.2 all-gather.10
  299.8 128.3 all-gather.8
  553.1 110.7 reduce-scatter.5
  666.8 119.4 reduce-scatter.7
  789.3 132.1 reduce-scatter.9
  924.6 91.9 reduce-scatter.11
  1019.9 87.6 reduce-scatter.13

commit v7 on v6

--- a/solution.py
+++ b/solution.py
@@ -445,6 +445,7 @@
 class Dispatch:
     def __init__(self, me, order, slots, landing, local_sem, send, recv, pass_send, pass_recv):
         self.me, self.chip, self.core, self.order = me, me // 2, lax.rem(me, 2), order
+        self.sending = stagger_order if order is stagger_order else chip_order
         self.slots, self.landing = slots, landing
         self.local_sem, self.send, self.recv = local_sem, send, recv
         self.pass_send, self.pass_recv = pass_send, pass_recv
@@ -469,7 +470,7 @@
         )
 
     def sends(self, step):
-        chip = chip_order(self.chip, step)
+        chip = self.sending(self.chip, step)
         targets = [2 * chip, 2 * chip + 1] if step else [self.me + 1 - 2 * self.core]
         return [self.direct(target) for target in targets]
 
@@ -835,6 +836,13 @@
     )(slots, gate_weight, up_weight, down_weight)
 
 
+def stagger_order(chip, step):
+    if step < 2:
+        return chip_order(chip, step)
+    end, middle = chip_order(chip, 5 - step), chip_order(chip, step)
+    return end + is_middle(chip) * (middle - end)
+
+
 def send_rows_body(
     slots,
     act_hbm,
@@ -855,25 +863,23 @@
 ):
     me = lax.axis_index("expert")
     enter(8, me)
-    dispatch = Dispatch(me, chip_order, slots, landing, local_sem.at[0], send, recv, pass_send, pass_recv)
+    dispatch = Dispatch(me, stagger_order, slots, landing, local_sem.at[0], send, recv, pass_send, pass_recv)
     dispatch.start_local()
-    dispatch.start((0, 1, 2, 3))
+    dispatch.start((0, 1, 2))
     block = landing.shape[1]
     width = stage.shape[1]
     parts = landing.shape[2] // width
 
     def span_of(step):
-        return pl.ds(pl.multiple_of(chip_order(me // 2, step) * block, 16), block)
+        return pl.ds(pl.multiple_of(stagger_order(me // 2, step) * block, 16), block)
 
     def act_copy(step):
         return pltpu.make_async_copy(
-            act_hbm.at[span_of(step), :],
-            act.at[step // 2, pl.ds(step % 2 * block, block), :],
-            act_sem.at[step],
+            act_hbm.at[span_of(step), :], act.at[pl.ds(step * block, block), :], act_sem.at[step]
         )
 
     def rows_copy(step):
-        chip = chip_order(me // 2, step)
+        chip = stagger_order(me // 2, step)
         return pltpu.make_async_copy(landing.at[chip], rows_out.at[chip], rows_sem.at[step])
 
     def stage_copy(part):
@@ -883,8 +889,7 @@
 
     for step in range(4):
         act_copy(step).start()
-    for pair in range(2):
-        steps = (2 * pair, 2 * pair + 1)
+    for steps in ((0, 1), (2,), (3,)):
         for step in steps:
             dispatch.arrive(step)
         chips = [dispatch.ready(step) for step in steps]
@@ -892,14 +897,24 @@
             rows_copy(step).start()
             act_copy(step).wait()
 
-        def one(part, carry, pair=pair, chips=chips):
+        def one(part, carry, steps=steps, chips=chips):
             columns = pl.ds(pl.multiple_of(part * width, 128), width)
-            rows = jnp.concatenate([landing[chip, :, columns] for chip in chips], axis=0)
+            rows = [landing[chip, :, columns] for chip in chips]
+            rows = rows[0] if len(rows) == 1 else jnp.concatenate(rows, axis=0)
             turned = rows.astype(jnp.float32).T.astype(jnp.bfloat16)
-            product = dot_nn(turned, act[pair])
+            product = dot_nn(turned, act[pl.ds(steps[0] * block, len(steps) * block), :])
             span = pl.ds(pl.multiple_of(part * width, 16), width)
-            if pair == 0:
+            if steps[0] == 0:
                 total[span, :] = product
+
+                @pl.when(part == 0)
+                def _():
+                    dispatch.sent((2,))
+                    dispatch.start((3,))
+
+                return carry
+            if steps[0] == 2:
+                total[span, :] += product
                 return carry
 
             @pl.when(part >= 2)
@@ -915,7 +930,7 @@
         stage_copy(part).wait()
     for step in range(4):
         rows_copy(step).wait()
-    dispatch.sent((0, 1, 2, 3))
+    dispatch.sent((0, 1, 3))
     dispatch.passed_on()
 
 
@@ -937,7 +952,7 @@
         ],
         scratch_shapes=[
             pltpu.VMEM((chips, block, depth), bf),
-            pltpu.VMEM((2, 2 * block, hidden_units), bf),
+            pltpu.VMEM((rows, hidden_units), bf),
             pltpu.VMEM((depth, hidden_units), jnp.float32),
             pltpu.VMEM((2, width, hidden_units), bf),
             dma((4,)),
@@ -1344,6 +1359,11 @@
         ),
         name="merge_return",
     )(plan, slots, grads, weights)
+
+
+def return_order(chip, step):
+    lower, upper = chip_order(chip, (2, 3, 1, 0)[step]), chip_order(chip, 3 - step)
+    return lower + chip // 2 * (upper - lower)
 
 
 def attention_send_body(
@@ -1421,7 +1441,7 @@
         load.wait()
 
     def group_of(step):
-        return chip_order(chip, 3 - step)
+        return return_order(chip, step)
 
     def span_of(step):
         return pl.ds(pl.multiple_of(group_of(step) * rows, 16), rows)
@@ -1525,11 +1545,13 @@
 
     for step in range(4):
         attend(step)
-        if step == 1:
+        if step == 0:
             loads[4].wait()
-        if step > 0:
-            settle(step - 1)
-    settle(3)
+        if step < 2:
+            settle(step)
+        elif step == 3:
+            settle(2)
+            settle(3)
     for step in range(4):
         swap(step).wait_send()
         own_copy(step).wait()
@@ -1775,12 +1797,8 @@
         kv_share.reshape(weight_rows, 2, 2, piece).transpose(0, 2, 1, 3).reshape(weight_rows, 4 * piece)
     )
     kv_gathered = lax.all_gather(kv_share, "expert", axis=0)
-    kv_gathered, hidden_sent = lax.optimization_barrier((kv_gathered, hidden))
-    hidden_all = lax.all_gather(hidden_sent, "expert", axis=0)
-    kv_half = lax.dynamic_slice_in_dim(kv_gathered, core * 2 * piece, 2 * piece, 2).reshape(D, 2 * piece)
-    kv_half, routes_sent = lax.optimization_barrier((kv_half, att_routes))
-    kv_blocks, block_order = spread_over_replicas(kv_half, my_replica, replicas)
-    all_routes = lax.all_gather(routes_sent, "expert", axis=0)
+    hidden_all = lax.all_gather(hidden, "expert", axis=0)
+    all_routes = lax.all_gather(att_routes, "expert", axis=0)
 
     tree_places = jnp.arange(token_count, dtype=jnp.int32)
     tree_segments, tree_depths = tree_layout(tree_places)
@@ -1806,7 +1824,10 @@
     att_gates = gate_values(hidden, att_router, att_first, att_second)
     ffn_picks, ffn_first, ffn_second = token_picks(ffn_routes, FFN_EXPERTS, ffn_capacity)
     prepared = (key_forward, key_backward, key_info, slot_tables, query_info, own_plan, att_picks, att_gates, ffn_picks)
-    hidden_all, kv_blocks, prepared = lax.optimization_barrier((hidden_all, kv_blocks, prepared))
+    kv_gathered, prepared = lax.optimization_barrier((kv_gathered, prepared))
+    kv_half = lax.dynamic_slice_in_dim(kv_gathered, core * 2 * piece, 2 * piece, 2).reshape(D, 2 * piece)
+    kv_blocks, block_order = spread_over_replicas(kv_half, my_replica, replicas)
+    hidden_all, kv_blocks = lax.optimization_barrier((hidden_all, kv_blocks))
     key_forward, key_backward, key_info, slot_tables, query_info, own_plan, att_picks, att_gates, ffn_picks = prepared
 
     queries, query_inputs = project_queries(own_plan, hidden_all, q_weight, slot_tables[0][0])

time: 1140 us -> 1140 us (level)
    all_gather x1, waiting for transfers between devices: 48.2 us -> 6.05 us  [body(): kv_gathered = lax.all_gather(kv_share, 'expert', axis=0)]
    ppermute x1, waiting for transfers between devices: 20 us -> 44.8 us  [spread_over_replicas(): lax.ppermute(block, 'dp', along)]
  transfers between devices with their start and end apart: 19 -> 19, of which waited for: 10 -> 11; matrix products, arithmetic and copies ran while one was open for 19% -> 18% of each run, Pallas kernels for 43% -> 44%
where the time goes in v7:
time: 1140 us; the launch traced here: 1130 us
  Pallas kernels  688 us (60%)
  waiting for transfers between devices  133 us (12%)
  matrix products  132 us (12%)
  other arithmetic  60.9 us (5%)
  blocking collectives  48.8 us (4%)
  local copies, waits for them, and re-layouts  32.8 us (3%)
  starting transfers between devices  17.1 us (2%)
  between operations  16.2 us (1%)
    pallas_call x1, Pallas kernels, ffn_forward(): pl.pallas_call(functools.partial(ffn_forward_body, chunk), in_specs=[any_...  147 us
    pallas_call x1, Pallas kernels, send_rows(): pl.pallas_call(send_rows_body, in_specs=[any_space] * 2, out_specs=[any_s...  93 us
    pallas_call x1, Pallas kernels, merge_return(): pl.pallas_call(functools.partial(merge_return_body, 'dp'), in_specs=[any_...  88.8 us
    pallas_call x1, Pallas kernels, attention_send(): pl.pallas_call(functools.partial(attention_send_body, HEAD ** (-0.5) * LO...  88 us
    pallas_call x1, Pallas kernels, ffn_backward(): pl.pallas_call(functools.partial(ffn_backward_body, chunk), in_specs=[any...  87.7 us
    pallas_call x1, Pallas kernels, attention_backward(): pl.pallas_call(functools.partial(attention_backward_body, sets, step_head...  83.3 us
    dot_general x4, matrix products, dot_tn(): lax.dot_general(left, right, (((0,), (0,)), ((), ())), preferred_element_...  74.6 us
    pallas_call x1, Pallas kernels, send_slots(): pl.pallas_call(send_slots_body, in_specs=[any_space] * 3, out_specs=[any_...  59 us
  transfers between devices with their start and end apart: 19, of which 11 were waited for; matrix products, arithmetic and copies ran while one was open for 18% of the time, Pallas kernels for 44%

profile of v7, /device:TPU:0, one launch (start us, length us, event | category | flops | bytes accessed | tf_op | source)
XLA Modules:
  0.0 1129.2 jit_solution(8190224733564404890)
XLA Ops:
  7.2 3.3 copy.63
  13.5 15.6 %all-gather.2 = s32[8,272,2]{1,2,0:T(2,128)S(1)} all-gather(s32[1,272,2]{1,2,0:T(2,128)S(1)} %bitcast.231), channel_id=2, replica_groups=mesh['dp'=4,'expert'=8] {'expert'}, dimensions={0}, use_global_device_ids=true | all-gather | bytes 19584 | tf_op jit(solution)/shard_map/all_gather | solution.py:1801
  37.4 2.6 multiply_cosine_fusion.1
  48.7 3.9 fusion.45
  55.7 6.0 all-gather.7.cloned.1.call-done
  66.6 44.8 %collective-permute-done.1 = bf16[2048,512]{1,0:T(8,128)(2,1)S(1)} collective-permute-done((bf16[2048,512]{1,0:T(8,128)(2,1)S(1)}, bf16[2048,512]{1,0:T(8,128)(2,1)S(1)}, u32[]{:S(2)}, u32[]{:S(2)}) %collective-permute-start.1) | collective-permute-done | bytes 2097184 | tf_op jit(solution)/shard_map/ppermute | solution.py:1747
  119.2 18.2 %collective-permute-done.2 = bf16[1024,512]{1,0:T(8,128)(2,1)} collective-permute-done((bf16[1024,512]{1,0:T(8,128)(2,1)}, bf16[1024,512]{1,0:T(8,128)(2,1)}, u32[]{:S(2)}, u32[]{:S(2)}) %collective-permute-start.2) | collective-permute-done | bytes 1048608 | tf_op jit(solution)/shard_map/ppermute | solution.py:1749
  137.4 2.9 collective-permute-done.3
  142.0 3.9 pad_maximum_fusion.weight_ref.weight_hbm
  145.9 3.1 all-gather.11.cloned.1.call-done
  149.0 15.1 %project_queries.1 = (bf16[704,2048]{1,0:T(8,128)(2,1)}, bf16[704,2048]{1,0:T(8,128)(2,1)}) custom-call(bf16[8,88,272]{2,1,0:T(8,128)(2,1)} %copy.69.plan_ref, bf16[8,272,2048]{2,1,0:T(8,128)(2,1)} %bitcast.208, bf16[2048,2048]{1,0:T(8,128)(2,1)} %weight_ref.1, f32[704,128]{1,0:T(8,128)} %pad_maximum_fusion.5.cos_ref.refs_13_, ...), custom_call_target="tpu_custom_call" | custom-call | tf_op jit(solution)/shard_map/project_queries/pallas_call | solution.py:292
  167.4 26.6 %project_keys_values.1 = (bf16[2176,1024]{1,0:T(8,128)(2,1)}, bf16[2176,1024]{1,0:T(8,128)(2,1)}) custom-call(s32[4]{0:T(128)} %iota_xor_fusion.order_ref, bf16[8,272,2048]{2,1,0:T(8,128)(2,1)} %bitcast.209, bf16[4,2048,512]{2,1,0:T(8,128)(2,1)} %pad_maximum_fusion.weight_ref.weight_hbm, f32[2176,128]{1,0:T(8,128)} %pad_maximum_fusion.2.cos_ref.refs_11_, ...), custom_call_target="tpu_custom_call" | custom-call | tf_op jit(solution)/shard_map/project_keys_values/pallas_call | solution.py:330
  195.2 88.0 %attention_send.1 = (bf16[704,1024]{1,0:T(8,128)(2,1)}, bf16[704,1024]{1,0:T(8,128)(2,1)}, bf16[704,2048]{1,0:T(8,128)(2,1)}, bf16[8,88,2048]{2,1,0:T(8,128)(2,1)}, f32[8,4,1,352]{3,2,1,0:T(1,128)}) custom-call(bf16[704,2048]{1,0:T(8,128)(2,1)} %get-tuple-element.84.query_hbm.refs_0_, bf16[704,1024]{1,0:T(8,128)(2,1)} %copy-done.12, ...), custom_call_target="tpu_custom_call" | custom-call | tf_op jit(solution)/shard_map/attention_send/pallas_call | solution.py:1575
  285.4 3.8 convolution_bitcast_fusion.2
  293.1 3.3 convolution_convert_fusion.5.slots
  296.4 146.6 %ffn_forward.1 = (bf16[1408,2048]{1,0:T(8,128)(2,1)}, bf16[1408,2816]{1,0:T(8,128)(2,1)}, bf16[1408,2816]{1,0:T(8,128)(2,1)}, bf16[1408,2816]{1,0:T(8,128)(2,1)}, bf16[4,176,2048]{2,1,0:T(8,128)(2,1)}) custom-call(bf16[4,176,2048]{2,1,0:T(8,128)(2,1)} %convolution_convert_fusion.5.slots, bf16[2048,2816]{1,0:T(8,128)(2,1)} %gate_hbm.3, ...), custom_call_target="tpu_custom_call" | custom-call | tf_op jit(solution)/shard_map/ffn_forward/pallas_call | solution.py:796
  443.1 3.9 convolution_bitcast_fusion.1
  450.6 4.0 bitcast_convert_fusion.1.slots
  454.7 93.0 %send_rows.1 = (bf16[4,352,2048]{2,1,0:T(8,128)(2,1)}, bf16[2048,2816]{1,0:T(8,128)(2,1)}) custom-call(bf16[4,176,2048]{2,1,0:T(8,128)(2,1)} %bitcast_convert_fusion.1.slots, bf16[1408,2816]{1,0:T(8,128)(2,1)} %get-tuple-element.97.act_hbm), custom_call_target="tpu_custom_call" | custom-call | tf_op jit(solution)/shard_map/send_rows/pallas_call | solution.py:945
  547.7 87.7 %ffn_backward.1 = (bf16[1408,2816]{1,0:T(8,128)(2,1)}, bf16[1408,2816]{1,0:T(8,128)(2,1)}, bf16[4,176,2048]{2,1,0:T(8,128)(2,1)}) custom-call(bf16[1408,2048]{1,0:T(8,128)(2,1)} %bitcast.215, bf16[1408,2816]{1,0:T(8,128)(2,1)} %get-tuple-element.101.gate_in, bf16[1408,2816]{1,0:T(8,128)(2,1)} %get-tuple-element.102.up_in, bf16[2048,2816]{1,0:T(8,128)(2,1)} %gate_hbm.3, ...), custom_call_target="tpu_custom_call" | custom-call | tf_op jit(solution)/shard_map/ffn_backward/pallas_call | solution.py:1127
  635.5 24.6 %convolution_convert_fusion = bf16[2048,2816]{1,0:T(8,128)(2,1)} fusion(bf16[1408,2048]{1,0:T(8,128)(2,1)} %get-tuple-element.104.rows_hbm, bf16[1408,2816]{1,0:T(8,128)(2,1)} %get-tuple-element.105), kind=kOutput, calls=%fused_computation | convolution fusion | flops 16246112256 | bytes 25231360 | tf_op jit(solution)/shard_map/dot_general | solution.py:1755
  660.3 3.9 convolution_bitcast_fusion
  664.2 2.9 multiply_reduce_fusion
  670.2 4.0 bitcast_convert_fusion.slots
  674.3 59.0 %send_slots.1 = (bf16[8,88,2048]{2,1,0:T(8,128)(2,1)}, bf16[2048,2816]{1,0:T(8,128)(2,1)}) custom-call(bf16[8,88,2048]{2,1,0:T(8,128)(2,1)} %bitcast_convert_fusion.slots, bf16[1408,2048]{1,0:T(8,128)(2,1)} %get-tuple-element.104.rows_hbm, bf16[1408,2816]{1,0:T(8,128)(2,1)} %get-tuple-element.109.grads_hbm), custom_call_target="tpu_custom_call" | custom-call | tf_op jit(solution)/shard_map/send_slots/pallas_call | solution.py:1222
  733.3 9.5 convolution_convert_fusion.4.refs_2_
  746.9 2.6 collective-permute-done.5.refs_3_
  749.6 83.3 %attention_backward.1 = (bf16[704,1024]{1,0:T(8,128)(2,1)}, bf16[704,1024]{1,0:T(8,128)(2,1)}, bf16[2176,2048]{1,0:T(8,128)(2,1)}) custom-call(s32[2]{0:T(128)} %pad_add_fusion.1.first_ref, bf16[704,2048]{1,0:T(8,128)(2,1)} %get-tuple-element.84.query_hbm.refs_0_, bf16[704,1024]{1,0:T(8,128)(2,1)} %copy-done.12, bf16[704,2048]{1,0:T(8,128)(2,1)} %copy-done.11, ...), custom_call_target="tpu_custom_call" | custom-call | tf_op jit(solution)/shard_map/attention_backward/pallas_call | solution.py:221
  832.9 26.5 %convolution_convert_fusion.2 = bf16[2048,2048]{1,0:T(8,128)(2,1)} fusion(bf16[2176,2048]{1,0:T(8,128)(2,1)} %all-gather.11.cloned.1.call-done, bf16[2176,2048]{1,0:T(8,128)(2,1)} %get-tuple-element.125.grads_hbm), kind=kOutput, calls=%fused_computation.4 | convolution fusion | flops 18257805312 | bytes 26214400 | tf_op jit(solution)/shard_map/dot_general | solution.py:1755
  859.8 3.3 collective-permute-done.6
  863.2 12.7 %convolution_convert_fusion.1 = bf16[2048,2048]{1,0:T(8,128)(2,1)} fusion(bf16[704,2048]{1,0:T(8,128)(2,1)S(1)} %copy-done.43, bf16[704,1024]{1,0:T(8,128)(2,1)} %collective-permute-done.6, bf16[704,1024]{1,0:T(8,128)(2,1)} %get-tuple-element.121, pred[]{:T(512)S(6)} %eq.225), kind=kOutput, calls=%fused_computation.3 | convolution fusion | flops 5922750464 | bytes 14155777 | tf_op jit(solution)/shard_map/dot_general | solution.py:1755
  881.9 3.3 constant_dynamic-slice_fusion
  885.1 3.1 collective-permute-start.9
  888.9 11.9 %convolution_convert_fusion.3 = bf16[704,2048]{1,0:T(8,128)(2,1)} fusion(bf16[2048,2048]{1,0:T(8,128)(2,1)} %weight_ref.1, bf16[704,1024]{1,0:T(8,128)(2,1)} %collective-permute-done.6, bf16[704,1024]{1,0:T(8,128)(2,1)S(1)} %copy-done.44, pred[]{:T(512)S(6)} %eq.225), kind=kOutput, calls=%fused_computation.18 | convolution fusion | flops 5919997952 | bytes 14155777 | tf_op jit(solution)/shard_map/dot_general | solution.py:2011
  900.8 16.1 %reduce-scatter.10.cloned.1.call-done = bf16[512,2816]{1,0:T(8,128)(2,1)} async-done(((bf16[2048,2816]{1,0:T(8,128)(2,1)}), bf16[512,2816]{1,0:T(8,128)(2,1)}) %reduce-scatter.10.cloned.1.call-update) | async-done | bytes 2883600 | tf_op jit(solution)/shard_map/reduce_scatter | solution.py:1972
  917.0 88.8 %merge_return.1 = bf16[4,272,2048]{2,1,0:T(8,128)(2,1)} custom-call(bf16[8,272,88]{2,1,0:T(8,128)(2,1)} %bitcast.216, bf16[8,88,2048]{2,1,0:T(8,128)(2,1)} %bitcast.220, bf16[2176,2048]{1,0:T(8,128)(2,1)} %get-tuple-element.125.grads_hbm, bf16[4,2048,512]{2,1,0:T(8,128)(2,1)} %pad_maximum_fusion.weight_ref.weight_hbm), custom_call_target="tpu_custom_call" | custom-call | tf_op jit(solution)/shard_map/merge_return/pallas_call | solution.py:1336
  1005.9 5.7 reduce-scatter.12.cloned.1.call-done
  1011.6 3.5 convert_reduce_fusion
  1015.1 3.2 fusion.21
  1021.4 10.8 fusion.4
  1032.3 33.1 %all_to_all.14 = f32[32,1,896]{2,1,0:T(1,128)S(1)} all-to-all(f32[32,1,896]{2,1,0:T(1,128)S(1)} %copy.72), channel_id=1, replica_groups=mesh['dp'=4,'expert'=8] {'dp','expert'}, dimensions={0} | all-to-all | bytes 229376 | tf_op jit(solution)/shard_map/all_to_all | solution.py:2057
  1065.4 4.4 all-to-all-start.1
  1069.8 5.0 convert_element_type.156
  1074.8 3.0 convert_element_type.154
  1077.8 24.8 %reduce-scatter.14.cloned.1.call-done = bf16[512,2048]{1,0:T(8,128)(2,1)} async-done(((bf16[2048,2048]{1,0:T(8,128)(2,1)}), bf16[512,2048]{1,0:T(8,128)(2,1)}) %reduce-scatter.14.cloned.1.call-update) | async-done | bytes 2097168 | tf_op jit(solution)/shard_map/reduce_scatter | solution.py:2010
  1102.6 4.3 convert_element_type.153
  1106.9 2.9 convert_element_type.155
  1113.7 5.2 all-to-all-done.1
  (244 shorter events, 75.1 us)
Async XLA Ops:
  7.2 24.9 %copy-start = (f32[2048,8]{0,1:T(8,128)S(1)}, f32[2048,8]{0,1:T(8,128)}, u32[]{:S(2)}) copy-start(f32[2048,8]{0,1:T(8,128)} %param.24) | copy-start | bytes 196612
  7.2 54.5 %all-gather.7.cloned.1.call-start = ((), (), s32[]{:S(2)}) async-start(), calls=%async_computation.7 | async-start | bytes 4718592 | tf_op jit(solution)/shard_map/all_gather | solution.py:1799
  11.7 137.4 %all-gather.11.cloned.1.call-start = ((), (), s32[]{:S(2)}) async-start(), calls=%async_computation.14 | async-start | bytes 10027008 | tf_op jit(solution)/shard_map/all_gather | solution.py:1800
  12.1 17.3 %copy-start.34 = (f32[272]{0:T(512)}, f32[272]{0:T(512)S(1)}, u32[]{:S(2)}) copy-start(f32[272]{0:T(512)S(1)} %add_rsqrt_fusion.1) | copy-start | bytes 3268
  12.1 22.3 %copy-start.40 = (s32[1,13]{1,0:T(1,128)S(1)}, s32[1,13]{1,0:T(1,128)}, u32[]{:S(2)}) copy-start(s32[1,13]{1,0:T(1,128)} %param.20) | copy-start | bytes 160
  13.5 441.2 %all-gather.9.cloned.1.call-start = ((), (), s32[]{:S(2)}) async-start(), calls=%async_computation.8 | async-start | bytes 14417920 | tf_op jit(solution)/shard_map/all_gather | solution.py:1860
  32.0 12.0 %copy-start.27 = (pred[2,8,272]{2,1,0:T(8,128)(4,1)}, pred[2,8,272]{2,1,0:T(8,128)(4,1)S(1)}, u32[]{:S(2)}) copy-start(pred[2,8,272]{2,1,0:T(8,128)(4,1)S(1)} %iota_compare_fusion.13) | copy-start | bytes 13060
  40.0 3.8 copy-start.41
  43.9 241.5 %copy-start.32 = (f32[272,2]{0,1:T(2,128)}, f32[272,2]{0,1:T(2,128)S(1)}, u32[]{:S(2)}) copy-start(f32[272,2]{0,1:T(2,128)S(1)} %broadcast_divide_fusion.1) | copy-start | bytes 6532
  63.5 47.8 %collective-permute-start.1 = (bf16[2048,512]{1,0:T(8,128)(2,1)S(1)}, bf16[2048,512]{1,0:T(8,128)(2,1)S(1)}, u32[]{:S(2)}, u32[]{:S(2)}) collective-permute-start(bf16[2048,512]{1,0:T(8,128)(2,1)S(1)} %bitcast.212), channel_id=1, source_target_pairs={{0,16},{8,24},{16,0},{24,8},{1,17},{9,25},{17,1},{25,9},{2,18},{10... | collective-permute-start | bytes 6291464 | tf_op jit(solution)/shard_map/ppermute | solution.py:1747
  65.1 48.9 %collective-permute-start = (bf16[2048,512]{1,0:T(8,128)(2,1)S(1)}, bf16[2048,512]{1,0:T(8,128)(2,1)S(1)}, u32[]{:S(2)}, u32[]{:S(2)}) collective-permute-start(bf16[2048,512]{1,0:T(8,128)(2,1)S(1)} %bitcast.213), channel_id=1, source_target_pairs={{0,8},{8,0},{16,24},{24,16},{1,9},{9,1},{17,25},{25,17},{2,10},{10... | collective-permute-start | bytes 6291464 | tf_op jit(solution)/shard_map/ppermute | solution.py:1747
  112.5 24.9 %collective-permute-start.2 = (bf16[1024,512]{1,0:T(8,128)(2,1)}, bf16[1024,512]{1,0:T(8,128)(2,1)}, u32[]{:S(2)}, u32[]{:S(2)}) collective-permute-start(bf16[1024,512]{1,0:T(8,128)(2,1)} %slice.152), channel_id=1, source_target_pairs={{0,8},{8,0},{16,24},{24,16},{1,9},{9,1},{17,25},{25,17},{2,10},{10... | collective-permute-start | bytes 3145736 | tf_op jit(solution)/shard_map/ppermute | solution.py:1749
  115.6 24.6 %collective-permute-start.3 = (bf16[1024,512]{1,0:T(8,128)(2,1)}, bf16[1024,512]{1,0:T(8,128)(2,1)}, u32[]{:S(2)}, u32[]{:S(2)}) collective-permute-start(bf16[1024,512]{1,0:T(8,128)(2,1)} %slice.153), channel_id=1, source_target_pairs={{0,16},{8,24},{16,0},{24,8},{1,17},{9,25},{17,1},{25,9},{2,18},{10... | collective-permute-start | bytes 3145736 | tf_op jit(solution)/shard_map/ppermute | solution.py:1749
  119.2 22.7 %copy-start.14 = (bf16[2048,512]{1,0:T(8,128)(2,1)S(1)}, bf16[2048,512]{1,0:T(8,128)(2,1)}, u32[]{:S(2)}) copy-start(bf16[2048,512]{1,0:T(8,128)(2,1)} %copy-done.13) | copy-start | bytes 6291460
  119.2 22.7 %copy-start.16 = (bf16[2048,512]{1,0:T(8,128)(2,1)S(1)}, bf16[2048,512]{1,0:T(8,128)(2,1)}, u32[]{:S(2)}) copy-start(bf16[2048,512]{1,0:T(8,128)(2,1)} %copy-done.15) | copy-start | bytes 6291460
  166.7 27.3 %collective-permute-start.4 = (bf16[704,1024]{1,0:T(8,128)(2,1)}, bf16[704,1024]{1,0:T(8,128)(2,1)S(1)}, u32[]{:S(2)}, u32[]{:S(2)}) collective-permute-start(bf16[704,1024]{1,0:T(8,128)(2,1)} %constant_dynamic-slice_fusion.5), channel_id=1, source_target_pairs={{0,1},{1,0},{2,3},{3,2},{4,5},{5,4},{6,7},{7,6},{8,9},{9,8},{10,11... | collective-permute-start | bytes 4325384 | tf_op jit(solution)/shard_map/ppermute | solution.py:1837
  283.3 391.0 %reduce-scatter.6.cloned.1.call-start = ((), (), s32[]{:S(2)}) async-start(), calls=%async_computation.9 | async-start | bytes 14417920 | tf_op jit(solution)/shard_map/reduce_scatter | solution.py:1931
  443.1 3.9 copy-start.19
  547.7 285.2 %reduce-scatter.8.cloned.1.call-start = ((), (), s32[]{:S(2)}) async-start(), calls=%async_computation.10 | async-start | bytes 14417920 | tf_op jit(solution)/shard_map/reduce_scatter | solution.py:1952
  660.1 256.9 %reduce-scatter.10.cloned.1.call-start = ((), (), s32[]{:S(2)}) async-start(), calls=%async_computation.11 | async-start | bytes 14417920 | tf_op jit(solution)/shard_map/reduce_scatter | solution.py:1972
  660.2 6.9 slice-start
  660.3 6.9 slice-start.1
  733.3 278.3 %reduce-scatter.12.cloned.1.call-start = ((), (), s32[]{:S(2)}) async-start(), calls=%async_computation.12 | async-start | bytes 10485760 | tf_op jit(solution)/shard_map/reduce_scatter | solution.py:2009
  742.8 6.7 copy-start.11
  744.3 5.3 collective-permute-start.5
  859.4 3.7 copy-start.43
  859.5 243.1 %reduce-scatter.14.cloned.1.call-start = ((), (), s32[]{:S(2)}) async-start(), calls=%async_computation.13 | async-start | bytes 10485760 | tf_op jit(solution)/shard_map/reduce_scatter | solution.py:2010
  859.5 3.6 collective-permute-start.6
  875.8 3.6 copy-start.33
  875.8 3.7 copy-start.8
  875.9 3.7 copy-start.28
  879.5 5.6 copy-start.36
  881.8 7.0 copy-start.44
  885.1 120.7 %collective-permute-start.9 = (bf16[704,512]{1,0:T(8,128)(2,1)}, bf16[704,512]{1,0:T(8,128)(2,1)S(1)}, u32[]{:S(2)}, u32[]{:S(2)}) collective-permute-start(bf16[704,512]{1,0:T(8,128)(2,1)} %get-tuple-element.231), channel_id=1, source_target_pairs={{0,24},{8,16},{16,8},{24,0},{1,25},{9,17},{17,9},{25,1},{2,26},{10... | collective-permute-start | bytes 2162696 | tf_op jit(solution)/shard_map/ppermute | solution.py:1985
  888.3 117.6 %collective-permute-start.8 = (bf16[704,512]{1,0:T(8,128)(2,1)}, bf16[704,512]{1,0:T(8,128)(2,1)S(1)}, u32[]{:S(2)}, u32[]{:S(2)}) collective-permute-start(bf16[704,512]{1,0:T(8,128)(2,1)} %get-tuple-element.232), channel_id=1, source_target_pairs={{0,16},{8,24},{16,0},{24,8},{1,17},{9,25},{17,1},{25,9},{2,18},{10... | collective-permute-start | bytes 2162696 | tf_op jit(solution)/shard_map/ppermute | solution.py:1985
  888.3 117.6 %collective-permute-start.7 = (bf16[704,512]{1,0:T(8,128)(2,1)S(1)}, bf16[704,512]{1,0:T(8,128)(2,1)S(1)}, u32[]{:S(2)}, u32[]{:S(2)}) collective-permute-start(bf16[704,512]{1,0:T(8,128)(2,1)S(1)} %get-tuple-element.233), channel_id=1, source_target_pairs={{0,8},{8,0},{16,24},{24,16},{1,9},{9,1},{17,25},{25,17},{2,10},{10... | collective-permute-start | bytes 2162696 | tf_op jit(solution)/shard_map/ppermute | solution.py:1985
  1005.8 5.8 copy-start.23
  1005.8 5.7 copy-start.24
  1005.8 5.7 copy-start.25
  1011.6 3.5 copy-start.2
  1011.6 3.5 copy-start.31
  1011.6 3.5 copy-start.35
  1011.6 3.5 copy-start.37
  1065.4 53.4 %all-to-all-start.1 = ((bf16[8,64,2048]{2,1,0:T(8,128)(2,1)}), bf16[8,64,2048]{2,1,0:T(8,128)(2,1)}, u32[]{:S(2)}, u32[]{:S(2)}) async-start(bf16[8,64,2048]{2,1,0:T(8,128)(2,1)} %bitcast.224), calls=%async_computation.5 | async-start | bytes 4194304 | tf_op jit(solution)/shard_map/all_to_all | solution.py:1723
  1069.8 5.0 copy-start.17
  1102.6 4.3 copy-start.18
  1106.9 2.9 copy-start.39
  1106.9 3.0 copy-start.6
  (18 other events, 29.7 us)
Sparse Core Ops, SparseCore 0:
  11.8 49.8 all-gather.6
  63.9 85.0 all-gather.10
  283.4 130.3 all-gather.8
  547.8 111.3 reduce-scatter.5
  662.1 119.5 reduce-scatter.7
  784.7 132.1 reduce-scatter.9
  920.0 91.4 reduce-scatter.11
  1014.9 87.6 reduce-scatter.13

commit v8 on v7

--- a/solution.py
+++ b/solution.py
@@ -39,6 +39,20 @@
             return carry
 
         lax.fori_loop(0, group + 1, one, 0)
+
+
+def fill_group_bias(bias_ref, key_ref, query_ref, keys, group):
+    place, own, parent, grand = (query_ref[group, n : n + 1, :] for n in range(4))
+
+    def one(block, carry):
+        at = pl.multiple_of(block * keys, 16)
+        key_place = key_ref[pl.ds(at, keys), 0:1]
+        key_segment = key_ref[pl.ds(at, keys), 1:2]
+        related = (key_segment == own) | (key_segment == parent) | (key_segment == grand)
+        bias_ref[block] = jnp.where(related & (key_place <= place), 0.0, -1e30)
+        return carry
+
+    lax.fori_loop(0, group + 1, one, 0)
 
 
 def group_rows(refs, group, rows, lanes):
@@ -74,7 +88,7 @@
             for head in range(step_heads):
                 top, total, mixed = carry[3 * head : 3 * head + 3]
                 scores = dot_nt(key_ref[pl.ds(at, keys), pl.ds(head * HEAD, HEAD)], queries[head])
-                scores = scores * scale + bias
+                scores = scores + bias
                 new_top = jnp.maximum(top, jnp.max(scores, axis=0, keepdims=True))
                 fade = jnp.exp2(top - new_top)
                 parts = jnp.exp2(scores - new_top)
@@ -109,6 +123,7 @@
     dkv_ref, bias_ref, flipped_ref, dk_acc, dv_acc = rest[sets:]
     half = dkv_ref.shape[1] // 2
     softmax_scale = scale / LOG2E
+    key_scale = 1.0 / LOG2E
 
     @pl.when(pl.program_id(0) == 0)
     def _():
@@ -141,7 +156,7 @@
                 lanes = pl.ds(head * HEAD, HEAD)
                 key_rows = key_ref[pl.ds(at, keys), lanes]
                 scores = dot_nt(key_rows, queries[head])
-                probs = jnp.exp2(scores * scale + (bias - tops[head]))
+                probs = jnp.exp2(scores + (bias - tops[head]))
                 grad_probs = dot_nt(value_ref[pl.ds(at, keys), lanes], grads[head])
                 grad_scores = (probs * (grad_probs - centres[head])).astype(jnp.bfloat16)
                 dv_acc[pl.ds(at, keys), lanes] += dot_nn(probs.astype(jnp.bfloat16), grads[head])
@@ -164,7 +179,7 @@
         first_lane = pl.multiple_of((pl.program_id(0) * step_heads + head) * HEAD, HEAD)
         for block in range(GROUPS):
             span = pl.ds(block * keys, keys)
-            turned = spin(dk_acc[span, lanes] * softmax_scale, key_cos[span, :], key_sin[span, :])
+            turned = spin(dk_acc[span, lanes] * key_scale, key_cos[span, :], key_sin[span, :])
             dkv_ref[span, pl.ds(first_lane, HEAD)] = turned.astype(jnp.bfloat16)
             dkv_ref[span, pl.ds(half + first_lane, HEAD)] = dv_acc[span, lanes].astype(jnp.bfloat16)
 
@@ -263,7 +278,7 @@
     )
 
 
-def project_body(plan_ref, hidden_ref, weight_ref, cos_ref, sin_ref, out_ref, x_ref):
+def project_body(scale, plan_ref, hidden_ref, weight_ref, cos_ref, sin_ref, out_ref, x_ref):
     sources, capacity = plan_ref.shape[0], plan_ref.shape[1]
     bundle = max(1, sources * capacity // GROUPS // capacity)
     tile = bundle * capacity
@@ -281,7 +296,7 @@
         product = dot_nn(x_ref[span, :], weight_ref[...])
         for lane in range(0, out_ref.shape[1], HEAD):
             turned = spin(product[:, lane : lane + HEAD], cos_ref[span, :], sin_ref[span, :])
-            out_ref[span, lane : lane + HEAD] = turned.astype(jnp.bfloat16)
+            out_ref[span, lane : lane + HEAD] = (turned * scale).astype(jnp.bfloat16)
 
 
 def project_queries(plan, hidden, weight, tables):
@@ -290,7 +305,7 @@
     rows = sources * capacity
     block = 512
     return pl.pallas_call(
-        project_body,
+        functools.partial(project_body, HEAD ** (-0.5) * LOG2E),
         grid=(columns // block,),
         in_specs=[
             pl.BlockSpec((sources, capacity, row_count), lambda j: (0, 0, 0)),
@@ -619,7 +634,8 @@
 
 def ffn_forward_body(
     chunk,
-    slots,
+    picks,
+    hidden,
     gate_hbm,
     up_hbm,
     down_hbm,
@@ -631,6 +647,7 @@
     gate,
     up,
     down,
+    slots,
     landing,
     pre_stage,
     act,
@@ -663,15 +680,25 @@
         me, crossing_order, (0, 3), kept, passing, passed, total, back, local_sem.at[1], swap_send, swap_recv, out_send, out_recv
     )
     middle = is_middle(me // 2)
-    dispatch.start_local()
-    dispatch.start((0, 1))
+    for load in loads:
+        load.start()
+
+    def pack(step):
+        chip = chip_order(me // 2, step)
+        slots[chip] = dot_nn(picks[chip], hidden[...]).astype(jnp.bfloat16)
+
+    pack(1)
+    dispatch.start((1,))
+    pack(2)
 
     @pl.when(middle == 1)
     def _():
         dispatch.start((2,))
 
-    for load in loads:
-        load.start()
+    pack(0)
+    dispatch.start_local()
+    dispatch.start((0,))
+    pack(3)
     block = landing.shape[1]
     hidden_units = gate.shape[1]
     chunks = hidden_units // chunk
@@ -689,7 +716,7 @@
 
     def act_copy(chip, step):
         span = pl.ds(pl.multiple_of(chip * block, 16), block)
-        return pltpu.make_async_copy(act.at[step % 2], act_out.at[span, :], act_sem.at[step % 2])
+        return pltpu.make_async_copy(act, act_out.at[span, :], act_sem.at[0])
 
     def rows_copy(chip, step):
         span = pl.ds(pl.multiple_of(chip * block, 16), block)
@@ -703,8 +730,8 @@
         if step == 0:
             loads[0].wait()
             loads[1].wait()
-        if step >= 2:
-            act_copy(crossing_order(me // 2, step - 2), step - 2).wait()
+        if step >= 1:
+            act_copy(crossing_order(me // 2, step - 1), step - 1).wait()
 
         def hidden_part(part, carry, chip=chip, step=step):
             slot = lax.rem(part + step * chunks, 2)
@@ -719,7 +746,7 @@
             raised = dot_nn(landing[chip], up[:, columns])
             pre_stage[slot, 0] = gated.astype(jnp.bfloat16)
             pre_stage[slot, 1] = raised.astype(jnp.bfloat16)
-            act[step % 2, :, columns] = (gated * jax.nn.sigmoid(gated) * raised).astype(jnp.bfloat16)
+            act[:, columns] = (gated * jax.nn.sigmoid(gated) * raised).astype(jnp.bfloat16)
             for copy in stage_copies(chip, part, slot):
                 copy.start()
             if step == 0:
@@ -746,13 +773,13 @@
 
         def far_part(part, carry, step=step):
             at = pl.multiple_of((1 - core) * half + part * width, 128)
-            product = dot_nt(act[step % 2], down[pl.ds(at, width), :])
+            product = dot_nt(act[...], down[pl.ds(at, width), :])
             passing[step % 2, :, pl.ds(pl.multiple_of(part * width, 128), width)] = product.astype(jnp.bfloat16)
             return carry
 
         def near_part(part, carry, step=step):
             at = pl.multiple_of(core * half + part * width, 128)
-            product = dot_nt(act[step % 2], down[pl.ds(at, width), :])
+            product = dot_nt(act[...], down[pl.ds(at, width), :])
             kept[:, pl.ds(pl.multiple_of(part * width, 128), width)] = product
             return carry
 
@@ -771,8 +798,7 @@
             dispatch.arrive(step + 1)
         lax.fori_loop(0, half // width, near_part, 0)
     collect.settle(3)
-    for step in (2, 3):
-        act_copy(crossing_order(me // 2, step), step).wait()
+    act_copy(crossing_order(me // 2, 3), 3).wait()
     for step in range(4):
         rows_copy(crossing_order(me // 2, step), step).wait()
     for slot in range(2):
@@ -783,8 +809,10 @@
     collect.finish()
 
 
-def ffn_forward(slots, gate_weight, up_weight, down_weight):
-    chips, capacity, depth = slots.shape
+def ffn_forward(picks, hidden, gate_weight, up_weight, down_weight):
+    chips, capacity, row_count = picks.shape
+    depth = hidden.shape[1]
+    here = pl.BlockSpec(memory_space=pltpu.VMEM)
     hidden_units = gate_weight.shape[1]
     block = 2 * capacity
     chunk = 256 if hidden_units % 256 == 0 else 128
@@ -795,7 +823,7 @@
     dma = pltpu.SemaphoreType.DMA
     return pl.pallas_call(
         functools.partial(ffn_forward_body, chunk),
-        in_specs=[any_space] * 4,
+        in_specs=[here] * 2 + [any_space] * 3,
         out_specs=[any_space] * 5,
         out_shape=[
             jax.ShapeDtypeStruct((rows, depth), bf),
@@ -808,9 +836,10 @@
             pltpu.VMEM((depth, hidden_units), bf),
             pltpu.VMEM((depth, hidden_units), bf),
             pltpu.VMEM((depth, hidden_units), bf),
+            pltpu.VMEM((chips, capacity, depth), bf),
             pltpu.VMEM((chips, block, depth), bf),
             pltpu.VMEM((2, 2, block, chunk), bf),
-            pltpu.VMEM((2, block, hidden_units), bf),
+            pltpu.VMEM((block, hidden_units), bf),
             pltpu.VMEM((block, half), jnp.float32),
             pltpu.VMEM((2, block, half), bf),
             pltpu.VMEM((chips, block, half), bf),
@@ -833,7 +862,7 @@
             collective_id=1, has_side_effects=True, vmem_limit_bytes=VMEM_BYTES
         ),
         name="ffn_forward",
-    )(slots, gate_weight, up_weight, down_weight)
+    )(picks, hidden, gate_weight, up_weight, down_weight)
 
 
 def stagger_order(chip, step):
@@ -844,10 +873,12 @@
 
 
 def send_rows_body(
-    slots,
+    picks,
+    pair,
     act_hbm,
     rows_out,
     grad_out,
+    slots,
     landing,
     act,
     total,
@@ -864,8 +895,18 @@
     me = lax.axis_index("expert")
     enter(8, me)
     dispatch = Dispatch(me, stagger_order, slots, landing, local_sem.at[0], send, recv, pass_send, pass_recv)
-    dispatch.start_local()
-    dispatch.start((0, 1, 2))
+
+    def pack(step):
+        chip = stagger_order(me // 2, step)
+        filled = dot_nn(picks[0, chip], pair[0]) + dot_nn(picks[1, chip], pair[1])
+        slots[chip] = filled.astype(jnp.bfloat16)
+
+    for step in (2, 1, 0):
+        pack(step)
+        if step == 0:
+            dispatch.start_local()
+        dispatch.start((step,))
+    pack(3)
     block = landing.shape[1]
     width = stage.shape[1]
     parts = landing.shape[2] // width
@@ -934,8 +975,10 @@
     dispatch.passed_on()
 
 
-def send_rows(slots, act):
-    chips, capacity, depth = slots.shape
+def send_rows(picks, pair, act):
+    unused, chips, capacity, row_count = picks.shape
+    depth = pair.shape[2]
+    here = pl.BlockSpec(memory_space=pltpu.VMEM)
     rows, hidden_units = act.shape
     block = 2 * capacity
     width = min(256, depth // 2)
@@ -944,13 +987,14 @@
     dma = pltpu.SemaphoreType.DMA
     return pl.pallas_call(
         send_rows_body,
-        in_specs=[any_space] * 2,
+        in_specs=[here] * 2 + [any_space],
         out_specs=[any_space] * 2,
         out_shape=[
             jax.ShapeDtypeStruct((chips, block, depth), bf),
             jax.ShapeDtypeStruct((depth, hidden_units), bf),
         ],
         scratch_shapes=[
+            pltpu.VMEM((chips, capacity, depth), bf),
             pltpu.VMEM((chips, block, depth), bf),
             pltpu.VMEM((rows, hidden_units), bf),
             pltpu.VMEM((depth, hidden_units), jnp.float32),
@@ -968,7 +1012,7 @@
             collective_id=2, has_side_effects=True, vmem_limit_bytes=VMEM_BYTES
         ),
         name="send_rows",
-    )(slots, act)
+    )(picks, pair, act)
 
 
 def ffn_backward_body(
@@ -1367,7 +1411,6 @@
 
 
 def attention_send_body(
-    scale,
     query_hbm,
     sibling_hbm,
     key_hbm,
@@ -1426,7 +1469,6 @@
     ]
     for load in loads:
         load.start()
-    fill_bias(bias_ref, key_info, query_info, keys)
     loads[0].wait()
 
     def flip(head, carry):
@@ -1488,8 +1530,8 @@
 
     def attend(step):
         group = group_of(step)
-        first_block = group * (group + 1) // 2
         span = span_of(step)
+        fill_group_bias(bias_ref, key_info, query_info, keys, group)
 
         def head_pair(pair, carry):
             lanes = [pl.ds(pl.multiple_of((2 * pair + n) * HEAD, HEAD), HEAD) for n in range(2)]
@@ -1497,11 +1539,11 @@
 
             def one(block, state):
                 at = pl.multiple_of(block * keys, 16)
-                bias = bias_ref[first_block + block]
+                bias = bias_ref[block]
                 result = []
                 for n in range(2):
                     top, total, mixed = state[3 * n : 3 * n + 3]
-                    scores = dot_nt(keys_v[pl.ds(at, keys), lanes[n]], parts[n]) * scale + bias
+                    scores = dot_nt(keys_v[pl.ds(at, keys), lanes[n]], parts[n]) + bias
                     new_top = jnp.maximum(top, jnp.max(scores, axis=0, keepdims=True))
                     fade = jnp.exp2(top - new_top)
                     probs = jnp.exp2(scores - new_top)
@@ -1573,7 +1615,7 @@
     bf = jnp.bfloat16
     dma = pltpu.SemaphoreType.DMA
     return pl.pallas_call(
-        functools.partial(attention_send_body, HEAD ** (-0.5) * LOG2E),
+        attention_send_body,
         in_specs=[any_space] * 5 + [here] * 2,
         out_specs=[any_space] * 4 + [here],
         out_shape=[
@@ -1589,7 +1631,7 @@
             pltpu.VMEM((tokens, half), bf),
             pltpu.VMEM((tokens, half), bf),
             pltpu.VMEM(out_weight.shape, bf),
-            pltpu.VMEM((GROUPS * (GROUPS + 1) // 2, keys, 2 * rows), jnp.float32),
+            pltpu.VMEM((GROUPS, keys, 2 * rows), jnp.float32),
             pltpu.VMEM((heads, GROUPS, HEAD, keys), bf),
             pltpu.VMEM((GROUPS, rows, half), bf),
             pltpu.VMEM((GROUPS, rows, half), bf),
@@ -1611,6 +1653,39 @@
         ),
         name="attention_send",
     )(queries, siblings, keys_all, values_all, out_weight, key_info, query_info)
+
+
+def swap_blocks_body(blocks, landing, local_sem, send, recv):
+    me = lax.axis_index("expert")
+    enter(8, me)
+
+    def outgoing(offset):
+        target = lax.rem(me + offset, 8)
+        return remote(blocks.at[target], landing.at[me], send.at[offset], recv.at[offset], target)
+
+    local = pltpu.make_async_copy(blocks.at[me], landing.at[me], local_sem)
+    for offset in range(1, 8):
+        outgoing(offset).start()
+    local.start()
+    local.wait()
+    for offset in range(1, 8):
+        outgoing(offset).wait_send()
+        place = landing.at[lax.rem(me + 8 - offset, 8)]
+        remote(place, place, send.at[offset], recv.at[offset], me).wait_recv()
+
+
+def swap_blocks(blocks):
+    any_space = pl.BlockSpec(memory_space=pl.ANY)
+    dma = pltpu.SemaphoreType.DMA
+    return pl.pallas_call(
+        swap_blocks_body,
+        in_specs=[any_space],
+        out_specs=any_space,
+        out_shape=jax.ShapeDtypeStruct(blocks.shape, blocks.dtype),
+        scratch_shapes=[dma, dma((8,)), dma((8,))],
+        compiler_params=pltpu.CompilerParams(collective_id=7, has_side_effects=True),
+        name="swap_blocks",
+    )(blocks)
 
 
 D = 2048
@@ -1823,12 +1898,13 @@
     att_picks, att_first, att_second = token_picks(att_routes, ATT_EXPERTS, att_capacity)
     att_gates = gate_values(hidden, att_router, att_first, att_second)
     ffn_picks, ffn_first, ffn_second = token_picks(ffn_routes, FFN_EXPERTS, ffn_capacity)
-    prepared = (key_forward, key_backward, key_info, slot_tables, query_info, own_plan, att_picks, att_gates, ffn_picks)
+    ffn_any = ffn_picks[0] + ffn_picks[1]
+    prepared = (key_forward, key_backward, key_info, slot_tables, query_info, own_plan, att_picks, att_gates, ffn_picks, ffn_any)
     kv_gathered, prepared = lax.optimization_barrier((kv_gathered, prepared))
     kv_half = lax.dynamic_slice_in_dim(kv_gathered, core * 2 * piece, 2 * piece, 2).reshape(D, 2 * piece)
     kv_blocks, block_order = spread_over_replicas(kv_half, my_replica, replicas)
     hidden_all, kv_blocks = lax.optimization_barrier((hidden_all, kv_blocks))
-    key_forward, key_backward, key_info, slot_tables, query_info, own_plan, att_picks, att_gates, ffn_picks = prepared
+    key_forward, key_backward, key_info, slot_tables, query_info, own_plan, att_picks, att_gates, ffn_picks, ffn_any = prepared
 
     queries, query_inputs = project_queries(own_plan, hidden_all, q_weight, slot_tables[0][0])
     keys_all, values_all = project_keys_values(hidden_all, kv_blocks, key_forward, block_order)
@@ -1887,16 +1963,17 @@
         back = exchange(rows.reshape(devices, ffn_capacity // ffn_copies, D))
         return read_slots(ffn_picks, back.reshape(FFN_EXPERTS, ffn_capacity, D))
 
-    ffn_slots = jnp.einsum(
-        "ecr,rd->ecd", ffn_picks[0] + ffn_picks[1], hidden_two, preferred_element_type=f32
-    ).astype(bf16)
     if fused:
         ffn_inputs, gate_pre, up_pre, activated, ffn_back = ffn_forward(
-            ffn_slots, gate_weight, up_weight, down_weight
+            ffn_any, hidden_two, gate_weight, up_weight, down_weight
         )
         ffn_branches = read_slots(ffn_picks, ffn_back)
     else:
-        ffn_inputs = to_experts(ffn_slots)
+        ffn_inputs = to_experts(
+            jnp.einsum(
+                "ecr,rd->ecd", ffn_picks[0] + ffn_picks[1], hidden_two, preferred_element_type=f32
+            ).astype(bf16)
+        )
         gate_pre = jnp.dot(ffn_inputs, gate_weight, preferred_element_type=f32)
         up_pre = jnp.dot(ffn_inputs, up_weight, preferred_element_type=f32)
         sigmoid_gate = jax.nn.sigmoid(gate_pre)
@@ -1919,13 +1996,12 @@
     grad_result = jnp.where(counted[:, None], (result - teacher.astype(f32)) * loss_factor, 0.0)
 
     ffn_gate_grad, ffn_scaled = pair_grads(ffn_gates, ffn_branches, grad_result)
-    ffn_grad_slots = fill_slots(ffn_picks, ffn_scaled)
     if fused:
-        ffn_grad_slots, att_everywhere = lax.optimization_barrier((ffn_grad_slots, att_everywhere))
-        grad_ffn_out, grad_down = send_rows(ffn_grad_slots, activated)
+        ffn_scaled, att_everywhere = lax.optimization_barrier((ffn_scaled, att_everywhere))
+        grad_ffn_out, grad_down = send_rows(ffn_picks, ffn_scaled, activated)
         grad_ffn_out = grad_ffn_out.reshape(-1, D)
     else:
-        grad_ffn_out = to_experts(ffn_grad_slots)
+        grad_ffn_out = to_experts(fill_slots(ffn_picks, ffn_scaled))
         grad_down = dot_tn(grad_ffn_out, activated).astype(bf16)
     grad_ffn_out, grad_down = lax.optimization_barrier((grad_ffn_out, grad_down))
     summed_down = lax.psum_scatter(grad_down, "dp", scatter_dimension=0, tiled=True)
@@ -2052,17 +2128,19 @@
     everyone = devices * replicas
     smalls = [grad_gain_one, grad_gain_two, grad_att_router, grad_ffn_router]
     packed = jnp.concatenate([small.reshape(everyone, -1) for small in smalls], axis=1)
+    kv_exchange = swap_blocks if fused else exchange
+    kv_rows = kv_exchange(summed_kv.reshape(devices, -1, 2 * half))
     packed, summed_o = lax.optimization_barrier((packed, summed_o))
     own_smalls = jnp.sum(
         lax.all_to_all(packed, ("dp", "expert"), split_axis=0, concat_axis=0, tiled=True), axis=0
     )
+    own_smalls, kv_rows, summed_q = lax.optimization_barrier((own_smalls, kv_rows, summed_q))
     share = D // everyone
     shared_gain_one = own_smalls[:share]
     shared_gain_two = own_smalls[share : 2 * share]
     shared_att_router = own_smalls[2 * share : (2 + ATT_EXPERTS) * share].reshape(share, ATT_EXPERTS)
     shared_ffn_router = own_smalls[(2 + ATT_EXPERTS) * share :].reshape(share, FFN_EXPERTS)
 
-    kv_rows = exchange(summed_kv.reshape(devices, -1, 2 * half))
     kv_sum = jnp.sum(kv_rows.astype(f32).reshape(devices // 2, 2, -1, 2 * half), axis=0)
     shared_kv = jnp.concatenate(
         [kv_sum[n, :, m * half : (m + 1) * half] for m in range(2) for n in range(2)], axis=1

time: 1140 us -> 1150 us (level)
  Pallas kernels: 688 us -> 749 us
  waiting for transfers between devices: 133 us -> 92.5 us
  blocking collectives: 48.8 us -> 15.6 us
  starting transfers between devices: 17.1 us -> 39.7 us
    pallas_call x4 -> x5, Pallas kernels: 343 us -> 396 us  [the longest x1 149 us: ffn_forward(): pl.pallas_call(functools.partial(ffn_forward_body, chunk), in_specs=[here...]
    all_to_all x1 -> x0, blocking collectives: 33.1 us -> none  [body(): lax.all_to_all(packed, ('dp', 'expert'), split_axis=0, concat_axis=0, til...]
    reduce_scatter x1, waiting for transfers between devices: 24.8 us -> 0.02 us  [body(): summed_q = lax.psum_scatter(grad_q, 'dp', scatter_dimension=0, tiled=True)]
    all_to_all x1, starting transfers between devices: 4.35 us -> 28.1 us  [body(): lax.all_to_all(packed, ('dp', 'expert'), split_axis=0, concat_axis=0, til...]
  transfers between devices with their start and end apart: 19 -> 19, of which waited for: 11 -> 8; matrix products, arithmetic and copies ran while one was open for 18% -> 17% of each run, Pallas kernels for 44% -> 48%
where the time goes in v8:
time: 1150 us; the launch traced here: 1130 us
  Pallas kernels  749 us (65%)
  matrix products  124 us (11%)
  waiting for transfers between devices  92.5 us (8%)
  other arithmetic  60.7 us (5%)
  starting transfers between devices  39.7 us (3%)
  local copies, waits for them, and re-layouts  36.6 us (3%)
  between operations  16.1 us (1%)
  blocking collectives  15.6 us (1%)
    pallas_call x1, Pallas kernels, ffn_forward(): pl.pallas_call(functools.partial(ffn_forward_body, chunk), in_specs=[here...  149 us
    pallas_call x1, Pallas kernels, send_rows(): pl.pallas_call(send_rows_body, in_specs=[here] * 2 + [any_space], out_spe...  103 us
    pallas_call x1, Pallas kernels, merge_return(): pl.pallas_call(functools.partial(merge_return_body, 'dp'), in_specs=[any_...  95.2 us
    pallas_call x1, Pallas kernels, attention_send(): pl.pallas_call(attention_send_body, in_specs=[any_space] * 5 + [here] * 2...  90.7 us
    pallas_call x1, Pallas kernels, ffn_backward(): pl.pallas_call(functools.partial(ffn_backward_body, chunk), in_specs=[any...  90.3 us
    pallas_call x1, Pallas kernels, attention_backward(): pl.pallas_call(functools.partial(attention_backward_body, sets, step_head...  82.8 us
    dot_general x4, matrix products, dot_tn(): lax.dot_general(left, right, (((0,), (0,)), ((), ())), preferred_element_...  74 us
    pallas_call x1, Pallas kernels, send_slots(): pl.pallas_call(send_slots_body, in_specs=[any_space] * 3, out_specs=[any_...  58 us
  transfers between devices with their start and end apart: 19, of which 8 were waited for; matrix products, arithmetic and copies ran while one was open for 17% of the time, Pallas kernels for 48%

profile of v8, /device:TPU:0, one launch (start us, length us, event | category | flops | bytes accessed | tf_op | source)
XLA Modules:
  0.0 1134.2 jit_solution(13762802978331125717)
XLA Ops:
  7.2 3.3 copy.61
  13.5 15.6 %all-gather.2 = s32[8,272,2]{1,2,0:T(2,128)S(1)} all-gather(s32[1,272,2]{1,2,0:T(2,128)S(1)} %bitcast.222), channel_id=2, replica_groups=mesh['dp'=4,'expert'=8] {'expert'}, dimensions={0}, use_global_device_ids=true | all-gather | bytes 19584 | tf_op jit(solution)/shard_map/all_gather | solution.py:1876
  32.1 2.3 select_reduce_fusion.6
  37.5 2.6 multiply_cosine_fusion.1
  48.6 3.9 fusion.39
  55.6 6.1 all-gather.7.cloned.1.call-done
  66.6 44.8 %collective-permute-done.1 = bf16[2048,512]{1,0:T(8,128)(2,1)S(1)} collective-permute-done((bf16[2048,512]{1,0:T(8,128)(2,1)S(1)}, bf16[2048,512]{1,0:T(8,128)(2,1)S(1)}, u32[]{:S(2)}, u32[]{:S(2)}) %collective-permute-start.1) | collective-permute-done | bytes 2097184 | tf_op jit(solution)/shard_map/ppermute | solution.py:1822
  117.1 2.1 copy.67.plan_ref
  119.2 18.2 %collective-permute-done.2 = bf16[1024,512]{1,0:T(8,128)(2,1)} collective-permute-done((bf16[1024,512]{1,0:T(8,128)(2,1)}, bf16[1024,512]{1,0:T(8,128)(2,1)}, u32[]{:S(2)}, u32[]{:S(2)}) %collective-permute-start.2) | collective-permute-done | bytes 1048608 | tf_op jit(solution)/shard_map/ppermute | solution.py:1824
  137.4 2.9 collective-permute-done.3
  142.0 3.9 pad_maximum_fusion.weight_ref.weight_hbm
  145.9 3.1 all-gather.11.cloned.1.call-done
  149.0 15.1 %project_queries.1 = (bf16[704,2048]{1,0:T(8,128)(2,1)}, bf16[704,2048]{1,0:T(8,128)(2,1)}) custom-call(bf16[8,88,272]{2,1,0:T(8,128)(2,1)} %copy.67.plan_ref, bf16[8,272,2048]{2,1,0:T(8,128)(2,1)} %bitcast.196, bf16[2048,2048]{1,0:T(8,128)(2,1)} %weight_ref.1, f32[704,128]{1,0:T(8,128)} %pad_maximum_fusion.6.cos_ref.refs_13_, ...), custom_call_target="tpu_custom_call" | custom-call | tf_op jit(solution)/shard_map/project_queries/pallas_call | solution.py:307
  164.1 2.6 constant_dynamic-slice_fusion.5
  167.4 26.6 %project_keys_values.1 = (bf16[2176,1024]{1,0:T(8,128)(2,1)}, bf16[2176,1024]{1,0:T(8,128)(2,1)}) custom-call(s32[4]{0:T(128)} %iota_xor_fusion.order_ref, bf16[8,272,2048]{2,1,0:T(8,128)(2,1)} %bitcast.197, bf16[4,2048,512]{2,1,0:T(8,128)(2,1)} %pad_maximum_fusion.weight_ref.weight_hbm, f32[2176,128]{1,0:T(8,128)} %pad_maximum_fusion.3.cos_ref.refs_11_, ...), custom_call_target="tpu_custom_call" | custom-call | tf_op jit(solution)/shard_map/project_keys_values/pallas_call | solution.py:345
  195.2 90.7 %attention_send.1 = (bf16[704,1024]{1,0:T(8,128)(2,1)}, bf16[704,1024]{1,0:T(8,128)(2,1)}, bf16[704,2048]{1,0:T(8,128)(2,1)}, bf16[8,88,2048]{2,1,0:T(8,128)(2,1)}, f32[8,4,1,352]{3,2,1,0:T(1,128)}) custom-call(bf16[704,2048]{1,0:T(8,128)(2,1)} %get-tuple-element.88.query_hbm.refs_0_, bf16[704,1024]{1,0:T(8,128)(2,1)} %copy-done.15, ...), custom_call_target="tpu_custom_call" | custom-call | tf_op jit(solution)/shard_map/attention_send/pallas_call | solution.py:1617
  288.1 3.8 convolution_bitcast_fusion.2
  295.9 149.2 %ffn_forward.1 = (bf16[1408,2048]{1,0:T(8,128)(2,1)}, bf16[1408,2816]{1,0:T(8,128)(2,1)}, bf16[1408,2816]{1,0:T(8,128)(2,1)}, bf16[1408,2816]{1,0:T(8,128)(2,1)}, bf16[4,176,2048]{2,1,0:T(8,128)(2,1)}) custom-call(bf16[4,176,272]{2,1,0:T(8,128)(2,1)} %fusion.38.picks, bf16[272,2048]{1,0:T(8,128)(2,1)} %copy-done.8, bf16[2048,2816]{1,0:T(8,128)(2,1)} %gate_hbm.3, ...), custom_call_target="tpu_custom_call" | custom-call | tf_op jit(solution)/shard_map/ffn_forward/pallas_call | solution.py:824
  445.1 4.2 convolution_bitcast_fusion.1
  449.3 2.3 multiply_reduce_fusion.5
  454.5 103.1 %send_rows.1 = (bf16[4,352,2048]{2,1,0:T(8,128)(2,1)}, bf16[2048,2816]{1,0:T(8,128)(2,1)}) custom-call(bf16[2,4,176,272]{3,2,1,0:T(8,128)(2,1)} %copy-done.11, bf16[2,272,2048]{2,1,0:T(8,128)(2,1)} %pad_maximum_fusion.2.pair, bf16[1408,2816]{1,0:T(8,128)(2,1)} %get-tuple-element.102.act_hbm), custom_call_target="tpu_custom_call" | custom-call | tf_op jit(solution)/shard_map/send_rows/pallas_call | solution.py:988
  557.7 90.3 %ffn_backward.1 = (bf16[1408,2816]{1,0:T(8,128)(2,1)}, bf16[1408,2816]{1,0:T(8,128)(2,1)}, bf16[4,176,2048]{2,1,0:T(8,128)(2,1)}) custom-call(bf16[1408,2048]{1,0:T(8,128)(2,1)} %bitcast.206, bf16[1408,2816]{1,0:T(8,128)(2,1)} %get-tuple-element.106.gate_in, bf16[1408,2816]{1,0:T(8,128)(2,1)} %get-tuple-element.107.up_in, bf16[2048,2816]{1,0:T(8,128)(2,1)} %gate_hbm.3, ...), custom_call_target="tpu_custom_call" | custom-call | tf_op jit(solution)/shard_map/ffn_backward/pallas_call | solution.py:1171
  648.0 24.7 %convolution_convert_fusion = bf16[2048,2816]{1,0:T(8,128)(2,1)} fusion(bf16[1408,2048]{1,0:T(8,128)(2,1)} %get-tuple-element.109.rows_hbm, bf16[1408,2816]{1,0:T(8,128)(2,1)} %get-tuple-element.110), kind=kOutput, calls=%fused_computation | convolution fusion | flops 16246112256 | bytes 25231360 | tf_op jit(solution)/shard_map/dot_general | solution.py:1830
  674.0 4.1 convolution_bitcast_fusion
  678.1 2.9 multiply_reduce_fusion
  684.1 4.0 bitcast_convert_fusion.slots
  688.1 58.0 %send_slots.1 = (bf16[8,88,2048]{2,1,0:T(8,128)(2,1)}, bf16[2048,2816]{1,0:T(8,128)(2,1)}) custom-call(bf16[8,88,2048]{2,1,0:T(8,128)(2,1)} %bitcast_convert_fusion.slots, bf16[1408,2048]{1,0:T(8,128)(2,1)} %get-tuple-element.109.rows_hbm, bf16[1408,2816]{1,0:T(8,128)(2,1)} %get-tuple-element.114.grads_hbm), custom_call_target="tpu_custom_call" | custom-call | tf_op jit(solution)/shard_map/send_slots/pallas_call | solution.py:1266
  746.2 9.4 convolution_convert_fusion.4.refs_2_
  759.0 2.6 collective-permute-done.5.refs_3_
  761.6 82.8 %attention_backward.1 = (bf16[704,1024]{1,0:T(8,128)(2,1)}, bf16[704,1024]{1,0:T(8,128)(2,1)}, bf16[2176,2048]{1,0:T(8,128)(2,1)}) custom-call(s32[2]{0:T(128)} %pad_add_fusion.1.first_ref, bf16[704,2048]{1,0:T(8,128)(2,1)} %get-tuple-element.88.query_hbm.refs_0_, bf16[704,1024]{1,0:T(8,128)(2,1)} %copy-done.15, bf16[704,2048]{1,0:T(8,128)(2,1)} %copy-done.14, ...), custom_call_target="tpu_custom_call" | custom-call | tf_op jit(solution)/shard_map/attention_backward/pallas_call | solution.py:236
  844.4 26.7 %convolution_convert_fusion.2 = bf16[2048,2048]{1,0:T(8,128)(2,1)} fusion(bf16[2176,2048]{1,0:T(8,128)(2,1)} %all-gather.11.cloned.1.call-done, bf16[2176,2048]{1,0:T(8,128)(2,1)} %get-tuple-element.130.grads_hbm), kind=kOutput, calls=%fused_computation.4 | convolution fusion | flops 18257805312 | bytes 26214400 | tf_op jit(solution)/shard_map/dot_general | solution.py:1830
  871.5 3.3 collective-permute-done.6
  874.8 11.9 %convolution_convert_fusion.1 = bf16[2048,2048]{1,0:T(8,128)(2,1)} fusion(bf16[704,2048]{1,0:T(8,128)(2,1)S(1)} %copy-done.41, bf16[704,1024]{1,0:T(8,128)(2,1)} %collective-permute-done.6, bf16[704,1024]{1,0:T(8,128)(2,1)} %get-tuple-element.126, pred[]{:T(512)S(6)} %eq.225), kind=kOutput, calls=%fused_computation.3 | convolution fusion | flops 5922750464 | bytes 14155777 | tf_op jit(solution)/shard_map/dot_general | solution.py:1830
  892.8 3.5 constant_dynamic-slice_fusion
  896.3 2.8 collective-permute-start.9
  899.8 3.4 convert_element_type.148
  903.1 3.3 convert_element_type.146
  908.2 9.8 convolution_convert_fusion.3
  918.0 11.3 reduce-scatter.10.cloned.1.call-done
  929.4 95.2 %merge_return.1 = bf16[4,272,2048]{2,1,0:T(8,128)(2,1)} custom-call(bf16[8,272,88]{2,1,0:T(8,128)(2,1)} %bitcast.207, bf16[8,88,2048]{2,1,0:T(8,128)(2,1)} %bitcast.211, bf16[2176,2048]{1,0:T(8,128)(2,1)} %get-tuple-element.130.grads_hbm, bf16[4,2048,512]{2,1,0:T(8,128)(2,1)} %pad_maximum_fusion.weight_ref.weight_hbm), custom_call_target="tpu_custom_call" | custom-call | tf_op jit(solution)/shard_map/merge_return/pallas_call | solution.py:1380
  1025.5 3.5 convert_reduce_fusion
  1029.0 3.9 fusion.21
  1034.8 10.7 fusion.4
  1046.2 28.1 %all-to-all-start = ((f32[32,1,896]{2,1,0:T(1,128)}), f32[32,1,896]{2,1,0:T(1,128)S(1)}, u32[]{:S(2)}, u32[]{:S(2)}) async-start(f32[32,1,896]{2,1,0:T(1,128)} %copy.70), calls=%async_computation.4 | async-start | bytes 229376 | tf_op jit(solution)/shard_map/all_to_all | solution.py:2135
  1074.3 3.2 fusion.20
  1077.6 38.4 %swap_blocks.1 = bf16[8,64,2048]{2,1,0:T(8,128)(2,1)} custom-call(bf16[8,64,2048]{2,1,0:T(8,128)(2,1)} %bitcast.215), custom_call_target="tpu_custom_call" | custom-call | tf_op jit(solution)/shard_map/swap_blocks/pallas_call | solution.py:1680
  1116.0 4.9 convert_element_type.147
  1123.6 2.5 convert_element_type.145
  (245 shorter events, 66.3 us)
Async XLA Ops:
  7.2 24.9 %copy-start = (f32[2048,8]{0,1:T(8,128)S(1)}, f32[2048,8]{0,1:T(8,128)}, u32[]{:S(2)}) copy-start(f32[2048,8]{0,1:T(8,128)} %param.24) | copy-start | bytes 196612
  7.2 54.5 %all-gather.7.cloned.1.call-start = ((), (), s32[]{:S(2)}) async-start(), calls=%async_computation.6 | async-start | bytes 4718592 | tf_op jit(solution)/shard_map/all_gather | solution.py:1874
  11.7 137.4 %all-gather.11.cloned.1.call-start = ((), (), s32[]{:S(2)}) async-start(), calls=%async_computation.13 | async-start | bytes 10027008 | tf_op jit(solution)/shard_map/all_gather | solution.py:1875
  12.1 17.3 %copy-start.35 = (f32[272]{0:T(512)}, f32[272]{0:T(512)S(1)}, u32[]{:S(2)}) copy-start(f32[272]{0:T(512)S(1)} %add_rsqrt_fusion.1) | copy-start | bytes 3268
  12.1 22.3 %copy-start.38 = (s32[1,13]{1,0:T(1,128)S(1)}, s32[1,13]{1,0:T(1,128)}, u32[]{:S(2)}) copy-start(s32[1,13]{1,0:T(1,128)} %param.20) | copy-start | bytes 160
  13.5 441.0 %all-gather.9.cloned.1.call-start = ((), (), s32[]{:S(2)}) async-start(), calls=%async_computation.7 | async-start | bytes 14417920 | tf_op jit(solution)/shard_map/all_gather | solution.py:1936
  32.0 12.0 %copy-start.28 = (pred[2,8,272]{2,1,0:T(8,128)(4,1)}, pred[2,8,272]{2,1,0:T(8,128)(4,1)S(1)}, u32[]{:S(2)}) copy-start(pred[2,8,272]{2,1,0:T(8,128)(4,1)S(1)} %iota_compare_fusion.13) | copy-start | bytes 13060
  40.0 3.8 copy-start.39
  43.9 244.2 %copy-start.33 = (f32[272,2]{0,1:T(2,128)}, f32[272,2]{0,1:T(2,128)S(1)}, u32[]{:S(2)}) copy-start(f32[272,2]{0,1:T(2,128)S(1)} %broadcast_divide_fusion.1) | copy-start | bytes 6532
  46.4 6.1 copy-start.11
  63.5 47.8 %collective-permute-start.1 = (bf16[2048,512]{1,0:T(8,128)(2,1)S(1)}, bf16[2048,512]{1,0:T(8,128)(2,1)S(1)}, u32[]{:S(2)}, u32[]{:S(2)}) collective-permute-start(bf16[2048,512]{1,0:T(8,128)(2,1)S(1)} %bitcast.203), channel_id=1, source_target_pairs={{0,16},{8,24},{16,0},{24,8},{1,17},{9,25},{17,1},{25,9},{2,18},{10... | collective-permute-start | bytes 6291464 | tf_op jit(solution)/shard_map/ppermute | solution.py:1822
  65.1 48.9 %collective-permute-start = (bf16[2048,512]{1,0:T(8,128)(2,1)S(1)}, bf16[2048,512]{1,0:T(8,128)(2,1)S(1)}, u32[]{:S(2)}, u32[]{:S(2)}) collective-permute-start(bf16[2048,512]{1,0:T(8,128)(2,1)S(1)} %bitcast.204), channel_id=1, source_target_pairs={{0,8},{8,0},{16,24},{24,16},{1,9},{9,1},{17,25},{25,17},{2,10},{10... | collective-permute-start | bytes 6291464 | tf_op jit(solution)/shard_map/ppermute | solution.py:1822
  111.4 2.6 copy-start.16
  112.5 24.9 %collective-permute-start.2 = (bf16[1024,512]{1,0:T(8,128)(2,1)}, bf16[1024,512]{1,0:T(8,128)(2,1)}, u32[]{:S(2)}, u32[]{:S(2)}) collective-permute-start(bf16[1024,512]{1,0:T(8,128)(2,1)} %slice.154), channel_id=1, source_target_pairs={{0,8},{8,0},{16,24},{24,16},{1,9},{9,1},{17,25},{25,17},{2,10},{10... | collective-permute-start | bytes 3145736 | tf_op jit(solution)/shard_map/ppermute | solution.py:1824
  115.6 24.6 %collective-permute-start.3 = (bf16[1024,512]{1,0:T(8,128)(2,1)}, bf16[1024,512]{1,0:T(8,128)(2,1)}, u32[]{:S(2)}, u32[]{:S(2)}) collective-permute-start(bf16[1024,512]{1,0:T(8,128)(2,1)} %slice.155), channel_id=1, source_target_pairs={{0,16},{8,24},{16,0},{24,8},{1,17},{9,25},{17,1},{25,9},{2,18},{10... | collective-permute-start | bytes 3145736 | tf_op jit(solution)/shard_map/ppermute | solution.py:1824
  119.2 22.7 %copy-start.17 = (bf16[2048,512]{1,0:T(8,128)(2,1)S(1)}, bf16[2048,512]{1,0:T(8,128)(2,1)}, u32[]{:S(2)}) copy-start(bf16[2048,512]{1,0:T(8,128)(2,1)} %copy-done.16) | copy-start | bytes 6291460
  119.2 22.7 %copy-start.19 = (bf16[2048,512]{1,0:T(8,128)(2,1)S(1)}, bf16[2048,512]{1,0:T(8,128)(2,1)}, u32[]{:S(2)}) copy-start(bf16[2048,512]{1,0:T(8,128)(2,1)} %copy-done.18) | copy-start | bytes 6291460
  166.7 27.3 %collective-permute-start.4 = (bf16[704,1024]{1,0:T(8,128)(2,1)}, bf16[704,1024]{1,0:T(8,128)(2,1)S(1)}, u32[]{:S(2)}, u32[]{:S(2)}) collective-permute-start(bf16[704,1024]{1,0:T(8,128)(2,1)} %constant_dynamic-slice_fusion.5), channel_id=1, source_target_pairs={{0,1},{1,0},{2,3},{3,2},{4,5},{5,4},{6,7},{7,6},{8,9},{9,8},{10,11... | collective-permute-start | bytes 4325384 | tf_op jit(solution)/shard_map/ppermute | solution.py:1913
  286.0 402.1 %reduce-scatter.6.cloned.1.call-start = ((), (), s32[]{:S(2)}) async-start(), calls=%async_computation.8 | async-start | bytes 14417920 | tf_op jit(solution)/shard_map/reduce_scatter | solution.py:2007
  445.1 4.2 copy-start.23
  557.7 286.7 %reduce-scatter.8.cloned.1.call-start = ((), (), s32[]{:S(2)}) async-start(), calls=%async_computation.9 | async-start | bytes 14417920 | tf_op jit(solution)/shard_map/reduce_scatter | solution.py:2028
  672.8 256.6 %reduce-scatter.10.cloned.1.call-start = ((), (), s32[]{:S(2)}) async-start(), calls=%async_computation.10 | async-start | bytes 14417920 | tf_op jit(solution)/shard_map/reduce_scatter | solution.py:2048
  672.9 8.1 slice-start
  674.0 7.0 slice-start.1
  678.1 2.9 copy-start.4
  746.2 278.5 %reduce-scatter.12.cloned.1.call-start = ((), (), s32[]{:S(2)}) async-start(), calls=%async_computation.11 | async-start | bytes 10485760 | tf_op jit(solution)/shard_map/reduce_scatter | solution.py:2085
  755.7 5.9 copy-start.14
  757.1 4.5 collective-permute-start.5
  871.1 3.7 copy-start.41
  871.2 249.8 %reduce-scatter.14.cloned.1.call-start = ((), (), s32[]{:S(2)}) async-start(), calls=%async_computation.12 | async-start | bytes 10485760 | tf_op jit(solution)/shard_map/reduce_scatter | solution.py:2086
  871.2 3.6 collective-permute-start.6
  886.8 3.6 copy-start.34
  886.8 3.7 copy-start.10
  886.8 3.7 copy-start.29
  892.8 7.0 copy-start.20
  896.3 128.3 %collective-permute-start.9 = (bf16[704,512]{1,0:T(8,128)(2,1)}, bf16[704,512]{1,0:T(8,128)(2,1)S(1)}, u32[]{:S(2)}, u32[]{:S(2)}) collective-permute-start(bf16[704,512]{1,0:T(8,128)(2,1)} %get-tuple-element.239), channel_id=1, source_target_pairs={{0,24},{8,16},{16,8},{24,0},{1,25},{9,17},{17,9},{25,1},{2,26},{10... | collective-permute-start | bytes 2162696 | tf_op jit(solution)/shard_map/ppermute | solution.py:2061
  899.1 125.5 %collective-permute-start.8 = (bf16[704,512]{1,0:T(8,128)(2,1)}, bf16[704,512]{1,0:T(8,128)(2,1)S(1)}, u32[]{:S(2)}, u32[]{:S(2)}) collective-permute-start(bf16[704,512]{1,0:T(8,128)(2,1)} %get-tuple-element.240), channel_id=1, source_target_pairs={{0,16},{8,24},{16,0},{24,8},{1,17},{9,25},{17,1},{25,9},{2,18},{10... | collective-permute-start | bytes 2162696 | tf_op jit(solution)/shard_map/ppermute | solution.py:2061
  899.2 3.9 copy-start.21
  899.2 125.4 %collective-permute-start.7 = (bf16[704,512]{1,0:T(8,128)(2,1)}, bf16[704,512]{1,0:T(8,128)(2,1)S(1)}, u32[]{:S(2)}, u32[]{:S(2)}) collective-permute-start(bf16[704,512]{1,0:T(8,128)(2,1)} %get-tuple-element.241), channel_id=1, source_target_pairs={{0,8},{8,0},{16,24},{24,16},{1,9},{9,1},{17,25},{25,17},{2,10},{10... | collective-permute-start | bytes 2162696 | tf_op jit(solution)/shard_map/ppermute | solution.py:2061
  899.8 6.7 slice-start.2
  903.1 4.8 slice-start.3
  903.1 5.1 copy-start.42
  1025.5 3.5 copy-start.2
  1025.5 3.5 copy-start.32
  1025.5 3.5 copy-start.36
  1034.7 39.6 %copy-start.6 = (f32[272,2048]{1,0:T(8,128)S(1)}, f32[272,2048]{1,0:T(8,128)}, u32[]{:S(2)}) copy-start(f32[272,2048]{1,0:T(8,128)} %copy-done.5) | copy-start | bytes 6684676
  1046.2 74.7 %all-to-all-start = ((f32[32,1,896]{2,1,0:T(1,128)}), f32[32,1,896]{2,1,0:T(1,128)S(1)}, u32[]{:S(2)}, u32[]{:S(2)}) async-start(f32[32,1,896]{2,1,0:T(1,128)} %copy.70), calls=%async_computation.4 | async-start | bytes 229376 | tf_op jit(solution)/shard_map/all_to_all | solution.py:2135
  1116.0 5.6 copy-start.13
  (18 other events, 26.0 us)
Sparse Core Ops, SparseCore 0:
  11.8 49.8 all-gather.6
  63.9 85.0 all-gather.10
  286.1 130.2 all-gather.8
  557.8 113.0 reduce-scatter.5
  673.8 119.5 reduce-scatter.7
  796.4 132.8 reduce-scatter.9
  932.4 90.9 reduce-scatter.11
  1026.8 87.6 reduce-scatter.13

commit v9 on v7

--- a/solution.py
+++ b/solution.py
@@ -1547,11 +1547,7 @@
         attend(step)
         if step == 0:
             loads[4].wait()
-        if step < 2:
-            settle(step)
-        elif step == 3:
-            settle(2)
-            settle(3)
+        settle(step)
     for step in range(4):
         swap(step).wait_send()
         own_copy(step).wait()
@@ -1613,6 +1609,39 @@
     )(queries, siblings, keys_all, values_all, out_weight, key_info, query_info)
 
 
+def swap_blocks_body(blocks, landing, local_sem, send, recv):
+    me = lax.axis_index("expert")
+    enter(8, me)
+
+    def outgoing(offset):
+        target = lax.rem(me + offset, 8)
+        return remote(blocks.at[target], landing.at[me], send.at[offset], recv.at[offset], target)
+
+    local = pltpu.make_async_copy(blocks.at[me], landing.at[me], local_sem)
+    for offset in range(1, 8):
+        outgoing(offset).start()
+    local.start()
+    local.wait()
+    for offset in range(1, 8):
+        outgoing(offset).wait_send()
+        place = landing.at[lax.rem(me + 8 - offset, 8)]
+        remote(place, place, send.at[offset], recv.at[offset], me).wait_recv()
+
+
+def swap_blocks(blocks):
+    any_space = pl.BlockSpec(memory_space=pl.ANY)
+    dma = pltpu.SemaphoreType.DMA
+    return pl.pallas_call(
+        swap_blocks_body,
+        in_specs=[any_space],
+        out_specs=any_space,
+        out_shape=jax.ShapeDtypeStruct(blocks.shape, blocks.dtype),
+        scratch_shapes=[dma, dma((8,)), dma((8,))],
+        compiler_params=pltpu.CompilerParams(collective_id=7, has_side_effects=True),
+        name="swap_blocks",
+    )(blocks)
+
+
 D = 2048
 HEADS = 16
 ATT_EXPERTS = 8
@@ -2053,16 +2082,18 @@
     smalls = [grad_gain_one, grad_gain_two, grad_att_router, grad_ffn_router]
     packed = jnp.concatenate([small.reshape(everyone, -1) for small in smalls], axis=1)
     packed, summed_o = lax.optimization_barrier((packed, summed_o))
+    kv_exchange = swap_blocks if fused else exchange
+    kv_rows = kv_exchange(summed_kv.reshape(devices, -1, 2 * half))
     own_smalls = jnp.sum(
         lax.all_to_all(packed, ("dp", "expert"), split_axis=0, concat_axis=0, tiled=True), axis=0
     )
+    own_smalls, kv_rows, summed_q = lax.optimization_barrier((own_smalls, kv_rows, summed_q))
     share = D // everyone
     shared_gain_one = own_smalls[:share]
     shared_gain_two = own_smalls[share : 2 * share]
     shared_att_router = own_smalls[2 * share : (2 + ATT_EXPERTS) * share].reshape(share, ATT_EXPERTS)
     shared_ffn_router = own_smalls[(2 + ATT_EXPERTS) * share :].reshape(share, FFN_EXPERTS)
 
-    kv_rows = exchange(summed_kv.reshape(devices, -1, 2 * half))
     kv_sum = jnp.sum(kv_rows.astype(f32).reshape(devices // 2, 2, -1, 2 * half), axis=0)
     shared_kv = jnp.concatenate(
         [kv_sum[n, :, m * half : (m + 1) * half] for m in range(2) for n in range(2)], axis=1

time: 1140 us -> 1130 us (level)
  waiting for transfers between devices: 133 us -> 91.8 us
  Pallas kernels: 688 us -> 729 us
  blocking collectives: 48.8 us -> 15.6 us
  starting transfers between devices: 17.1 us -> 41 us
    pallas_call x0 -> x1, Pallas kernels: none -> 38.4 us  [swap_blocks(): pl.pallas_call(swap_blocks_body, in_specs=[any_space], out_specs=any_spac...]
    all_to_all x1 -> x0, blocking collectives: 33.1 us -> none  [body(): lax.all_to_all(packed, ('dp', 'expert'), split_axis=0, concat_axis=0, til...]
    reduce_scatter x1, waiting for transfers between devices: 24.8 us -> 0.02 us  [body(): summed_q = lax.psum_scatter(grad_q, 'dp', scatter_dimension=0, tiled=True)]
    all_to_all x1, starting transfers between devices: 4.35 us -> 28.2 us  [body(): lax.all_to_all(packed, ('dp', 'expert'), split_axis=0, concat_axis=0, til...]
  transfers between devices with their start and end apart: 19 -> 19, of which waited for: 11 -> 8; matrix products, arithmetic and copies ran while one was open for 18% -> 18% of each run, Pallas kernels for 44% -> 48%
where the time goes in v9:
time: 1130 us; the launch traced here: 1120 us
  Pallas kernels  729 us (65%)
  matrix products  130 us (12%)
  waiting for transfers between devices  91.8 us (8%)
  other arithmetic  59.2 us (5%)
  starting transfers between devices  41 us (4%)
  local copies, waits for them, and re-layouts  35.4 us (3%)
  between operations  16.1 us (1%)
  blocking collectives  15.6 us (1%)
    pallas_call x1, Pallas kernels, ffn_forward(): pl.pallas_call(functools.partial(ffn_forward_body, chunk), in_specs=[any_...  147 us
    pallas_call x1, Pallas kernels, merge_return(): pl.pallas_call(functools.partial(merge_return_body, 'dp'), in_specs=[any_...  94.9 us
    pallas_call x1, Pallas kernels, send_rows(): pl.pallas_call(send_rows_body, in_specs=[any_space] * 2, out_specs=[any_s...  93 us
    pallas_call x1, Pallas kernels, ffn_backward(): pl.pallas_call(functools.partial(ffn_backward_body, chunk), in_specs=[any...  87.7 us
    pallas_call x1, Pallas kernels, attention_send(): pl.pallas_call(functools.partial(attention_send_body, HEAD ** (-0.5) * LO...  84.2 us
    pallas_call x1, Pallas kernels, attention_backward(): pl.pallas_call(functools.partial(attention_backward_body, sets, step_head...  83.3 us
    dot_general x4, matrix products, dot_tn(): lax.dot_general(left, right, (((0,), (0,)), ((), ())), preferred_element_...  73.8 us
    pallas_call x1, Pallas kernels, send_slots(): pl.pallas_call(send_slots_body, in_specs=[any_space] * 3, out_specs=[any_...  59 us
  transfers between devices with their start and end apart: 19, of which 8 were waited for; matrix products, arithmetic and copies ran while one was open for 18% of the time, Pallas kernels for 48%

profile of v9, /device:TPU:0, one launch (start us, length us, event | category | flops | bytes accessed | tf_op | source)
XLA Modules:
  0.0 1118.5 jit_solution(18440577603630254299)
XLA Ops:
  7.2 3.3 copy.63
  13.5 15.6 %all-gather.2 = s32[8,272,2]{1,2,0:T(2,128)S(1)} all-gather(s32[1,272,2]{1,2,0:T(2,128)S(1)} %bitcast.234), channel_id=2, replica_groups=mesh['dp'=4,'expert'=8] {'expert'}, dimensions={0}, use_global_device_ids=true | all-gather | bytes 19584 | tf_op jit(solution)/shard_map/all_gather | solution.py:1830
  32.1 2.3 select_reduce_fusion.6
  37.4 2.6 multiply_cosine_fusion.1
  48.7 3.9 fusion.45
  55.7 6.0 all-gather.7.cloned.1.call-done
  66.6 44.8 %collective-permute-done.1 = bf16[2048,512]{1,0:T(8,128)(2,1)S(1)} collective-permute-done((bf16[2048,512]{1,0:T(8,128)(2,1)S(1)}, bf16[2048,512]{1,0:T(8,128)(2,1)S(1)}, u32[]{:S(2)}, u32[]{:S(2)}) %collective-permute-start.1) | collective-permute-done | bytes 2097184 | tf_op jit(solution)/shard_map/ppermute | solution.py:1776
  119.2 18.2 %collective-permute-done.2 = bf16[1024,512]{1,0:T(8,128)(2,1)} collective-permute-done((bf16[1024,512]{1,0:T(8,128)(2,1)}, bf16[1024,512]{1,0:T(8,128)(2,1)}, u32[]{:S(2)}, u32[]{:S(2)}) %collective-permute-start.2) | collective-permute-done | bytes 1048608 | tf_op jit(solution)/shard_map/ppermute | solution.py:1778
  137.4 2.9 collective-permute-done.3
  142.0 3.9 pad_maximum_fusion.weight_ref.weight_hbm
  145.9 3.1 all-gather.11.cloned.1.call-done
  149.0 15.1 %project_queries.1 = (bf16[704,2048]{1,0:T(8,128)(2,1)}, bf16[704,2048]{1,0:T(8,128)(2,1)}) custom-call(bf16[8,88,272]{2,1,0:T(8,128)(2,1)} %copy.69.plan_ref, bf16[8,272,2048]{2,1,0:T(8,128)(2,1)} %bitcast.208, bf16[2048,2048]{1,0:T(8,128)(2,1)} %weight_ref.1, f32[704,128]{1,0:T(8,128)} %pad_maximum_fusion.5.cos_ref.refs_13_, ...), custom_call_target="tpu_custom_call" | custom-call | tf_op jit(solution)/shard_map/project_queries/pallas_call | solution.py:292
  164.1 2.6 constant_dynamic-slice_fusion.5
  167.4 26.6 %project_keys_values.1 = (bf16[2176,1024]{1,0:T(8,128)(2,1)}, bf16[2176,1024]{1,0:T(8,128)(2,1)}) custom-call(s32[4]{0:T(128)} %iota_xor_fusion.order_ref, bf16[8,272,2048]{2,1,0:T(8,128)(2,1)} %bitcast.209, bf16[4,2048,512]{2,1,0:T(8,128)(2,1)} %pad_maximum_fusion.weight_ref.weight_hbm, f32[2176,128]{1,0:T(8,128)} %pad_maximum_fusion.2.cos_ref.refs_11_, ...), custom_call_target="tpu_custom_call" | custom-call | tf_op jit(solution)/shard_map/project_keys_values/pallas_call | solution.py:330
  195.2 84.2 %attention_send.1 = (bf16[704,1024]{1,0:T(8,128)(2,1)}, bf16[704,1024]{1,0:T(8,128)(2,1)}, bf16[704,2048]{1,0:T(8,128)(2,1)}, bf16[8,88,2048]{2,1,0:T(8,128)(2,1)}, f32[8,4,1,352]{3,2,1,0:T(1,128)}) custom-call(bf16[704,2048]{1,0:T(8,128)(2,1)} %get-tuple-element.87.query_hbm.refs_0_, bf16[704,1024]{1,0:T(8,128)(2,1)} %copy-done.13, ...), custom_call_target="tpu_custom_call" | custom-call | tf_op jit(solution)/shard_map/attention_send/pallas_call | solution.py:1571
  281.6 3.8 convolution_bitcast_fusion.2
  289.4 3.3 convolution_convert_fusion.5.slots
  292.6 147.0 %ffn_forward.1 = (bf16[1408,2048]{1,0:T(8,128)(2,1)}, bf16[1408,2816]{1,0:T(8,128)(2,1)}, bf16[1408,2816]{1,0:T(8,128)(2,1)}, bf16[1408,2816]{1,0:T(8,128)(2,1)}, bf16[4,176,2048]{2,1,0:T(8,128)(2,1)}) custom-call(bf16[4,176,2048]{2,1,0:T(8,128)(2,1)} %convolution_convert_fusion.5.slots, bf16[2048,2816]{1,0:T(8,128)(2,1)} %gate_hbm.3, ...), custom_call_target="tpu_custom_call" | custom-call | tf_op jit(solution)/shard_map/ffn_forward/pallas_call | solution.py:796
  439.7 3.9 convolution_bitcast_fusion.1
  447.2 4.0 bitcast_convert_fusion.1.slots
  451.2 93.0 %send_rows.1 = (bf16[4,352,2048]{2,1,0:T(8,128)(2,1)}, bf16[2048,2816]{1,0:T(8,128)(2,1)}) custom-call(bf16[4,176,2048]{2,1,0:T(8,128)(2,1)} %bitcast_convert_fusion.1.slots, bf16[1408,2816]{1,0:T(8,128)(2,1)} %get-tuple-element.100.act_hbm), custom_call_target="tpu_custom_call" | custom-call | tf_op jit(solution)/shard_map/send_rows/pallas_call | solution.py:945
  544.3 87.7 %ffn_backward.1 = (bf16[1408,2816]{1,0:T(8,128)(2,1)}, bf16[1408,2816]{1,0:T(8,128)(2,1)}, bf16[4,176,2048]{2,1,0:T(8,128)(2,1)}) custom-call(bf16[1408,2048]{1,0:T(8,128)(2,1)} %bitcast.218, bf16[1408,2816]{1,0:T(8,128)(2,1)} %get-tuple-element.104.gate_in, bf16[1408,2816]{1,0:T(8,128)(2,1)} %get-tuple-element.105.up_in, bf16[2048,2816]{1,0:T(8,128)(2,1)} %gate_hbm.3, ...), custom_call_target="tpu_custom_call" | custom-call | tf_op jit(solution)/shard_map/ffn_backward/pallas_call | solution.py:1127
  632.0 24.6 %convolution_convert_fusion = bf16[2048,2816]{1,0:T(8,128)(2,1)} fusion(bf16[1408,2048]{1,0:T(8,128)(2,1)} %get-tuple-element.107.rows_hbm, bf16[1408,2816]{1,0:T(8,128)(2,1)} %get-tuple-element.108), kind=kOutput, calls=%fused_computation | convolution fusion | flops 16246112256 | bytes 25231360 | tf_op jit(solution)/shard_map/dot_general | solution.py:1784
  656.9 3.9 convolution_bitcast_fusion
  660.8 2.9 multiply_reduce_fusion
  666.8 4.0 bitcast_convert_fusion.slots
  670.8 59.0 %send_slots.1 = (bf16[8,88,2048]{2,1,0:T(8,128)(2,1)}, bf16[2048,2816]{1,0:T(8,128)(2,1)}) custom-call(bf16[8,88,2048]{2,1,0:T(8,128)(2,1)} %bitcast_convert_fusion.slots, bf16[1408,2048]{1,0:T(8,128)(2,1)} %get-tuple-element.107.rows_hbm, bf16[1408,2816]{1,0:T(8,128)(2,1)} %get-tuple-element.112.grads_hbm), custom_call_target="tpu_custom_call" | custom-call | tf_op jit(solution)/shard_map/send_slots/pallas_call | solution.py:1222
  729.9 9.5 convolution_convert_fusion.4.refs_2_
  743.5 2.6 collective-permute-done.5.refs_3_
  746.1 83.3 %attention_backward.1 = (bf16[704,1024]{1,0:T(8,128)(2,1)}, bf16[704,1024]{1,0:T(8,128)(2,1)}, bf16[2176,2048]{1,0:T(8,128)(2,1)}) custom-call(s32[2]{0:T(128)} %pad_add_fusion.1.first_ref, bf16[704,2048]{1,0:T(8,128)(2,1)} %get-tuple-element.87.query_hbm.refs_0_, bf16[704,1024]{1,0:T(8,128)(2,1)} %copy-done.13, bf16[704,2048]{1,0:T(8,128)(2,1)} %copy-done.12, ...), custom_call_target="tpu_custom_call" | custom-call | tf_op jit(solution)/shard_map/attention_backward/pallas_call | solution.py:221
  829.5 26.6 %convolution_convert_fusion.2 = bf16[2048,2048]{1,0:T(8,128)(2,1)} fusion(bf16[2176,2048]{1,0:T(8,128)(2,1)} %all-gather.11.cloned.1.call-done, bf16[2176,2048]{1,0:T(8,128)(2,1)} %get-tuple-element.128.grads_hbm), kind=kOutput, calls=%fused_computation.4 | convolution fusion | flops 18257805312 | bytes 26214400 | tf_op jit(solution)/shard_map/dot_general | solution.py:1784
  856.7 3.2 collective-permute-done.6
  859.9 11.9 %convolution_convert_fusion.1 = bf16[2048,2048]{1,0:T(8,128)(2,1)} fusion(bf16[704,2048]{1,0:T(8,128)(2,1)S(1)} %copy-done.40, bf16[704,1024]{1,0:T(8,128)(2,1)} %collective-permute-done.6, bf16[704,1024]{1,0:T(8,128)(2,1)} %get-tuple-element.124, pred[]{:T(512)S(6)} %eq.225), kind=kOutput, calls=%fused_computation.3 | convolution fusion | flops 5922750464 | bytes 14155777 | tf_op jit(solution)/shard_map/dot_general | solution.py:1784
  877.9 3.4 constant_dynamic-slice_fusion
  881.2 3.1 collective-permute-start.9
  884.9 3.3 convert_element_type.156
  888.2 3.3 convert_element_type.154
  893.4 9.8 convolution_convert_fusion.3
  903.2 10.7 reduce-scatter.10.cloned.1.call-done
  913.9 94.9 %merge_return.1 = bf16[4,272,2048]{2,1,0:T(8,128)(2,1)} custom-call(bf16[8,272,88]{2,1,0:T(8,128)(2,1)} %bitcast.219, bf16[8,88,2048]{2,1,0:T(8,128)(2,1)} %bitcast.223, bf16[2176,2048]{1,0:T(8,128)(2,1)} %get-tuple-element.128.grads_hbm, bf16[4,2048,512]{2,1,0:T(8,128)(2,1)} %pad_maximum_fusion.weight_ref.weight_hbm), custom_call_target="tpu_custom_call" | custom-call | tf_op jit(solution)/shard_map/merge_return/pallas_call | solution.py:1336
  1009.7 3.5 convert_reduce_fusion
  1013.2 3.9 fusion.21
  1019.0 10.7 fusion.4
  1030.5 28.2 %all-to-all-start = ((f32[32,1,896]{2,1,0:T(1,128)}), f32[32,1,896]{2,1,0:T(1,128)S(1)}, u32[]{:S(2)}, u32[]{:S(2)}) async-start(f32[32,1,896]{2,1,0:T(1,128)} %copy.72), calls=%async_computation.4 | async-start | bytes 229376 | tf_op jit(solution)/shard_map/all_to_all | solution.py:2088
  1058.7 3.2 fusion.20
  1061.9 38.4 %swap_blocks.1 = bf16[8,64,2048]{2,1,0:T(8,128)(2,1)} custom-call(bf16[8,64,2048]{2,1,0:T(8,128)(2,1)} %bitcast.227), custom_call_target="tpu_custom_call" | custom-call | tf_op jit(solution)/shard_map/swap_blocks/pallas_call | solution.py:1634
  1100.3 4.9 convert_element_type.155
  1107.9 2.5 convert_element_type.153
  (243 shorter events, 69.1 us)
Async XLA Ops:
  7.2 24.9 %copy-start = (f32[2048,8]{0,1:T(8,128)S(1)}, f32[2048,8]{0,1:T(8,128)}, u32[]{:S(2)}) copy-start(f32[2048,8]{0,1:T(8,128)} %param.24) | copy-start | bytes 196612
  7.2 54.5 %all-gather.7.cloned.1.call-start = ((), (), s32[]{:S(2)}) async-start(), calls=%async_computation.6 | async-start | bytes 4718592 | tf_op jit(solution)/shard_map/all_gather | solution.py:1828
  11.7 137.4 %all-gather.11.cloned.1.call-start = ((), (), s32[]{:S(2)}) async-start(), calls=%async_computation.13 | async-start | bytes 10027008 | tf_op jit(solution)/shard_map/all_gather | solution.py:1829
  12.1 17.3 %copy-start.34 = (f32[272]{0:T(512)}, f32[272]{0:T(512)S(1)}, u32[]{:S(2)}) copy-start(f32[272]{0:T(512)S(1)} %add_rsqrt_fusion.1) | copy-start | bytes 3268
  12.1 22.3 %copy-start.37 = (s32[1,13]{1,0:T(1,128)S(1)}, s32[1,13]{1,0:T(1,128)}, u32[]{:S(2)}) copy-start(s32[1,13]{1,0:T(1,128)} %param.20) | copy-start | bytes 160
  13.5 437.8 %all-gather.9.cloned.1.call-start = ((), (), s32[]{:S(2)}) async-start(), calls=%async_computation.7 | async-start | bytes 14417920 | tf_op jit(solution)/shard_map/all_gather | solution.py:1889
  32.0 12.0 %copy-start.27 = (pred[2,8,272]{2,1,0:T(8,128)(4,1)}, pred[2,8,272]{2,1,0:T(8,128)(4,1)S(1)}, u32[]{:S(2)}) copy-start(pred[2,8,272]{2,1,0:T(8,128)(4,1)S(1)} %iota_compare_fusion.13) | copy-start | bytes 13060
  40.0 3.8 copy-start.38
  43.9 237.7 %copy-start.32 = (f32[272,2]{0,1:T(2,128)}, f32[272,2]{0,1:T(2,128)S(1)}, u32[]{:S(2)}) copy-start(f32[272,2]{0,1:T(2,128)S(1)} %broadcast_divide_fusion.1) | copy-start | bytes 6532
  63.5 47.8 %collective-permute-start.1 = (bf16[2048,512]{1,0:T(8,128)(2,1)S(1)}, bf16[2048,512]{1,0:T(8,128)(2,1)S(1)}, u32[]{:S(2)}, u32[]{:S(2)}) collective-permute-start(bf16[2048,512]{1,0:T(8,128)(2,1)S(1)} %bitcast.215), channel_id=1, source_target_pairs={{0,16},{8,24},{16,0},{24,8},{1,17},{9,25},{17,1},{25,9},{2,18},{10... | collective-permute-start | bytes 6291464 | tf_op jit(solution)/shard_map/ppermute | solution.py:1776
  65.1 48.9 %collective-permute-start = (bf16[2048,512]{1,0:T(8,128)(2,1)S(1)}, bf16[2048,512]{1,0:T(8,128)(2,1)S(1)}, u32[]{:S(2)}, u32[]{:S(2)}) collective-permute-start(bf16[2048,512]{1,0:T(8,128)(2,1)S(1)} %bitcast.216), channel_id=1, source_target_pairs={{0,8},{8,0},{16,24},{24,16},{1,9},{9,1},{17,25},{25,17},{2,10},{10... | collective-permute-start | bytes 6291464 | tf_op jit(solution)/shard_map/ppermute | solution.py:1776
  111.4 2.6 copy-start.14
  112.5 24.9 %collective-permute-start.2 = (bf16[1024,512]{1,0:T(8,128)(2,1)}, bf16[1024,512]{1,0:T(8,128)(2,1)}, u32[]{:S(2)}, u32[]{:S(2)}) collective-permute-start(bf16[1024,512]{1,0:T(8,128)(2,1)} %slice.152), channel_id=1, source_target_pairs={{0,8},{8,0},{16,24},{24,16},{1,9},{9,1},{17,25},{25,17},{2,10},{10... | collective-permute-start | bytes 3145736 | tf_op jit(solution)/shard_map/ppermute | solution.py:1778
  115.6 24.6 %collective-permute-start.3 = (bf16[1024,512]{1,0:T(8,128)(2,1)}, bf16[1024,512]{1,0:T(8,128)(2,1)}, u32[]{:S(2)}, u32[]{:S(2)}) collective-permute-start(bf16[1024,512]{1,0:T(8,128)(2,1)} %slice.153), channel_id=1, source_target_pairs={{0,16},{8,24},{16,0},{24,8},{1,17},{9,25},{17,1},{25,9},{2,18},{10... | collective-permute-start | bytes 3145736 | tf_op jit(solution)/shard_map/ppermute | solution.py:1778
  119.2 22.7 %copy-start.15 = (bf16[2048,512]{1,0:T(8,128)(2,1)S(1)}, bf16[2048,512]{1,0:T(8,128)(2,1)}, u32[]{:S(2)}) copy-start(bf16[2048,512]{1,0:T(8,128)(2,1)} %copy-done.14) | copy-start | bytes 6291460
  119.2 22.7 %copy-start.17 = (bf16[2048,512]{1,0:T(8,128)(2,1)S(1)}, bf16[2048,512]{1,0:T(8,128)(2,1)}, u32[]{:S(2)}) copy-start(bf16[2048,512]{1,0:T(8,128)(2,1)} %copy-done.16) | copy-start | bytes 6291460
  166.7 27.3 %collective-permute-start.4 = (bf16[704,1024]{1,0:T(8,128)(2,1)}, bf16[704,1024]{1,0:T(8,128)(2,1)S(1)}, u32[]{:S(2)}, u32[]{:S(2)}) collective-permute-start(bf16[704,1024]{1,0:T(8,128)(2,1)} %constant_dynamic-slice_fusion.5), channel_id=1, source_target_pairs={{0,1},{1,0},{2,3},{3,2},{4,5},{5,4},{6,7},{7,6},{8,9},{9,8},{10,11... | collective-permute-start | bytes 4325384 | tf_op jit(solution)/shard_map/ppermute | solution.py:1866
  279.5 2.1 copy-start.22
  279.5 391.3 %reduce-scatter.6.cloned.1.call-start = ((), (), s32[]{:S(2)}) async-start(), calls=%async_computation.8 | async-start | bytes 14417920 | tf_op jit(solution)/shard_map/reduce_scatter | solution.py:1960
  439.7 3.9 copy-start.21
  544.3 285.2 %reduce-scatter.8.cloned.1.call-start = ((), (), s32[]{:S(2)}) async-start(), calls=%async_computation.9 | async-start | bytes 14417920 | tf_op jit(solution)/shard_map/reduce_scatter | solution.py:1981
  656.7 257.2 %reduce-scatter.10.cloned.1.call-start = ((), (), s32[]{:S(2)}) async-start(), calls=%async_computation.10 | async-start | bytes 14417920 | tf_op jit(solution)/shard_map/reduce_scatter | solution.py:2001
  656.8 6.9 slice-start
  656.8 6.9 slice-start.1
  660.8 2.9 copy-start.4
  729.9 279.0 %reduce-scatter.12.cloned.1.call-start = ((), (), s32[]{:S(2)}) async-start(), calls=%async_computation.11 | async-start | bytes 10485760 | tf_op jit(solution)/shard_map/reduce_scatter | solution.py:2038
  739.4 6.7 copy-start.12
  740.9 5.3 collective-permute-start.5
  856.1 3.8 copy-start.40
  856.2 249.2 %reduce-scatter.14.cloned.1.call-start = ((), (), s32[]{:S(2)}) async-start(), calls=%async_computation.12 | async-start | bytes 10485760 | tf_op jit(solution)/shard_map/reduce_scatter | solution.py:2039
  856.2 3.7 collective-permute-start.6
  871.8 3.6 copy-start.33
  871.9 3.7 copy-start.8
  871.9 3.7 copy-start.28
  877.9 7.0 copy-start.18
  881.2 127.6 %collective-permute-start.9 = (bf16[704,512]{1,0:T(8,128)(2,1)}, bf16[704,512]{1,0:T(8,128)(2,1)S(1)}, u32[]{:S(2)}, u32[]{:S(2)}) collective-permute-start(bf16[704,512]{1,0:T(8,128)(2,1)} %get-tuple-element.237), channel_id=1, source_target_pairs={{0,24},{8,16},{16,8},{24,0},{1,25},{9,17},{17,9},{25,1},{2,26},{10... | collective-permute-start | bytes 2162696 | tf_op jit(solution)/shard_map/ppermute | solution.py:2014
  884.3 124.5 %collective-permute-start.8 = (bf16[704,512]{1,0:T(8,128)(2,1)}, bf16[704,512]{1,0:T(8,128)(2,1)S(1)}, u32[]{:S(2)}, u32[]{:S(2)}) collective-permute-start(bf16[704,512]{1,0:T(8,128)(2,1)} %get-tuple-element.238), channel_id=1, source_target_pairs={{0,16},{8,24},{16,0},{24,8},{1,17},{9,25},{17,1},{25,9},{2,18},{10... | collective-permute-start | bytes 2162696 | tf_op jit(solution)/shard_map/ppermute | solution.py:2014
  884.3 3.9 copy-start.19
  884.3 124.6 %collective-permute-start.7 = (bf16[704,512]{1,0:T(8,128)(2,1)}, bf16[704,512]{1,0:T(8,128)(2,1)S(1)}, u32[]{:S(2)}, u32[]{:S(2)}) collective-permute-start(bf16[704,512]{1,0:T(8,128)(2,1)} %get-tuple-element.239), channel_id=1, source_target_pairs={{0,8},{8,0},{16,24},{24,16},{1,9},{9,1},{17,25},{25,17},{2,10},{10... | collective-permute-start | bytes 2162696 | tf_op jit(solution)/shard_map/ppermute | solution.py:2014
  884.9 6.7 slice-start.2
  888.2 4.8 slice-start.3
  888.2 5.1 copy-start.41
  1009.7 3.5 copy-start.2
  1009.7 3.5 copy-start.31
  1009.7 3.5 copy-start.35
  1019.0 39.6 %copy-start.6 = (f32[272,2048]{1,0:T(8,128)S(1)}, f32[272,2048]{1,0:T(8,128)}, u32[]{:S(2)}) copy-start(f32[272,2048]{1,0:T(8,128)} %copy-done.5) | copy-start | bytes 6684676
  1030.5 74.8 %all-to-all-start = ((f32[32,1,896]{2,1,0:T(1,128)}), f32[32,1,896]{2,1,0:T(1,128)S(1)}, u32[]{:S(2)}, u32[]{:S(2)}) async-start(f32[32,1,896]{2,1,0:T(1,128)} %copy.72), calls=%async_computation.4 | async-start | bytes 229376 | tf_op jit(solution)/shard_map/all_to_all | solution.py:2088
  1100.3 5.6 copy-start.11
  (17 other events, 24.5 us)
Sparse Core Ops, SparseCore 0:
  11.8 49.8 all-gather.6
  63.9 85.0 all-gather.10
  279.6 130.6 all-gather.8
  544.4 111.2 reduce-scatter.5
  658.6 119.5 reduce-scatter.7
  781.2 132.6 reduce-scatter.9
  917.0 90.6 reduce-scatter.11
  1011.0 87.6 reduce-scatter.13

commit v10 on v9

--- a/solution.py
+++ b/solution.py
@@ -471,7 +471,7 @@
 
     def sends(self, step):
         chip = self.sending(self.chip, step)
-        targets = [2 * chip, 2 * chip + 1] if step else [self.me + 1 - 2 * self.core]
+        targets = [2 * chip + self.core, 2 * chip + 1 - self.core] if step else [self.me + 1 - 2 * self.core]
         return [self.direct(target) for target in targets]
 
     def local(self):
@@ -576,7 +576,7 @@
 
     def each(self, step, own, other):
         chip = self.block(step)
-        for source in (2 * chip, 2 * chip + 1):
+        for source in (2 * chip + self.core, 2 * chip + 1 - self.core):
             if step not in self.own_steps:
                 other(source)
                 continue
@@ -1473,18 +1473,8 @@
         return pltpu.make_async_copy(sending.at[step, n], back.at[me], local_sem)
 
     def each(step, own, other):
-        for n in range(2):
-            if step < 3:
-                other(n)
-                continue
-
-            @pl.when(core == n)
-            def _(n=n):
-                own(n)
-
-            @pl.when(core != n)
-            def _(n=n):
-                other(n)
+        (own if step == 3 else other)(core)
+        other(1 - core)
 
     def attend(step):
         group = group_of(step)

time: 1130 us -> 1120 us (level)
    pallas_call x1, Pallas kernels: 93 us -> 79.8 us  [send_rows(): pl.pallas_call(send_rows_body, in_specs=[any_space] * 2, out_specs=[any_s...]
  transfers between devices with their start and end apart: 19 -> 19, of which waited for: 8 -> 8; matrix products, arithmetic and copies ran while one was open for 18% -> 18% of each run, Pallas kernels for 48% -> 49%
where the time goes in v10:
time: 1120 us; the launch traced here: 1110 us
  Pallas kernels  718 us (64%)
  matrix products  130 us (12%)
  waiting for transfers between devices  91.4 us (8%)
  other arithmetic  59.1 us (5%)
  starting transfers between devices  40.5 us (4%)
  local copies, waits for them, and re-layouts  35.6 us (3%)
  between operations  16.1 us (1%)
  blocking collectives  15.6 us (1%)
    pallas_call x1, Pallas kernels, ffn_forward(): pl.pallas_call(functools.partial(ffn_forward_body, chunk), in_specs=[any_...  148 us
    pallas_call x1, Pallas kernels, merge_return(): pl.pallas_call(functools.partial(merge_return_body, 'dp'), in_specs=[any_...  95.8 us
    pallas_call x1, Pallas kernels, ffn_backward(): pl.pallas_call(functools.partial(ffn_backward_body, chunk), in_specs=[any...  94.7 us
    pallas_call x1, Pallas kernels, attention_send(): pl.pallas_call(functools.partial(attention_send_body, HEAD ** (-0.5) * LO...  84.2 us
    pallas_call x1, Pallas kernels, attention_backward(): pl.pallas_call(functools.partial(attention_backward_body, sets, step_head...  83.3 us
    pallas_call x1, Pallas kernels, send_rows(): pl.pallas_call(send_rows_body, in_specs=[any_space] * 2, out_specs=[any_s...  79.8 us
    dot_general x4, matrix products, dot_tn(): lax.dot_general(left, right, (((0,), (0,)), ((), ())), preferred_element_...  74 us
    pallas_call x1, Pallas kernels, send_slots(): pl.pallas_call(send_slots_body, in_specs=[any_space] * 3, out_specs=[any_...  51.6 us
  transfers between devices with their start and end apart: 19, of which 8 were waited for; matrix products, arithmetic and copies ran while one was open for 18% of the time, Pallas kernels for 49%

profile of v10, /device:TPU:0, one launch (start us, length us, event | category | flops | bytes accessed | tf_op | source)
XLA Modules:
  0.0 1106.3 jit_solution(2858912476833515534)
XLA Ops:
  7.2 3.3 copy.63
  13.5 15.6 %all-gather.2 = s32[8,272,2]{1,2,0:T(2,128)S(1)} all-gather(s32[1,272,2]{1,2,0:T(2,128)S(1)} %bitcast.234), channel_id=2, replica_groups=mesh['dp'=4,'expert'=8] {'expert'}, dimensions={0}, use_global_device_ids=true | all-gather | bytes 19584 | tf_op jit(solution)/shard_map/all_gather | solution.py:1820
  32.1 2.3 select_reduce_fusion.6
  37.4 2.6 multiply_cosine_fusion.1
  48.7 3.9 fusion.45
  55.7 6.0 all-gather.7.cloned.1.call-done
  66.6 44.8 %collective-permute-done.1 = bf16[2048,512]{1,0:T(8,128)(2,1)S(1)} collective-permute-done((bf16[2048,512]{1,0:T(8,128)(2,1)S(1)}, bf16[2048,512]{1,0:T(8,128)(2,1)S(1)}, u32[]{:S(2)}, u32[]{:S(2)}) %collective-permute-start.1) | collective-permute-done | bytes 2097184 | tf_op jit(solution)/shard_map/ppermute | solution.py:1766
  119.2 18.2 %collective-permute-done.2 = bf16[1024,512]{1,0:T(8,128)(2,1)} collective-permute-done((bf16[1024,512]{1,0:T(8,128)(2,1)}, bf16[1024,512]{1,0:T(8,128)(2,1)}, u32[]{:S(2)}, u32[]{:S(2)}) %collective-permute-start.2) | collective-permute-done | bytes 1048608 | tf_op jit(solution)/shard_map/ppermute | solution.py:1768
  137.4 2.9 collective-permute-done.3
  142.0 3.9 pad_maximum_fusion.weight_ref.weight_hbm
  145.9 3.1 all-gather.11.cloned.1.call-done
  149.0 15.1 %project_queries.1 = (bf16[704,2048]{1,0:T(8,128)(2,1)}, bf16[704,2048]{1,0:T(8,128)(2,1)}) custom-call(bf16[8,88,272]{2,1,0:T(8,128)(2,1)} %copy.69.plan_ref, bf16[8,272,2048]{2,1,0:T(8,128)(2,1)} %bitcast.208, bf16[2048,2048]{1,0:T(8,128)(2,1)} %weight_ref.1, f32[704,128]{1,0:T(8,128)} %pad_maximum_fusion.5.cos_ref.refs_13_, ...), custom_call_target="tpu_custom_call" | custom-call | tf_op jit(solution)/shard_map/project_queries/pallas_call | solution.py:292
  164.1 2.6 constant_dynamic-slice_fusion.5
  167.4 26.6 %project_keys_values.1 = (bf16[2176,1024]{1,0:T(8,128)(2,1)}, bf16[2176,1024]{1,0:T(8,128)(2,1)}) custom-call(s32[4]{0:T(128)} %iota_xor_fusion.order_ref, bf16[8,272,2048]{2,1,0:T(8,128)(2,1)} %bitcast.209, bf16[4,2048,512]{2,1,0:T(8,128)(2,1)} %pad_maximum_fusion.weight_ref.weight_hbm, f32[2176,128]{1,0:T(8,128)} %pad_maximum_fusion.2.cos_ref.refs_11_, ...), custom_call_target="tpu_custom_call" | custom-call | tf_op jit(solution)/shard_map/project_keys_values/pallas_call | solution.py:330
  195.2 84.2 %attention_send.1 = (bf16[704,1024]{1,0:T(8,128)(2,1)}, bf16[704,1024]{1,0:T(8,128)(2,1)}, bf16[704,2048]{1,0:T(8,128)(2,1)}, bf16[8,88,2048]{2,1,0:T(8,128)(2,1)}, f32[8,4,1,352]{3,2,1,0:T(1,128)}) custom-call(bf16[704,2048]{1,0:T(8,128)(2,1)} %get-tuple-element.87.query_hbm.refs_0_, bf16[704,1024]{1,0:T(8,128)(2,1)} %copy-done.13, ...), custom_call_target="tpu_custom_call" | custom-call | tf_op jit(solution)/shard_map/attention_send/pallas_call | solution.py:1561
  281.6 3.8 convolution_bitcast_fusion.2
  289.4 3.3 convolution_convert_fusion.5.slots
  292.6 148.0 %ffn_forward.1 = (bf16[1408,2048]{1,0:T(8,128)(2,1)}, bf16[1408,2816]{1,0:T(8,128)(2,1)}, bf16[1408,2816]{1,0:T(8,128)(2,1)}, bf16[1408,2816]{1,0:T(8,128)(2,1)}, bf16[4,176,2048]{2,1,0:T(8,128)(2,1)}) custom-call(bf16[4,176,2048]{2,1,0:T(8,128)(2,1)} %convolution_convert_fusion.5.slots, bf16[2048,2816]{1,0:T(8,128)(2,1)} %gate_hbm.3, ...), custom_call_target="tpu_custom_call" | custom-call | tf_op jit(solution)/shard_map/ffn_forward/pallas_call | solution.py:796
  440.8 3.9 convolution_bitcast_fusion.1
  448.3 4.0 bitcast_convert_fusion.1.slots
  452.3 79.8 %send_rows.1 = (bf16[4,352,2048]{2,1,0:T(8,128)(2,1)}, bf16[2048,2816]{1,0:T(8,128)(2,1)}) custom-call(bf16[4,176,2048]{2,1,0:T(8,128)(2,1)} %bitcast_convert_fusion.1.slots, bf16[1408,2816]{1,0:T(8,128)(2,1)} %get-tuple-element.100.act_hbm), custom_call_target="tpu_custom_call" | custom-call | tf_op jit(solution)/shard_map/send_rows/pallas_call | solution.py:945
  532.2 94.7 %ffn_backward.1 = (bf16[1408,2816]{1,0:T(8,128)(2,1)}, bf16[1408,2816]{1,0:T(8,128)(2,1)}, bf16[4,176,2048]{2,1,0:T(8,128)(2,1)}) custom-call(bf16[1408,2048]{1,0:T(8,128)(2,1)} %bitcast.218, bf16[1408,2816]{1,0:T(8,128)(2,1)} %get-tuple-element.104.gate_in, bf16[1408,2816]{1,0:T(8,128)(2,1)} %get-tuple-element.105.up_in, bf16[2048,2816]{1,0:T(8,128)(2,1)} %gate_hbm.3, ...), custom_call_target="tpu_custom_call" | custom-call | tf_op jit(solution)/shard_map/ffn_backward/pallas_call | solution.py:1127
  626.9 24.8 %convolution_convert_fusion = bf16[2048,2816]{1,0:T(8,128)(2,1)} fusion(bf16[1408,2048]{1,0:T(8,128)(2,1)} %get-tuple-element.107.rows_hbm, bf16[1408,2816]{1,0:T(8,128)(2,1)} %get-tuple-element.108), kind=kOutput, calls=%fused_computation | convolution fusion | flops 16246112256 | bytes 25231360 | tf_op jit(solution)/shard_map/dot_general | solution.py:1774
  652.0 3.9 convolution_bitcast_fusion
  655.9 2.9 multiply_reduce_fusion
  662.0 4.0 bitcast_convert_fusion.slots
  666.0 51.6 %send_slots.1 = (bf16[8,88,2048]{2,1,0:T(8,128)(2,1)}, bf16[2048,2816]{1,0:T(8,128)(2,1)}) custom-call(bf16[8,88,2048]{2,1,0:T(8,128)(2,1)} %bitcast_convert_fusion.slots, bf16[1408,2048]{1,0:T(8,128)(2,1)} %get-tuple-element.107.rows_hbm, bf16[1408,2816]{1,0:T(8,128)(2,1)} %get-tuple-element.112.grads_hbm), custom_call_target="tpu_custom_call" | custom-call | tf_op jit(solution)/shard_map/send_slots/pallas_call | solution.py:1222
  717.7 9.5 convolution_convert_fusion.4.refs_2_
  731.5 2.6 collective-permute-done.5.refs_3_
  734.1 83.3 %attention_backward.1 = (bf16[704,1024]{1,0:T(8,128)(2,1)}, bf16[704,1024]{1,0:T(8,128)(2,1)}, bf16[2176,2048]{1,0:T(8,128)(2,1)}) custom-call(s32[2]{0:T(128)} %pad_add_fusion.1.first_ref, bf16[704,2048]{1,0:T(8,128)(2,1)} %get-tuple-element.87.query_hbm.refs_0_, bf16[704,1024]{1,0:T(8,128)(2,1)} %copy-done.13, bf16[704,2048]{1,0:T(8,128)(2,1)} %copy-done.12, ...), custom_call_target="tpu_custom_call" | custom-call | tf_op jit(solution)/shard_map/attention_backward/pallas_call | solution.py:221
  817.5 26.6 %convolution_convert_fusion.2 = bf16[2048,2048]{1,0:T(8,128)(2,1)} fusion(bf16[2176,2048]{1,0:T(8,128)(2,1)} %all-gather.11.cloned.1.call-done, bf16[2176,2048]{1,0:T(8,128)(2,1)} %get-tuple-element.128.grads_hbm), kind=kOutput, calls=%fused_computation.4 | convolution fusion | flops 18257805312 | bytes 26214400 | tf_op jit(solution)/shard_map/dot_general | solution.py:1774
  844.7 3.2 collective-permute-done.6
  847.9 11.9 %convolution_convert_fusion.1 = bf16[2048,2048]{1,0:T(8,128)(2,1)} fusion(bf16[704,2048]{1,0:T(8,128)(2,1)S(1)} %copy-done.40, bf16[704,1024]{1,0:T(8,128)(2,1)} %collective-permute-done.6, bf16[704,1024]{1,0:T(8,128)(2,1)} %get-tuple-element.124, pred[]{:T(512)S(6)} %eq.225), kind=kOutput, calls=%fused_computation.3 | convolution fusion | flops 5922750464 | bytes 14155777 | tf_op jit(solution)/shard_map/dot_general | solution.py:1774
  865.9 3.3 constant_dynamic-slice_fusion
  869.2 3.0 collective-permute-start.9
  872.8 3.3 convert_element_type.156
  876.1 3.3 convert_element_type.154
  881.3 9.8 convolution_convert_fusion.3
  891.1 10.4 reduce-scatter.10.cloned.1.call-done
  901.5 95.8 %merge_return.1 = bf16[4,272,2048]{2,1,0:T(8,128)(2,1)} custom-call(bf16[8,272,88]{2,1,0:T(8,128)(2,1)} %bitcast.219, bf16[8,88,2048]{2,1,0:T(8,128)(2,1)} %bitcast.223, bf16[2176,2048]{1,0:T(8,128)(2,1)} %get-tuple-element.128.grads_hbm, bf16[4,2048,512]{2,1,0:T(8,128)(2,1)} %pad_maximum_fusion.weight_ref.weight_hbm), custom_call_target="tpu_custom_call" | custom-call | tf_op jit(solution)/shard_map/merge_return/pallas_call | solution.py:1336
  998.2 3.5 convert_reduce_fusion
  1001.7 3.9 fusion.21
  1007.4 10.7 fusion.4
  1018.9 27.5 %all-to-all-start = ((f32[32,1,896]{2,1,0:T(1,128)}), f32[32,1,896]{2,1,0:T(1,128)S(1)}, u32[]{:S(2)}, u32[]{:S(2)}) async-start(f32[32,1,896]{2,1,0:T(1,128)} %copy.72), calls=%async_computation.4 | async-start | bytes 229376 | tf_op jit(solution)/shard_map/all_to_all | solution.py:2078
  1046.4 3.2 fusion.20
  1049.7 38.4 %swap_blocks.1 = bf16[8,64,2048]{2,1,0:T(8,128)(2,1)} custom-call(bf16[8,64,2048]{2,1,0:T(8,128)(2,1)} %bitcast.227), custom_call_target="tpu_custom_call" | custom-call | tf_op jit(solution)/shard_map/swap_blocks/pallas_call | solution.py:1624
  1088.1 4.9 convert_element_type.155
  1095.7 2.5 convert_element_type.153
  (243 shorter events, 69.4 us)
Async XLA Ops:
  7.2 24.9 %copy-start = (f32[2048,8]{0,1:T(8,128)S(1)}, f32[2048,8]{0,1:T(8,128)}, u32[]{:S(2)}) copy-start(f32[2048,8]{0,1:T(8,128)} %param.24) | copy-start | bytes 196612
  7.2 54.5 %all-gather.7.cloned.1.call-start = ((), (), s32[]{:S(2)}) async-start(), calls=%async_computation.6 | async-start | bytes 4718592 | tf_op jit(solution)/shard_map/all_gather | solution.py:1818
  11.7 137.4 %all-gather.11.cloned.1.call-start = ((), (), s32[]{:S(2)}) async-start(), calls=%async_computation.13 | async-start | bytes 10027008 | tf_op jit(solution)/shard_map/all_gather | solution.py:1819
  12.1 17.3 %copy-start.34 = (f32[272]{0:T(512)}, f32[272]{0:T(512)S(1)}, u32[]{:S(2)}) copy-start(f32[272]{0:T(512)S(1)} %add_rsqrt_fusion.1) | copy-start | bytes 3268
  12.1 22.3 %copy-start.37 = (s32[1,13]{1,0:T(1,128)S(1)}, s32[1,13]{1,0:T(1,128)}, u32[]{:S(2)}) copy-start(s32[1,13]{1,0:T(1,128)} %param.20) | copy-start | bytes 160
  13.5 438.8 %all-gather.9.cloned.1.call-start = ((), (), s32[]{:S(2)}) async-start(), calls=%async_computation.7 | async-start | bytes 14417920 | tf_op jit(solution)/shard_map/all_gather | solution.py:1879
  32.0 12.0 %copy-start.27 = (pred[2,8,272]{2,1,0:T(8,128)(4,1)}, pred[2,8,272]{2,1,0:T(8,128)(4,1)S(1)}, u32[]{:S(2)}) copy-start(pred[2,8,272]{2,1,0:T(8,128)(4,1)S(1)} %iota_compare_fusion.13) | copy-start | bytes 13060
  40.0 3.8 copy-start.38
  43.9 237.7 %copy-start.32 = (f32[272,2]{0,1:T(2,128)}, f32[272,2]{0,1:T(2,128)S(1)}, u32[]{:S(2)}) copy-start(f32[272,2]{0,1:T(2,128)S(1)} %broadcast_divide_fusion.1) | copy-start | bytes 6532
  63.5 47.8 %collective-permute-start.1 = (bf16[2048,512]{1,0:T(8,128)(2,1)S(1)}, bf16[2048,512]{1,0:T(8,128)(2,1)S(1)}, u32[]{:S(2)}, u32[]{:S(2)}) collective-permute-start(bf16[2048,512]{1,0:T(8,128)(2,1)S(1)} %bitcast.215), channel_id=1, source_target_pairs={{0,16},{8,24},{16,0},{24,8},{1,17},{9,25},{17,1},{25,9},{2,18},{10... | collective-permute-start | bytes 6291464 | tf_op jit(solution)/shard_map/ppermute | solution.py:1766
  65.1 48.9 %collective-permute-start = (bf16[2048,512]{1,0:T(8,128)(2,1)S(1)}, bf16[2048,512]{1,0:T(8,128)(2,1)S(1)}, u32[]{:S(2)}, u32[]{:S(2)}) collective-permute-start(bf16[2048,512]{1,0:T(8,128)(2,1)S(1)} %bitcast.216), channel_id=1, source_target_pairs={{0,8},{8,0},{16,24},{24,16},{1,9},{9,1},{17,25},{25,17},{2,10},{10... | collective-permute-start | bytes 6291464 | tf_op jit(solution)/shard_map/ppermute | solution.py:1766
  111.4 2.6 copy-start.14
  112.5 24.9 %collective-permute-start.2 = (bf16[1024,512]{1,0:T(8,128)(2,1)}, bf16[1024,512]{1,0:T(8,128)(2,1)}, u32[]{:S(2)}, u32[]{:S(2)}) collective-permute-start(bf16[1024,512]{1,0:T(8,128)(2,1)} %slice.152), channel_id=1, source_target_pairs={{0,8},{8,0},{16,24},{24,16},{1,9},{9,1},{17,25},{25,17},{2,10},{10... | collective-permute-start | bytes 3145736 | tf_op jit(solution)/shard_map/ppermute | solution.py:1768
  115.6 24.6 %collective-permute-start.3 = (bf16[1024,512]{1,0:T(8,128)(2,1)}, bf16[1024,512]{1,0:T(8,128)(2,1)}, u32[]{:S(2)}, u32[]{:S(2)}) collective-permute-start(bf16[1024,512]{1,0:T(8,128)(2,1)} %slice.153), channel_id=1, source_target_pairs={{0,16},{8,24},{16,0},{24,8},{1,17},{9,25},{17,1},{25,9},{2,18},{10... | collective-permute-start | bytes 3145736 | tf_op jit(solution)/shard_map/ppermute | solution.py:1768
  119.2 22.7 %copy-start.15 = (bf16[2048,512]{1,0:T(8,128)(2,1)S(1)}, bf16[2048,512]{1,0:T(8,128)(2,1)}, u32[]{:S(2)}) copy-start(bf16[2048,512]{1,0:T(8,128)(2,1)} %copy-done.14) | copy-start | bytes 6291460
  119.2 22.7 %copy-start.17 = (bf16[2048,512]{1,0:T(8,128)(2,1)S(1)}, bf16[2048,512]{1,0:T(8,128)(2,1)}, u32[]{:S(2)}) copy-start(bf16[2048,512]{1,0:T(8,128)(2,1)} %copy-done.16) | copy-start | bytes 6291460
  166.7 27.3 %collective-permute-start.4 = (bf16[704,1024]{1,0:T(8,128)(2,1)}, bf16[704,1024]{1,0:T(8,128)(2,1)S(1)}, u32[]{:S(2)}, u32[]{:S(2)}) collective-permute-start(bf16[704,1024]{1,0:T(8,128)(2,1)} %constant_dynamic-slice_fusion.5), channel_id=1, source_target_pairs={{0,1},{1,0},{2,3},{3,2},{4,5},{5,4},{6,7},{7,6},{8,9},{9,8},{10,11... | collective-permute-start | bytes 4325384 | tf_op jit(solution)/shard_map/ppermute | solution.py:1856
  279.5 386.5 %reduce-scatter.6.cloned.1.call-start = ((), (), s32[]{:S(2)}) async-start(), calls=%async_computation.8 | async-start | bytes 14417920 | tf_op jit(solution)/shard_map/reduce_scatter | solution.py:1950
  440.7 3.9 copy-start.21
  532.1 285.3 %reduce-scatter.8.cloned.1.call-start = ((), (), s32[]{:S(2)}) async-start(), calls=%async_computation.9 | async-start | bytes 14417920 | tf_op jit(solution)/shard_map/reduce_scatter | solution.py:1971
  651.8 249.8 %reduce-scatter.10.cloned.1.call-start = ((), (), s32[]{:S(2)}) async-start(), calls=%async_computation.10 | async-start | bytes 14417920 | tf_op jit(solution)/shard_map/reduce_scatter | solution.py:1991
  651.9 6.9 slice-start
  651.9 6.9 slice-start.1
  655.9 2.9 copy-start.4
  659.9 2.1 copy-start.23
  717.6 279.7 %reduce-scatter.12.cloned.1.call-start = ((), (), s32[]{:S(2)}) async-start(), calls=%async_computation.11 | async-start | bytes 10485760 | tf_op jit(solution)/shard_map/reduce_scatter | solution.py:2028
  727.2 6.9 copy-start.12
  728.6 5.5 collective-permute-start.5
  844.1 3.8 copy-start.40
  844.1 249.0 %reduce-scatter.14.cloned.1.call-start = ((), (), s32[]{:S(2)}) async-start(), calls=%async_computation.12 | async-start | bytes 10485760 | tf_op jit(solution)/shard_map/reduce_scatter | solution.py:2029
  844.2 3.8 collective-permute-start.6
  859.9 3.6 copy-start.33
  859.9 3.7 copy-start.8
  859.9 3.7 copy-start.28
  865.9 6.9 copy-start.18
  869.2 128.1 %collective-permute-start.9 = (bf16[704,512]{1,0:T(8,128)(2,1)}, bf16[704,512]{1,0:T(8,128)(2,1)S(1)}, u32[]{:S(2)}, u32[]{:S(2)}) collective-permute-start(bf16[704,512]{1,0:T(8,128)(2,1)} %get-tuple-element.237), channel_id=1, source_target_pairs={{0,24},{8,16},{16,8},{24,0},{1,25},{9,17},{17,9},{25,1},{2,26},{10... | collective-permute-start | bytes 2162696 | tf_op jit(solution)/shard_map/ppermute | solution.py:2004
  872.2 125.1 %collective-permute-start.8 = (bf16[704,512]{1,0:T(8,128)(2,1)}, bf16[704,512]{1,0:T(8,128)(2,1)S(1)}, u32[]{:S(2)}, u32[]{:S(2)}) collective-permute-start(bf16[704,512]{1,0:T(8,128)(2,1)} %get-tuple-element.238), channel_id=1, source_target_pairs={{0,16},{8,24},{16,0},{24,8},{1,17},{9,25},{17,1},{25,9},{2,18},{10... | collective-permute-start | bytes 2162696 | tf_op jit(solution)/shard_map/ppermute | solution.py:2004
  872.3 3.8 copy-start.19
  872.3 125.0 %collective-permute-start.7 = (bf16[704,512]{1,0:T(8,128)(2,1)}, bf16[704,512]{1,0:T(8,128)(2,1)S(1)}, u32[]{:S(2)}, u32[]{:S(2)}) collective-permute-start(bf16[704,512]{1,0:T(8,128)(2,1)} %get-tuple-element.239), channel_id=1, source_target_pairs={{0,8},{8,0},{16,24},{24,16},{1,9},{9,1},{17,25},{25,17},{2,10},{10... | collective-permute-start | bytes 2162696 | tf_op jit(solution)/shard_map/ppermute | solution.py:2004
  872.8 6.7 slice-start.2
  876.1 4.8 slice-start.3
  876.1 5.2 copy-start.41
  998.2 3.5 copy-start.2
  998.2 3.5 copy-start.31
  998.2 3.5 copy-start.35
  1007.4 39.0 %copy-start.6 = (f32[272,2048]{1,0:T(8,128)S(1)}, f32[272,2048]{1,0:T(8,128)}, u32[]{:S(2)}) copy-start(f32[272,2048]{1,0:T(8,128)} %copy-done.5) | copy-start | bytes 6684676
  1018.9 74.1 %all-to-all-start = ((f32[32,1,896]{2,1,0:T(1,128)}), f32[32,1,896]{2,1,0:T(1,128)S(1)}, u32[]{:S(2)}, u32[]{:S(2)}) async-start(f32[32,1,896]{2,1,0:T(1,128)} %copy.72), calls=%async_computation.4 | async-start | bytes 229376 | tf_op jit(solution)/shard_map/all_to_all | solution.py:2078
  1088.1 5.6 copy-start.11
  (17 other events, 24.6 us)
Sparse Core Ops, SparseCore 0:
  11.8 49.8 all-gather.6
  63.9 85.0 all-gather.10
  279.6 131.1 all-gather.8
  532.2 111.1 reduce-scatter.5
  651.9 114.1 reduce-scatter.7
  769.0 132.4 reduce-scatter.9
  904.6 90.7 reduce-scatter.11
  998.8 87.6 reduce-scatter.13

commit v11 on v10

--- a/solution.py
+++ b/solution.py
@@ -502,7 +502,7 @@
 
     def arrive(self, step):
         chip = self.order(self.chip, step)
-        for source in (2 * chip, 2 * chip + 1):
+        for source in (2 * chip + self.core, 2 * chip + 1 - self.core):
             offset = lax.rem(self.me - source + 8, 8)
 
             @pl.when(offset == 0)

time: 1120 us -> 1120 us (level)
  no operation moved by 1% of the time
where the time goes in v11:
time: 1120 us; the launch traced here: 1110 us
  Pallas kernels  717 us (64%)
  matrix products  130 us (12%)
  waiting for transfers between devices  91.4 us (8%)
  other arithmetic  59.1 us (5%)
  starting transfers between devices  40.6 us (4%)
  local copies, waits for them, and re-layouts  35.6 us (3%)
  between operations  16.1 us (1%)
  blocking collectives  15.6 us (1%)
    pallas_call x1, Pallas kernels, ffn_forward(): pl.pallas_call(functools.partial(ffn_forward_body, chunk), in_specs=[any_...  148 us
    pallas_call x1, Pallas kernels, merge_return(): pl.pallas_call(functools.partial(merge_return_body, 'dp'), in_specs=[any_...  95.8 us
    pallas_call x1, Pallas kernels, ffn_backward(): pl.pallas_call(functools.partial(ffn_backward_body, chunk), in_specs=[any...  94.7 us
    pallas_call x1, Pallas kernels, attention_send(): pl.pallas_call(functools.partial(attention_send_body, HEAD ** (-0.5) * LO...  84.2 us
    pallas_call x1, Pallas kernels, attention_backward(): pl.pallas_call(functools.partial(attention_backward_body, sets, step_head...  83.3 us
    pallas_call x1, Pallas kernels, send_rows(): pl.pallas_call(send_rows_body, in_specs=[any_space] * 2, out_specs=[any_s...  79.3 us
    dot_general x4, matrix products, dot_tn(): lax.dot_general(left, right, (((0,), (0,)), ((), ())), preferred_element_...  74 us
    pallas_call x1, Pallas kernels, send_slots(): pl.pallas_call(send_slots_body, in_specs=[any_space] * 3, out_specs=[any_...  51.6 us
  transfers between devices with their start and end apart: 19, of which 8 were waited for; matrix products, arithmetic and copies ran while one was open for 18% of the time, Pallas kernels for 49%

profile of v11, /device:TPU:0, one launch (start us, length us, event | category | flops | bytes accessed | tf_op | source)
XLA Modules:
  0.0 1105.9 jit_solution(14120942747121749973)
XLA Ops:
  7.2 3.3 copy.63
  13.5 15.6 %all-gather.2 = s32[8,272,2]{1,2,0:T(2,128)S(1)} all-gather(s32[1,272,2]{1,2,0:T(2,128)S(1)} %bitcast.234), channel_id=2, replica_groups=mesh['dp'=4,'expert'=8] {'expert'}, dimensions={0}, use_global_device_ids=true | all-gather | bytes 19584 | tf_op jit(solution)/shard_map/all_gather | solution.py:1820
  37.4 2.6 multiply_cosine_fusion.1
  48.7 3.9 fusion.45
  55.7 6.0 all-gather.7.cloned.1.call-done
  66.6 44.8 %collective-permute-done.1 = bf16[2048,512]{1,0:T(8,128)(2,1)S(1)} collective-permute-done((bf16[2048,512]{1,0:T(8,128)(2,1)S(1)}, bf16[2048,512]{1,0:T(8,128)(2,1)S(1)}, u32[]{:S(2)}, u32[]{:S(2)}) %collective-permute-start.1) | collective-permute-done | bytes 2097184 | tf_op jit(solution)/shard_map/ppermute | solution.py:1766
  119.2 18.2 %collective-permute-done.2 = bf16[1024,512]{1,0:T(8,128)(2,1)} collective-permute-done((bf16[1024,512]{1,0:T(8,128)(2,1)}, bf16[1024,512]{1,0:T(8,128)(2,1)}, u32[]{:S(2)}, u32[]{:S(2)}) %collective-permute-start.2) | collective-permute-done | bytes 1048608 | tf_op jit(solution)/shard_map/ppermute | solution.py:1768
  137.4 2.9 collective-permute-done.3
  142.0 3.9 pad_maximum_fusion.weight_ref.weight_hbm
  145.9 3.1 all-gather.11.cloned.1.call-done
  149.0 15.1 %project_queries.1 = (bf16[704,2048]{1,0:T(8,128)(2,1)}, bf16[704,2048]{1,0:T(8,128)(2,1)}) custom-call(bf16[8,88,272]{2,1,0:T(8,128)(2,1)} %copy.69.plan_ref, bf16[8,272,2048]{2,1,0:T(8,128)(2,1)} %bitcast.208, bf16[2048,2048]{1,0:T(8,128)(2,1)} %weight_ref.1, f32[704,128]{1,0:T(8,128)} %pad_maximum_fusion.5.cos_ref.refs_13_, ...), custom_call_target="tpu_custom_call" | custom-call | tf_op jit(solution)/shard_map/project_queries/pallas_call | solution.py:292
  164.1 2.6 constant_dynamic-slice_fusion.5
  167.4 26.6 %project_keys_values.1 = (bf16[2176,1024]{1,0:T(8,128)(2,1)}, bf16[2176,1024]{1,0:T(8,128)(2,1)}) custom-call(s32[4]{0:T(128)} %iota_xor_fusion.order_ref, bf16[8,272,2048]{2,1,0:T(8,128)(2,1)} %bitcast.209, bf16[4,2048,512]{2,1,0:T(8,128)(2,1)} %pad_maximum_fusion.weight_ref.weight_hbm, f32[2176,128]{1,0:T(8,128)} %pad_maximum_fusion.2.cos_ref.refs_11_, ...), custom_call_target="tpu_custom_call" | custom-call | tf_op jit(solution)/shard_map/project_keys_values/pallas_call | solution.py:330
  195.2 84.2 %attention_send.1 = (bf16[704,1024]{1,0:T(8,128)(2,1)}, bf16[704,1024]{1,0:T(8,128)(2,1)}, bf16[704,2048]{1,0:T(8,128)(2,1)}, bf16[8,88,2048]{2,1,0:T(8,128)(2,1)}, f32[8,4,1,352]{3,2,1,0:T(1,128)}) custom-call(bf16[704,2048]{1,0:T(8,128)(2,1)} %get-tuple-element.87.query_hbm.refs_0_, bf16[704,1024]{1,0:T(8,128)(2,1)} %copy-done.13, ...), custom_call_target="tpu_custom_call" | custom-call | tf_op jit(solution)/shard_map/attention_send/pallas_call | solution.py:1561
  281.6 3.8 convolution_bitcast_fusion.2
  289.4 3.3 convolution_convert_fusion.5.slots
  292.6 148.0 %ffn_forward.1 = (bf16[1408,2048]{1,0:T(8,128)(2,1)}, bf16[1408,2816]{1,0:T(8,128)(2,1)}, bf16[1408,2816]{1,0:T(8,128)(2,1)}, bf16[1408,2816]{1,0:T(8,128)(2,1)}, bf16[4,176,2048]{2,1,0:T(8,128)(2,1)}) custom-call(bf16[4,176,2048]{2,1,0:T(8,128)(2,1)} %convolution_convert_fusion.5.slots, bf16[2048,2816]{1,0:T(8,128)(2,1)} %gate_hbm.3, ...), custom_call_target="tpu_custom_call" | custom-call | tf_op jit(solution)/shard_map/ffn_forward/pallas_call | solution.py:796
  440.8 3.9 convolution_bitcast_fusion.1
  448.3 4.0 bitcast_convert_fusion.1.slots
  452.3 79.3 %send_rows.1 = (bf16[4,352,2048]{2,1,0:T(8,128)(2,1)}, bf16[2048,2816]{1,0:T(8,128)(2,1)}) custom-call(bf16[4,176,2048]{2,1,0:T(8,128)(2,1)} %bitcast_convert_fusion.1.slots, bf16[1408,2816]{1,0:T(8,128)(2,1)} %get-tuple-element.100.act_hbm), custom_call_target="tpu_custom_call" | custom-call | tf_op jit(solution)/shard_map/send_rows/pallas_call | solution.py:945
  531.7 94.7 %ffn_backward.1 = (bf16[1408,2816]{1,0:T(8,128)(2,1)}, bf16[1408,2816]{1,0:T(8,128)(2,1)}, bf16[4,176,2048]{2,1,0:T(8,128)(2,1)}) custom-call(bf16[1408,2048]{1,0:T(8,128)(2,1)} %bitcast.218, bf16[1408,2816]{1,0:T(8,128)(2,1)} %get-tuple-element.104.gate_in, bf16[1408,2816]{1,0:T(8,128)(2,1)} %get-tuple-element.105.up_in, bf16[2048,2816]{1,0:T(8,128)(2,1)} %gate_hbm.3, ...), custom_call_target="tpu_custom_call" | custom-call | tf_op jit(solution)/shard_map/ffn_backward/pallas_call | solution.py:1127
  626.4 24.8 %convolution_convert_fusion = bf16[2048,2816]{1,0:T(8,128)(2,1)} fusion(bf16[1408,2048]{1,0:T(8,128)(2,1)} %get-tuple-element.107.rows_hbm, bf16[1408,2816]{1,0:T(8,128)(2,1)} %get-tuple-element.108), kind=kOutput, calls=%fused_computation | convolution fusion | flops 16246112256 | bytes 25231360 | tf_op jit(solution)/shard_map/dot_general | solution.py:1774
  651.5 3.9 convolution_bitcast_fusion
  655.4 2.9 multiply_reduce_fusion
  661.5 4.0 bitcast_convert_fusion.slots
  665.5 51.6 %send_slots.1 = (bf16[8,88,2048]{2,1,0:T(8,128)(2,1)}, bf16[2048,2816]{1,0:T(8,128)(2,1)}) custom-call(bf16[8,88,2048]{2,1,0:T(8,128)(2,1)} %bitcast_convert_fusion.slots, bf16[1408,2048]{1,0:T(8,128)(2,1)} %get-tuple-element.107.rows_hbm, bf16[1408,2816]{1,0:T(8,128)(2,1)} %get-tuple-element.112.grads_hbm), custom_call_target="tpu_custom_call" | custom-call | tf_op jit(solution)/shard_map/send_slots/pallas_call | solution.py:1222
  717.2 9.5 convolution_convert_fusion.4.refs_2_
  728.2 2.3 collective-permute-start.5
  731.0 2.6 collective-permute-done.5.refs_3_
  733.6 83.3 %attention_backward.1 = (bf16[704,1024]{1,0:T(8,128)(2,1)}, bf16[704,1024]{1,0:T(8,128)(2,1)}, bf16[2176,2048]{1,0:T(8,128)(2,1)}) custom-call(s32[2]{0:T(128)} %pad_add_fusion.1.first_ref, bf16[704,2048]{1,0:T(8,128)(2,1)} %get-tuple-element.87.query_hbm.refs_0_, bf16[704,1024]{1,0:T(8,128)(2,1)} %copy-done.13, bf16[704,2048]{1,0:T(8,128)(2,1)} %copy-done.12, ...), custom_call_target="tpu_custom_call" | custom-call | tf_op jit(solution)/shard_map/attention_backward/pallas_call | solution.py:221
  817.0 26.6 %convolution_convert_fusion.2 = bf16[2048,2048]{1,0:T(8,128)(2,1)} fusion(bf16[2176,2048]{1,0:T(8,128)(2,1)} %all-gather.11.cloned.1.call-done, bf16[2176,2048]{1,0:T(8,128)(2,1)} %get-tuple-element.128.grads_hbm), kind=kOutput, calls=%fused_computation.4 | convolution fusion | flops 18257805312 | bytes 26214400 | tf_op jit(solution)/shard_map/dot_general | solution.py:1774
  844.2 3.2 collective-permute-done.6
  847.4 11.9 %convolution_convert_fusion.1 = bf16[2048,2048]{1,0:T(8,128)(2,1)} fusion(bf16[704,2048]{1,0:T(8,128)(2,1)S(1)} %copy-done.40, bf16[704,1024]{1,0:T(8,128)(2,1)} %collective-permute-done.6, bf16[704,1024]{1,0:T(8,128)(2,1)} %get-tuple-element.124, pred[]{:T(512)S(6)} %eq.225), kind=kOutput, calls=%fused_computation.3 | convolution fusion | flops 5922750464 | bytes 14155777 | tf_op jit(solution)/shard_map/dot_general | solution.py:1774
  865.4 3.3 constant_dynamic-slice_fusion
  868.7 3.0 collective-permute-start.9
  872.3 3.3 convert_element_type.156
  875.7 3.3 convert_element_type.154
  880.9 9.8 convolution_convert_fusion.3
  890.7 10.4 reduce-scatter.10.cloned.1.call-done
  901.1 95.8 %merge_return.1 = bf16[4,272,2048]{2,1,0:T(8,128)(2,1)} custom-call(bf16[8,272,88]{2,1,0:T(8,128)(2,1)} %bitcast.219, bf16[8,88,2048]{2,1,0:T(8,128)(2,1)} %bitcast.223, bf16[2176,2048]{1,0:T(8,128)(2,1)} %get-tuple-element.128.grads_hbm, bf16[4,2048,512]{2,1,0:T(8,128)(2,1)} %pad_maximum_fusion.weight_ref.weight_hbm), custom_call_target="tpu_custom_call" | custom-call | tf_op jit(solution)/shard_map/merge_return/pallas_call | solution.py:1336
  997.8 3.5 convert_reduce_fusion
  1001.3 3.9 fusion.21
  1007.0 10.7 fusion.4
  1018.4 27.6 %all-to-all-start = ((f32[32,1,896]{2,1,0:T(1,128)}), f32[32,1,896]{2,1,0:T(1,128)S(1)}, u32[]{:S(2)}, u32[]{:S(2)}) async-start(f32[32,1,896]{2,1,0:T(1,128)} %copy.72), calls=%async_computation.4 | async-start | bytes 229376 | tf_op jit(solution)/shard_map/all_to_all | solution.py:2078
  1046.0 3.2 fusion.20
  1049.2 38.4 %swap_blocks.1 = bf16[8,64,2048]{2,1,0:T(8,128)(2,1)} custom-call(bf16[8,64,2048]{2,1,0:T(8,128)(2,1)} %bitcast.227), custom_call_target="tpu_custom_call" | custom-call | tf_op jit(solution)/shard_map/swap_blocks/pallas_call | solution.py:1624
  1087.6 4.9 convert_element_type.155
  1095.3 2.5 convert_element_type.153
  (243 shorter events, 69.4 us)
Async XLA Ops:
  7.2 24.9 %copy-start = (f32[2048,8]{0,1:T(8,128)S(1)}, f32[2048,8]{0,1:T(8,128)}, u32[]{:S(2)}) copy-start(f32[2048,8]{0,1:T(8,128)} %param.24) | copy-start | bytes 196612
  7.2 54.5 %all-gather.7.cloned.1.call-start = ((), (), s32[]{:S(2)}) async-start(), calls=%async_computation.6 | async-start | bytes 4718592 | tf_op jit(solution)/shard_map/all_gather | solution.py:1818
  11.7 137.4 %all-gather.11.cloned.1.call-start = ((), (), s32[]{:S(2)}) async-start(), calls=%async_computation.13 | async-start | bytes 10027008 | tf_op jit(solution)/shard_map/all_gather | solution.py:1819
  12.1 17.3 %copy-start.34 = (f32[272]{0:T(512)}, f32[272]{0:T(512)S(1)}, u32[]{:S(2)}) copy-start(f32[272]{0:T(512)S(1)} %add_rsqrt_fusion.1) | copy-start | bytes 3268
  12.1 22.3 %copy-start.37 = (s32[1,13]{1,0:T(1,128)S(1)}, s32[1,13]{1,0:T(1,128)}, u32[]{:S(2)}) copy-start(s32[1,13]{1,0:T(1,128)} %param.20) | copy-start | bytes 160
  13.5 438.9 %all-gather.9.cloned.1.call-start = ((), (), s32[]{:S(2)}) async-start(), calls=%async_computation.7 | async-start | bytes 14417920 | tf_op jit(solution)/shard_map/all_gather | solution.py:1879
  32.0 12.0 %copy-start.27 = (pred[2,8,272]{2,1,0:T(8,128)(4,1)}, pred[2,8,272]{2,1,0:T(8,128)(4,1)S(1)}, u32[]{:S(2)}) copy-start(pred[2,8,272]{2,1,0:T(8,128)(4,1)S(1)} %iota_compare_fusion.13) | copy-start | bytes 13060
  40.0 3.8 copy-start.38
  43.9 237.7 %copy-start.32 = (f32[272,2]{0,1:T(2,128)}, f32[272,2]{0,1:T(2,128)S(1)}, u32[]{:S(2)}) copy-start(f32[272,2]{0,1:T(2,128)S(1)} %broadcast_divide_fusion.1) | copy-start | bytes 6532
  63.5 47.8 %collective-permute-start.1 = (bf16[2048,512]{1,0:T(8,128)(2,1)S(1)}, bf16[2048,512]{1,0:T(8,128)(2,1)S(1)}, u32[]{:S(2)}, u32[]{:S(2)}) collective-permute-start(bf16[2048,512]{1,0:T(8,128)(2,1)S(1)} %bitcast.215), channel_id=1, source_target_pairs={{0,16},{8,24},{16,0},{24,8},{1,17},{9,25},{17,1},{25,9},{2,18},{10... | collective-permute-start | bytes 6291464 | tf_op jit(solution)/shard_map/ppermute | solution.py:1766
  65.1 48.9 %collective-permute-start = (bf16[2048,512]{1,0:T(8,128)(2,1)S(1)}, bf16[2048,512]{1,0:T(8,128)(2,1)S(1)}, u32[]{:S(2)}, u32[]{:S(2)}) collective-permute-start(bf16[2048,512]{1,0:T(8,128)(2,1)S(1)} %bitcast.216), channel_id=1, source_target_pairs={{0,8},{8,0},{16,24},{24,16},{1,9},{9,1},{17,25},{25,17},{2,10},{10... | collective-permute-start | bytes 6291464 | tf_op jit(solution)/shard_map/ppermute | solution.py:1766
  111.4 2.6 copy-start.14
  112.5 24.9 %collective-permute-start.2 = (bf16[1024,512]{1,0:T(8,128)(2,1)}, bf16[1024,512]{1,0:T(8,128)(2,1)}, u32[]{:S(2)}, u32[]{:S(2)}) collective-permute-start(bf16[1024,512]{1,0:T(8,128)(2,1)} %slice.152), channel_id=1, source_target_pairs={{0,8},{8,0},{16,24},{24,16},{1,9},{9,1},{17,25},{25,17},{2,10},{10... | collective-permute-start | bytes 3145736 | tf_op jit(solution)/shard_map/ppermute | solution.py:1768
  115.6 24.6 %collective-permute-start.3 = (bf16[1024,512]{1,0:T(8,128)(2,1)}, bf16[1024,512]{1,0:T(8,128)(2,1)}, u32[]{:S(2)}, u32[]{:S(2)}) collective-permute-start(bf16[1024,512]{1,0:T(8,128)(2,1)} %slice.153), channel_id=1, source_target_pairs={{0,16},{8,24},{16,0},{24,8},{1,17},{9,25},{17,1},{25,9},{2,18},{10... | collective-permute-start | bytes 3145736 | tf_op jit(solution)/shard_map/ppermute | solution.py:1768
  119.2 22.7 %copy-start.15 = (bf16[2048,512]{1,0:T(8,128)(2,1)S(1)}, bf16[2048,512]{1,0:T(8,128)(2,1)}, u32[]{:S(2)}) copy-start(bf16[2048,512]{1,0:T(8,128)(2,1)} %copy-done.14) | copy-start | bytes 6291460
  119.2 22.7 %copy-start.17 = (bf16[2048,512]{1,0:T(8,128)(2,1)S(1)}, bf16[2048,512]{1,0:T(8,128)(2,1)}, u32[]{:S(2)}) copy-start(bf16[2048,512]{1,0:T(8,128)(2,1)} %copy-done.16) | copy-start | bytes 6291460
  166.7 27.3 %collective-permute-start.4 = (bf16[704,1024]{1,0:T(8,128)(2,1)}, bf16[704,1024]{1,0:T(8,128)(2,1)S(1)}, u32[]{:S(2)}, u32[]{:S(2)}) collective-permute-start(bf16[704,1024]{1,0:T(8,128)(2,1)} %constant_dynamic-slice_fusion.5), channel_id=1, source_target_pairs={{0,1},{1,0},{2,3},{3,2},{4,5},{5,4},{6,7},{7,6},{8,9},{9,8},{10,11... | collective-permute-start | bytes 4325384 | tf_op jit(solution)/shard_map/ppermute | solution.py:1856
  279.5 386.1 %reduce-scatter.6.cloned.1.call-start = ((), (), s32[]{:S(2)}) async-start(), calls=%async_computation.8 | async-start | bytes 14417920 | tf_op jit(solution)/shard_map/reduce_scatter | solution.py:1950
  440.8 3.9 copy-start.21
  531.6 285.4 %reduce-scatter.8.cloned.1.call-start = ((), (), s32[]{:S(2)}) async-start(), calls=%async_computation.9 | async-start | bytes 14417920 | tf_op jit(solution)/shard_map/reduce_scatter | solution.py:1971
  651.3 249.8 %reduce-scatter.10.cloned.1.call-start = ((), (), s32[]{:S(2)}) async-start(), calls=%async_computation.10 | async-start | bytes 14417920 | tf_op jit(solution)/shard_map/reduce_scatter | solution.py:1991
  651.4 6.9 slice-start
  651.4 6.9 slice-start.1
  655.4 2.9 copy-start.4
  659.4 2.1 copy-start.23
  717.2 279.8 %reduce-scatter.12.cloned.1.call-start = ((), (), s32[]{:S(2)}) async-start(), calls=%async_computation.11 | async-start | bytes 10485760 | tf_op jit(solution)/shard_map/reduce_scatter | solution.py:2028
  726.7 6.9 copy-start.12
  728.2 5.5 collective-permute-start.5
  843.6 3.8 copy-start.40
  843.6 249.0 %reduce-scatter.14.cloned.1.call-start = ((), (), s32[]{:S(2)}) async-start(), calls=%async_computation.12 | async-start | bytes 10485760 | tf_op jit(solution)/shard_map/reduce_scatter | solution.py:2029
  843.7 3.8 collective-permute-start.6
  859.4 3.6 copy-start.33
  859.4 3.7 copy-start.8
  859.4 3.7 copy-start.28
  865.4 6.9 copy-start.18
  868.7 128.1 %collective-permute-start.9 = (bf16[704,512]{1,0:T(8,128)(2,1)}, bf16[704,512]{1,0:T(8,128)(2,1)S(1)}, u32[]{:S(2)}, u32[]{:S(2)}) collective-permute-start(bf16[704,512]{1,0:T(8,128)(2,1)} %get-tuple-element.237), channel_id=1, source_target_pairs={{0,24},{8,16},{16,8},{24,0},{1,25},{9,17},{17,9},{25,1},{2,26},{10... | collective-permute-start | bytes 2162696 | tf_op jit(solution)/shard_map/ppermute | solution.py:2004
  871.8 125.1 %collective-permute-start.8 = (bf16[704,512]{1,0:T(8,128)(2,1)}, bf16[704,512]{1,0:T(8,128)(2,1)S(1)}, u32[]{:S(2)}, u32[]{:S(2)}) collective-permute-start(bf16[704,512]{1,0:T(8,128)(2,1)} %get-tuple-element.238), channel_id=1, source_target_pairs={{0,16},{8,24},{16,0},{24,8},{1,17},{9,25},{17,1},{25,9},{2,18},{10... | collective-permute-start | bytes 2162696 | tf_op jit(solution)/shard_map/ppermute | solution.py:2004
  871.8 3.9 copy-start.19
  871.8 125.1 %collective-permute-start.7 = (bf16[704,512]{1,0:T(8,128)(2,1)}, bf16[704,512]{1,0:T(8,128)(2,1)S(1)}, u32[]{:S(2)}, u32[]{:S(2)}) collective-permute-start(bf16[704,512]{1,0:T(8,128)(2,1)} %get-tuple-element.239), channel_id=1, source_target_pairs={{0,8},{8,0},{16,24},{24,16},{1,9},{9,1},{17,25},{25,17},{2,10},{10... | collective-permute-start | bytes 2162696 | tf_op jit(solution)/shard_map/ppermute | solution.py:2004
  872.3 6.7 slice-start.2
  875.7 4.8 slice-start.3
  875.7 5.2 copy-start.41
  997.7 3.5 copy-start.2
  997.7 3.5 copy-start.31
  997.8 3.5 copy-start.35
  1007.0 39.0 %copy-start.6 = (f32[272,2048]{1,0:T(8,128)S(1)}, f32[272,2048]{1,0:T(8,128)}, u32[]{:S(2)}) copy-start(f32[272,2048]{1,0:T(8,128)} %copy-done.5) | copy-start | bytes 6684676
  1018.4 74.1 %all-to-all-start = ((f32[32,1,896]{2,1,0:T(1,128)}), f32[32,1,896]{2,1,0:T(1,128)S(1)}, u32[]{:S(2)}, u32[]{:S(2)}) async-start(f32[32,1,896]{2,1,0:T(1,128)} %copy.72), calls=%async_computation.4 | async-start | bytes 229376 | tf_op jit(solution)/shard_map/all_to_all | solution.py:2078
  1087.6 5.6 copy-start.11
  (17 other events, 24.7 us)
Sparse Core Ops, SparseCore 0:
  11.8 49.8 all-gather.6
  63.9 85.0 all-gather.10
  279.6 131.1 all-gather.8
  531.8 111.1 reduce-scatter.5
  651.4 114.1 reduce-scatter.7
  768.6 132.4 reduce-scatter.9
  904.1 90.7 reduce-scatter.11
  998.3 87.6 reduce-scatter.13
